TPU v7x, 256 devices: a whole 4x4x8 slice. The times are simulated.
256 devices in a mesh: rep: 32 (over y, z_lo, x), tp: 8 (over z_hi, core).
Axes of the slice: x: 4, y: 4, z: 8 (z_hi: 4, z_lo: 2; z = z_hi * 2 + z_lo), core: 2. Of those that a mesh axis runs over, the one named last changes fastest.
Arguments:
- tokens: bfloat16 [4096, 4096], P('rep'), may hold values from -6 to 6
- targets: bfloat16 [4096, 4096], P('rep'), may hold values from -6 to 6
- frozen_in_matrix: bfloat16 [4096, 8192], P('rep', 'tp'), may hold values from -6 to 6
- base_out: bfloat16 [8192, 4096], P('tp', 'rep'), may hold values from -6 to 6
- factor_down: bfloat16 [32, 16, 4096], P('rep'), may hold values from -6 to 6
- factor_up: bfloat16 [32, 16, 8192], P('rep', None, 'tp'), may hold values from -0.75 to 0.75
Outputs:
- merged: float32 [4096, 8192], P('rep', 'tp')
- new_down: float32 [32, 16, 4096], P('rep')
- new_up: float32 [32, 16, 8192], P('rep', None, 'tp')
All inputs are finite; a program needn't handle non-finite values.
Results may differ from a plain program's by a relative error of at most 0.014.
The roundings to bfloat16 on the way count: a program that leaves them out, or rounds other values in their place, can miss the bound.
Values may be sent and summed in bfloat16 or wider, within the bound.
No kernel may reach another device: no remote copies, remote signals or barrier semaphores. Data moves between devices by JAX's collectives and lax.ppermute only.
A program may use at most 128 MiB of HBM per device.

v0:
```python
import jax
import jax.numpy as jnp
from jax import lax
from jax.sharding import Mesh
from jax.sharding import PartitionSpec as P

MODEL_WIDTH = 4096
FF = 8192
REP = ("rep_0", "rep_1", "rep_2")


adapter_scale = 2.0
rate_down = 25.0
rate_up = 0.75


def laid_out(tiles, dim):
    tiles = jnp.moveaxis(tiles, 0, dim)
    dims = tiles.shape
    return tiles.reshape(*dims[:dim], dims[dim] * dims[dim + 1], *dims[dim + 2 :])


def gather_in_order(value, axes, turns):
    tiles = value[None]
    for k in turns:
        tiles = lax.all_gather(tiles, axes[k], axis=0, tiled=True)
    held = [lax.axis_size(axes[k]) for k in reversed(turns)]
    tiles = tiles.reshape(*held, *value.shape)
    turned = sorted(range(len(turns)), key=lambda place: turns[len(turns) - 1 - place])
    return tiles.transpose(*turned, *range(len(turns), tiles.ndim)).reshape(-1, *value.shape)


def whole_of(value, axes, turns, dim):
    return laid_out(gather_in_order(value, axes, turns), dim)


def split_up(value, dim, devices):
    before, after = (value.shape[:dim], value.shape[dim + 1 :])
    return jnp.moveaxis(value.reshape(*before, devices, -1, *after), dim, 0)


def summed_on_arrival(value, axis, dim):
    tiles = split_up(value, dim, lax.axis_size(axis))
    arrived = lax.all_to_all(tiles, axis, split_axis=0, concat_axis=0, tiled=True)
    return arrived.sum(axis=0)


def from_everyone(value, axis):
    devices = lax.axis_size(axis)
    return lax.all_to_all(
        jnp.broadcast_to(value[None], (devices, *value.shape)), axis, 0, 0, tiled=True
    )


def gathered_copies(value, axis, dim):
    return laid_out(from_everyone(value, axis), dim)


def taken_together(value, axis):
    return from_everyone(value, axis).astype(jnp.float32).sum(axis=0)


def shards(tokens, targets, frozen_in_matrix, base_out, factor_down, factor_up):
    tok_count = tokens.shape[0]
    factor_a = factor_down[0]
    second_factor = factor_up[0]
    projection_result = jnp.einsum(
        "td,rd->tr", tokens, factor_a, preferred_element_type=jnp.float32
    ).astype(jnp.bfloat16)
    leading_item = jnp.dot(
        tokens,
        lax.all_gather(frozen_in_matrix, REP, axis=0, tiled=True),
        preferred_element_type=jnp.float32,
    )
    preact = (
        leading_item
        + adapter_scale
        * jnp.dot(projection_result, second_factor, preferred_element_type=jnp.float32)
    ) * MODEL_WIDTH ** (-0.5)
    hidden = jnp.maximum(preact, 0.0).astype(jnp.bfloat16)
    whole_out = whole_of(base_out, REP, (1, 0, 2), 1)
    partial_value = jnp.dot(hidden, whole_out, preferred_element_type=jnp.float32)
    scaled = partial_value * FF ** (-0.5)
    share = summed_on_arrival(scaled, "tp", 0)
    share_rows = share.shape[0]
    row_begin = lax.axis_index("tp") * share_rows
    my_targets = lax.dynamic_slice_in_dim(targets, row_begin, share_rows, 0)
    grad_share = ((share - my_targets.astype(jnp.float32)) / tok_count).astype(jnp.bfloat16)
    out_grad = gathered_copies(grad_share, "tp", 0)
    hid_full = jnp.einsum("td,fd->tf", out_grad, whole_out, preferred_element_type=jnp.float32)
    hidden_gradient = jnp.where(preact > 0, hid_full * FF ** (-0.5), 0.0).astype(jnp.bfloat16)
    up_gradient = (
        adapter_scale
        * MODEL_WIDTH ** (-0.5)
        * jnp.einsum(
            "tr,tf->rf", projection_result, hidden_gradient, preferred_element_type=jnp.float32
        )
    )
    back_local = jnp.einsum(
        "tf,rf->tr", hidden_gradient, second_factor, preferred_element_type=jnp.float32
    )
    tokens_wide = tokens.astype(jnp.float32)
    replica_gradient = jnp.dot(back_local.T, tokens_wide, precision=lax.Precision.HIGHEST)
    down_gradient = (
        adapter_scale
        * MODEL_WIDTH ** (-0.5)
        * taken_together(replica_gradient.astype(jnp.bfloat16), "tp").astype(jnp.float32)
    )
    new_a = factor_a.astype(jnp.float32) - rate_down * down_gradient
    new_b = second_factor.astype(jnp.float32) - rate_up * up_gradient
    up_transport = new_b.astype(jnp.bfloat16)[None]
    down_transport = new_a.astype(jnp.bfloat16)[None]
    all_ups = gathered_copies(up_transport, REP, 0)
    row_count = frozen_in_matrix.shape[0]
    my_downs = lax.all_to_all(down_transport, REP, split_axis=2, concat_axis=0, tiled=True)
    replica_list = lax.axis_size(REP)
    stacked_down = my_downs.reshape(replica_list * my_downs.shape[1], row_count)
    stacked_up = all_ups.reshape(replica_list * all_ups.shape[1], all_ups.shape[2])
    weight_delta = jnp.einsum(
        "kd,kf->df", stacked_down, stacked_up, preferred_element_type=jnp.float32
    )
    merged = frozen_in_matrix.astype(jnp.float32) + adapter_scale / replica_list * weight_delta
    return (merged, new_a[None], new_b[None])


def solution(mesh):
    split = Mesh(mesh.devices.reshape(4, 2, 4, mesh.shape["tp"]), ("rep_0", "rep_1", "rep_2", "tp"))
    in_specs = (
        P(REP, None),
        P(REP, None),
        P(REP, "tp"),
        P("tp", REP),
        P(REP, None, None),
        P(REP, None, "tp"),
    )
    out_specs = (P(REP, "tp"), P(REP, None, None), P(REP, None, "tp"))
    return jax.shard_map(
        shards, mesh=split, in_specs=in_specs, out_specs=out_specs, check_vma=False
    )
```

profile of v0, /device:TPU:2, one launch (start us, length us, event | category | flops | bytes accessed | tf_op | source)
XLA Modules:
  0.0 523.4 jit_solution(6009717544488256002)
XLA Ops:
  7.2 0.0 copy-start
  7.2 0.0 all-gather.7.cloned.1.call-start
  7.2 11.0 %all-gather = bf16[2048,128]{1,0:T(8,128)(2,1)} all-gather(bf16[1024,128]{1,0:T(8,128)(2,1)} %param.9), channel_id=2, replica_groups=mesh['rep_0'=4,'rep_1'=2,'rep_2'=4,'tp'=8] {'rep_1'}, dimensions={0}, use_global_device_ids=true | all-gather | bytes 786432 | tf_op jit(solution)/shard_map/all_gather | solution.py:26
  18.2 0.0 all-gather.7.cloned.1.call-update
  18.2 0.0 all-gather.9.cloned.1.call-start
  18.3 35.6 %all-gather.7.cloned.1.call-done = bf16[8,1024,128]{2,1,0:T(8,128)(2,1)} async-done(((bf16[2,1024,128]{2,1,0:T(8,128)(2,1)}), bf16[8,1024,128]{2,1,0:T(8,128)(2,1)}) %all-gather.7.cloned.1.call-update) | async-done | bytes 2097168 | tf_op jit(solution)/shard_map/all_gather | solution.py:26
  53.9 0.0 all-gather.9.cloned.1.call-update
  53.9 0.0 all-gather.5.cloned.1.call-start
  53.9 0.7 all-gather.5.cloned.1.call-update
  54.6 0.0 copy-done
  54.6 1.3 convolution_convert_fusion.1
  55.9 85.5 %all-gather.9.cloned.1.call-done = bf16[32,1024,128]{2,1,0:T(8,128)(2,1)} async-done(((bf16[8,1024,128]{2,1,0:T(8,128)(2,1)}), bf16[32,1024,128]{2,1,0:T(8,128)(2,1)}) %all-gather.9.cloned.1.call-update) | async-done | bytes 8388624 | tf_op jit(solution)/shard_map/all_gather | solution.py:26
  141.4 7.5 %copy.18 = bf16[4,2,4,1024,128]{4,3,2,1,0:T(8,128)(2,1)} copy(bf16[4,2,4,1024,128]{4,3,1,0,2:T(8,128)(2,1)} %bitcast.62) | data formatting | bytes 16777216 | tf_op jit(solution)/shard_map/transpose | solution.py:30
  148.9 11.6 %copy.19 = bf16[1024,32,128]{0,2,1:T(8,128)(2,1)} copy(bf16[1024,32,128]{2,0,1:T(8,128)(2,1)} %bitcast.61) | data formatting | bytes 16777216 | tf_op jit(solution)/shard_map/transpose | solution.py:18
  160.5 153.7 %all-gather.5.cloned.1.call-done = bf16[4096,1024]{1,0:T(8,128)(2,1)} async-done(((bf16[128,1024]{1,0:T(8,128)(2,1)}), bf16[4096,1024]{1,0:T(8,128)(2,1)}) %all-gather.5.cloned.1.call-update) | async-done | bytes 8388624 | tf_op jit(solution)/shard_map/all_gather | solution.py:72
  314.2 4.8 fusion.17
  319.0 0.0 copy-done.4
  319.0 0.2 fusion.3
  319.3 0.0 copy-start.2
  319.3 0.7 copy-done.1
  320.0 4.2 convolution_multiply_fusion
  324.2 0.0 copy-done.2
  324.2 6.5 %all-to-all-start = ((f32[8,16,4096]{2,1,0:T(8,128)}), f32[8,16,4096]{2,1,0:T(8,128)S(1)}, u32[]{:S(2)}, u32[]{:S(2)}) async-start(f32[8,16,4096]{2,1,0:T(8,128)} %bitcast.65), calls=%async_computation | async-start | bytes 4194304 | tf_op jit(solution)/shard_map/all_to_all | solution.py:44
  330.7 45.3 %all-to-all-done = f32[8,16,4096]{2,1,0:T(8,128)S(1)} async-done(((f32[8,16,4096]{2,1,0:T(8,128)}), f32[8,16,4096]{2,1,0:T(8,128)S(1)}, u32[]{:S(2)}, u32[]{:S(2)}) %all-to-all-start) | async-done | bytes 2097184 | tf_op jit(solution)/shard_map/all_to_all | solution.py:44
  376.0 0.1 reduce_sum.18
  376.1 0.9 multiply_convert_fusion
  377.1 0.1 broadcast_in_dim.13
  377.2 32.1 %all_to_all.35 = bf16[8,16,4096]{2,1,0:T(8,128)(2,1)S(1)} all-to-all(bf16[8,16,4096]{2,1,0:T(8,128)(2,1)S(1)} %broadcast_in_dim.13), channel_id=1, replica_groups=mesh['rep_0'=4,'rep_1'=2,'rep_2'=4,'tp'=8] {'tp'}, dimensions={0} | all-to-all | bytes 2097152 | tf_op jit(solution)/shard_map/all_to_all | solution.py:50
  409.3 4.8 fusion.5
  414.2 0.2 fusion.11
  414.3 0.5 convolution_convert_fusion
  414.9 0.1 broadcast_in_dim.14
  415.0 32.0 %all_to_all.36 = bf16[8,16,4096]{2,1,0:T(8,128)(2,1)S(1)} all-to-all(bf16[8,16,4096]{2,1,0:T(8,128)(2,1)S(1)} %broadcast_in_dim.14), channel_id=1, replica_groups=mesh['rep_0'=4,'rep_1'=2,'rep_2'=4,'tp'=8] {'tp'}, dimensions={0} | all-to-all | bytes 2097152 | tf_op jit(solution)/shard_map/all_to_all | solution.py:50
  447.0 0.1 convert_reduce_fusion
  447.1 0.7 fusion.15
  447.9 2.7 copy.20
  450.5 0.5 broadcast.26
  451.0 23.4 %reduce = bf16[4096,16]{1,0:T(8,128)(2,1)} reduce(bf16[4096,1,16]{2,1,0:T(2,128)(2,1)S(1)} %bitcast.63, bf16[]{:T(256)} %broadcast.26), dimensions={1}, to_apply=%bitcast.42.reduce_sub_computation | reduce | bytes 262146
  474.4 3.1 reshape.53
  477.5 7.7 %all-to-all-start.3 = ((bf16[32,2,1024]{2,1,0:T(2,128)(2,1)}), bf16[32,2,1024]{2,1,0:T(2,128)(2,1)S(1)}, u32[]{:S(2)}, u32[]{:S(2)}) async-start(bf16[32,2,1024]{2,1,0:T(2,128)(2,1)} %reshape.53), calls=%async_computation.3 | async-start | bytes 262144 | tf_op jit(solution)/shard_map/all_to_all | solution.py:115
  485.2 1.5 fusion.16
  486.8 6.1 %all-to-all-done.3 = bf16[32,2,1024]{2,1,0:T(2,128)(2,1)S(1)} async-done(((bf16[32,2,1024]{2,1,0:T(2,128)(2,1)}), bf16[32,2,1024]{2,1,0:T(2,128)(2,1)S(1)}, u32[]{:S(2)}, u32[]{:S(2)}) %all-to-all-start.3) | async-done | bytes 131104 | tf_op jit(solution)/shard_map/all_to_all | solution.py:115
  492.8 1.1 broadcast_in_dim.15
  494.0 5.6 %all-to-all-start.4 = ((bf16[32,1,16,1024]{3,2,1,0:T(8,128)(2,1)}), bf16[32,1,16,1024]{3,2,1,0:T(8,128)(2,1)}, u32[]{:S(2)}, u32[]{:S(2)}) async-start(bf16[32,1,16,1024]{3,2,1,0:T(8,128)(2,1)} %broadcast_in_dim.15), calls=%async_computation.4 | async-start | bytes 2097152 | tf_op jit(solution)/shard_map/all_to_all | solution.py:50
  499.5 1.8 reshape.54
  501.4 2.0 copy.21
  503.4 10.7 %all-to-all-done.4 = bf16[32,1,16,1024]{3,2,1,0:T(8,128)(2,1)} async-done(((bf16[32,1,16,1024]{3,2,1,0:T(8,128)(2,1)}), bf16[32,1,16,1024]{3,2,1,0:T(8,128)(2,1)}, u32[]{:S(2)}, u32[]{:S(2)}) %all-to-all-start.4) | async-done | bytes 1048608 | tf_op jit(solution)/shard_map/all_to_all | solution.py:50
  514.1 2.8 fusion.1
  (5 shorter events, 0.0 us)
Async XLA Ops:
  7.2 47.4 %copy-start = (bf16[128,4096]{1,0:T(8,128)(2,1)S(1)}, bf16[128,4096]{1,0:T(8,128)(2,1)}, u32[]{:S(2)}) copy-start(bf16[128,4096]{1,0:T(8,128)(2,1)} %param.6) | copy-start | bytes 3145732
  7.2 46.7 %all-gather.7.cloned.1.call-start = ((), (), s32[]{:S(2)}) async-start(), calls=%async_computation.6 | async-start | bytes 2621440 | tf_op jit(solution)/shard_map/all_gather | solution.py:26
  18.2 123.2 %all-gather.9.cloned.1.call-start = ((), (), s32[]{:S(2)}) async-start(), calls=%async_computation.7 | async-start | bytes 10485760 | tf_op jit(solution)/shard_map/all_gather | solution.py:26
  53.9 260.4 %all-gather.5.cloned.1.call-start = ((), (), s32[]{:S(2)}) async-start(), calls=%async_computation.5 | async-start | bytes 8650752 | tf_op jit(solution)/shard_map/all_gather | solution.py:72
  160.5 158.5 %copy-start.4 = (bf16[1,16,1024]{2,1,0:T(8,128)(2,1)S(1)}, bf16[1,16,1024]{2,1,0:T(8,128)(2,1)}, u32[]{:S(2)}) copy-start(bf16[1,16,1024]{2,1,0:T(8,128)(2,1)} %param.11) | copy-start | bytes 98308
  314.2 5.8 %copy-start.1 = (bf16[1024,32,128]{0,2,1:T(8,128)(2,1)S(1)}, bf16[1024,32,128]{0,2,1:T(8,128)(2,1)}, u32[]{:S(2)}) copy-start(bf16[1024,32,128]{0,2,1:T(8,128)(2,1)} %copy.19) | copy-start | bytes 25165828
  319.3 4.9 copy-start.2
  324.2 51.8 %all-to-all-start = ((f32[8,16,4096]{2,1,0:T(8,128)}), f32[8,16,4096]{2,1,0:T(8,128)S(1)}, u32[]{:S(2)}, u32[]{:S(2)}) async-start(f32[8,16,4096]{2,1,0:T(8,128)} %bitcast.65), calls=%async_computation | async-start | bytes 4194304 | tf_op jit(solution)/shard_map/all_to_all | solution.py:44
  409.3 37.8 %copy-start.3 = (bf16[1,16,4096]{2,1,0:T(8,128)(2,1)S(1)}, bf16[1,16,4096]{2,1,0:T(8,128)(2,1)}, u32[]{:S(2)}) copy-start(bf16[1,16,4096]{2,1,0:T(8,128)(2,1)} %param.10) | copy-start | bytes 393220
  477.5 15.3 %all-to-all-start.3 = ((bf16[32,2,1024]{2,1,0:T(2,128)(2,1)}), bf16[32,2,1024]{2,1,0:T(2,128)(2,1)S(1)}, u32[]{:S(2)}, u32[]{:S(2)}) async-start(bf16[32,2,1024]{2,1,0:T(2,128)(2,1)} %reshape.53), calls=%async_computation.3 | async-start | bytes 262144 | tf_op jit(solution)/shard_map/all_to_all | solution.py:115
  494.0 20.1 %all-to-all-start.4 = ((bf16[32,1,16,1024]{3,2,1,0:T(8,128)(2,1)}), bf16[32,1,16,1024]{3,2,1,0:T(8,128)(2,1)}, u32[]{:S(2)}, u32[]{:S(2)}) async-start(bf16[32,1,16,1024]{3,2,1,0:T(8,128)(2,1)} %broadcast_in_dim.15), calls=%async_computation.4 | async-start | bytes 2097152 | tf_op jit(solution)/shard_map/all_to_all | solution.py:50
Sparse Core Ops, SparseCore 0:
  18.4 35.4 all-gather.6
  55.7 85.6 all-gather.8
  143.2 171.0 all-gather.4
where the time goes:
time: 524 us; the launch traced here: 523 us
  waiting for transfers between devices  338 us (65%)
  blocking collectives  75.1 us (14%)
  local copies, waits for them, and re-layouts  31.3 us (6%)
  other arithmetic  25.3 us (5%)
  matrix products  20.4 us (4%)
  starting transfers between devices  19.9 us (4%)
  between operations  13.9 us (3%)
    all_gather x1, waiting for transfers between devices, shards(): lax.all_gather(frozen_in_matrix, REP, axis=0, tiled=True)  154 us
    all_gather x2, waiting for transfers between devices, gather_in_order(): tiles = lax.all_gather(tiles, axes[k], axis=0, tiled=True)  121 us
    all_to_all x2, blocking collectives, from_everyone(): lax.all_to_all(jnp.broadcast_to(value[None], (devices, *value.shape)), ax...  64.1 us
    all_to_all x1, waiting for transfers between devices, summed_on_arrival(): lax.all_to_all(tiles, axis, split_axis=0, concat_axis=0, tiled=True)  45.3 us
    unnamed x1, other arithmetic  23.4 us
    transpose x1, local copies, waits for them, and re-layouts, laid_out(): tiles = jnp.moveaxis(tiles, 0, dim)  11.6 us
    all_gather x1, blocking collectives, gather_in_order(): tiles = lax.all_gather(tiles, axes[k], axis=0, tiled=True)  11 us
    all_to_all x1, waiting for transfers between devices, from_everyone(): lax.all_to_all(jnp.broadcast_to(value[None], (devices, *value.shape)), ax...  10.7 us
  transfers between devices with their start and end apart: 6, of which 6 were waited for; matrix products, arithmetic and copies ran while one was open for 5% of the time, Pallas kernels for 0%

commit v1 on v0

v1 whole, which is shorter than its diff:
```python
import jax
import jax.numpy as jnp
from jax import lax
from jax.experimental import pallas as pl
from jax.experimental.pallas import tpu as pltpu
from jax.sharding import Mesh
from jax.sharding import PartitionSpec as P

MODEL_WIDTH = 4096
FF = 8192
TOK = 128
RANK = 16
ROWS = 16
BLOCK = 128
HID = 512
SIDE = MODEL_WIDTH // 2
REP = ("y", "l", "x")
Z = ("l", "h")
ADAPTER_SCALE = 2.0
RATE_DOWN = 25.0
RATE_UP = 0.75
BF16 = jnp.bfloat16
F32 = jnp.float32

RING = (0, -1, 1, 2)


def dot(a, b):
    return jnp.dot(a, b, preferred_element_type=F32)


def dot_nt(a, b):
    return lax.dot_general(a, b, (((1,), (1,)), ((), ())), preferred_element_type=F32)


def dot_tn(a, b):
    return lax.dot_general(a, b, (((0,), (0,)), ((), ())), preferred_element_type=F32)


def shift(value, axis, by):
    n = lax.axis_size(axis)
    return lax.ppermute(value, axis, [(i, (i + by) % n) for i in range(n)])


def partner(value, axis):
    return lax.ppermute(value, axis, [(0, 1), (1, 0)])


def near_z(value):
    def place(z):
        return (z % 2) * 4 + (z % 8) // 2

    return lax.ppermute(
        value, Z, [(place(z), place(z + 1 if z % 2 else z - 1)) for z in range(8)]
    )


def call(kernel, out_shape, *args, scratch=(), name):
    vmem = pl.BlockSpec(memory_space=pltpu.VMEM)
    many = isinstance(out_shape, tuple)
    return pl.pallas_call(
        kernel,
        out_shape=out_shape,
        in_specs=[vmem] * len(args),
        out_specs=(vmem,) * len(out_shape) if many else vmem,
        scratch_shapes=scratch,
        name=name,
    )(*args)


def shape(*dims, dtype=BF16):
    return jax.ShapeDtypeStruct(dims, dtype)


def lanes(start, size):
    return pl.ds(pl.multiple_of(start, BLOCK), size)


def token_row(i):
    h, c = lax.axis_index("h"), lax.axis_index("c")
    j, e = (i // 2) % 4, i % 2
    return pl.multiple_of((((h + j) % 4) * 2 + (c + e) % 2) * ROWS, ROWS)


def column(dy, side, dx):
    y, x = lax.axis_index("y"), lax.axis_index("x")
    return (((y + dy) % 4) * 8 + side * 4 + (x + dx) % 4) * BLOCK


def split_kernel(w_in_ref, w_out_ref, own_ref, send_ref):
    l = lax.axis_index("l")
    for ref, side in ((own_ref, l), (send_ref, 1 - l)):
        ref[:TOK] = w_in_ref[:, lanes(side * HID, HID)]
        ref[TOK:] = w_out_ref[lanes(side * HID, HID), :].T


def arrange_kernel(own_ref, oth_ref, pown_ref, poth_ref, x_ref, p_ref):
    l = lax.axis_index("l")
    cols = [column(dy, l, dx) for dy in RING for dx in RING]
    cols += [column(dy, 1 - l, dx) for dx in RING for dy in RING]
    p_ref[...] = jnp.zeros_like(p_ref)
    for i in range(16):
        src, psrc = (own_ref, pown_ref) if i < 8 else (oth_ref, poth_ref)
        row = token_row(i)
        lane = 0 if i < 8 else RANK
        p_ref[i * ROWS : (i + 1) * ROWS, lane : lane + RANK] = psrc[pl.ds(row, ROWS), :]
        for j in range(32):
            x_ref[i * ROWS : (i + 1) * ROWS, j * BLOCK : (j + 1) * BLOCK] = src[
                pl.ds(row, ROWS), lanes(cols[j], BLOCK)
            ]


def hidden_kernel(x_ref, p_ref, b_ref, *refs):
    pieces, (hidden_ref, mask_ref) = refs[:8], refs[8:]
    total = ADAPTER_SCALE * dot(p_ref[...], b_ref[...])
    for k, piece in enumerate(pieces):
        total = total + dot(x_ref[:, k * HID : (k + 1) * HID], piece[...])
    preact = total * MODEL_WIDTH ** (-0.5)
    hidden_ref[...] = jnp.maximum(preact, 0.0).astype(BF16)
    mask_ref[...] = jnp.where(preact > 0, 1.0, 0.0).astype(BF16)


def output_kernel(hidden_ref, *refs):
    pieces, (keep_ref, send_ref) = refs[:8], refs[8:]
    l = lax.axis_index("l")
    for k, piece in enumerate(pieces):
        part = dot_nt(hidden_ref[...], piece[...]).reshape(8, 2, ROWS, HID)
        if k < 4:
            places = [(l * SIDE + k * HID, 0, HID)]
        else:
            places = [
                ((1 - l) * SIDE + (j * 4 + k - 4) * BLOCK, j * BLOCK, BLOCK) for j in range(4)
            ]
        for to, begin, size in places:
            keep_ref[:, :, lanes(to, size)] = part[:, 0, :, begin : begin + size]
            send_ref[:, :, lanes(to, size)] = part[:, 1, :, begin : begin + size].astype(BF16)


def finish_kernel(mine_ref, r1_ref, r2_ref, r3_ref, targets_ref, out_ref):
    h, c = lax.axis_index("h"), lax.axis_index("c")
    row = pl.multiple_of((h * 2 + c) * ROWS, ROWS)
    j = 0
    for side in range(2):
        for dy in RING:
            for dx in RING:
                here = slice(j * BLOCK, (j + 1) * BLOCK)
                total = mine_ref[:, here]
                for ref in (r1_ref, r2_ref, r3_ref):
                    total = total + ref[:, here].astype(F32)
                target = targets_ref[pl.ds(row, ROWS), lanes(column(dy, side, dx), BLOCK)]
                grad = (total * FF ** (-0.5) - target.astype(F32)) / TOK
                out_ref[:, here] = grad.astype(BF16)
                j += 1


def backward_kernel(q_ref, qc_ref, left_ref, leftc_ref, right_ref, rightc_ref, mask_ref, p_own_ref,
                    p_oth_ref, b_ref, *refs):
    pieces, (up_own_ref, up_oth_ref, wire_ref, back_ref, grad_ref, own_ref, oth_ref) = refs[:8], refs[8:]
    l = lax.axis_index("l")
    for i in range(16):
        j, e = (i // 2) % 4, i % 2
        here = slice(i * ROWS, (i + 1) * ROWS)
        if i < 8:
            grad_ref[here, :] = (q_ref, qc_ref)[e][j]
        else:
            turned = (j + 1 + 2 * l) % 4
            grad_ref[here, :SIDE] = (left_ref, leftc_ref)[e][j]
            grad_ref[here, SIDE:] = (right_ref, rightc_ref)[e][turned]
    total = None
    for k, piece in enumerate(pieces):
        if k < 4:
            part = grad_ref[:, lanes(l * SIDE + k * HID, HID)]
        else:
            part = jnp.concatenate(
                [
                    grad_ref[:, lanes((1 - l) * SIDE + (j * 4 + k - 4) * BLOCK, BLOCK)]
                    for j in range(4)
                ],
                axis=1,
            )
        term = dot(part, piece[...])
        total = term if total is None else total + term
    total = jnp.where(mask_ref[...].astype(F32) > 0, total * FF ** (-0.5), 0.0).astype(BF16)
    for i in range(16):
        ref = own_ref if i < 8 else oth_ref
        ref[pl.ds(token_row(i), ROWS), :] = total[i * ROWS : (i + 1) * ROWS]
    scale = ADAPTER_SCALE * MODEL_WIDTH ** (-0.5)
    sides = (
        (l, own_ref, p_own_ref, up_own_ref, b_ref[:RANK]),
        (1 - l, oth_ref, p_oth_ref, up_oth_ref, b_ref[RANK:]),
    )
    for side, hid_ref, p_ref, up_ref, b in sides:
        up = b.astype(F32) - RATE_UP * (scale * dot(p_ref[...], hid_ref[...]))
        up_ref[...] = up
        wire_ref[side] = up.astype(BF16)
        back = dot_nt(b, hid_ref[...])
        for k in range(8):
            back_ref[side * 8 + k] = back


def down_kernel(back_ref, x_ref, a_ref, new_ref, wire_ref):
    terms = [back_ref[k] for k in range(16)]
    while len(terms) > 1:
        terms = [terms[k] + terms[k + 1] for k in range(0, len(terms), 2)]
    rest = terms[0]
    parts = []
    for _ in range(3):
        parts.append(rest.astype(BF16))
        rest = rest - parts[-1].astype(F32)
    stacked = jnp.concatenate(parts, axis=0)
    scale = ADAPTER_SCALE * MODEL_WIDTH ** (-0.5)
    for k in range(8):
        here = slice(k * HID, (k + 1) * HID)
        grad = dot(stacked, x_ref[:, here])
        grad = grad[:RANK] + grad[RANK : 2 * RANK] + grad[2 * RANK :]
        new = a_ref[:, here].astype(F32) - RATE_DOWN * (scale * grad)
        new_ref[:, here] = new
        for j in range(4):
            wire_ref[k * 4 + j] = new[:, j * BLOCK : (j + 1) * BLOCK].astype(BF16)


def merge_kernel(down_ref, up_ref, w_ref, out_ref, d_ref, u_ref):
    for y in range(4):
        for x in range(4):
            for l in range(2):
                at = ((y * 4 + x) * 2 + l) * RANK
                d_ref[at : at + RANK, :] = down_ref[y * 8 + l * 4 + x]
    for side in range(2):
        for y in range(4):
            for x in range(4):
                for l in range(2):
                    at = ((y * 4 + x) * 2 + l) * RANK
                    u_ref[at : at + RANK, :] = up_ref[y * 8 + side * 4 + x, l]
        here = slice(side * HID, (side + 1) * HID)
        delta = dot_tn(d_ref[...], u_ref[...])
        out_ref[:, here] = w_ref[:, here].astype(F32) + ADAPTER_SCALE / 32 * delta


def ring(value, axis, upward):
    below = shift(value, axis, 1)
    above = shift(value, axis, -1)
    far = shift(below, axis, 1) if upward else shift(above, axis, -1)
    return [value, below, above, far]


def ring_direct(value, axis):
    return [value, shift(value, axis, 1), shift(value, axis, -1), shift(value, axis, 2)]


def shards(tokens, targets, w_in, w_out, factor_down, factor_up):
    l = lax.axis_index("l")
    a = factor_down[0]
    b = factor_up[0]

    w_own, w_send = call(
        split_kernel, (shape(2 * TOK, HID), shape(2 * TOK, HID)), w_in, w_out, name="split"
    )
    line_own = ring_direct(w_own, "x")
    w_oth = partner(w_send, "l")
    line_oth = ring_direct(w_oth, "y")

    projected = dot_nt(tokens, a).astype(BF16)
    p_own = projected.T
    b_own = jnp.where(l == 0, b[:, :HID], b[:, HID:])
    b_send = jnp.where(l == 0, b[:, HID:], b[:, :HID])
    arrived = partner(jnp.concatenate([b_send, p_own], axis=1), "l")
    b_oth, p_oth = arrived[:, :HID], arrived[:, HID:]
    b_both = jnp.concatenate([b_own, b_oth], axis=0)
    tokens_oth = near_z(tokens)

    def joined(line, begin):
        return jnp.concatenate([block[begin : begin + TOK] for block in line], axis=0)

    in_pieces = ring(joined(line_own, 0), "y", True) + ring(joined(line_oth, 0), "x", True)
    out_pieces = ring(joined(line_own, TOK), "y", False) + ring(joined(line_oth, TOK), "x", False)

    x_rel, p_rel = call(
        arrange_kernel,
        (shape(2 * TOK, MODEL_WIDTH), shape(2 * TOK, 2 * RANK)),
        tokens, tokens_oth, projected, p_oth.T,
        name="arrange",
    )
    hidden, mask = call(
        hidden_kernel,
        (shape(2 * TOK, HID), shape(2 * TOK, HID)),
        x_rel, p_rel, b_both, *in_pieces,
        name="hidden",
    )
    keep, send = call(
        output_kernel,
        (shape(8, ROWS, MODEL_WIDTH, dtype=F32), shape(8, ROWS, MODEL_WIDTH)),
        hidden, *out_pieces,
        name="output",
    )

    summed = keep + partner(send, "c").astype(F32)
    away = summed[4:].astype(BF16)
    left = partner(away[:, :, :SIDE], "l")
    right = away[:, :, SIDE:]
    right = near_z(jnp.where(l == 0, jnp.roll(right, 1, 0), jnp.roll(right, -1, 0)))
    summed = summed[:4] + jnp.concatenate([left, right], axis=2).astype(F32)
    steps = [shift(summed[j].astype(BF16), "h", j) for j in (1, 2, 3)]
    grad_rows = call(
        finish_kernel, shape(ROWS, MODEL_WIDTH), summed[0], *steps, targets, name="finish"
    )

    q = jnp.stack([grad_rows] + [shift(grad_rows, "h", -j) for j in (1, 2, 3)])
    left = partner(q[:, :, :SIDE], "l")
    right = near_z(q[:, :, SIDE:])
    q_far, left_far, right_far = partner(q, "c"), partner(left, "c"), partner(right, "c")

    up_own, up_oth, up_wire, back = call(
        backward_kernel,
        (
            shape(RANK, HID, dtype=F32),
            shape(RANK, HID, dtype=F32),
            shape(2, RANK, HID),
            shape(16, RANK, TOK, dtype=F32),
        ),
        q, q_far, left, left_far, right, right_far, mask, p_own, p_oth, b_both, *out_pieces,
        scratch=[
            pltpu.VMEM((2 * TOK, MODEL_WIDTH), BF16),
            pltpu.VMEM((TOK, HID), BF16),
            pltpu.VMEM((TOK, HID), BF16),
        ],
        name="backward",
    )
    ups = lax.all_gather(up_wire, REP, axis=0)
    back = lax.all_to_all(back, ("l", "h", "c"), 0, 0, tiled=True)
    new_a, wire = call(
        down_kernel,
        (shape(RANK, MODEL_WIDTH, dtype=F32), shape(32, RANK, BLOCK)),
        back, tokens, a,
        name="down",
    )
    downs = lax.all_to_all(wire, REP, 0, 0, tiled=True)
    up_arrived = partner(up_oth, "l")
    new_b = jnp.where(
        l == 0,
        jnp.concatenate([up_own, up_arrived], axis=1),
        jnp.concatenate([up_arrived, up_own], axis=1),
    )
    merged = call(
        merge_kernel,
        shape(TOK, 2 * HID, dtype=F32),
        downs, ups, w_in,
        scratch=[pltpu.VMEM((32 * RANK, BLOCK), BF16), pltpu.VMEM((32 * RANK, HID), BF16)],
        name="merge",
    )
    return merged, new_a[None], new_b[None]


def solution(mesh):
    split = Mesh(mesh.devices.reshape(4, 2, 4, 4, 2), ("y", "l", "x", "h", "c"))
    tp = ("h", "c")
    in_specs = (
        P(REP, None),
        P(REP, None),
        P(REP, tp),
        P(tp, REP),
        P(REP, None, None),
        P(REP, None, tp),
    )
    out_specs = (P(REP, tp), P(REP, None, None), P(REP, None, tp))
    return jax.shard_map(
        shards, mesh=split, in_specs=in_specs, out_specs=out_specs, check_vma=False
    )
```

time: 524 us -> 333 us (0.64)
  waiting for transfers between devices: 338 us -> 196 us
  blocking collectives: 75.1 us -> 13.7 us
  starting transfers between devices: 19.9 us -> 66.5 us
  Pallas kernels: 0 us -> 27.8 us
  local copies, waits for them, and re-layouts: 31.3 us -> 7.37 us
  other arithmetic: 25.3 us -> 5.34 us
  matrix products: 20.4 us -> 1.6 us
    all_gather x3 -> x1, waiting for transfers between devices: 275 us -> 119 us  [shards(): ups = lax.all_gather(up_wire, REP, axis=0)]
    ppermute x0 -> x36, waiting for transfers between devices: none -> 74.9 us  [the longest x24 50.1 us: shift(): return lax.ppermute(value, axis, [(i, (i + by) % n) for i in range(n)])]
    all_to_all x3 -> x1, waiting for transfers between devices: 62.1 us -> 2.25 us  [shards(): downs = lax.all_to_all(wire, REP, 0, 0, tiled=True)]
    ppermute x0 -> x36, starting transfers between devices: none -> 58.1 us  [the longest x24 40.4 us: shift(): return lax.ppermute(value, axis, [(i, (i + by) % n) for i in range(n)])]
    all_to_all x2 -> x1, blocking collectives: 64.1 us -> 13.7 us  [shards(): back = lax.all_to_all(back, ('l', 'h', 'c'), 0, 0, tiled=True)]
    pallas_call x0 -> x8, Pallas kernels: none -> 27.8 us  [call(): pl.pallas_call(kernel, out_shape=out_shape, in_specs=[vmem] * len(args),...]
    unnamed x1 -> x0, other arithmetic: 23.4 us -> none
    dot_general x9 -> x1, matrix products: 20.4 us -> 1.6 us  [dot_nt(): lax.dot_general(a, b, (((1,), (1,)), ((), ())), preferred_element_type=F32)]
  transfers between devices with their start and end apart: 6 -> 38, of which waited for: 6 -> 22; matrix products, arithmetic and copies ran while one was open for 5% -> 2% of each run, Pallas kernels for 0% -> 3%
where the time goes in v1:
time: 333 us
  waiting for transfers between devices  196 us (59%)
  starting transfers between devices  66.5 us (20%)
  Pallas kernels  27.8 us (8%)
  between operations  14.5 us (4%)
  blocking collectives  13.7 us (4%)
  local copies, waits for them, and re-layouts  7.37 us (2%)
  other arithmetic  5.34 us (2%)
    all_gather x1, waiting for transfers between devices, shards(): ups = lax.all_gather(up_wire, REP, axis=0)  119 us
    ppermute x24, waiting for transfers between devices, shift(): return lax.ppermute(value, axis, [(i, (i + by) % n) for i in range(n)])  50.1 us
    ppermute x24, starting transfers between devices, shift(): return lax.ppermute(value, axis, [(i, (i + by) % n) for i in range(n)])  40.4 us
    pallas_call x8, Pallas kernels, call(): pl.pallas_call(kernel, out_shape=out_shape, in_specs=[vmem] * len(args),...  27.8 us
    ppermute x9, waiting for transfers between devices, partner(): return lax.ppermute(value, axis, [(0, 1), (1, 0)])  16.9 us
    all_to_all x1, blocking collectives, shards(): back = lax.all_to_all(back, ('l', 'h', 'c'), 0, 0, tiled=True)  13.7 us
    ppermute x3, starting transfers between devices, near_z(): lax.ppermute(value, Z, [(place(z), place(z + 1 if z % 2 else z - 1)) for...  12.6 us
    all_to_all x1, starting transfers between devices, shards(): downs = lax.all_to_all(wire, REP, 0, 0, tiled=True)  8.32 us
  transfers between devices with their start and end apart: 38, of which 22 were waited for; matrix products, arithmetic and copies ran while one was open for 2% of the time, Pallas kernels for 3%

profile of v1, /device:TPU:2, one launch (start us, length us, event | category | flops | bytes accessed | tf_op | source)
XLA Modules:
  0.0 332.5 jit_solution(576391111089798818)
XLA Ops:
  7.2 1.9 split.1
  11.4 2.1 collective-permute-start.4
  13.5 1.7 collective-permute-start.8
  15.2 4.9 %collective-permute-start = (bf16[128,4096]{1,0:T(8,128)(2,1)}, bf16[128,4096]{1,0:T(8,128)(2,1)}, u32[]{:S(2)}, u32[]{:S(2)}) collective-permute-start(bf16[128,4096]{1,0:T(8,128)(2,1)} %x_ref.1), channel_id=1, source_target_pairs={{0,38},{32,2},{2,32},{34,4},{4,34},{36,6},{6,36},{38,0},{1,39},{33... | collective-permute-start | bytes 3145736 | tf_op jit(solution)/shard_map/ppermute | solution.py:53
  22.9 2.0 collective-permute-done.4
  24.9 1.7 collective-permute-start.5
  26.6 1.7 collective-permute-start.6
  28.6 2.9 collective-permute-start.10
  31.5 12.9 %collective-permute-done.9 = bf16[256,512]{1,0:T(8,128)(2,1)S(1)} collective-permute-done((bf16[256,512]{1,0:T(8,128)(2,1)S(1)}, bf16[256,512]{1,0:T(8,128)(2,1)S(1)}, u32[]{:S(2)}, u32[]{:S(2)}) %collective-permute-start.9) | collective-permute-done | bytes 262176 | tf_op jit(solution)/shard_map/ppermute | solution.py:42
  44.5 1.9 collective-permute-start.11
  47.6 4.8 %collective-permute-done.11 = bf16[256,512]{1,0:T(8,128)(2,1)S(1)} collective-permute-done((bf16[256,512]{1,0:T(8,128)(2,1)S(1)}, bf16[256,512]{1,0:T(8,128)(2,1)S(1)}, u32[]{:S(2)}, u32[]{:S(2)}) %collective-permute-start.11) | collective-permute-done | bytes 262176 | tf_op jit(solution)/shard_map/ppermute | solution.py:42
  52.3 1.8 collective-permute-start.1
  54.2 1.9 collective-permute-done.1
  56.2 2.0 collective-permute-start.13
  58.2 2.4 collective-permute-start.19
  60.7 1.8 collective-permute-done.16.refs_2_
  63.8 2.5 collective-permute-done.12.refs_5_
  66.6 4.5 %collective-permute-done.13.refs_6_ = bf16[512,512]{1,0:T(8,128)(2,1)S(1)} collective-permute-done((bf16[512,512]{1,0:T(8,128)(2,1)S(1)}, bf16[512,512]{1,0:T(8,128)(2,1)S(1)}, u32[]{:S(2)}, u32[]{:S(2)}) %collective-permute-start.13) | collective-permute-done | bytes 524320 | tf_op jit(solution)/shard_map/ppermute | solution.py:42
  72.1 1.8 collective-permute-start.18
  73.9 3.4 %collective-permute-done.19.refs_6_ = bf16[512,512]{1,0:T(8,128)(2,1)S(1)} collective-permute-done((bf16[512,512]{1,0:T(8,128)(2,1)S(1)}, bf16[512,512]{1,0:T(8,128)(2,1)S(1)}, u32[]{:S(2)}, u32[]{:S(2)}) %collective-permute-start.19) | collective-permute-done | bytes 524320 | tf_op jit(solution)/shard_map/ppermute | solution.py:42
  77.3 1.9 collective-permute-start.17
  84.4 3.6 %arrange.1 = (bf16[256,4096]{1,0:T(8,128)(2,1)}, bf16[256,32]{1,0:T(8,128)(2,1)}) custom-call(bf16[128,4096]{1,0:T(8,128)(2,1)} %x_ref.1, bf16[128,4096]{1,0:T(8,128)(2,1)} %collective-permute-done.oth_ref, bf16[128,16]{1,0:T(8,128)(2,1)} %copy.11.pown_ref, bf16[128,16]{1,0:T(8,128)(2,1)} %copy.12.poth_ref), custom_call_target="tpu_custom_call" | custom-call | tf_op jit(solution)/shard_map/arrange/pallas_call | solution.py:61
  88.0 5.0 %hidden.1 = (bf16[256,512]{1,0:T(8,128)(2,1)}, bf16[256,512]{1,0:T(8,128)(2,1)}) custom-call(bf16[256,4096]{1,0:T(8,128)(2,1)} %get-tuple-element.17.x_ref, bf16[256,32]{1,0:T(8,128)(2,1)} %get-tuple-element.18.p_ref, bf16[32,512]{1,0:T(8,128)(2,1)} %pad_maximum_fusion.5.b_ref, bf16[512,512]{1,0:T(8,128)(2,1)} %copy-done.7, bf16[512,512]{1,0:T(8,128)(2,1)} %copy-done.9, ...), custom_call_target="tpu_custom_call" | custom-call | tf_op jit(solution)/shard_map/hidden/pallas_call | solution.py:61
  93.9 5.2 %output.1 = (f32[8,16,4096]{2,1,0:T(8,128)}, bf16[8,16,4096]{2,1,0:T(8,128)(2,1)}) custom-call(bf16[256,512]{1,0:T(8,128)(2,1)} %get-tuple-element.21.hidden_ref, bf16[512,512]{1,0:T(8,128)(2,1)} %copy-done, bf16[512,512]{1,0:T(8,128)(2,1)} %copy-done.5, bf16[512,512]{1,0:T(8,128)(2,1)} %copy-done.3, bf16[512,512]{1,0:T(8,128)(2,1)} %collective-permute-done.17.refs_3_, ...), custom_call_target="tpu_custom_call" | custom-call | tf_op jit(solution)/shard_map/output/pallas_call | solution.py:61
  99.1 2.9 collective-permute-done.21
  102.0 1.9 fusion.2
  104.0 5.8 %collective-permute-start.23 = (bf16[4,16,2048]{2,1,0:T(8,128)(2,1)S(1)}, bf16[4,16,2048]{2,1,0:T(8,128)(2,1)S(1)}, u32[]{:S(2)}, u32[]{:S(2)}) collective-permute-start(bf16[4,16,2048]{2,1,0:T(8,128)(2,1)S(1)} %maximum_select_fusion), channel_id=1, source_target_pairs={{0,38},{32,2},{2,32},{34,4},{4,34},{36,6},{6,36},{38,0},{1,39},{33... | collective-permute-start | bytes 786440 | tf_op jit(solution)/shard_map/ppermute | solution.py:53
  109.8 6.6 %collective-permute-done.23 = bf16[4,16,2048]{2,1,0:T(8,128)(2,1)S(1)} collective-permute-done((bf16[4,16,2048]{2,1,0:T(8,128)(2,1)S(1)}, bf16[4,16,2048]{2,1,0:T(8,128)(2,1)S(1)}, u32[]{:S(2)}, u32[]{:S(2)}) %collective-permute-start.23) | collective-permute-done | bytes 262176 | tf_op jit(solution)/shard_map/ppermute | solution.py:53
  118.9 3.1 collective-permute-start.25
  122.0 3.1 collective-permute-start.26
  125.8 5.7 %collective-permute-done.24.r1_ref = bf16[16,4096]{1,0:T(8,128)(2,1)S(1)} collective-permute-done((bf16[16,4096]{1,0:T(8,128)(2,1)S(1)}, bf16[16,4096]{1,0:T(8,128)(2,1)S(1)}, u32[]{:S(2)}, u32[]{:S(2)}) %collective-permute-start.24) | collective-permute-done | bytes 131104 | tf_op jit(solution)/shard_map/ppermute | solution.py:42
  131.6 3.6 %collective-permute-done.26.r3_ref = bf16[16,4096]{1,0:T(8,128)(2,1)S(1)} collective-permute-done((bf16[16,4096]{1,0:T(8,128)(2,1)S(1)}, bf16[16,4096]{1,0:T(8,128)(2,1)S(1)}, u32[]{:S(2)}, u32[]{:S(2)}) %collective-permute-start.26) | collective-permute-done | bytes 131104 | tf_op jit(solution)/shard_map/ppermute | solution.py:42
  135.9 2.3 finish.1
  138.1 2.8 collective-permute-start.28
  140.9 2.4 collective-permute-start.29
  143.3 1.8 collective-permute-start.27
  145.1 5.4 %collective-permute-done.28 = bf16[16,4096]{1,0:T(8,128)(2,1)S(1)} collective-permute-done((bf16[16,4096]{1,0:T(8,128)(2,1)}, bf16[16,4096]{1,0:T(8,128)(2,1)S(1)}, u32[]{:S(2)}, u32[]{:S(2)}) %collective-permute-start.28) | collective-permute-done | bytes 131104 | tf_op jit(solution)/shard_map/ppermute | solution.py:42
  150.5 3.5 %collective-permute-done.29 = bf16[16,4096]{1,0:T(8,128)(2,1)S(1)} collective-permute-done((bf16[16,4096]{1,0:T(8,128)(2,1)}, bf16[16,4096]{1,0:T(8,128)(2,1)S(1)}, u32[]{:S(2)}, u32[]{:S(2)}) %collective-permute-start.29) | collective-permute-done | bytes 131104 | tf_op jit(solution)/shard_map/ppermute | solution.py:42
  155.1 1.9 collective-permute-start.33
  157.0 6.4 %collective-permute-done.31.left_ref = bf16[4,16,2048]{2,1,0:T(8,128)(2,1)S(1)} collective-permute-done((bf16[4,16,2048]{2,1,0:T(8,128)(2,1)S(1)}, bf16[4,16,2048]{2,1,0:T(8,128)(2,1)S(1)}, u32[]{:S(2)}, u32[]{:S(2)}) %collective-permute-start.31) | collective-permute-done | bytes 262176 | tf_op jit(solution)/shard_map/ppermute | solution.py:46
  167.0 5.2 %backward.1 = (f32[16,512]{1,0:T(8,128)}, f32[16,512]{1,0:T(8,128)}, bf16[2,16,512]{2,1,0:T(8,128)(2,1)}, f32[16,16,128]{2,1,0:T(8,128)}) custom-call(bf16[4,16,4096]{2,1,0:T(8,128)(2,1)} %copy-done.2, bf16[4,16,4096]{2,1,0:T(8,128)(2,1)} %copy-done.13, bf16[4,16,2048]{2,1,0:T(8,128)(2,1)} %copy-done.15, bf16[4,16,2048]{2,1,0:T(8,128)(2,1)} %copy-done.17, ...), custom_call_target="tpu_custom_call" | custom-call | tf_op jit(solution)/shard_map/backward/pallas_call | solution.py:61
  172.3 13.7 %all_to_all.10.back_ref = f32[16,16,128]{2,1,0:T(8,128)} all-to-all(f32[16,16,128]{2,1,0:T(8,128)} %get-tuple-element.25), channel_id=1, replica_groups=mesh['y'=4,'l'=2,'x'=4,'h'=4,'c'=2] {'l','h','c'}, dimensions={0} | all-to-all | bytes 262144 | tf_op jit(solution)/shard_map/all_to_all | solution.py:329
  185.9 2.3 down.1
  188.2 8.3 %all-to-all-start.1 = ((bf16[32,16,128]{2,1,0:T(8,128)(2,1)}), bf16[32,16,128]{2,1,0:T(8,128)(2,1)S(1)}, u32[]{:S(2)}, u32[]{:S(2)}) async-start(bf16[32,16,128]{2,1,0:T(8,128)(2,1)} %get-tuple-element.26), calls=%async_computation.1 | async-start | bytes 262144 | tf_op jit(solution)/shard_map/all_to_all | solution.py:336
  198.1 2.8 collective-permute-done.35
  202.4 2.3 all-to-all-done.1.down_ref
  204.7 118.6 %all-gather.3.cloned.1.call-done = bf16[64,16,512]{2,1,0:T(8,128)(2,1)} async-done(((bf16[2,16,512]{2,1,0:T(8,128)(2,1)}), bf16[64,16,512]{2,1,0:T(8,128)(2,1)}) %all-gather.3.cloned.1.call-update) | async-done | bytes 1048592 | tf_op jit(solution)/shard_map/all_gather | solution.py:328
  323.2 2.4 merge.1
  (117 shorter events, 27.4 us)
Async XLA Ops:
  7.2 316.1 %all-gather.3.cloned.1.call-start = ((), (), s32[]{:S(2)}) async-start(), calls=%async_computation.2 | async-start | bytes 1081344 | tf_op jit(solution)/shard_map/all_gather | solution.py:328
  9.1 13.7 %collective-permute-start.2 = (bf16[256,512]{1,0:T(8,128)(2,1)}, bf16[256,512]{1,0:T(8,128)(2,1)S(1)}, u32[]{:S(2)}, u32[]{:S(2)}) collective-permute-start(bf16[256,512]{1,0:T(8,128)(2,1)} %get-tuple-element.19), channel_id=1, source_target_pairs={{0,8},{8,16},{16,24},{24,0},{1,9},{9,17},{17,25},{25,1},{2,10},{10... | collective-permute-start | bytes 786440 | tf_op jit(solution)/shard_map/ppermute | solution.py:42
  10.6 12.2 %collective-permute-start.3 = (bf16[256,512]{1,0:T(8,128)(2,1)}, bf16[256,512]{1,0:T(8,128)(2,1)S(1)}, u32[]{:S(2)}, u32[]{:S(2)}) collective-permute-start(bf16[256,512]{1,0:T(8,128)(2,1)} %get-tuple-element.19), channel_id=1, source_target_pairs={{0,24},{8,0},{16,8},{24,16},{1,25},{9,1},{17,9},{25,17},{2,26},{10... | collective-permute-start | bytes 786440 | tf_op jit(solution)/shard_map/ppermute | solution.py:42
  11.4 13.4 %collective-permute-start.4 = (bf16[256,512]{1,0:T(8,128)(2,1)}, bf16[256,512]{1,0:T(8,128)(2,1)S(1)}, u32[]{:S(2)}, u32[]{:S(2)}) collective-permute-start(bf16[256,512]{1,0:T(8,128)(2,1)} %get-tuple-element.19), channel_id=1, source_target_pairs={{0,16},{8,24},{16,0},{24,8},{1,17},{9,25},{17,1},{25,9},{2,18},{10... | collective-permute-start | bytes 786440 | tf_op jit(solution)/shard_map/ppermute | solution.py:42
  13.5 14.8 %collective-permute-start.8 = (bf16[256,512]{1,0:T(8,128)(2,1)}, bf16[256,512]{1,0:T(8,128)(2,1)S(1)}, u32[]{:S(2)}, u32[]{:S(2)}) collective-permute-start(bf16[256,512]{1,0:T(8,128)(2,1)} %get-tuple-element.20), channel_id=1, source_target_pairs={{0,32},{32,0},{1,33},{33,1},{2,34},{34,2},{3,35},{35,3},{4,36},{36... | collective-permute-start | bytes 786440 | tf_op jit(solution)/shard_map/ppermute | solution.py:46
  15.2 56.9 %collective-permute-start = (bf16[128,4096]{1,0:T(8,128)(2,1)}, bf16[128,4096]{1,0:T(8,128)(2,1)}, u32[]{:S(2)}, u32[]{:S(2)}) collective-permute-start(bf16[128,4096]{1,0:T(8,128)(2,1)} %x_ref.1), channel_id=1, source_target_pairs={{0,38},{32,2},{2,32},{34,4},{4,34},{36,6},{6,36},{38,0},{1,39},{33... | collective-permute-start | bytes 3145736 | tf_op jit(solution)/shard_map/ppermute | solution.py:53
  22.7 59.0 %copy-start.22 = (bf16[128,16]{0,1:T(8,128)(2,1)}, bf16[128,16]{0,1:T(8,128)(2,1)S(1)}, u32[]{:S(2)}) copy-start(bf16[128,16]{0,1:T(8,128)(2,1)S(1)} %convolution_convert_fusion) | copy-start | bytes 12292
  24.9 29.3 %copy-start.7 = (bf16[512,512]{1,0:T(8,128)(2,1)}, bf16[512,512]{1,0:T(8,128)(2,1)S(1)}, u32[]{:S(2)}) copy-start(bf16[512,512]{1,0:T(8,128)(2,1)S(1)} %pad_maximum_fusion.refs_0_) | copy-start | bytes 1572868
  24.9 31.3 %collective-permute-start.5 = (bf16[512,512]{1,0:T(8,128)(2,1)S(1)}, bf16[512,512]{1,0:T(8,128)(2,1)S(1)}, u32[]{:S(2)}, u32[]{:S(2)}) collective-permute-start(bf16[512,512]{1,0:T(8,128)(2,1)S(1)} %pad_maximum_fusion.refs_0_), channel_id=1, source_target_pairs={{0,64},{64,128},{128,192},{192,0},{1,65},{65,129},{129,193},{193,1... | collective-permute-start | bytes 1572872 | tf_op jit(solution)/shard_map/ppermute | solution.py:42
  26.6 31.6 %collective-permute-start.6 = (bf16[512,512]{1,0:T(8,128)(2,1)S(1)}, bf16[512,512]{1,0:T(8,128)(2,1)S(1)}, u32[]{:S(2)}, u32[]{:S(2)}) collective-permute-start(bf16[512,512]{1,0:T(8,128)(2,1)S(1)} %pad_maximum_fusion.refs_0_), channel_id=1, source_target_pairs={{0,192},{64,0},{128,64},{192,128},{1,193},{65,1},{129,65},{193,129... | collective-permute-start | bytes 1572872 | tf_op jit(solution)/shard_map/ppermute | solution.py:42
  28.2 16.2 %collective-permute-start.9 = (bf16[256,512]{1,0:T(8,128)(2,1)S(1)}, bf16[256,512]{1,0:T(8,128)(2,1)S(1)}, u32[]{:S(2)}, u32[]{:S(2)}) collective-permute-start(bf16[256,512]{1,0:T(8,128)(2,1)S(1)} %collective-permute-done.8), channel_id=1, source_target_pairs={{0,64},{64,128},{128,192},{192,0},{1,65},{65,129},{129,193},{193,1... | collective-permute-start | bytes 786440 | tf_op jit(solution)/shard_map/ppermute | solution.py:42
  28.6 17.8 %collective-permute-start.10 = (bf16[256,512]{1,0:T(8,128)(2,1)S(1)}, bf16[256,512]{1,0:T(8,128)(2,1)S(1)}, u32[]{:S(2)}, u32[]{:S(2)}) collective-permute-start(bf16[256,512]{1,0:T(8,128)(2,1)S(1)} %collective-permute-done.8), channel_id=1, source_target_pairs={{0,192},{64,0},{128,64},{192,128},{1,193},{65,1},{129,65},{193,129... | collective-permute-start | bytes 786440 | tf_op jit(solution)/shard_map/ppermute | solution.py:42
  31.5 56.4 %copy-start = (bf16[512,512]{1,0:T(8,128)(2,1)}, bf16[512,512]{1,0:T(8,128)(2,1)S(1)}, u32[]{:S(2)}) copy-start(bf16[512,512]{1,0:T(8,128)(2,1)S(1)} %pad_maximum_fusion.2.refs_0_) | copy-start | bytes 1572868
  44.5 7.9 %collective-permute-start.11 = (bf16[256,512]{1,0:T(8,128)(2,1)S(1)}, bf16[256,512]{1,0:T(8,128)(2,1)S(1)}, u32[]{:S(2)}, u32[]{:S(2)}) collective-permute-start(bf16[256,512]{1,0:T(8,128)(2,1)S(1)} %collective-permute-done.8), channel_id=1, source_target_pairs={{0,128},{64,192},{128,0},{192,64},{1,129},{65,193},{129,1},{193,65... | collective-permute-start | bytes 786440 | tf_op jit(solution)/shard_map/ppermute | solution.py:42
  46.4 16.0 %collective-permute-start.16 = (bf16[512,512]{1,0:T(8,128)(2,1)S(1)}, bf16[512,512]{1,0:T(8,128)(2,1)S(1)}, u32[]{:S(2)}, u32[]{:S(2)}) collective-permute-start(bf16[512,512]{1,0:T(8,128)(2,1)S(1)} %pad_maximum_fusion.2.refs_0_), channel_id=1, source_target_pairs={{0,192},{64,0},{128,64},{192,128},{1,193},{65,1},{129,65},{193,129... | collective-permute-start | bytes 1572872 | tf_op jit(solution)/shard_map/ppermute | solution.py:42
  52.3 3.8 %collective-permute-start.1 = (bf16[16,640]{1,0:T(8,128)(2,1)S(1)}, bf16[16,640]{1,0:T(8,128)(2,1)S(1)}, u32[]{:S(2)}, u32[]{:S(2)}) collective-permute-start(bf16[16,640]{1,0:T(8,128)(2,1)S(1)} %pad_maximum_fusion.6), channel_id=1, source_target_pairs={{0,32},{32,0},{1,33},{33,1},{2,34},{34,2},{3,35},{35,3},{4,36},{36... | collective-permute-start | bytes 61448 | tf_op jit(solution)/shard_map/ppermute | solution.py:46
  54.2 25.0 %copy-start.8 = (bf16[512,512]{1,0:T(8,128)(2,1)}, bf16[512,512]{1,0:T(8,128)(2,1)S(1)}, u32[]{:S(2)}) copy-start(bf16[512,512]{1,0:T(8,128)(2,1)S(1)} %pad_maximum_fusion.1.refs_4_) | copy-start | bytes 1572868
  56.1 10.2 %collective-permute-start.12 = (bf16[512,512]{1,0:T(8,128)(2,1)S(1)}, bf16[512,512]{1,0:T(8,128)(2,1)}, u32[]{:S(2)}, u32[]{:S(2)}) collective-permute-start(bf16[512,512]{1,0:T(8,128)(2,1)S(1)} %pad_maximum_fusion.1.refs_4_), channel_id=1, source_target_pairs={{0,8},{8,16},{16,24},{24,0},{1,9},{9,17},{17,25},{25,1},{2,10},{10... | collective-permute-start | bytes 1572872 | tf_op jit(solution)/shard_map/ppermute | solution.py:42
  56.2 23.0 %copy-start.9 = (bf16[512,512]{1,0:T(8,128)(2,1)}, bf16[512,512]{1,0:T(8,128)(2,1)S(1)}, u32[]{:S(2)}) copy-start(bf16[512,512]{1,0:T(8,128)(2,1)S(1)} %collective-permute-done.5.refs_1_) | copy-start | bytes 1572868
  56.2 14.9 %collective-permute-start.13 = (bf16[512,512]{1,0:T(8,128)(2,1)S(1)}, bf16[512,512]{1,0:T(8,128)(2,1)S(1)}, u32[]{:S(2)}, u32[]{:S(2)}) collective-permute-start(bf16[512,512]{1,0:T(8,128)(2,1)S(1)} %pad_maximum_fusion.1.refs_4_), channel_id=1, source_target_pairs={{0,24},{8,0},{16,8},{24,16},{1,25},{9,1},{17,9},{25,17},{2,26},{10... | collective-permute-start | bytes 1572872 | tf_op jit(solution)/shard_map/ppermute | solution.py:42
  58.2 34.7 %copy-start.1 = (bf16[512,512]{1,0:T(8,128)(2,1)}, bf16[512,512]{1,0:T(8,128)(2,1)S(1)}, u32[]{:S(2)}) copy-start(bf16[512,512]{1,0:T(8,128)(2,1)S(1)} %pad_maximum_fusion.3.refs_4_) | copy-start | bytes 1572868
  58.2 21.0 %copy-start.10 = (bf16[512,512]{1,0:T(8,128)(2,1)}, bf16[512,512]{1,0:T(8,128)(2,1)S(1)}, u32[]{:S(2)}) copy-start(bf16[512,512]{1,0:T(8,128)(2,1)S(1)} %collective-permute-done.6.refs_2_) | copy-start | bytes 1572868
  58.2 19.1 %collective-permute-start.19 = (bf16[512,512]{1,0:T(8,128)(2,1)S(1)}, bf16[512,512]{1,0:T(8,128)(2,1)S(1)}, u32[]{:S(2)}, u32[]{:S(2)}) collective-permute-start(bf16[512,512]{1,0:T(8,128)(2,1)S(1)} %pad_maximum_fusion.3.refs_4_), channel_id=1, source_target_pairs={{0,24},{8,0},{16,8},{24,16},{1,25},{9,1},{17,9},{25,17},{2,26},{10... | collective-permute-start | bytes 1572872 | tf_op jit(solution)/shard_map/ppermute | solution.py:42
  62.5 30.5 %copy-start.3 = (bf16[512,512]{1,0:T(8,128)(2,1)}, bf16[512,512]{1,0:T(8,128)(2,1)S(1)}, u32[]{:S(2)}) copy-start(bf16[512,512]{1,0:T(8,128)(2,1)S(1)} %collective-permute-done.16.refs_2_) | copy-start | bytes 1572868
  62.5 16.7 %collective-permute-start.7 = (bf16[512,512]{1,0:T(8,128)(2,1)S(1)}, bf16[512,512]{1,0:T(8,128)(2,1)S(1)}, u32[]{:S(2)}, u32[]{:S(2)}) collective-permute-start(bf16[512,512]{1,0:T(8,128)(2,1)S(1)} %collective-permute-done.5.refs_1_), channel_id=1, source_target_pairs={{0,64},{64,128},{128,192},{192,0},{1,65},{65,129},{129,193},{193,1... | collective-permute-start | bytes 1572872 | tf_op jit(solution)/shard_map/ppermute | solution.py:42
  66.3 21.6 %collective-permute-start.14 = (bf16[512,512]{1,0:T(8,128)(2,1)}, bf16[512,512]{1,0:T(8,128)(2,1)}, u32[]{:S(2)}, u32[]{:S(2)}) collective-permute-start(bf16[512,512]{1,0:T(8,128)(2,1)} %collective-permute-done.12.refs_5_), channel_id=1, source_target_pairs={{0,8},{8,16},{16,24},{24,0},{1,9},{9,17},{17,25},{25,1},{2,10},{10... | collective-permute-start | bytes 1572872 | tf_op jit(solution)/shard_map/ppermute | solution.py:42
  71.1 21.9 %collective-permute-start.15 = (bf16[512,512]{1,0:T(8,128)(2,1)S(1)}, bf16[512,512]{1,0:T(8,128)(2,1)S(1)}, u32[]{:S(2)}, u32[]{:S(2)}) collective-permute-start(bf16[512,512]{1,0:T(8,128)(2,1)S(1)} %pad_maximum_fusion.2.refs_0_), channel_id=1, source_target_pairs={{0,64},{64,128},{128,192},{192,0},{1,65},{65,129},{129,193},{193,1... | collective-permute-start | bytes 1572872 | tf_op jit(solution)/shard_map/ppermute | solution.py:42
  72.1 20.8 %collective-permute-start.18 = (bf16[512,512]{1,0:T(8,128)(2,1)S(1)}, bf16[512,512]{1,0:T(8,128)(2,1)S(1)}, u32[]{:S(2)}, u32[]{:S(2)}) collective-permute-start(bf16[512,512]{1,0:T(8,128)(2,1)S(1)} %pad_maximum_fusion.3.refs_4_), channel_id=1, source_target_pairs={{0,8},{8,16},{16,24},{24,0},{1,9},{9,17},{17,25},{25,1},{2,10},{10... | collective-permute-start | bytes 1572872 | tf_op jit(solution)/shard_map/ppermute | solution.py:42
  77.3 15.6 %copy-start.4 = (bf16[512,512]{1,0:T(8,128)(2,1)}, bf16[512,512]{1,0:T(8,128)(2,1)S(1)}, u32[]{:S(2)}) copy-start(bf16[512,512]{1,0:T(8,128)(2,1)S(1)} %collective-permute-done.19.refs_6_) | copy-start | bytes 1572868
  77.3 15.7 %collective-permute-start.17 = (bf16[512,512]{1,0:T(8,128)(2,1)S(1)}, bf16[512,512]{1,0:T(8,128)(2,1)}, u32[]{:S(2)}, u32[]{:S(2)}) collective-permute-start(bf16[512,512]{1,0:T(8,128)(2,1)S(1)} %collective-permute-done.16.refs_2_), channel_id=1, source_target_pairs={{0,192},{64,0},{128,64},{192,128},{1,193},{65,1},{129,65},{193,129... | collective-permute-start | bytes 1572872 | tf_op jit(solution)/shard_map/ppermute | solution.py:42
  80.1 12.9 %collective-permute-start.20 = (bf16[512,512]{1,0:T(8,128)(2,1)S(1)}, bf16[512,512]{1,0:T(8,128)(2,1)}, u32[]{:S(2)}, u32[]{:S(2)}) collective-permute-start(bf16[512,512]{1,0:T(8,128)(2,1)S(1)} %collective-permute-done.19.refs_6_), channel_id=1, source_target_pairs={{0,24},{8,0},{16,8},{24,16},{1,25},{9,1},{17,9},{25,17},{2,26},{10... | collective-permute-start | bytes 1572872 | tf_op jit(solution)/shard_map/ppermute | solution.py:42
  99.1 2.9 collective-permute-start.21
  104.0 12.4 %collective-permute-start.23 = (bf16[4,16,2048]{2,1,0:T(8,128)(2,1)S(1)}, bf16[4,16,2048]{2,1,0:T(8,128)(2,1)S(1)}, u32[]{:S(2)}, u32[]{:S(2)}) collective-permute-start(bf16[4,16,2048]{2,1,0:T(8,128)(2,1)S(1)} %maximum_select_fusion), channel_id=1, source_target_pairs={{0,38},{32,2},{2,32},{34,4},{4,34},{36,6},{6,36},{38,0},{1,39},{33... | collective-permute-start | bytes 786440 | tf_op jit(solution)/shard_map/ppermute | solution.py:53
  109.8 8.1 %collective-permute-start.22 = (bf16[4,16,2048]{2,1,0:T(8,128)(2,1)S(1)}, bf16[4,16,2048]{2,1,0:T(8,128)(2,1)S(1)}, u32[]{:S(2)}, u32[]{:S(2)}) collective-permute-start(bf16[4,16,2048]{2,1,0:T(8,128)(2,1)S(1)} %slice.168), channel_id=1, source_target_pairs={{0,32},{32,0},{1,33},{33,1},{2,34},{34,2},{3,35},{35,3},{4,36},{36... | collective-permute-start | bytes 786440 | tf_op jit(solution)/shard_map/ppermute | solution.py:46
  118.1 13.5 %collective-permute-start.24 = (bf16[16,4096]{1,0:T(8,128)(2,1)S(1)}, bf16[16,4096]{1,0:T(8,128)(2,1)S(1)}, u32[]{:S(2)}, u32[]{:S(2)}) collective-permute-start(bf16[16,4096]{1,0:T(8,128)(2,1)S(1)} %get-tuple-element.43), channel_id=1, source_target_pairs={{0,2},{2,4},{4,6},{6,0},{1,3},{3,5},{5,7},{7,1},{8,10},{10,12},{12... | collective-permute-start | bytes 393224 | tf_op jit(solution)/shard_map/ppermute | solution.py:42
  118.9 12.7 %collective-permute-start.25 = (bf16[16,4096]{1,0:T(8,128)(2,1)S(1)}, bf16[16,4096]{1,0:T(8,128)(2,1)S(1)}, u32[]{:S(2)}, u32[]{:S(2)}) collective-permute-start(bf16[16,4096]{1,0:T(8,128)(2,1)S(1)} %get-tuple-element.42), channel_id=1, source_target_pairs={{0,4},{2,6},{4,0},{6,2},{1,5},{3,7},{5,1},{7,3},{8,12},{10,14},{12... | collective-permute-start | bytes 393224 | tf_op jit(solution)/shard_map/ppermute | solution.py:42
  122.0 13.2 %collective-permute-start.26 = (bf16[16,4096]{1,0:T(8,128)(2,1)S(1)}, bf16[16,4096]{1,0:T(8,128)(2,1)S(1)}, u32[]{:S(2)}, u32[]{:S(2)}) collective-permute-start(bf16[16,4096]{1,0:T(8,128)(2,1)S(1)} %get-tuple-element.41), channel_id=1, source_target_pairs={{0,6},{2,0},{4,2},{6,4},{1,7},{3,1},{5,3},{7,5},{8,14},{10,8},{12,... | collective-permute-start | bytes 393224 | tf_op jit(solution)/shard_map/ppermute | solution.py:42
  138.1 12.3 %collective-permute-start.28 = (bf16[16,4096]{1,0:T(8,128)(2,1)}, bf16[16,4096]{1,0:T(8,128)(2,1)S(1)}, u32[]{:S(2)}, u32[]{:S(2)}) collective-permute-start(bf16[16,4096]{1,0:T(8,128)(2,1)} %finish.1), channel_id=1, source_target_pairs={{0,4},{2,6},{4,0},{6,2},{1,5},{3,7},{5,1},{7,3},{8,12},{10,14},{12... | collective-permute-start | bytes 393224 | tf_op jit(solution)/shard_map/ppermute | solution.py:42
  140.9 13.0 %collective-permute-start.29 = (bf16[16,4096]{1,0:T(8,128)(2,1)}, bf16[16,4096]{1,0:T(8,128)(2,1)S(1)}, u32[]{:S(2)}, u32[]{:S(2)}) collective-permute-start(bf16[16,4096]{1,0:T(8,128)(2,1)} %finish.1), channel_id=1, source_target_pairs={{0,2},{2,4},{4,6},{6,0},{1,3},{3,5},{5,7},{7,1},{8,10},{10,12},{12... | collective-permute-start | bytes 393224 | tf_op jit(solution)/shard_map/ppermute | solution.py:42
  143.3 10.6 %collective-permute-start.27 = (bf16[16,4096]{1,0:T(8,128)(2,1)}, bf16[16,4096]{1,0:T(8,128)(2,1)S(1)}, u32[]{:S(2)}, u32[]{:S(2)}) collective-permute-start(bf16[16,4096]{1,0:T(8,128)(2,1)} %finish.1), channel_id=1, source_target_pairs={{0,6},{2,0},{4,2},{6,4},{1,7},{3,1},{5,3},{7,5},{8,14},{10,8},{12,... | collective-permute-start | bytes 393224 | tf_op jit(solution)/shard_map/ppermute | solution.py:42
  155.0 8.3 %collective-permute-start.31 = (bf16[4,16,2048]{2,1,0:T(8,128)(2,1)S(1)}, bf16[4,16,2048]{2,1,0:T(8,128)(2,1)S(1)}, u32[]{:S(2)}, u32[]{:S(2)}) collective-permute-start(bf16[4,16,2048]{2,1,0:T(8,128)(2,1)S(1)} %get-tuple-element.40), channel_id=1, source_target_pairs={{0,32},{32,0},{1,33},{33,1},{2,34},{34,2},{3,35},{35,3},{4,36},{36... | collective-permute-start | bytes 786440 | tf_op jit(solution)/shard_map/ppermute | solution.py:46
  155.1 9.5 %collective-permute-start.33 = (bf16[4,16,2048]{2,1,0:T(8,128)(2,1)S(1)}, bf16[4,16,2048]{2,1,0:T(8,128)(2,1)S(1)}, u32[]{:S(2)}, u32[]{:S(2)}) collective-permute-start(bf16[4,16,2048]{2,1,0:T(8,128)(2,1)S(1)} %get-tuple-element.39), channel_id=1, source_target_pairs={{0,38},{32,2},{2,32},{34,4},{4,34},{36,6},{6,36},{38,0},{1,39},{33... | collective-permute-start | bytes 786440 | tf_op jit(solution)/shard_map/ppermute | solution.py:53
  157.0 9.2 %collective-permute-start.30 = (bf16[4,16,4096]{2,1,0:T(8,128)(2,1)S(1)}, bf16[4,16,4096]{2,1,0:T(8,128)(2,1)S(1)}, u32[]{:S(2)}, u32[]{:S(2)}) collective-permute-start(bf16[4,16,4096]{2,1,0:T(8,128)(2,1)S(1)} %pad_maximum_fusion.4.q_ref), channel_id=1, source_target_pairs={{0,1},{1,0},{2,3},{3,2},{4,5},{5,4},{6,7},{7,6},{8,9},{9,8},{10,11... | collective-permute-start | bytes 1572872 | tf_op jit(solution)/shard_map/ppermute | solution.py:46
  163.3 1.5 collective-permute-start.32
  164.6 1.5 collective-permute-start.34
  188.2 16.4 %all-to-all-start.1 = ((bf16[32,16,128]{2,1,0:T(8,128)(2,1)}), bf16[32,16,128]{2,1,0:T(8,128)(2,1)S(1)}, u32[]{:S(2)}, u32[]{:S(2)}) async-start(bf16[32,16,128]{2,1,0:T(8,128)(2,1)} %get-tuple-element.26), calls=%async_computation.1 | async-start | bytes 262144 | tf_op jit(solution)/shard_map/all_to_all | solution.py:336
  196.6 4.4 %collective-permute-start.35 = (f32[16,512]{1,0:T(8,128)}, f32[16,512]{1,0:T(8,128)S(1)}, u32[]{:S(2)}, u32[]{:S(2)}) collective-permute-start(f32[16,512]{1,0:T(8,128)} %get-tuple-element.30), channel_id=1, source_target_pairs={{0,32},{32,0},{1,33},{33,1},{2,34},{34,2},{3,35},{35,3},{4,36},{36... | collective-permute-start | bytes 98312 | tf_op jit(solution)/shard_map/ppermute | solution.py:46
  204.7 118.6 %copy-start.14 = (bf16[32,16,128]{2,1,0:T(8,128)(2,1)}, bf16[32,16,128]{2,1,0:T(8,128)(2,1)S(1)}, u32[]{:S(2)}) copy-start(bf16[32,16,128]{2,1,0:T(8,128)(2,1)S(1)} %all-to-all-done.1.down_ref) | copy-start | bytes 393220
  (14 other events, 52.9 us)
Sparse Core Ops, SparseCore 0:
  172.4 150.8 all-gather.2

commit v2 on v1

--- a/solution.py
+++ b/solution.py
@@ -87,33 +87,57 @@
     return (((y + dy) % 4) * 8 + side * 4 + (x + dx) % 4) * BLOCK
 
 
-def split_kernel(w_in_ref, w_out_ref, own_ref, send_ref):
+def send_kernel(w_in_ref, w_out_ref, b_ref, send_ref):
+    other = (1 - lax.axis_index("l")) * HID
+    send_ref[:TOK] = w_in_ref[:, lanes(other, HID)]
+    send_ref[TOK : 2 * TOK] = w_out_ref[lanes(other, HID), :].T
+    send_ref[2 * TOK :] = b_ref[:, lanes(other, HID)]
+
+
+def own_kernel(w_in_ref, w_out_ref, b_ref, send_ref, in_ref, out_ref, b_own_ref):
+    mine = lax.axis_index("l") * HID
+    in_ref[...] = w_in_ref[:, lanes(mine, HID)]
+    out_ref[...] = w_out_ref[lanes(mine, HID), :].T
+    b_own_ref[...] = b_ref[:, lanes(mine, HID)]
+
+
+def pack_kernel(tokens_ref, a_ref, out_ref):
+    out_ref[:TOK] = tokens_ref[...]
+    out_ref[TOK:, :TOK] = dot_nt(a_ref[...], tokens_ref[...]).astype(BF16)
+
+
+def arrange_kernel(own_ref, oth_ref, x_ref, p_ref, turned_ref):
     l = lax.axis_index("l")
-    for ref, side in ((own_ref, l), (send_ref, 1 - l)):
-        ref[:TOK] = w_in_ref[:, lanes(side * HID, HID)]
-        ref[TOK:] = w_out_ref[lanes(side * HID, HID), :].T
-
-
-def arrange_kernel(own_ref, oth_ref, pown_ref, poth_ref, x_ref, p_ref):
-    l = lax.axis_index("l")
+    for k, ref in enumerate((own_ref, oth_ref)):
+        turned_ref[k] = ref[TOK:, :TOK].astype(F32).T.astype(BF16)
     cols = [column(dy, l, dx) for dy in RING for dx in RING]
     cols += [column(dy, 1 - l, dx) for dx in RING for dy in RING]
     p_ref[...] = jnp.zeros_like(p_ref)
     for i in range(16):
-        src, psrc = (own_ref, pown_ref) if i < 8 else (oth_ref, poth_ref)
+        src = own_ref if i < 8 else oth_ref
         row = token_row(i)
         lane = 0 if i < 8 else RANK
-        p_ref[i * ROWS : (i + 1) * ROWS, lane : lane + RANK] = psrc[pl.ds(row, ROWS), :]
+        p_ref[i * ROWS : (i + 1) * ROWS, lane : lane + RANK] = turned_ref[
+            i // 8, pl.ds(row, ROWS), :
+        ]
         for j in range(32):
             x_ref[i * ROWS : (i + 1) * ROWS, j * BLOCK : (j + 1) * BLOCK] = src[
                 pl.ds(row, ROWS), lanes(cols[j], BLOCK)
             ]
 
 
-def hidden_kernel(x_ref, p_ref, b_ref, *refs):
-    pieces, (hidden_ref, mask_ref) = refs[:8], refs[8:]
-    total = ADAPTER_SCALE * dot(p_ref[...], b_ref[...])
-    for k, piece in enumerate(pieces):
+def near_kernel(x_ref, p_ref, b_own_ref, b_oth_ref, *refs):
+    pieces, total_ref = refs[:6], refs[6]
+    b = jnp.concatenate([b_own_ref[...], b_oth_ref[...]], axis=0)
+    total = ADAPTER_SCALE * dot(p_ref[...], b)
+    for k, piece in zip((0, 1, 2, 4, 5, 6), pieces):
+        total = total + dot(x_ref[:, k * HID : (k + 1) * HID], piece[...])
+    total_ref[...] = total
+
+
+def hidden_kernel(x_ref, total_ref, own_ref, oth_ref, hidden_ref, mask_ref):
+    total = total_ref[...]
+    for k, piece in ((3, own_ref), (7, oth_ref)):
         total = total + dot(x_ref[:, k * HID : (k + 1) * HID], piece[...])
     preact = total * MODEL_WIDTH ** (-0.5)
     hidden_ref[...] = jnp.maximum(preact, 0.0).astype(BF16)
@@ -126,11 +150,9 @@
     for k, piece in enumerate(pieces):
         part = dot_nt(hidden_ref[...], piece[...]).reshape(8, 2, ROWS, HID)
         if k < 4:
-            places = [(l * SIDE + k * HID, 0, HID)]
+            places = [(l * SIDE + (j * 4 + k) * BLOCK, j * BLOCK, BLOCK) for j in range(4)]
         else:
-            places = [
-                ((1 - l) * SIDE + (j * 4 + k - 4) * BLOCK, j * BLOCK, BLOCK) for j in range(4)
-            ]
+            places = [((1 - l) * SIDE + (k - 4) * HID, 0, HID)]
         for to, begin, size in places:
             keep_ref[:, :, lanes(to, size)] = part[:, 0, :, begin : begin + size]
             send_ref[:, :, lanes(to, size)] = part[:, 1, :, begin : begin + size].astype(BF16)
@@ -153,8 +175,8 @@
                 j += 1
 
 
-def backward_kernel(q_ref, qc_ref, left_ref, leftc_ref, right_ref, rightc_ref, mask_ref, p_own_ref,
-                    p_oth_ref, b_ref, *refs):
+def backward_kernel(q_ref, qc_ref, left_ref, leftc_ref, right_ref, rightc_ref, mask_ref, own_pack_ref,
+                    oth_pack_ref, b_own_ref, b_oth_ref, *refs):
     pieces, (up_own_ref, up_oth_ref, wire_ref, back_ref, grad_ref, own_ref, oth_ref) = refs[:8], refs[8:]
     l = lax.axis_index("l")
     for i in range(16):
@@ -169,15 +191,12 @@
     total = None
     for k, piece in enumerate(pieces):
         if k < 4:
-            part = grad_ref[:, lanes(l * SIDE + k * HID, HID)]
-        else:
             part = jnp.concatenate(
-                [
-                    grad_ref[:, lanes((1 - l) * SIDE + (j * 4 + k - 4) * BLOCK, BLOCK)]
-                    for j in range(4)
-                ],
+                [grad_ref[:, lanes(l * SIDE + (j * 4 + k) * BLOCK, BLOCK)] for j in range(4)],
                 axis=1,
             )
+        else:
+            part = grad_ref[:, lanes((1 - l) * SIDE + (k - 4) * HID, HID)]
         term = dot(part, piece[...])
         total = term if total is None else total + term
     total = jnp.where(mask_ref[...].astype(F32) > 0, total * FF ** (-0.5), 0.0).astype(BF16)
@@ -186,8 +205,8 @@
         ref[pl.ds(token_row(i), ROWS), :] = total[i * ROWS : (i + 1) * ROWS]
     scale = ADAPTER_SCALE * MODEL_WIDTH ** (-0.5)
     sides = (
-        (l, own_ref, p_own_ref, up_own_ref, b_ref[:RANK]),
-        (1 - l, oth_ref, p_oth_ref, up_oth_ref, b_ref[RANK:]),
+        (l, own_ref, own_pack_ref, up_own_ref, b_own_ref[...]),
+        (1 - l, oth_ref, oth_pack_ref, up_oth_ref, b_oth_ref[...]),
     )
     for side, hid_ref, p_ref, up_ref, b in sides:
         up = b.astype(F32) - RATE_UP * (scale * dot(p_ref[...], hid_ref[...]))
@@ -198,7 +217,7 @@
             back_ref[side * 8 + k] = back
 
 
-def down_kernel(back_ref, x_ref, a_ref, new_ref, wire_ref):
+def down_kernel(back_ref, x_ref, a_ref, up_ref, new_ref, wire_ref):
     terms = [back_ref[k] for k in range(16)]
     while len(terms) > 1:
         terms = [terms[k] + terms[k + 1] for k in range(0, len(terms), 2)]
@@ -216,31 +235,35 @@
         new = a_ref[:, here].astype(F32) - RATE_DOWN * (scale * grad)
         new_ref[:, here] = new
         for j in range(4):
-            wire_ref[k * 4 + j] = new[:, j * BLOCK : (j + 1) * BLOCK].astype(BF16)
-
-
-def merge_kernel(down_ref, up_ref, w_ref, out_ref, d_ref, u_ref):
+            wire_ref[k * 4 + j, :, :BLOCK] = new[:, j * BLOCK : (j + 1) * BLOCK].astype(BF16)
+            for l in range(2):
+                begin = BLOCK + l * HID
+                wire_ref[k * 4 + j, :, begin : begin + HID] = up_ref[l]
+
+
+def merge_kernel(wire_ref, w_ref, out_ref, d_ref, u_ref):
     for y in range(4):
         for x in range(4):
             for l in range(2):
                 at = ((y * 4 + x) * 2 + l) * RANK
-                d_ref[at : at + RANK, :] = down_ref[y * 8 + l * 4 + x]
+                d_ref[at : at + RANK, :] = wire_ref[y * 8 + l * 4 + x, :, :BLOCK]
     for side in range(2):
         for y in range(4):
             for x in range(4):
                 for l in range(2):
                     at = ((y * 4 + x) * 2 + l) * RANK
-                    u_ref[at : at + RANK, :] = up_ref[y * 8 + side * 4 + x, l]
+                    begin = BLOCK + l * HID
+                    u_ref[at : at + RANK, :] = wire_ref[
+                        y * 8 + side * 4 + x, :, begin : begin + HID
+                    ]
         here = slice(side * HID, (side + 1) * HID)
         delta = dot_tn(d_ref[...], u_ref[...])
         out_ref[:, here] = w_ref[:, here].astype(F32) + ADAPTER_SCALE / 32 * delta
 
 
-def ring(value, axis, upward):
-    below = shift(value, axis, 1)
-    above = shift(value, axis, -1)
-    far = shift(below, axis, 1) if upward else shift(above, axis, -1)
-    return [value, below, above, far]
+def ring(value, axis):
+    below, above = shift(value, axis, 1), shift(value, axis, -1)
+    return [value, below, above, shift(below, axis, 1)]
 
 
 def ring_direct(value, axis):
@@ -252,38 +275,50 @@
     a = factor_down[0]
     b = factor_up[0]
 
-    w_own, w_send = call(
-        split_kernel, (shape(2 * TOK, HID), shape(2 * TOK, HID)), w_in, w_out, name="split"
-    )
-    line_own = ring_direct(w_own, "x")
+    w_send = call(send_kernel, shape(2 * TOK + RANK, HID), w_in, w_out, b, name="send")
     w_oth = partner(w_send, "l")
-    line_oth = ring_direct(w_oth, "y")
-
-    projected = dot_nt(tokens, a).astype(BF16)
-    p_own = projected.T
-    b_own = jnp.where(l == 0, b[:, :HID], b[:, HID:])
-    b_send = jnp.where(l == 0, b[:, HID:], b[:, :HID])
-    arrived = partner(jnp.concatenate([b_send, p_own], axis=1), "l")
-    b_oth, p_oth = arrived[:, :HID], arrived[:, HID:]
-    b_both = jnp.concatenate([b_own, b_oth], axis=0)
-    tokens_oth = near_z(tokens)
-
-    def joined(line, begin):
-        return jnp.concatenate([block[begin : begin + TOK] for block in line], axis=0)
-
-    in_pieces = ring(joined(line_own, 0), "y", True) + ring(joined(line_oth, 0), "x", True)
-    out_pieces = ring(joined(line_own, TOK), "y", False) + ring(joined(line_oth, TOK), "x", False)
+    in_own, out_own, b_own = call(
+        own_kernel,
+        (shape(TOK, HID), shape(TOK, HID), shape(RANK, HID)),
+        w_in, w_out, b, w_send,
+        name="own",
+    )
+    b_oth = w_oth[2 * TOK :]
+    packed = call(pack_kernel, shape(TOK + RANK, MODEL_WIDTH), tokens, a, name="pack")
+    packed_oth = near_z(packed)
+    in_own = jnp.concatenate(ring(in_own, "x"), axis=0)
+    out_own = jnp.concatenate(ring(out_own, "y"), axis=0)
+    in_oth = jnp.concatenate(ring_direct(w_oth[:TOK], "y"), axis=0)
+    out_oth = jnp.concatenate(ring_direct(w_oth[TOK : 2 * TOK], "x"), axis=0)
 
     x_rel, p_rel = call(
         arrange_kernel,
         (shape(2 * TOK, MODEL_WIDTH), shape(2 * TOK, 2 * RANK)),
-        tokens, tokens_oth, projected, p_oth.T,
+        packed, packed_oth,
+        scratch=[pltpu.VMEM((2, TOK, RANK), BF16)],
         name="arrange",
+    )
+
+    in_a = [in_own, shift(in_own, "y", 1), shift(in_own, "y", -1)]
+    in_b = [in_oth, shift(in_oth, "x", 1), shift(in_oth, "x", -1)]
+    out_a = [out_own, shift(out_own, "x", 1), shift(out_own, "x", -1)]
+    out_b = [out_oth, shift(out_oth, "y", 1), shift(out_oth, "y", -1)]
+    in_a_far = shift(in_a[1], "y", 1)
+    in_b_far = shift(in_b[1], "x", 1)
+    out_a_far = shift(out_a[2], "x", -1)
+    out_b_far = shift(out_b[2], "y", -1)
+    out_pieces = out_a + [out_a_far] + out_b + [out_b_far]
+
+    total = call(
+        near_kernel,
+        shape(2 * TOK, HID, dtype=F32),
+        x_rel, p_rel, b_own, b_oth, *in_a, *in_b,
+        name="near",
     )
     hidden, mask = call(
         hidden_kernel,
         (shape(2 * TOK, HID), shape(2 * TOK, HID)),
-        x_rel, p_rel, b_both, *in_pieces,
+        x_rel, total, in_a_far, in_b_far,
         name="hidden",
     )
     keep, send = call(
@@ -317,7 +352,8 @@
             shape(2, RANK, HID),
             shape(16, RANK, TOK, dtype=F32),
         ),
-        q, q_far, left, left_far, right, right_far, mask, p_own, p_oth, b_both, *out_pieces,
+        q, q_far, left, left_far, right, right_far, mask, packed[TOK:, :TOK],
+        packed_oth[TOK:, :TOK], b_own, b_oth, *out_pieces,
         scratch=[
             pltpu.VMEM((2 * TOK, MODEL_WIDTH), BF16),
             pltpu.VMEM((TOK, HID), BF16),
@@ -325,15 +361,14 @@
         ],
         name="backward",
     )
-    ups = lax.all_gather(up_wire, REP, axis=0)
     back = lax.all_to_all(back, ("l", "h", "c"), 0, 0, tiled=True)
     new_a, wire = call(
         down_kernel,
-        (shape(RANK, MODEL_WIDTH, dtype=F32), shape(32, RANK, BLOCK)),
-        back, tokens, a,
+        (shape(RANK, MODEL_WIDTH, dtype=F32), shape(32, RANK, BLOCK + 2 * HID)),
+        back, tokens, a, up_wire,
         name="down",
     )
-    downs = lax.all_to_all(wire, REP, 0, 0, tiled=True)
+    wires = lax.all_to_all(wire, REP, 0, 0, tiled=True)
     up_arrived = partner(up_oth, "l")
     new_b = jnp.where(
         l == 0,
@@ -343,7 +378,7 @@
     merged = call(
         merge_kernel,
         shape(TOK, 2 * HID, dtype=F32),
-        downs, ups, w_in,
+        wires, w_in,
         scratch=[pltpu.VMEM((32 * RANK, BLOCK), BF16), pltpu.VMEM((32 * RANK, HID), BF16)],
         name="merge",
     )

time: 333 us -> 218 us (0.65)
  waiting for transfers between devices: 196 us -> 89.6 us
  between operations: 14.5 us -> 1.04 us
  Pallas kernels: 27.8 us -> 35.5 us
    all_gather x1 -> x0, waiting for transfers between devices: 119 us -> none  [shards(): ups = lax.all_gather(up_wire, REP, axis=0)]
    pallas_call x8 -> x11, Pallas kernels: 27.8 us -> 35.5 us  [call(): pl.pallas_call(kernel, out_shape=out_shape, in_specs=[vmem] * len(args),...]
    ppermute x24 -> x30, waiting for transfers between devices: 50.1 us -> 55.5 us  [shift(): return lax.ppermute(value, axis, [(i, (i + by) % n) for i in range(n)])]
    ppermute x3, waiting for transfers between devices: 7.91 us -> 12.7 us  [near_z(): lax.ppermute(value, Z, [(place(z), place(z + 1 if z % 2 else z - 1)) for...]
    ppermute x24 -> x30, starting transfers between devices: 40.4 us -> 43.4 us  [shift(): return lax.ppermute(value, axis, [(i, (i + by) % n) for i in range(n)])]
    ppermute x9 -> x8, waiting for transfers between devices: 16.9 us -> 19.1 us  [partner(): return lax.ppermute(value, axis, [(0, 1), (1, 0)])]
  transfers between devices with their start and end apart: 38 -> 42, of which waited for: 22 -> 20; matrix products, arithmetic and copies ran while one was open for 2% -> 3% of each run, Pallas kernels for 3% -> 6%
where the time goes in v2:
time: 218 us; the launch traced here: 216 us
  waiting for transfers between devices  89.6 us (41%)
  starting transfers between devices  63.3 us (29%)
  Pallas kernels  35.5 us (16%)
  blocking collectives  13.7 us (6%)
  local copies, waits for them, and re-layouts  9.51 us (4%)
  other arithmetic  3.78 us (2%)
    ppermute x30, waiting for transfers between devices, shift(): return lax.ppermute(value, axis, [(i, (i + by) % n) for i in range(n)])  55.5 us
    ppermute x30, starting transfers between devices, shift(): return lax.ppermute(value, axis, [(i, (i + by) % n) for i in range(n)])  43.4 us
    pallas_call x11, Pallas kernels, call(): pl.pallas_call(kernel, out_shape=out_shape, in_specs=[vmem] * len(args),...  35.5 us
    ppermute x8, waiting for transfers between devices, partner(): return lax.ppermute(value, axis, [(0, 1), (1, 0)])  19.1 us
    all_to_all x1, blocking collectives, shards(): back = lax.all_to_all(back, ('l', 'h', 'c'), 0, 0, tiled=True)  13.7 us
    ppermute x3, waiting for transfers between devices, near_z(): lax.ppermute(value, Z, [(place(z), place(z + 1 if z % 2 else z - 1)) for...  12.7 us
    ppermute x3, starting transfers between devices, near_z(): lax.ppermute(value, Z, [(place(z), place(z + 1 if z % 2 else z - 1)) for...  9.55 us
    unnamed x53, local copies, waits for them, and re-layouts  5.47 us
  transfers between devices with their start and end apart: 42, of which 20 were waited for; matrix products, arithmetic and copies ran while one was open for 3% of the time, Pallas kernels for 6%

profile of v2, /device:TPU:2, one launch (start us, length us, event | category | flops | bytes accessed | tf_op | source)
XLA Modules:
  0.0 216.5 jit_solution(6236274502445419903)
XLA Ops:
  0.6 1.8 send.1.send_ref
  2.5 1.9 own.1
  6.6 2.8 %collective-permute-start.15 = (bf16[128,512]{1,0:T(8,128)(2,1)}, bf16[128,512]{1,0:T(8,128)(2,1)S(1)}, u32[]{:S(2)}, u32[]{:S(2)}) collective-permute-start(bf16[128,512]{1,0:T(8,128)(2,1)} %get-tuple-element.23), channel_id=1, source_target_pairs={{0,192},{64,0},{128,64},{192,128},{1,193},{65,1},{129,65},{193,129... | collective-permute-start | bytes 393224 | tf_op jit(solution)/shard_map/ppermute | solution.py:42
  9.4 1.9 collective-permute-start.1
  12.3 2.7 %pack.1.own_ref = bf16[144,4096]{1,0:T(8,128)(2,1)} custom-call(bf16[128,4096]{1,0:T(8,128)(2,1)} %x_ref.1, bf16[16,4096]{1,0:T(8,128)(2,1)} %bitcast.18), custom_call_target="tpu_custom_call" | custom-call | tf_op jit(solution)/shard_map/pack/pallas_call | solution.py:61
  15.0 4.9 %collective-permute-start = (bf16[144,4096]{1,0:T(8,128)(2,1)}, bf16[144,4096]{1,0:T(8,128)(2,1)S(1)}, u32[]{:S(2)}, u32[]{:S(2)}) collective-permute-start(bf16[144,4096]{1,0:T(8,128)(2,1)} %pack.1.own_ref), channel_id=1, source_target_pairs={{0,38},{32,2},{2,32},{34,4},{4,34},{36,6},{6,36},{38,0},{1,39},{33... | collective-permute-start | bytes 3538952 | tf_op jit(solution)/shard_map/ppermute | solution.py:53
  19.9 1.6 collective-permute-start.4
  22.3 2.4 %collective-permute-start.22 = (bf16[128,512]{1,0:T(8,128)(2,1)S(1)}, bf16[128,512]{1,0:T(8,128)(2,1)S(1)}, u32[]{:S(2)}, u32[]{:S(2)}) collective-permute-start(bf16[128,512]{1,0:T(8,128)(2,1)S(1)} %get-tuple-element.46), channel_id=1, source_target_pairs={{0,16},{8,24},{16,0},{24,8},{1,17},{9,25},{17,1},{25,9},{2,18},{10... | collective-permute-start | bytes 393224 | tf_op jit(solution)/shard_map/ppermute | solution.py:42
  25.6 2.2 collective-permute-done.16
  27.8 2.0 collective-permute-start.9
  33.4 2.2 %collective-permute-done.9 = bf16[128,512]{1,0:T(8,128)(2,1)S(1)} collective-permute-done((bf16[128,512]{1,0:T(8,128)(2,1)S(1)}, bf16[128,512]{1,0:T(8,128)(2,1)S(1)}, u32[]{:S(2)}, u32[]{:S(2)}) %collective-permute-start.9) | collective-permute-done | bytes 131104 | tf_op jit(solution)/shard_map/ppermute | solution.py:42
  35.6 2.1 collective-permute-start.8
  37.7 8.2 %collective-permute-done.8 = bf16[128,512]{1,0:T(8,128)(2,1)S(1)} collective-permute-done((bf16[128,512]{1,0:T(8,128)(2,1)S(1)}, bf16[128,512]{1,0:T(8,128)(2,1)S(1)}, u32[]{:S(2)}, u32[]{:S(2)}) %collective-permute-start.8) | collective-permute-done | bytes 131104 | tf_op jit(solution)/shard_map/ppermute | solution.py:42
  45.9 6.1 %collective-permute-done.7 = bf16[128,512]{1,0:T(8,128)(2,1)S(1)} collective-permute-done((bf16[128,512]{1,0:T(8,128)(2,1)S(1)}, bf16[128,512]{1,0:T(8,128)(2,1)S(1)}, u32[]{:S(2)}, u32[]{:S(2)}) %collective-permute-start.7) | collective-permute-done | bytes 131104 | tf_op jit(solution)/shard_map/ppermute | solution.py:42
  53.3 4.0 %collective-permute-done.20 = bf16[128,512]{1,0:T(8,128)(2,1)S(1)} collective-permute-done((bf16[128,512]{1,0:T(8,128)(2,1)S(1)}, bf16[128,512]{1,0:T(8,128)(2,1)S(1)}, u32[]{:S(2)}, u32[]{:S(2)}) %collective-permute-start.20) | collective-permute-done | bytes 131104 | tf_op jit(solution)/shard_map/ppermute | solution.py:42
  57.3 2.8 %collective-permute-start.11 = (bf16[512,512]{1,0:T(8,128)(2,1)S(1)}, bf16[512,512]{1,0:T(8,128)(2,1)S(1)}, u32[]{:S(2)}, u32[]{:S(2)}) collective-permute-start(bf16[512,512]{1,0:T(8,128)(2,1)S(1)} %pad_maximum_fusion.refs_3_), channel_id=1, source_target_pairs={{0,24},{8,0},{16,8},{24,16},{1,25},{9,1},{17,9},{25,17},{2,26},{10... | collective-permute-start | bytes 1572872 | tf_op jit(solution)/shard_map/ppermute | solution.py:42
  60.3 1.6 collective-permute-start.24
  62.4 5.5 %collective-permute-done.11.refs_5_ = bf16[512,512]{1,0:T(8,128)(2,1)S(1)} collective-permute-done((bf16[512,512]{1,0:T(8,128)(2,1)S(1)}, bf16[512,512]{1,0:T(8,128)(2,1)S(1)}, u32[]{:S(2)}, u32[]{:S(2)}) %collective-permute-start.11) | collective-permute-done | bytes 524320 | tf_op jit(solution)/shard_map/ppermute | solution.py:42
  68.5 6.6 %collective-permute-done.10.refs_4_ = bf16[512,512]{1,0:T(8,128)(2,1)} collective-permute-done((bf16[512,512]{1,0:T(8,128)(2,1)S(1)}, bf16[512,512]{1,0:T(8,128)(2,1)}, u32[]{:S(2)}, u32[]{:S(2)}) %collective-permute-start.10) | collective-permute-done | bytes 524320 | tf_op jit(solution)/shard_map/ppermute | solution.py:42
  76.5 1.9 collective-permute-start.19
  79.3 1.9 collective-permute-start.25
  81.8 3.7 %arrange.1 = (bf16[256,4096]{1,0:T(8,128)(2,1)}, bf16[256,32]{1,0:T(8,128)(2,1)}) custom-call(bf16[144,4096]{1,0:T(8,128)(2,1)} %pack.1.own_ref, bf16[144,4096]{1,0:T(8,128)(2,1)} %copy-done.9), custom_call_target="tpu_custom_call" | custom-call | tf_op jit(solution)/shard_map/arrange/pallas_call | solution.py:61
  85.5 4.4 %near.1.total_ref = f32[256,512]{1,0:T(8,128)} custom-call(bf16[256,4096]{1,0:T(8,128)(2,1)} %get-tuple-element.18.x_ref, bf16[256,32]{1,0:T(8,128)(2,1)} %get-tuple-element.19.p_ref, bf16[16,512]{1,0:T(8,128)(2,1)} %get-tuple-element.20.b_own_ref, bf16[16,512]{1,0:T(8,128)(2,1)} %slice.87.b_oth_ref, bf16[512,512]{1,0:T(8,128)(2,1)} %copy-done.10, ...), custom_call_target="tpu_custom_call" | custom-call | tf_op jit(solution)/shard_map/near/pallas_call | solution.py:61
  89.9 1.5 collective-permute-done.13.oth_ref
  91.5 3.3 %hidden.1 = (bf16[256,512]{1,0:T(8,128)(2,1)}, bf16[256,512]{1,0:T(8,128)(2,1)}) custom-call(bf16[256,4096]{1,0:T(8,128)(2,1)} %get-tuple-element.18.x_ref, f32[256,512]{1,0:T(8,128)} %near.1.total_ref, bf16[512,512]{1,0:T(8,128)(2,1)} %copy-done.13, bf16[512,512]{1,0:T(8,128)(2,1)} %collective-permute-done.13.oth_ref), custom_call_target="tpu_custom_call" | custom-call | tf_op jit(solution)/shard_map/hidden/pallas_call | solution.py:61
  95.7 5.2 %output.1 = (f32[8,16,4096]{2,1,0:T(8,128)}, bf16[8,16,4096]{2,1,0:T(8,128)(2,1)}) custom-call(bf16[256,512]{1,0:T(8,128)(2,1)} %get-tuple-element.22.hidden_ref, bf16[512,512]{1,0:T(8,128)(2,1)} %copy-done.3, bf16[512,512]{1,0:T(8,128)(2,1)} %copy-done.6, bf16[512,512]{1,0:T(8,128)(2,1)} %copy-done.4, bf16[512,512]{1,0:T(8,128)(2,1)} %collective-permute-done.19.refs_3_, ...), custom_call_target="tpu_custom_call" | custom-call | tf_op jit(solution)/shard_map/output/pallas_call | solution.py:61
  100.8 2.9 %collective-permute-done.26 = bf16[8,16,4096]{2,1,0:T(8,128)(2,1)S(1)} collective-permute-done((bf16[8,16,4096]{2,1,0:T(8,128)(2,1)}, bf16[8,16,4096]{2,1,0:T(8,128)(2,1)S(1)}, u32[]{:S(2)}, u32[]{:S(2)}) %collective-permute-start.26) | collective-permute-done | bytes 1048608 | tf_op jit(solution)/shard_map/ppermute | solution.py:46
  103.7 1.9 fusion.1
  105.8 1.8 collective-permute-start.28
  107.6 7.9 %collective-permute-done.28 = bf16[4,16,2048]{2,1,0:T(8,128)(2,1)S(1)} collective-permute-done((bf16[4,16,2048]{2,1,0:T(8,128)(2,1)S(1)}, bf16[4,16,2048]{2,1,0:T(8,128)(2,1)S(1)}, u32[]{:S(2)}, u32[]{:S(2)}) %collective-permute-start.28) | collective-permute-done | bytes 262176 | tf_op jit(solution)/shard_map/ppermute | solution.py:53
  117.2 3.0 %collective-permute-start.30 = (bf16[16,4096]{1,0:T(8,128)(2,1)S(1)}, bf16[16,4096]{1,0:T(8,128)(2,1)S(1)}, u32[]{:S(2)}, u32[]{:S(2)}) collective-permute-start(bf16[16,4096]{1,0:T(8,128)(2,1)S(1)} %get-tuple-element.44), channel_id=1, source_target_pairs={{0,4},{2,6},{4,0},{6,2},{1,5},{3,7},{5,1},{7,3},{8,12},{10,14},{12... | collective-permute-start | bytes 393224 | tf_op jit(solution)/shard_map/ppermute | solution.py:42
  123.8 5.6 %collective-permute-done.30.r2_ref = bf16[16,4096]{1,0:T(8,128)(2,1)S(1)} collective-permute-done((bf16[16,4096]{1,0:T(8,128)(2,1)S(1)}, bf16[16,4096]{1,0:T(8,128)(2,1)S(1)}, u32[]{:S(2)}, u32[]{:S(2)}) %collective-permute-start.30) | collective-permute-done | bytes 131104 | tf_op jit(solution)/shard_map/ppermute | solution.py:42
  131.1 2.3 %finish.1 = bf16[16,4096]{1,0:T(8,128)(2,1)} custom-call(f32[16,4096]{1,0:T(8,128)} %slice_bitcast_fusion.mine_ref, bf16[16,4096]{1,0:T(8,128)(2,1)} %copy-done.21, bf16[16,4096]{1,0:T(8,128)(2,1)} %copy-done.20, bf16[16,4096]{1,0:T(8,128)(2,1)} %copy-done.19, bf16[128,4096]{1,0:T(8,128)(2,1)} %targets_ref.1), custom_call_target="tpu_custom_call" | custom-call | tf_op jit(solution)/shard_map/finish/pallas_call | solution.py:61
  134.3 2.9 %collective-permute-start.33 = (bf16[16,4096]{1,0:T(8,128)(2,1)}, bf16[16,4096]{1,0:T(8,128)(2,1)S(1)}, u32[]{:S(2)}, u32[]{:S(2)}) collective-permute-start(bf16[16,4096]{1,0:T(8,128)(2,1)} %finish.1), channel_id=1, source_target_pairs={{0,4},{2,6},{4,0},{6,2},{1,5},{3,7},{5,1},{7,3},{8,12},{10,14},{12... | collective-permute-start | bytes 393224 | tf_op jit(solution)/shard_map/ppermute | solution.py:42
  137.1 3.4 %collective-permute-start.32 = (bf16[16,4096]{1,0:T(8,128)(2,1)}, bf16[16,4096]{1,0:T(8,128)(2,1)S(1)}, u32[]{:S(2)}, u32[]{:S(2)}) collective-permute-start(bf16[16,4096]{1,0:T(8,128)(2,1)} %finish.1), channel_id=1, source_target_pairs={{0,6},{2,0},{4,2},{6,4},{1,7},{3,1},{5,3},{7,5},{8,14},{10,8},{12,... | collective-permute-start | bytes 393224 | tf_op jit(solution)/shard_map/ppermute | solution.py:42
  140.5 6.5 %collective-permute-done.34 = bf16[16,4096]{1,0:T(8,128)(2,1)S(1)} collective-permute-done((bf16[16,4096]{1,0:T(8,128)(2,1)}, bf16[16,4096]{1,0:T(8,128)(2,1)S(1)}, u32[]{:S(2)}, u32[]{:S(2)}) %collective-permute-start.34) | collective-permute-done | bytes 131104 | tf_op jit(solution)/shard_map/ppermute | solution.py:42
  147.0 4.6 %collective-permute-done.32 = bf16[16,4096]{1,0:T(8,128)(2,1)S(1)} collective-permute-done((bf16[16,4096]{1,0:T(8,128)(2,1)}, bf16[16,4096]{1,0:T(8,128)(2,1)S(1)}, u32[]{:S(2)}, u32[]{:S(2)}) %collective-permute-start.32) | collective-permute-done | bytes 131104 | tf_op jit(solution)/shard_map/ppermute | solution.py:42
  152.7 2.8 %collective-permute-start.38 = (bf16[4,16,2048]{2,1,0:T(8,128)(2,1)S(1)}, bf16[4,16,2048]{2,1,0:T(8,128)(2,1)S(1)}, u32[]{:S(2)}, u32[]{:S(2)}) collective-permute-start(bf16[4,16,2048]{2,1,0:T(8,128)(2,1)S(1)} %get-tuple-element.41), channel_id=1, source_target_pairs={{0,38},{32,2},{2,32},{34,4},{4,34},{36,6},{6,36},{38,0},{1,39},{33... | collective-permute-start | bytes 786440 | tf_op jit(solution)/shard_map/ppermute | solution.py:53
  155.5 1.6 collective-permute-start.36
  157.1 4.9 %collective-permute-done.38.right_ref = bf16[4,16,2048]{2,1,0:T(8,128)(2,1)S(1)} collective-permute-done((bf16[4,16,2048]{2,1,0:T(8,128)(2,1)S(1)}, bf16[4,16,2048]{2,1,0:T(8,128)(2,1)S(1)}, u32[]{:S(2)}, u32[]{:S(2)}) %collective-permute-start.38) | collective-permute-done | bytes 262176 | tf_op jit(solution)/shard_map/ppermute | solution.py:53
  167.0 5.2 %backward.1 = (f32[16,512]{1,0:T(8,128)}, f32[16,512]{1,0:T(8,128)}, bf16[2,16,512]{2,1,0:T(8,128)(2,1)}, f32[16,16,128]{2,1,0:T(8,128)}) custom-call(bf16[4,16,4096]{2,1,0:T(8,128)(2,1)} %copy-done.1, bf16[4,16,4096]{2,1,0:T(8,128)(2,1)} %copy-done.14, bf16[4,16,2048]{2,1,0:T(8,128)(2,1)} %copy-done.16, bf16[4,16,2048]{2,1,0:T(8,128)(2,1)} %copy-done.18, ...), custom_call_target="tpu_custom_call" | custom-call | tf_op jit(solution)/shard_map/backward/pallas_call | solution.py:61
  172.2 13.7 %all_to_all.10.back_ref = f32[16,16,128]{2,1,0:T(8,128)} all-to-all(f32[16,16,128]{2,1,0:T(8,128)} %get-tuple-element.27), channel_id=1, replica_groups=mesh['y'=4,'l'=2,'x'=4,'h'=4,'c'=2] {'l','h','c'}, dimensions={0} | all-to-all | bytes 262144 | tf_op jit(solution)/shard_map/all_to_all | solution.py:364
  185.9 2.7 %down.1 = (f32[16,4096]{1,0:T(8,128)}, bf16[32,16,1152]{2,1,0:T(8,128)(2,1)}) custom-call(f32[16,16,128]{2,1,0:T(8,128)} %all_to_all.10.back_ref, bf16[128,4096]{1,0:T(8,128)(2,1)} %x_ref.1, bf16[16,4096]{1,0:T(8,128)(2,1)} %bitcast.19, bf16[2,16,512]{2,1,0:T(8,128)(2,1)} %get-tuple-element.28.up_ref), custom_call_target="tpu_custom_call" | custom-call | tf_op jit(solution)/shard_map/down/pallas_call | solution.py:61
  188.6 5.3 %all-to-all-start.1 = ((bf16[32,16,1152]{2,1,0:T(8,128)(2,1)}), bf16[32,16,1152]{2,1,0:T(8,128)(2,1)S(1)}, u32[]{:S(2)}, u32[]{:S(2)}) async-start(bf16[32,16,1152]{2,1,0:T(8,128)(2,1)} %get-tuple-element.29), calls=%async_computation.1 | async-start | bytes 2359296 | tf_op jit(solution)/shard_map/all_to_all | solution.py:371
  193.9 1.6 collective-permute-start.40
  195.5 14.5 %collective-permute-done.40 = f32[16,512]{1,0:T(8,128)S(1)} collective-permute-done((f32[16,512]{1,0:T(8,128)S(1)}, f32[16,512]{1,0:T(8,128)S(1)}, u32[]{:S(2)}, u32[]{:S(2)}) %collective-permute-start.40) | collective-permute-done | bytes 32800 | tf_op jit(solution)/shard_map/ppermute | solution.py:46
  210.6 2.4 %all-to-all-done.1.wire_ref = bf16[32,16,1152]{2,1,0:T(8,128)(2,1)S(1)} async-done(((bf16[32,16,1152]{2,1,0:T(8,128)(2,1)}), bf16[32,16,1152]{2,1,0:T(8,128)(2,1)S(1)}, u32[]{:S(2)}, u32[]{:S(2)}) %all-to-all-start.1) | async-done | bytes 1179680 | tf_op jit(solution)/shard_map/all_to_all | solution.py:371
  214.0 2.4 %merge.1 = f32[128,1024]{1,0:T(8,128)} custom-call(bf16[32,16,1152]{2,1,0:T(8,128)(2,1)} %copy-done.2, bf16[128,1024]{1,0:T(8,128)(2,1)} %w_ref.1), custom_call_target="tpu_custom_call" | custom-call | tf_op jit(solution)/shard_map/merge/pallas_call | solution.py:61
  (120 shorter events, 30.5 us)
Async XLA Ops:
  4.3 10.6 %collective-permute-start.2 = (bf16[128,512]{1,0:T(8,128)(2,1)}, bf16[128,512]{1,0:T(8,128)(2,1)S(1)}, u32[]{:S(2)}, u32[]{:S(2)}) collective-permute-start(bf16[128,512]{1,0:T(8,128)(2,1)} %get-tuple-element.21), channel_id=1, source_target_pairs={{0,8},{8,16},{16,24},{24,0},{1,9},{9,17},{17,25},{25,1},{2,10},{10... | collective-permute-start | bytes 393224 | tf_op jit(solution)/shard_map/ppermute | solution.py:42
  5.8 15.7 %collective-permute-start.3 = (bf16[128,512]{1,0:T(8,128)(2,1)}, bf16[128,512]{1,0:T(8,128)(2,1)S(1)}, u32[]{:S(2)}, u32[]{:S(2)}) collective-permute-start(bf16[128,512]{1,0:T(8,128)(2,1)} %get-tuple-element.21), channel_id=1, source_target_pairs={{0,24},{8,0},{16,8},{24,16},{1,25},{9,1},{17,9},{25,17},{2,26},{10... | collective-permute-start | bytes 393224 | tf_op jit(solution)/shard_map/ppermute | solution.py:42
  6.6 15.6 %collective-permute-start.15 = (bf16[128,512]{1,0:T(8,128)(2,1)}, bf16[128,512]{1,0:T(8,128)(2,1)S(1)}, u32[]{:S(2)}, u32[]{:S(2)}) collective-permute-start(bf16[128,512]{1,0:T(8,128)(2,1)} %get-tuple-element.23), channel_id=1, source_target_pairs={{0,192},{64,0},{128,64},{192,128},{1,193},{65,1},{129,65},{193,129... | collective-permute-start | bytes 393224 | tf_op jit(solution)/shard_map/ppermute | solution.py:42
  9.4 10.5 %collective-permute-start.14 = (bf16[128,512]{1,0:T(8,128)(2,1)}, bf16[128,512]{1,0:T(8,128)(2,1)S(1)}, u32[]{:S(2)}, u32[]{:S(2)}) collective-permute-start(bf16[128,512]{1,0:T(8,128)(2,1)} %get-tuple-element.23), channel_id=1, source_target_pairs={{0,64},{64,128},{128,192},{192,0},{1,65},{65,129},{129,193},{193,1... | collective-permute-start | bytes 393224 | tf_op jit(solution)/shard_map/ppermute | solution.py:42
  9.4 12.8 %collective-permute-start.1 = (bf16[272,512]{1,0:T(8,128)(2,1)}, bf16[272,512]{1,0:T(8,128)(2,1)S(1)}, u32[]{:S(2)}, u32[]{:S(2)}) collective-permute-start(bf16[272,512]{1,0:T(8,128)(2,1)} %send.1.send_ref), channel_id=1, source_target_pairs={{0,32},{32,0},{1,33},{33,1},{2,34},{34,2},{3,35},{35,3},{4,36},{36... | collective-permute-start | bytes 835592 | tf_op jit(solution)/shard_map/ppermute | solution.py:46
  15.0 61.6 %collective-permute-start = (bf16[144,4096]{1,0:T(8,128)(2,1)}, bf16[144,4096]{1,0:T(8,128)(2,1)S(1)}, u32[]{:S(2)}, u32[]{:S(2)}) collective-permute-start(bf16[144,4096]{1,0:T(8,128)(2,1)} %pack.1.own_ref), channel_id=1, source_target_pairs={{0,38},{32,2},{2,32},{34,4},{4,34},{36,6},{6,36},{38,0},{1,39},{33... | collective-permute-start | bytes 3538952 | tf_op jit(solution)/shard_map/ppermute | solution.py:53
  19.9 9.8 %collective-permute-start.4 = (bf16[128,512]{1,0:T(8,128)(2,1)S(1)}, bf16[128,512]{1,0:T(8,128)(2,1)S(1)}, u32[]{:S(2)}, u32[]{:S(2)}) collective-permute-start(bf16[128,512]{1,0:T(8,128)(2,1)S(1)} %collective-permute-done.2), channel_id=1, source_target_pairs={{0,8},{8,16},{16,24},{24,0},{1,9},{9,17},{17,25},{25,1},{2,10},{10... | collective-permute-start | bytes 393224 | tf_op jit(solution)/shard_map/ppermute | solution.py:42
  21.5 6.3 %collective-permute-start.16 = (bf16[128,512]{1,0:T(8,128)(2,1)S(1)}, bf16[128,512]{1,0:T(8,128)(2,1)S(1)}, u32[]{:S(2)}, u32[]{:S(2)}) collective-permute-start(bf16[128,512]{1,0:T(8,128)(2,1)S(1)} %collective-permute-done.14), channel_id=1, source_target_pairs={{0,64},{64,128},{128,192},{192,0},{1,65},{65,129},{129,193},{193,1... | collective-permute-start | bytes 393224 | tf_op jit(solution)/shard_map/ppermute | solution.py:42
  22.3 9.0 %collective-permute-start.22 = (bf16[128,512]{1,0:T(8,128)(2,1)S(1)}, bf16[128,512]{1,0:T(8,128)(2,1)S(1)}, u32[]{:S(2)}, u32[]{:S(2)}) collective-permute-start(bf16[128,512]{1,0:T(8,128)(2,1)S(1)} %get-tuple-element.46), channel_id=1, source_target_pairs={{0,16},{8,24},{16,0},{24,8},{1,17},{9,25},{17,1},{25,9},{2,18},{10... | collective-permute-start | bytes 393224 | tf_op jit(solution)/shard_map/ppermute | solution.py:42
  24.7 8.2 %collective-permute-start.21 = (bf16[128,512]{1,0:T(8,128)(2,1)S(1)}, bf16[128,512]{1,0:T(8,128)(2,1)S(1)}, u32[]{:S(2)}, u32[]{:S(2)}) collective-permute-start(bf16[128,512]{1,0:T(8,128)(2,1)S(1)} %get-tuple-element.46), channel_id=1, source_target_pairs={{0,24},{8,0},{16,8},{24,16},{1,25},{9,1},{17,9},{25,17},{2,26},{10... | collective-permute-start | bytes 393224 | tf_op jit(solution)/shard_map/ppermute | solution.py:42
  27.8 7.9 %collective-permute-start.9 = (bf16[128,512]{1,0:T(8,128)(2,1)S(1)}, bf16[128,512]{1,0:T(8,128)(2,1)S(1)}, u32[]{:S(2)}, u32[]{:S(2)}) collective-permute-start(bf16[128,512]{1,0:T(8,128)(2,1)S(1)} %get-tuple-element.47), channel_id=1, source_target_pairs={{0,128},{64,192},{128,0},{192,64},{1,129},{65,193},{129,1},{193,65... | collective-permute-start | bytes 393224 | tf_op jit(solution)/shard_map/ppermute | solution.py:42
  29.7 55.8 %copy-start.3 = (bf16[512,512]{1,0:T(8,128)(2,1)}, bf16[512,512]{1,0:T(8,128)(2,1)S(1)}, u32[]{:S(2)}) copy-start(bf16[512,512]{1,0:T(8,128)(2,1)S(1)} %constant_dynamic-update-slice_fusion.4.refs_0_) | copy-start | bytes 1572868
  29.8 30.4 %collective-permute-start.18 = (bf16[512,512]{1,0:T(8,128)(2,1)S(1)}, bf16[512,512]{1,0:T(8,128)(2,1)S(1)}, u32[]{:S(2)}, u32[]{:S(2)}) collective-permute-start(bf16[512,512]{1,0:T(8,128)(2,1)S(1)} %constant_dynamic-update-slice_fusion.4.refs_0_), channel_id=1, source_target_pairs={{0,24},{8,0},{16,8},{24,16},{1,25},{9,1},{17,9},{25,17},{2,26},{10... | collective-permute-start | bytes 1572872 | tf_op jit(solution)/shard_map/ppermute | solution.py:42
  31.3 31.1 %copy-start.10 = (bf16[512,512]{1,0:T(8,128)(2,1)}, bf16[512,512]{1,0:T(8,128)(2,1)S(1)}, u32[]{:S(2)}) copy-start(bf16[512,512]{1,0:T(8,128)(2,1)S(1)} %constant_dynamic-update-slice_fusion.refs_0_) | copy-start | bytes 1572868
  31.3 28.9 %collective-permute-start.6 = (bf16[512,512]{1,0:T(8,128)(2,1)S(1)}, bf16[512,512]{1,0:T(8,128)(2,1)}, u32[]{:S(2)}, u32[]{:S(2)}) collective-permute-start(bf16[512,512]{1,0:T(8,128)(2,1)S(1)} %constant_dynamic-update-slice_fusion.refs_0_), channel_id=1, source_target_pairs={{0,192},{64,0},{128,64},{192,128},{1,193},{65,1},{129,65},{193,129... | collective-permute-start | bytes 1572872 | tf_op jit(solution)/shard_map/ppermute | solution.py:42
  32.8 29.1 %collective-permute-start.5 = (bf16[512,512]{1,0:T(8,128)(2,1)S(1)}, bf16[512,512]{1,0:T(8,128)(2,1)S(1)}, u32[]{:S(2)}, u32[]{:S(2)}) collective-permute-start(bf16[512,512]{1,0:T(8,128)(2,1)S(1)} %constant_dynamic-update-slice_fusion.refs_0_), channel_id=1, source_target_pairs={{0,64},{64,128},{128,192},{192,0},{1,65},{65,129},{129,193},{193,1... | collective-permute-start | bytes 1572872 | tf_op jit(solution)/shard_map/ppermute | solution.py:42
  35.6 10.3 %collective-permute-start.8 = (bf16[128,512]{1,0:T(8,128)(2,1)S(1)}, bf16[128,512]{1,0:T(8,128)(2,1)S(1)}, u32[]{:S(2)}, u32[]{:S(2)}) collective-permute-start(bf16[128,512]{1,0:T(8,128)(2,1)S(1)} %get-tuple-element.47), channel_id=1, source_target_pairs={{0,192},{64,0},{128,64},{192,128},{1,193},{65,1},{129,65},{193,129... | collective-permute-start | bytes 393224 | tf_op jit(solution)/shard_map/ppermute | solution.py:42
  45.9 6.2 %collective-permute-start.7 = (bf16[128,512]{1,0:T(8,128)(2,1)S(1)}, bf16[128,512]{1,0:T(8,128)(2,1)S(1)}, u32[]{:S(2)}, u32[]{:S(2)}) collective-permute-start(bf16[128,512]{1,0:T(8,128)(2,1)S(1)} %get-tuple-element.47), channel_id=1, source_target_pairs={{0,64},{64,128},{128,192},{192,0},{1,65},{65,129},{129,193},{193,1... | collective-permute-start | bytes 393224 | tf_op jit(solution)/shard_map/ppermute | solution.py:42
  52.1 5.2 %collective-permute-start.20 = (bf16[128,512]{1,0:T(8,128)(2,1)S(1)}, bf16[128,512]{1,0:T(8,128)(2,1)S(1)}, u32[]{:S(2)}, u32[]{:S(2)}) collective-permute-start(bf16[128,512]{1,0:T(8,128)(2,1)S(1)} %get-tuple-element.46), channel_id=1, source_target_pairs={{0,8},{8,16},{16,24},{24,0},{1,9},{9,17},{17,25},{25,1},{2,10},{10... | collective-permute-start | bytes 393224 | tf_op jit(solution)/shard_map/ppermute | solution.py:42
  53.3 25.2 %copy-start.8 = (bf16[512,512]{1,0:T(8,128)(2,1)}, bf16[512,512]{1,0:T(8,128)(2,1)S(1)}, u32[]{:S(2)}) copy-start(bf16[512,512]{1,0:T(8,128)(2,1)S(1)} %pad_maximum_fusion.refs_3_) | copy-start | bytes 1572868
  57.3 10.6 %collective-permute-start.11 = (bf16[512,512]{1,0:T(8,128)(2,1)S(1)}, bf16[512,512]{1,0:T(8,128)(2,1)S(1)}, u32[]{:S(2)}, u32[]{:S(2)}) collective-permute-start(bf16[512,512]{1,0:T(8,128)(2,1)S(1)} %pad_maximum_fusion.refs_3_), channel_id=1, source_target_pairs={{0,24},{8,0},{16,8},{24,16},{1,25},{9,1},{17,9},{25,17},{2,26},{10... | collective-permute-start | bytes 1572872 | tf_op jit(solution)/shard_map/ppermute | solution.py:42
  60.1 29.8 %copy-start = (bf16[512,512]{1,0:T(8,128)(2,1)}, bf16[512,512]{1,0:T(8,128)(2,1)S(1)}, u32[]{:S(2)}) copy-start(bf16[512,512]{1,0:T(8,128)(2,1)S(1)} %pad_maximum_fusion.1.refs_4_) | copy-start | bytes 1572868
  60.1 29.7 %copy-start.4 = (bf16[512,512]{1,0:T(8,128)(2,1)}, bf16[512,512]{1,0:T(8,128)(2,1)S(1)}, u32[]{:S(2)}) copy-start(bf16[512,512]{1,0:T(8,128)(2,1)S(1)} %collective-permute-done.18.refs_2_) | copy-start | bytes 1572868
  60.2 14.9 %collective-permute-start.10 = (bf16[512,512]{1,0:T(8,128)(2,1)S(1)}, bf16[512,512]{1,0:T(8,128)(2,1)}, u32[]{:S(2)}, u32[]{:S(2)}) collective-permute-start(bf16[512,512]{1,0:T(8,128)(2,1)S(1)} %pad_maximum_fusion.refs_3_), channel_id=1, source_target_pairs={{0,8},{8,16},{16,24},{24,0},{1,9},{9,17},{17,25},{25,1},{2,10},{10... | collective-permute-start | bytes 1572872 | tf_op jit(solution)/shard_map/ppermute | solution.py:42
  60.3 14.8 %collective-permute-start.24 = (bf16[512,512]{1,0:T(8,128)(2,1)S(1)}, bf16[512,512]{1,0:T(8,128)(2,1)S(1)}, u32[]{:S(2)}, u32[]{:S(2)}) collective-permute-start(bf16[512,512]{1,0:T(8,128)(2,1)S(1)} %pad_maximum_fusion.1.refs_4_), channel_id=1, source_target_pairs={{0,192},{64,0},{128,64},{192,128},{1,193},{65,1},{129,65},{193,129... | collective-permute-start | bytes 1572872 | tf_op jit(solution)/shard_map/ppermute | solution.py:42
  61.9 16.6 %collective-permute-start.12 = (bf16[512,512]{1,0:T(8,128)(2,1)S(1)}, bf16[512,512]{1,0:T(8,128)(2,1)S(1)}, u32[]{:S(2)}, u32[]{:S(2)}) collective-permute-start(bf16[512,512]{1,0:T(8,128)(2,1)S(1)} %collective-permute-done.5.refs_1_), channel_id=1, source_target_pairs={{0,64},{64,128},{128,192},{192,0},{1,65},{65,129},{129,193},{193,1... | collective-permute-start | bytes 1572872 | tf_op jit(solution)/shard_map/ppermute | solution.py:42
  67.9 26.9 %collective-permute-start.17 = (bf16[512,512]{1,0:T(8,128)(2,1)S(1)}, bf16[512,512]{1,0:T(8,128)(2,1)S(1)}, u32[]{:S(2)}, u32[]{:S(2)}) collective-permute-start(bf16[512,512]{1,0:T(8,128)(2,1)S(1)} %constant_dynamic-update-slice_fusion.4.refs_0_), channel_id=1, source_target_pairs={{0,8},{8,16},{16,24},{24,0},{1,9},{9,17},{17,25},{25,1},{2,10},{10... | collective-permute-start | bytes 1572872 | tf_op jit(solution)/shard_map/ppermute | solution.py:42
  75.1 16.4 %collective-permute-start.13 = (bf16[512,512]{1,0:T(8,128)(2,1)}, bf16[512,512]{1,0:T(8,128)(2,1)}, u32[]{:S(2)}, u32[]{:S(2)}) collective-permute-start(bf16[512,512]{1,0:T(8,128)(2,1)} %collective-permute-done.10.refs_4_), channel_id=1, source_target_pairs={{0,8},{8,16},{16,24},{24,0},{1,9},{9,17},{17,25},{25,1},{2,10},{10... | collective-permute-start | bytes 1572872 | tf_op jit(solution)/shard_map/ppermute | solution.py:42
  75.1 19.6 %collective-permute-start.23 = (bf16[512,512]{1,0:T(8,128)(2,1)S(1)}, bf16[512,512]{1,0:T(8,128)(2,1)S(1)}, u32[]{:S(2)}, u32[]{:S(2)}) collective-permute-start(bf16[512,512]{1,0:T(8,128)(2,1)S(1)} %pad_maximum_fusion.1.refs_4_), channel_id=1, source_target_pairs={{0,64},{64,128},{128,192},{192,0},{1,65},{65,129},{129,193},{193,1... | collective-permute-start | bytes 1572872 | tf_op jit(solution)/shard_map/ppermute | solution.py:42
  76.5 18.2 %collective-permute-start.19 = (bf16[512,512]{1,0:T(8,128)(2,1)S(1)}, bf16[512,512]{1,0:T(8,128)(2,1)}, u32[]{:S(2)}, u32[]{:S(2)}) collective-permute-start(bf16[512,512]{1,0:T(8,128)(2,1)S(1)} %collective-permute-done.18.refs_2_), channel_id=1, source_target_pairs={{0,24},{8,0},{16,8},{24,16},{1,25},{9,1},{17,9},{25,17},{2,26},{10... | collective-permute-start | bytes 1572872 | tf_op jit(solution)/shard_map/ppermute | solution.py:42
  79.3 15.5 %collective-permute-start.25 = (bf16[512,512]{1,0:T(8,128)(2,1)S(1)}, bf16[512,512]{1,0:T(8,128)(2,1)}, u32[]{:S(2)}, u32[]{:S(2)}) collective-permute-start(bf16[512,512]{1,0:T(8,128)(2,1)S(1)} %collective-permute-done.24.refs_6_), channel_id=1, source_target_pairs={{0,192},{64,0},{128,64},{192,128},{1,193},{65,1},{129,65},{193,129... | collective-permute-start | bytes 1572872 | tf_op jit(solution)/shard_map/ppermute | solution.py:42
  100.8 2.9 %collective-permute-start.26 = (bf16[8,16,4096]{2,1,0:T(8,128)(2,1)}, bf16[8,16,4096]{2,1,0:T(8,128)(2,1)S(1)}, u32[]{:S(2)}, u32[]{:S(2)}) collective-permute-start(bf16[8,16,4096]{2,1,0:T(8,128)(2,1)} %get-tuple-element.25), channel_id=1, source_target_pairs={{0,1},{1,0},{2,3},{3,2},{4,5},{5,4},{6,7},{7,6},{8,9},{9,8},{10,11... | collective-permute-start | bytes 3145736 | tf_op jit(solution)/shard_map/ppermute | solution.py:46
  105.8 9.6 %collective-permute-start.28 = (bf16[4,16,2048]{2,1,0:T(8,128)(2,1)S(1)}, bf16[4,16,2048]{2,1,0:T(8,128)(2,1)S(1)}, u32[]{:S(2)}, u32[]{:S(2)}) collective-permute-start(bf16[4,16,2048]{2,1,0:T(8,128)(2,1)S(1)} %maximum_select_fusion), channel_id=1, source_target_pairs={{0,38},{32,2},{2,32},{34,4},{4,34},{36,6},{6,36},{38,0},{1,39},{33... | collective-permute-start | bytes 786440 | tf_op jit(solution)/shard_map/ppermute | solution.py:53
  107.5 8.1 %collective-permute-start.27 = (bf16[4,16,2048]{2,1,0:T(8,128)(2,1)S(1)}, bf16[4,16,2048]{2,1,0:T(8,128)(2,1)S(1)}, u32[]{:S(2)}, u32[]{:S(2)}) collective-permute-start(bf16[4,16,2048]{2,1,0:T(8,128)(2,1)S(1)} %slice.91), channel_id=1, source_target_pairs={{0,32},{32,0},{1,33},{33,1},{2,34},{34,2},{3,35},{35,3},{4,36},{36... | collective-permute-start | bytes 786440 | tf_op jit(solution)/shard_map/ppermute | solution.py:46
  115.8 8.0 %collective-permute-start.31 = (bf16[16,4096]{1,0:T(8,128)(2,1)S(1)}, bf16[16,4096]{1,0:T(8,128)(2,1)S(1)}, u32[]{:S(2)}, u32[]{:S(2)}) collective-permute-start(bf16[16,4096]{1,0:T(8,128)(2,1)S(1)} %get-tuple-element.43), channel_id=1, source_target_pairs={{0,6},{2,0},{4,2},{6,4},{1,7},{3,1},{5,3},{7,5},{8,14},{10,8},{12,... | collective-permute-start | bytes 393224 | tf_op jit(solution)/shard_map/ppermute | solution.py:42
  117.2 12.3 %collective-permute-start.30 = (bf16[16,4096]{1,0:T(8,128)(2,1)S(1)}, bf16[16,4096]{1,0:T(8,128)(2,1)S(1)}, u32[]{:S(2)}, u32[]{:S(2)}) collective-permute-start(bf16[16,4096]{1,0:T(8,128)(2,1)S(1)} %get-tuple-element.44), channel_id=1, source_target_pairs={{0,4},{2,6},{4,0},{6,2},{1,5},{3,7},{5,1},{7,3},{8,12},{10,14},{12... | collective-permute-start | bytes 393224 | tf_op jit(solution)/shard_map/ppermute | solution.py:42
  120.2 10.2 %collective-permute-start.29 = (bf16[16,4096]{1,0:T(8,128)(2,1)S(1)}, bf16[16,4096]{1,0:T(8,128)(2,1)S(1)}, u32[]{:S(2)}, u32[]{:S(2)}) collective-permute-start(bf16[16,4096]{1,0:T(8,128)(2,1)S(1)} %get-tuple-element.45), channel_id=1, source_target_pairs={{0,2},{2,4},{4,6},{6,0},{1,3},{3,5},{5,7},{7,1},{8,10},{10,12},{12... | collective-permute-start | bytes 393224 | tf_op jit(solution)/shard_map/ppermute | solution.py:42
  133.3 13.7 %collective-permute-start.34 = (bf16[16,4096]{1,0:T(8,128)(2,1)}, bf16[16,4096]{1,0:T(8,128)(2,1)S(1)}, u32[]{:S(2)}, u32[]{:S(2)}) collective-permute-start(bf16[16,4096]{1,0:T(8,128)(2,1)} %finish.1), channel_id=1, source_target_pairs={{0,2},{2,4},{4,6},{6,0},{1,3},{3,5},{5,7},{7,1},{8,10},{10,12},{12... | collective-permute-start | bytes 393224 | tf_op jit(solution)/shard_map/ppermute | solution.py:42
  134.3 12.8 %collective-permute-start.33 = (bf16[16,4096]{1,0:T(8,128)(2,1)}, bf16[16,4096]{1,0:T(8,128)(2,1)S(1)}, u32[]{:S(2)}, u32[]{:S(2)}) collective-permute-start(bf16[16,4096]{1,0:T(8,128)(2,1)} %finish.1), channel_id=1, source_target_pairs={{0,4},{2,6},{4,0},{6,2},{1,5},{3,7},{5,1},{7,3},{8,12},{10,14},{12... | collective-permute-start | bytes 393224 | tf_op jit(solution)/shard_map/ppermute | solution.py:42
  137.1 14.5 %collective-permute-start.32 = (bf16[16,4096]{1,0:T(8,128)(2,1)}, bf16[16,4096]{1,0:T(8,128)(2,1)S(1)}, u32[]{:S(2)}, u32[]{:S(2)}) collective-permute-start(bf16[16,4096]{1,0:T(8,128)(2,1)} %finish.1), channel_id=1, source_target_pairs={{0,6},{2,0},{4,2},{6,4},{1,7},{3,1},{5,3},{7,5},{8,14},{10,8},{12,... | collective-permute-start | bytes 393224 | tf_op jit(solution)/shard_map/ppermute | solution.py:42
  152.7 9.2 %collective-permute-start.38 = (bf16[4,16,2048]{2,1,0:T(8,128)(2,1)S(1)}, bf16[4,16,2048]{2,1,0:T(8,128)(2,1)S(1)}, u32[]{:S(2)}, u32[]{:S(2)}) collective-permute-start(bf16[4,16,2048]{2,1,0:T(8,128)(2,1)S(1)} %get-tuple-element.41), channel_id=1, source_target_pairs={{0,38},{32,2},{2,32},{34,4},{4,34},{36,6},{6,36},{38,0},{1,39},{33... | collective-permute-start | bytes 786440 | tf_op jit(solution)/shard_map/ppermute | solution.py:53
  155.5 7.9 %collective-permute-start.36 = (bf16[4,16,2048]{2,1,0:T(8,128)(2,1)S(1)}, bf16[4,16,2048]{2,1,0:T(8,128)(2,1)S(1)}, u32[]{:S(2)}, u32[]{:S(2)}) collective-permute-start(bf16[4,16,2048]{2,1,0:T(8,128)(2,1)S(1)} %get-tuple-element.42), channel_id=1, source_target_pairs={{0,32},{32,0},{1,33},{33,1},{2,34},{34,2},{3,35},{35,3},{4,36},{36... | collective-permute-start | bytes 786440 | tf_op jit(solution)/shard_map/ppermute | solution.py:46
  157.1 8.9 %collective-permute-start.35 = (bf16[4,16,4096]{2,1,0:T(8,128)(2,1)S(1)}, bf16[4,16,4096]{2,1,0:T(8,128)(2,1)S(1)}, u32[]{:S(2)}, u32[]{:S(2)}) collective-permute-start(bf16[4,16,4096]{2,1,0:T(8,128)(2,1)S(1)} %pad_maximum_fusion.2.q_ref), channel_id=1, source_target_pairs={{0,1},{1,0},{2,3},{3,2},{4,5},{5,4},{6,7},{7,6},{8,9},{9,8},{10,11... | collective-permute-start | bytes 1572872 | tf_op jit(solution)/shard_map/ppermute | solution.py:46
  161.9 4.0 %collective-permute-start.39 = (bf16[4,16,2048]{2,1,0:T(8,128)(2,1)S(1)}, bf16[4,16,2048]{2,1,0:T(8,128)(2,1)S(1)}, u32[]{:S(2)}, u32[]{:S(2)}) collective-permute-start(bf16[4,16,2048]{2,1,0:T(8,128)(2,1)S(1)} %collective-permute-done.38.right_ref), channel_id=1, source_target_pairs={{0,1},{1,0},{2,3},{3,2},{4,5},{5,4},{6,7},{7,6},{8,9},{9,8},{10,11... | collective-permute-start | bytes 786440 | tf_op jit(solution)/shard_map/ppermute | solution.py:46
  163.4 2.6 %collective-permute-start.37 = (bf16[4,16,2048]{2,1,0:T(8,128)(2,1)S(1)}, bf16[4,16,2048]{2,1,0:T(8,128)(2,1)S(1)}, u32[]{:S(2)}, u32[]{:S(2)}) collective-permute-start(bf16[4,16,2048]{2,1,0:T(8,128)(2,1)S(1)} %collective-permute-done.36.left_ref), channel_id=1, source_target_pairs={{0,1},{1,0},{2,3},{3,2},{4,5},{5,4},{6,7},{7,6},{8,9},{9,8},{10,11... | collective-permute-start | bytes 786440 | tf_op jit(solution)/shard_map/ppermute | solution.py:46
  172.2 37.8 %copy-start.22 = (f32[16,512]{1,0:T(8,128)S(1)}, f32[16,512]{1,0:T(8,128)}, u32[]{:S(2)}) copy-start(f32[16,512]{1,0:T(8,128)} %get-tuple-element.31) | copy-start | bytes 98308
  188.6 24.4 %all-to-all-start.1 = ((bf16[32,16,1152]{2,1,0:T(8,128)(2,1)}), bf16[32,16,1152]{2,1,0:T(8,128)(2,1)S(1)}, u32[]{:S(2)}, u32[]{:S(2)}) async-start(bf16[32,16,1152]{2,1,0:T(8,128)(2,1)} %get-tuple-element.29), calls=%async_computation.1 | async-start | bytes 2359296 | tf_op jit(solution)/shard_map/all_to_all | solution.py:371
  193.9 16.1 %collective-permute-start.40 = (f32[16,512]{1,0:T(8,128)S(1)}, f32[16,512]{1,0:T(8,128)S(1)}, u32[]{:S(2)}, u32[]{:S(2)}) collective-permute-start(f32[16,512]{1,0:T(8,128)S(1)} %copy-done.23), channel_id=1, source_target_pairs={{0,32},{32,0},{1,33},{33,1},{2,34},{34,2},{3,35},{35,3},{4,36},{36... | collective-permute-start | bytes 98312 | tf_op jit(solution)/shard_map/ppermute | solution.py:46
  (18 other events, 105.4 us)

commit v3 on v2

--- a/solution.py
+++ b/solution.py
@@ -55,17 +55,18 @@
     )
 
 
-def call(kernel, out_shape, *args, scratch=(), name):
+def call(kernel, out_shape, *args, scratch=(), after=(), name):
     vmem = pl.BlockSpec(memory_space=pltpu.VMEM)
+    wait = pl.BlockSpec(memory_space=pl.ANY)
     many = isinstance(out_shape, tuple)
     return pl.pallas_call(
         kernel,
         out_shape=out_shape,
-        in_specs=[vmem] * len(args),
+        in_specs=[vmem] * len(args) + [wait] * len(after),
         out_specs=(vmem,) * len(out_shape) if many else vmem,
         scratch_shapes=scratch,
         name=name,
-    )(*args)
+    )(*args, *after)
 
 
 def shape(*dims, dtype=BF16):
@@ -78,7 +79,7 @@
 
 def token_row(i):
     h, c = lax.axis_index("h"), lax.axis_index("c")
-    j, e = (i // 2) % 4, i % 2
+    j, e = i % 4, i // 8
     return pl.multiple_of((((h + j) % 4) * 2 + (c + e) % 2) * ROWS, ROWS)
 
 
@@ -106,19 +107,21 @@
     out_ref[TOK:, :TOK] = dot_nt(a_ref[...], tokens_ref[...]).astype(BF16)
 
 
-def arrange_kernel(own_ref, oth_ref, x_ref, p_ref, turned_ref):
+def arrange_kernel(own_ref, oth_ref, x_ref, p_ref, pt_ref, turned_ref):
     l = lax.axis_index("l")
     for k, ref in enumerate((own_ref, oth_ref)):
+        pt_ref[k] = ref[TOK:, :TOK]
         turned_ref[k] = ref[TOK:, :TOK].astype(F32).T.astype(BF16)
     cols = [column(dy, l, dx) for dy in RING for dx in RING]
     cols += [column(dy, 1 - l, dx) for dx in RING for dy in RING]
     p_ref[...] = jnp.zeros_like(p_ref)
     for i in range(16):
-        src = own_ref if i < 8 else oth_ref
+        side = (i // 4) % 2
+        src = oth_ref if side else own_ref
         row = token_row(i)
-        lane = 0 if i < 8 else RANK
+        lane = side * RANK
         p_ref[i * ROWS : (i + 1) * ROWS, lane : lane + RANK] = turned_ref[
-            i // 8, pl.ds(row, ROWS), :
+            side, pl.ds(row, ROWS), :
         ]
         for j in range(32):
             x_ref[i * ROWS : (i + 1) * ROWS, j * BLOCK : (j + 1) * BLOCK] = src[
@@ -141,21 +144,23 @@
         total = total + dot(x_ref[:, k * HID : (k + 1) * HID], piece[...])
     preact = total * MODEL_WIDTH ** (-0.5)
     hidden_ref[...] = jnp.maximum(preact, 0.0).astype(BF16)
-    mask_ref[...] = jnp.where(preact > 0, 1.0, 0.0).astype(BF16)
+    mask = jnp.where(preact > 0, 1.0, 0.0).astype(BF16)
+    for i in range(16):
+        mask_ref[(i // 4) % 2, pl.ds(token_row(i), ROWS), :] = mask[i * ROWS : (i + 1) * ROWS]
 
 
 def output_kernel(hidden_ref, *refs):
-    pieces, (keep_ref, send_ref) = refs[:8], refs[8:]
+    pieces, out_ref = refs[:8], refs[-1]
     l = lax.axis_index("l")
+    rows = slice(0, TOK) if out_ref.dtype == F32 else slice(TOK, 2 * TOK)
     for k, piece in enumerate(pieces):
-        part = dot_nt(hidden_ref[...], piece[...]).reshape(8, 2, ROWS, HID)
+        part = dot_nt(hidden_ref[rows], piece[...]).astype(out_ref.dtype).reshape(8, ROWS, HID)
         if k < 4:
-            places = [(l * SIDE + (j * 4 + k) * BLOCK, j * BLOCK, BLOCK) for j in range(4)]
+            for j in range(4):
+                to = l * SIDE + (j * 4 + k) * BLOCK
+                out_ref[:, :, lanes(to, BLOCK)] = part[:, :, j * BLOCK : (j + 1) * BLOCK]
         else:
-            places = [((1 - l) * SIDE + (k - 4) * HID, 0, HID)]
-        for to, begin, size in places:
-            keep_ref[:, :, lanes(to, size)] = part[:, 0, :, begin : begin + size]
-            send_ref[:, :, lanes(to, size)] = part[:, 1, :, begin : begin + size].astype(BF16)
+            out_ref[:, :, lanes((1 - l) * SIDE + (k - 4) * HID, HID)] = part
 
 
 def finish_kernel(mine_ref, r1_ref, r2_ref, r3_ref, targets_ref, out_ref):
@@ -175,19 +180,8 @@
                 j += 1
 
 
-def backward_kernel(q_ref, qc_ref, left_ref, leftc_ref, right_ref, rightc_ref, mask_ref, own_pack_ref,
-                    oth_pack_ref, b_own_ref, b_oth_ref, *refs):
-    pieces, (up_own_ref, up_oth_ref, wire_ref, back_ref, grad_ref, own_ref, oth_ref) = refs[:8], refs[8:]
+def backward(grad_ref, mask, pt, b, pieces):
     l = lax.axis_index("l")
-    for i in range(16):
-        j, e = (i // 2) % 4, i % 2
-        here = slice(i * ROWS, (i + 1) * ROWS)
-        if i < 8:
-            grad_ref[here, :] = (q_ref, qc_ref)[e][j]
-        else:
-            turned = (j + 1 + 2 * l) % 4
-            grad_ref[here, :SIDE] = (left_ref, leftc_ref)[e][j]
-            grad_ref[here, SIDE:] = (right_ref, rightc_ref)[e][turned]
     total = None
     for k, piece in enumerate(pieces):
         if k < 4:
@@ -199,22 +193,35 @@
             part = grad_ref[:, lanes((1 - l) * SIDE + (k - 4) * HID, HID)]
         term = dot(part, piece[...])
         total = term if total is None else total + term
-    total = jnp.where(mask_ref[...].astype(F32) > 0, total * FF ** (-0.5), 0.0).astype(BF16)
-    for i in range(16):
-        ref = own_ref if i < 8 else oth_ref
-        ref[pl.ds(token_row(i), ROWS), :] = total[i * ROWS : (i + 1) * ROWS]
+    hid = jnp.where(mask.astype(F32) > 0, total * FF ** (-0.5), 0.0).astype(BF16)
     scale = ADAPTER_SCALE * MODEL_WIDTH ** (-0.5)
-    sides = (
-        (l, own_ref, own_pack_ref, up_own_ref, b_own_ref[...]),
-        (1 - l, oth_ref, oth_pack_ref, up_oth_ref, b_oth_ref[...]),
-    )
-    for side, hid_ref, p_ref, up_ref, b in sides:
-        up = b.astype(F32) - RATE_UP * (scale * dot(p_ref[...], hid_ref[...]))
-        up_ref[...] = up
-        wire_ref[side] = up.astype(BF16)
-        back = dot_nt(b, hid_ref[...])
-        for k in range(8):
-            back_ref[side * 8 + k] = back
+    return b.astype(F32) - RATE_UP * (scale * dot(pt, hid)), dot_nt(b, hid)
+
+
+def backward_own_kernel(q_ref, qc_ref, mask_ref, pt_ref, b_ref, *refs):
+    pieces, (up_ref, back_ref, grad_ref) = refs[:8], refs[8:]
+    for e, ref in enumerate((q_ref, qc_ref)):
+        for j in range(4):
+            grad_ref[pl.ds(token_row(e * 8 + j), ROWS), :] = ref[j]
+    up_ref[...], back_ref[...] = backward(grad_ref, mask_ref[0], pt_ref[0], b_ref[...], pieces)
+
+
+def backward_oth_kernel(left_ref, leftc_ref, right_ref, rightc_ref, mask_ref, pt_ref, b_ref,
+                        up_own_ref, back_own_ref, *refs):
+    pieces, (up_ref, wire_ref, back_ref, grad_ref) = refs[:8], refs[8:]
+    l = lax.axis_index("l")
+    for e, (left, right) in enumerate(((left_ref, right_ref), (leftc_ref, rightc_ref))):
+        for j in range(4):
+            rows = pl.ds(token_row(e * 8 + 4 + j), ROWS)
+            grad_ref[rows, :SIDE] = left[j]
+            grad_ref[rows, SIDE:] = right[(j + 1 + 2 * l) % 4]
+    up, back = backward(grad_ref, mask_ref[1], pt_ref[1], b_ref[...], pieces)
+    up_ref[...] = up
+    wire_ref[l] = up_own_ref[...].astype(BF16)
+    wire_ref[1 - l] = up.astype(BF16)
+    for k in range(8):
+        back_ref[l * 8 + k] = back_own_ref[...]
+        back_ref[(1 - l) * 8 + k] = back
 
 
 def down_kernel(back_ref, x_ref, a_ref, up_ref, new_ref, wire_ref):
@@ -291,9 +298,9 @@
     in_oth = jnp.concatenate(ring_direct(w_oth[:TOK], "y"), axis=0)
     out_oth = jnp.concatenate(ring_direct(w_oth[TOK : 2 * TOK], "x"), axis=0)
 
-    x_rel, p_rel = call(
+    x_rel, p_rel, pt = call(
         arrange_kernel,
-        (shape(2 * TOK, MODEL_WIDTH), shape(2 * TOK, 2 * RANK)),
+        (shape(2 * TOK, MODEL_WIDTH), shape(2 * TOK, 2 * RANK), shape(2, RANK, TOK)),
         packed, packed_oth,
         scratch=[pltpu.VMEM((2, TOK, RANK), BF16)],
         name="arrange",
@@ -303,32 +310,38 @@
     in_b = [in_oth, shift(in_oth, "x", 1), shift(in_oth, "x", -1)]
     out_a = [out_own, shift(out_own, "x", 1), shift(out_own, "x", -1)]
     out_b = [out_oth, shift(out_oth, "y", 1), shift(out_oth, "y", -1)]
+    in_a[1], x_rel, p_rel = lax.optimization_barrier((in_a[1], x_rel, p_rel))
     in_a_far = shift(in_a[1], "y", 1)
     in_b_far = shift(in_b[1], "x", 1)
-    out_a_far = shift(out_a[2], "x", -1)
-    out_b_far = shift(out_b[2], "y", -1)
-    out_pieces = out_a + [out_a_far] + out_b + [out_b_far]
-
     total = call(
         near_kernel,
         shape(2 * TOK, HID, dtype=F32),
         x_rel, p_rel, b_own, b_oth, *in_a, *in_b,
         name="near",
     )
+    out_a[2], out_b[2], total = lax.optimization_barrier((out_a[2], out_b[2], total))
+    out_a_far = shift(out_a[2], "x", -1)
+    out_b_far = shift(out_b[2], "y", -1)
+    out_pieces = out_a + [out_a_far] + out_b + [out_b_far]
     hidden, mask = call(
         hidden_kernel,
-        (shape(2 * TOK, HID), shape(2 * TOK, HID)),
+        (shape(2 * TOK, HID), shape(2, TOK, HID)),
         x_rel, total, in_a_far, in_b_far,
         name="hidden",
     )
-    keep, send = call(
+    send = call(
+        output_kernel, shape(8, ROWS, MODEL_WIDTH), hidden, *out_pieces, name="output_send"
+    )
+    arrived = partner(send, "c")
+    keep = call(
         output_kernel,
-        (shape(8, ROWS, MODEL_WIDTH, dtype=F32), shape(8, ROWS, MODEL_WIDTH)),
+        shape(8, ROWS, MODEL_WIDTH, dtype=F32),
         hidden, *out_pieces,
-        name="output",
-    )
-
-    summed = keep + partner(send, "c").astype(F32)
+        after=[send],
+        name="output_keep",
+    )
+
+    summed = keep + arrived.astype(F32)
     away = summed[4:].astype(BF16)
     left = partner(away[:, :, :SIDE], "l")
     right = away[:, :, SIDE:]
@@ -344,22 +357,23 @@
     right = near_z(q[:, :, SIDE:])
     q_far, left_far, right_far = partner(q, "c"), partner(left, "c"), partner(right, "c")
 
-    up_own, up_oth, up_wire, back = call(
-        backward_kernel,
+    up_own, back_own = call(
+        backward_own_kernel,
+        (shape(RANK, HID, dtype=F32), shape(RANK, TOK, dtype=F32)),
+        q, q_far, mask, pt, b_own, *out_pieces,
+        scratch=[pltpu.VMEM((TOK, MODEL_WIDTH), BF16)],
+        name="backward_own",
+    )
+    up_oth, up_wire, back = call(
+        backward_oth_kernel,
         (
-            shape(RANK, HID, dtype=F32),
             shape(RANK, HID, dtype=F32),
             shape(2, RANK, HID),
             shape(16, RANK, TOK, dtype=F32),
         ),
-        q, q_far, left, left_far, right, right_far, mask, packed[TOK:, :TOK],
-        packed_oth[TOK:, :TOK], b_own, b_oth, *out_pieces,
-        scratch=[
-            pltpu.VMEM((2 * TOK, MODEL_WIDTH), BF16),
-            pltpu.VMEM((TOK, HID), BF16),
-            pltpu.VMEM((TOK, HID), BF16),
-        ],
-        name="backward",
+        left, left_far, right, right_far, mask, pt, b_oth, up_own, back_own, *out_pieces,
+        scratch=[pltpu.VMEM((TOK, MODEL_WIDTH), BF16)],
+        name="backward_oth",
     )
     back = lax.all_to_all(back, ("l", "h", "c"), 0, 0, tiled=True)
     new_a, wire = call(

time: 218 us -> 221 us (1.014)
  Pallas kernels: 35.5 us -> 43.1 us
  starting transfers between devices: 63.3 us -> 68.1 us
  waiting for transfers between devices: 89.6 us -> 85.2 us
  local copies, waits for them, and re-layouts: 9.51 us -> 5.81 us
    pallas_call x11 -> x13, Pallas kernels: 35.5 us -> 43.1 us  [call(): pl.pallas_call(kernel, out_shape=out_shape, in_specs=[vmem] * len(args) +...]
    ppermute x30, waiting for transfers between devices: 55.5 us -> 50.9 us  [shift(): return lax.ppermute(value, axis, [(i, (i + by) % n) for i in range(n)])]
    ppermute x30, starting transfers between devices: 43.4 us -> 47.3 us  [shift(): return lax.ppermute(value, axis, [(i, (i + by) % n) for i in range(n)])]
    all_to_all x1, starting transfers between devices: 5.3 us -> 7.98 us  [shards(): wires = lax.all_to_all(wire, REP, 0, 0, tiled=True)]
    ppermute x3, starting transfers between devices: 9.55 us -> 6.97 us  [near_z(): lax.ppermute(value, Z, [(place(z), place(z + 1 if z % 2 else z - 1)) for...]
    slice x3 -> x1, local copies, waits for them, and re-layouts: 2.56 us -> 0.02 us  [shards(): in_oth = jnp.concatenate(ring_direct(w_oth[:TOK], 'y'), axis=0)]
    unnamed x53 -> x49, local copies, waits for them, and re-layouts: 5.47 us -> 4.31 us
  transfers between devices with their start and end apart: 42 -> 42, of which waited for: 20 -> 19; matrix products, arithmetic and copies ran while one was open for 3% -> 1% of each run, Pallas kernels for 6% -> 11%
where the time goes in v3:
time: 221 us
  waiting for transfers between devices  85.2 us (39%)
  starting transfers between devices  68.1 us (31%)
  Pallas kernels  43.1 us (20%)
  blocking collectives  13.8 us (6%)
  local copies, waits for them, and re-layouts  5.81 us (3%)
  other arithmetic  3.79 us (2%)
    ppermute x30, waiting for transfers between devices, shift(): return lax.ppermute(value, axis, [(i, (i + by) % n) for i in range(n)])  50.9 us
    ppermute x30, starting transfers between devices, shift(): return lax.ppermute(value, axis, [(i, (i + by) % n) for i in range(n)])  47.3 us
    pallas_call x13, Pallas kernels, call(): pl.pallas_call(kernel, out_shape=out_shape, in_specs=[vmem] * len(args) +...  43.1 us
    ppermute x8, waiting for transfers between devices, partner(): return lax.ppermute(value, axis, [(0, 1), (1, 0)])  19.7 us
    all_to_all x1, blocking collectives, shards(): back = lax.all_to_all(back, ('l', 'h', 'c'), 0, 0, tiled=True)  13.8 us
    ppermute x3, waiting for transfers between devices, near_z(): lax.ppermute(value, Z, [(place(z), place(z + 1 if z % 2 else z - 1)) for...  12.2 us
    all_to_all x1, starting transfers between devices, shards(): wires = lax.all_to_all(wire, REP, 0, 0, tiled=True)  7.98 us
    ppermute x3, starting transfers between devices, near_z(): lax.ppermute(value, Z, [(place(z), place(z + 1 if z % 2 else z - 1)) for...  6.97 us
  transfers between devices with their start and end apart: 42, of which 19 were waited for; matrix products, arithmetic and copies ran while one was open for 1% of the time, Pallas kernels for 11%

profile of v3, /device:TPU:2, one launch (start us, length us, event | category | flops | bytes accessed | tf_op | source)
XLA Modules:
  0.0 220.8 jit_solution(10579390372140826333)
XLA Ops:
  0.6 1.8 send.1.send_ref
  2.5 1.9 collective-permute-start.9
  4.4 1.9 own.1
  8.3 2.6 %pack.1.own_ref = bf16[144,4096]{1,0:T(8,128)(2,1)} custom-call(bf16[128,4096]{1,0:T(8,128)(2,1)} %x_ref.1, bf16[16,4096]{1,0:T(8,128)(2,1)} %bitcast.18), custom_call_target="tpu_custom_call" | custom-call | tf_op jit(solution)/shard_map/pack/pallas_call | solution.py:62
  10.9 5.0 %collective-permute-start.4 = (bf16[144,4096]{1,0:T(8,128)(2,1)}, bf16[144,4096]{1,0:T(8,128)(2,1)}, u32[]{:S(2)}, u32[]{:S(2)}) collective-permute-start(bf16[144,4096]{1,0:T(8,128)(2,1)} %pack.1.own_ref), channel_id=1, source_target_pairs={{0,38},{32,2},{2,32},{34,4},{4,34},{36,6},{6,36},{38,0},{1,39},{33... | collective-permute-start | bytes 3538952 | tf_op jit(solution)/shard_map/ppermute | solution.py:53
  15.9 1.6 collective-permute-start.2
  17.5 1.7 collective-permute-start.15
  19.2 1.7 collective-permute-start.16
  20.9 2.0 collective-permute-start.17
  23.6 1.9 collective-permute-done.15
  33.3 10.3 %collective-permute-done.7 = bf16[128,512]{1,0:T(8,128)(2,1)S(1)} collective-permute-done((bf16[128,512]{1,0:T(8,128)(2,1)S(1)}, bf16[128,512]{1,0:T(8,128)(2,1)S(1)}, u32[]{:S(2)}, u32[]{:S(2)}) %collective-permute-start.7) | collective-permute-done | bytes 131104 | tf_op jit(solution)/shard_map/ppermute | solution.py:42
  44.2 2.1 collective-permute-start.12
  46.3 2.7 %collective-permute-done.11 = bf16[128,512]{1,0:T(8,128)(2,1)S(1)} collective-permute-done((bf16[128,512]{1,0:T(8,128)(2,1)S(1)}, bf16[128,512]{1,0:T(8,128)(2,1)S(1)}, u32[]{:S(2)}, u32[]{:S(2)}) %collective-permute-start.11) | collective-permute-done | bytes 131104 | tf_op jit(solution)/shard_map/ppermute | solution.py:42
  50.7 2.9 %collective-permute-start.19 = (bf16[512,512]{1,0:T(8,128)(2,1)S(1)}, bf16[512,512]{1,0:T(8,128)(2,1)}, u32[]{:S(2)}, u32[]{:S(2)}) collective-permute-start(bf16[512,512]{1,0:T(8,128)(2,1)S(1)} %pad_maximum_fusion.1.refs_3_), channel_id=1, source_target_pairs={{0,24},{8,0},{16,8},{24,16},{1,25},{9,1},{17,9},{25,17},{2,26},{10... | collective-permute-start | bytes 1572872 | tf_op jit(solution)/shard_map/ppermute | solution.py:42
  53.6 2.2 collective-permute-start.8
  55.8 2.3 %collective-permute-start.13 = (bf16[512,512]{1,0:T(8,128)(2,1)S(1)}, bf16[512,512]{1,0:T(8,128)(2,1)S(1)}, u32[]{:S(2)}, u32[]{:S(2)}) collective-permute-start(bf16[512,512]{1,0:T(8,128)(2,1)S(1)} %pad_maximum_fusion.refs_4_), channel_id=1, source_target_pairs={{0,192},{64,0},{128,64},{192,128},{1,193},{65,1},{129,65},{193,129... | collective-permute-start | bytes 1572872 | tf_op jit(solution)/shard_map/ppermute | solution.py:42
  58.7 3.7 %arrange.1 = (bf16[256,4096]{1,0:T(8,128)(2,1)}, bf16[256,32]{1,0:T(8,128)(2,1)}, bf16[2,16,128]{2,1,0:T(8,128)(2,1)}) custom-call(bf16[144,4096]{1,0:T(8,128)(2,1)} %pack.1.own_ref, bf16[144,4096]{1,0:T(8,128)(2,1)} %collective-permute-done.4.oth_ref), custom_call_target="tpu_custom_call" | custom-call | tf_op jit(solution)/shard_map/arrange/pallas_call | solution.py:62
  66.2 4.4 %near.1.total_ref = f32[256,512]{1,0:T(8,128)} custom-call(bf16[256,4096]{1,0:T(8,128)(2,1)} %get-tuple-element.27.x_ref, bf16[256,32]{1,0:T(8,128)(2,1)} %get-tuple-element.29.p_ref, bf16[16,512]{1,0:T(8,128)(2,1)} %get-tuple-element.30.b_own_ref.b_ref, bf16[16,512]{1,0:T(8,128)(2,1)} %slice.80.b_oth_ref.b_ref, bf16[512,512]{1,0:T(8,128)(2,1)} %copy-done.9, ...), custom_call_target="tpu_custom_call" | custom-call | tf_op jit(solution)/shard_map/near/pallas_call | solution.py:62
  70.5 3.5 %collective-permute-done.8.refs_2_ = bf16[512,512]{1,0:T(8,128)(2,1)S(1)} collective-permute-done((bf16[512,512]{1,0:T(8,128)(2,1)S(1)}, bf16[512,512]{1,0:T(8,128)(2,1)S(1)}, u32[]{:S(2)}, u32[]{:S(2)}) %collective-permute-start.8) | collective-permute-done | bytes 524320 | tf_op jit(solution)/shard_map/ppermute | solution.py:42
  74.0 2.6 %collective-permute-start.23 = (bf16[512,512]{1,0:T(8,128)(2,1)S(1)}, bf16[512,512]{1,0:T(8,128)(2,1)}, u32[]{:S(2)}, u32[]{:S(2)}) collective-permute-start(bf16[512,512]{1,0:T(8,128)(2,1)S(1)} %collective-permute-done.8.refs_2_), channel_id=1, source_target_pairs={{0,24},{8,0},{16,8},{24,16},{1,25},{9,1},{17,9},{25,17},{2,26},{10... | collective-permute-start | bytes 1572872 | tf_op jit(solution)/shard_map/ppermute | solution.py:42
  76.6 3.1 %collective-permute-start.25 = (bf16[512,512]{1,0:T(8,128)(2,1)S(1)}, bf16[512,512]{1,0:T(8,128)(2,1)}, u32[]{:S(2)}, u32[]{:S(2)}) collective-permute-start(bf16[512,512]{1,0:T(8,128)(2,1)S(1)} %collective-permute-done.13.refs_6_), channel_id=1, source_target_pairs={{0,192},{64,0},{128,64},{192,128},{1,193},{65,1},{129,65},{193,129... | collective-permute-start | bytes 1572872 | tf_op jit(solution)/shard_map/ppermute | solution.py:42
  79.8 7.9 %collective-permute-done.20.own_ref = bf16[512,512]{1,0:T(8,128)(2,1)} collective-permute-done((bf16[512,512]{1,0:T(8,128)(2,1)}, bf16[512,512]{1,0:T(8,128)(2,1)}, u32[]{:S(2)}, u32[]{:S(2)}) %collective-permute-start.20) | collective-permute-done | bytes 524320 | tf_op jit(solution)/shard_map/ppermute | solution.py:42
  87.7 3.3 %hidden.1 = (bf16[256,512]{1,0:T(8,128)(2,1)}, bf16[2,128,512]{2,1,0:T(8,128)(2,1)}) custom-call(bf16[256,4096]{1,0:T(8,128)(2,1)} %get-tuple-element.27.x_ref, f32[256,512]{1,0:T(8,128)} %near.1.total_ref, bf16[512,512]{1,0:T(8,128)(2,1)} %collective-permute-done.20.own_ref, bf16[512,512]{1,0:T(8,128)(2,1)} %collective-permute-done.21.oth_ref), custom_call_target="tpu_custom_call" | custom-call | tf_op jit(solution)/shard_map/hidden/pallas_call | solution.py:62
  92.0 4.7 %output_send.1.refs_8_ = bf16[8,16,4096]{2,1,0:T(8,128)(2,1)} custom-call(bf16[256,512]{1,0:T(8,128)(2,1)} %get-tuple-element.33.hidden_ref, bf16[512,512]{1,0:T(8,128)(2,1)} %copy-done.1, bf16[512,512]{1,0:T(8,128)(2,1)} %copy-done.4, bf16[512,512]{1,0:T(8,128)(2,1)} %copy-done.2, bf16[512,512]{1,0:T(8,128)(2,1)} %collective-permute-done.23.refs_3_, ...), custom_call_target="tpu_custom_call" | custom-call | tf_op jit(solution)/shard_map/output_send/pallas_call | solution.py:62
  96.7 5.0 %output_keep.1 = f32[8,16,4096]{2,1,0:T(8,128)} custom-call(bf16[256,512]{1,0:T(8,128)(2,1)} %get-tuple-element.33.hidden_ref, bf16[512,512]{1,0:T(8,128)(2,1)} %copy-done.1, bf16[512,512]{1,0:T(8,128)(2,1)} %copy-done.4, bf16[512,512]{1,0:T(8,128)(2,1)} %copy-done.2, bf16[512,512]{1,0:T(8,128)(2,1)} %collective-permute-done.23.refs_3_, ...), custom_call_target="tpu_custom_call" | custom-call | tf_op jit(solution)/shard_map/output_keep/pallas_call | solution.py:62
  101.7 1.9 fusion.1
  104.2 9.6 %collective-permute-done.28 = bf16[4,16,2048]{2,1,0:T(8,128)(2,1)S(1)} collective-permute-done((bf16[4,16,2048]{2,1,0:T(8,128)(2,1)S(1)}, bf16[4,16,2048]{2,1,0:T(8,128)(2,1)S(1)}, u32[]{:S(2)}, u32[]{:S(2)}) %collective-permute-start.28) | collective-permute-done | bytes 262176 | tf_op jit(solution)/shard_map/ppermute | solution.py:53
  114.0 3.8 %collective-permute-start.30 = (bf16[16,4096]{1,0:T(8,128)(2,1)S(1)}, bf16[16,4096]{1,0:T(8,128)(2,1)S(1)}, u32[]{:S(2)}, u32[]{:S(2)}) collective-permute-start(bf16[16,4096]{1,0:T(8,128)(2,1)S(1)} %get-tuple-element.56), channel_id=1, source_target_pairs={{0,4},{2,6},{4,0},{6,2},{1,5},{3,7},{5,1},{7,3},{8,12},{10,14},{12... | collective-permute-start | bytes 393224 | tf_op jit(solution)/shard_map/ppermute | solution.py:42
  117.9 3.4 %collective-permute-start.31 = (bf16[16,4096]{1,0:T(8,128)(2,1)S(1)}, bf16[16,4096]{1,0:T(8,128)(2,1)S(1)}, u32[]{:S(2)}, u32[]{:S(2)}) collective-permute-start(bf16[16,4096]{1,0:T(8,128)(2,1)S(1)} %get-tuple-element.55), channel_id=1, source_target_pairs={{0,6},{2,0},{4,2},{6,4},{1,7},{3,1},{5,3},{7,5},{8,14},{10,8},{12,... | collective-permute-start | bytes 393224 | tf_op jit(solution)/shard_map/ppermute | solution.py:42
  122.0 6.1 %collective-permute-done.29.r1_ref = bf16[16,4096]{1,0:T(8,128)(2,1)S(1)} collective-permute-done((bf16[16,4096]{1,0:T(8,128)(2,1)S(1)}, bf16[16,4096]{1,0:T(8,128)(2,1)S(1)}, u32[]{:S(2)}, u32[]{:S(2)}) %collective-permute-start.29) | collective-permute-done | bytes 131104 | tf_op jit(solution)/shard_map/ppermute | solution.py:42
  128.0 2.8 %collective-permute-done.31.r3_ref = bf16[16,4096]{1,0:T(8,128)(2,1)S(1)} collective-permute-done((bf16[16,4096]{1,0:T(8,128)(2,1)S(1)}, bf16[16,4096]{1,0:T(8,128)(2,1)S(1)}, u32[]{:S(2)}, u32[]{:S(2)}) %collective-permute-start.31) | collective-permute-done | bytes 131104 | tf_op jit(solution)/shard_map/ppermute | solution.py:42
  131.5 2.2 %finish.1 = bf16[16,4096]{1,0:T(8,128)(2,1)} custom-call(f32[16,4096]{1,0:T(8,128)} %slice_bitcast_fusion.mine_ref, bf16[16,4096]{1,0:T(8,128)(2,1)} %copy-done.16, bf16[16,4096]{1,0:T(8,128)(2,1)} %copy-done.17, bf16[16,4096]{1,0:T(8,128)(2,1)} %copy-done.18, bf16[128,4096]{1,0:T(8,128)(2,1)} %targets_ref.1), custom_call_target="tpu_custom_call" | custom-call | tf_op jit(solution)/shard_map/finish/pallas_call | solution.py:62
  133.7 3.3 %collective-permute-start.32 = (bf16[16,4096]{1,0:T(8,128)(2,1)}, bf16[16,4096]{1,0:T(8,128)(2,1)S(1)}, u32[]{:S(2)}, u32[]{:S(2)}) collective-permute-start(bf16[16,4096]{1,0:T(8,128)(2,1)} %finish.1), channel_id=1, source_target_pairs={{0,6},{2,0},{4,2},{6,4},{1,7},{3,1},{5,3},{7,5},{8,14},{10,8},{12,... | collective-permute-start | bytes 393224 | tf_op jit(solution)/shard_map/ppermute | solution.py:42
  137.1 3.2 %collective-permute-start.33 = (bf16[16,4096]{1,0:T(8,128)(2,1)}, bf16[16,4096]{1,0:T(8,128)(2,1)S(1)}, u32[]{:S(2)}, u32[]{:S(2)}) collective-permute-start(bf16[16,4096]{1,0:T(8,128)(2,1)} %finish.1), channel_id=1, source_target_pairs={{0,4},{2,6},{4,0},{6,2},{1,5},{3,7},{5,1},{7,3},{8,12},{10,14},{12... | collective-permute-start | bytes 393224 | tf_op jit(solution)/shard_map/ppermute | solution.py:42
  140.4 3.8 %collective-permute-done.32 = bf16[16,4096]{1,0:T(8,128)(2,1)S(1)} collective-permute-done((bf16[16,4096]{1,0:T(8,128)(2,1)}, bf16[16,4096]{1,0:T(8,128)(2,1)S(1)}, u32[]{:S(2)}, u32[]{:S(2)}) %collective-permute-start.32) | collective-permute-done | bytes 131104 | tf_op jit(solution)/shard_map/ppermute | solution.py:42
  144.2 6.9 %collective-permute-done.33 = bf16[16,4096]{1,0:T(8,128)(2,1)S(1)} collective-permute-done((bf16[16,4096]{1,0:T(8,128)(2,1)}, bf16[16,4096]{1,0:T(8,128)(2,1)S(1)}, u32[]{:S(2)}, u32[]{:S(2)}) %collective-permute-start.33) | collective-permute-done | bytes 131104 | tf_op jit(solution)/shard_map/ppermute | solution.py:42
  152.2 2.2 collective-permute-start.35
  154.4 1.6 collective-permute-start.37
  155.9 5.4 %collective-permute-done.35.left_ref = bf16[4,16,2048]{2,1,0:T(8,128)(2,1)S(1)} collective-permute-done((bf16[4,16,2048]{2,1,0:T(8,128)(2,1)S(1)}, bf16[4,16,2048]{2,1,0:T(8,128)(2,1)S(1)}, u32[]{:S(2)}, u32[]{:S(2)}) %collective-permute-start.35) | collective-permute-done | bytes 262176 | tf_op jit(solution)/shard_map/ppermute | solution.py:46
  161.3 2.7 %collective-permute-done.37.right_ref = bf16[4,16,2048]{2,1,0:T(8,128)(2,1)S(1)} collective-permute-done((bf16[4,16,2048]{2,1,0:T(8,128)(2,1)S(1)}, bf16[4,16,2048]{2,1,0:T(8,128)(2,1)S(1)}, u32[]{:S(2)}, u32[]{:S(2)}) %collective-permute-start.37) | collective-permute-done | bytes 262176 | tf_op jit(solution)/shard_map/ppermute | solution.py:53
  164.8 4.1 %backward_own.1 = (f32[16,512]{1,0:T(8,128)}, f32[16,128]{1,0:T(8,128)}) custom-call(bf16[4,16,4096]{2,1,0:T(8,128)(2,1)} %copy-done.7, bf16[4,16,4096]{2,1,0:T(8,128)(2,1)} %copy-done.10, bf16[2,128,512]{2,1,0:T(8,128)(2,1)} %get-tuple-element.36.mask_ref, bf16[2,16,128]{2,1,0:T(8,128)(2,1)} %get-tuple-element.37.pt_ref, ...), custom_call_target="tpu_custom_call" | custom-call | tf_op jit(solution)/shard_map/backward_own/pallas_call | solution.py:62
  169.8 4.2 %backward_oth.1 = (f32[16,512]{1,0:T(8,128)}, bf16[2,16,512]{2,1,0:T(8,128)(2,1)}, f32[16,16,128]{2,1,0:T(8,128)}) custom-call(bf16[4,16,2048]{2,1,0:T(8,128)(2,1)} %copy-done.11, bf16[4,16,2048]{2,1,0:T(8,128)(2,1)} %copy-done.13, bf16[4,16,2048]{2,1,0:T(8,128)(2,1)} %copy-done.12, bf16[4,16,2048]{2,1,0:T(8,128)(2,1)} %copy-done.14, ...), custom_call_target="tpu_custom_call" | custom-call | tf_op jit(solution)/shard_map/backward_oth/pallas_call | solution.py:62
  174.0 13.8 %all_to_all.10.back_ref = f32[16,16,128]{2,1,0:T(8,128)} all-to-all(f32[16,16,128]{2,1,0:T(8,128)} %get-tuple-element.40), channel_id=1, replica_groups=mesh['y'=4,'l'=2,'x'=4,'h'=4,'c'=2] {'l','h','c'}, dimensions={0} | all-to-all | bytes 262144 | tf_op jit(solution)/shard_map/all_to_all | solution.py:378
  187.9 2.7 %down.1 = (f32[16,4096]{1,0:T(8,128)}, bf16[32,16,1152]{2,1,0:T(8,128)(2,1)}) custom-call(f32[16,16,128]{2,1,0:T(8,128)} %all_to_all.10.back_ref, bf16[128,4096]{1,0:T(8,128)(2,1)} %x_ref.1, bf16[16,4096]{1,0:T(8,128)(2,1)} %bitcast.19, bf16[2,16,512]{2,1,0:T(8,128)(2,1)} %get-tuple-element.41.up_ref), custom_call_target="tpu_custom_call" | custom-call | tf_op jit(solution)/shard_map/down/pallas_call | solution.py:62
  190.5 8.0 %all-to-all-start.1 = ((bf16[32,16,1152]{2,1,0:T(8,128)(2,1)}), bf16[32,16,1152]{2,1,0:T(8,128)(2,1)S(1)}, u32[]{:S(2)}, u32[]{:S(2)}) async-start(bf16[32,16,1152]{2,1,0:T(8,128)(2,1)} %get-tuple-element.42), calls=%async_computation.1 | async-start | bytes 2359296 | tf_op jit(solution)/shard_map/all_to_all | solution.py:385
  200.1 14.3 %collective-permute-done.40 = f32[16,512]{1,0:T(8,128)S(1)} collective-permute-done((f32[16,512]{1,0:T(8,128)S(1)}, f32[16,512]{1,0:T(8,128)S(1)}, u32[]{:S(2)}, u32[]{:S(2)}) %collective-permute-start.40) | collective-permute-done | bytes 32800 | tf_op jit(solution)/shard_map/ppermute | solution.py:46
  215.0 2.3 %all-to-all-done.1.wire_ref = bf16[32,16,1152]{2,1,0:T(8,128)(2,1)S(1)} async-done(((bf16[32,16,1152]{2,1,0:T(8,128)(2,1)}), bf16[32,16,1152]{2,1,0:T(8,128)(2,1)S(1)}, u32[]{:S(2)}, u32[]{:S(2)}) %all-to-all-start.1) | async-done | bytes 1179680 | tf_op jit(solution)/shard_map/all_to_all | solution.py:385
  218.4 2.4 %merge.1 = f32[128,1024]{1,0:T(8,128)} custom-call(bf16[32,16,1152]{2,1,0:T(8,128)(2,1)} %copy-done.6, bf16[128,1024]{1,0:T(8,128)(2,1)} %w_ref.1), custom_call_target="tpu_custom_call" | custom-call | tf_op jit(solution)/shard_map/merge/pallas_call | solution.py:62
  (116 shorter events, 26.4 us)
Async XLA Ops:
  2.5 15.0 %collective-permute-start.9 = (bf16[272,512]{1,0:T(8,128)(2,1)}, bf16[272,512]{1,0:T(8,128)(2,1)S(1)}, u32[]{:S(2)}, u32[]{:S(2)}) collective-permute-start(bf16[272,512]{1,0:T(8,128)(2,1)} %send.1.send_ref), channel_id=1, source_target_pairs={{0,32},{32,0},{1,33},{33,1},{2,34},{34,2},{3,35},{35,3},{4,36},{36... | collective-permute-start | bytes 835592 | tf_op jit(solution)/shard_map/ppermute | solution.py:46
  6.3 9.7 %collective-permute-start = (bf16[128,512]{1,0:T(8,128)(2,1)}, bf16[128,512]{1,0:T(8,128)(2,1)S(1)}, u32[]{:S(2)}, u32[]{:S(2)}) collective-permute-start(bf16[128,512]{1,0:T(8,128)(2,1)} %get-tuple-element.24), channel_id=1, source_target_pairs={{0,8},{8,16},{16,24},{24,0},{1,9},{9,17},{17,25},{25,1},{2,10},{10... | collective-permute-start | bytes 393224 | tf_op jit(solution)/shard_map/ppermute | solution.py:42
  7.7 13.1 %collective-permute-start.1 = (bf16[128,512]{1,0:T(8,128)(2,1)}, bf16[128,512]{1,0:T(8,128)(2,1)S(1)}, u32[]{:S(2)}, u32[]{:S(2)}) collective-permute-start(bf16[128,512]{1,0:T(8,128)(2,1)} %get-tuple-element.24), channel_id=1, source_target_pairs={{0,24},{8,0},{16,8},{24,16},{1,25},{9,1},{17,9},{25,17},{2,26},{10... | collective-permute-start | bytes 393224 | tf_op jit(solution)/shard_map/ppermute | solution.py:42
  10.9 47.2 %collective-permute-start.4 = (bf16[144,4096]{1,0:T(8,128)(2,1)}, bf16[144,4096]{1,0:T(8,128)(2,1)}, u32[]{:S(2)}, u32[]{:S(2)}) collective-permute-start(bf16[144,4096]{1,0:T(8,128)(2,1)} %pack.1.own_ref), channel_id=1, source_target_pairs={{0,38},{32,2},{2,32},{34,4},{4,34},{36,6},{6,36},{38,0},{1,39},{33... | collective-permute-start | bytes 3538952 | tf_op jit(solution)/shard_map/ppermute | solution.py:53
  15.9 6.9 %collective-permute-start.2 = (bf16[128,512]{1,0:T(8,128)(2,1)S(1)}, bf16[128,512]{1,0:T(8,128)(2,1)S(1)}, u32[]{:S(2)}, u32[]{:S(2)}) collective-permute-start(bf16[128,512]{1,0:T(8,128)(2,1)S(1)} %collective-permute-done), channel_id=1, source_target_pairs={{0,8},{8,16},{16,24},{24,0},{1,9},{9,17},{17,25},{25,1},{2,10},{10... | collective-permute-start | bytes 393224 | tf_op jit(solution)/shard_map/ppermute | solution.py:42
  17.5 8.0 %collective-permute-start.15 = (bf16[128,512]{1,0:T(8,128)(2,1)S(1)}, bf16[128,512]{1,0:T(8,128)(2,1)S(1)}, u32[]{:S(2)}, u32[]{:S(2)}) collective-permute-start(bf16[128,512]{1,0:T(8,128)(2,1)S(1)} %get-tuple-element.58), channel_id=1, source_target_pairs={{0,64},{64,128},{128,192},{192,0},{1,65},{65,129},{129,193},{193,1... | collective-permute-start | bytes 393224 | tf_op jit(solution)/shard_map/ppermute | solution.py:42
  19.2 7.8 %collective-permute-start.16 = (bf16[128,512]{1,0:T(8,128)(2,1)S(1)}, bf16[128,512]{1,0:T(8,128)(2,1)S(1)}, u32[]{:S(2)}, u32[]{:S(2)}) collective-permute-start(bf16[128,512]{1,0:T(8,128)(2,1)S(1)} %get-tuple-element.58), channel_id=1, source_target_pairs={{0,192},{64,0},{128,64},{192,128},{1,193},{65,1},{129,65},{193,129... | collective-permute-start | bytes 393224 | tf_op jit(solution)/shard_map/ppermute | solution.py:42
  20.9 8.3 %collective-permute-start.17 = (bf16[128,512]{1,0:T(8,128)(2,1)S(1)}, bf16[128,512]{1,0:T(8,128)(2,1)S(1)}, u32[]{:S(2)}, u32[]{:S(2)}) collective-permute-start(bf16[128,512]{1,0:T(8,128)(2,1)S(1)} %get-tuple-element.58), channel_id=1, source_target_pairs={{0,128},{64,192},{128,0},{192,64},{1,129},{65,193},{129,1},{193,65... | collective-permute-start | bytes 393224 | tf_op jit(solution)/shard_map/ppermute | solution.py:42
  22.9 8.4 %collective-permute-start.5 = (bf16[128,512]{1,0:T(8,128)(2,1)S(1)}, bf16[128,512]{1,0:T(8,128)(2,1)S(1)}, u32[]{:S(2)}, u32[]{:S(2)}) collective-permute-start(bf16[128,512]{1,0:T(8,128)(2,1)S(1)} %copy-done.19), channel_id=1, source_target_pairs={{0,64},{64,128},{128,192},{192,0},{1,65},{65,129},{129,193},{193,1... | collective-permute-start | bytes 393224 | tf_op jit(solution)/shard_map/ppermute | solution.py:42
  23.6 38.8 %copy-start.9 = (bf16[512,512]{1,0:T(8,128)(2,1)}, bf16[512,512]{1,0:T(8,128)(2,1)S(1)}, u32[]{:S(2)}) copy-start(bf16[512,512]{1,0:T(8,128)(2,1)S(1)} %constant_dynamic-update-slice_fusion.refs_0_) | copy-start | bytes 1572868
  25.6 6.5 %collective-permute-start.6 = (bf16[128,512]{1,0:T(8,128)(2,1)S(1)}, bf16[128,512]{1,0:T(8,128)(2,1)S(1)}, u32[]{:S(2)}, u32[]{:S(2)}) collective-permute-start(bf16[128,512]{1,0:T(8,128)(2,1)S(1)} %copy-done.19), channel_id=1, source_target_pairs={{0,192},{64,0},{128,64},{192,128},{1,193},{65,1},{129,65},{193,129... | collective-permute-start | bytes 393224 | tf_op jit(solution)/shard_map/ppermute | solution.py:42
  26.9 26.7 %collective-permute-start.3 = (bf16[512,512]{1,0:T(8,128)(2,1)S(1)}, bf16[512,512]{1,0:T(8,128)(2,1)}, u32[]{:S(2)}, u32[]{:S(2)}) collective-permute-start(bf16[512,512]{1,0:T(8,128)(2,1)S(1)} %constant_dynamic-update-slice_fusion.refs_0_), channel_id=1, source_target_pairs={{0,64},{64,128},{128,192},{192,0},{1,65},{65,129},{129,193},{193,1... | collective-permute-start | bytes 1572872 | tf_op jit(solution)/shard_map/ppermute | solution.py:42
  29.2 33.2 %copy-start.8 = (bf16[512,512]{1,0:T(8,128)(2,1)}, bf16[512,512]{1,0:T(8,128)(2,1)S(1)}, u32[]{:S(2)}) copy-start(bf16[512,512]{1,0:T(8,128)(2,1)S(1)} %pad_maximum_fusion.1.refs_3_) | copy-start | bytes 1572868
  29.2 26.6 %collective-permute-start.18 = (bf16[512,512]{1,0:T(8,128)(2,1)S(1)}, bf16[512,512]{1,0:T(8,128)(2,1)}, u32[]{:S(2)}, u32[]{:S(2)}) collective-permute-start(bf16[512,512]{1,0:T(8,128)(2,1)S(1)} %pad_maximum_fusion.1.refs_3_), channel_id=1, source_target_pairs={{0,8},{8,16},{16,24},{24,0},{1,9},{9,17},{17,25},{25,1},{2,10},{10... | collective-permute-start | bytes 1572872 | tf_op jit(solution)/shard_map/ppermute | solution.py:42
  31.3 12.3 %collective-permute-start.7 = (bf16[128,512]{1,0:T(8,128)(2,1)S(1)}, bf16[128,512]{1,0:T(8,128)(2,1)S(1)}, u32[]{:S(2)}, u32[]{:S(2)}) collective-permute-start(bf16[128,512]{1,0:T(8,128)(2,1)S(1)} %collective-permute-done.5), channel_id=1, source_target_pairs={{0,64},{64,128},{128,192},{192,0},{1,65},{65,129},{129,193},{193,1... | collective-permute-start | bytes 393224 | tf_op jit(solution)/shard_map/ppermute | solution.py:42
  32.1 12.1 %collective-permute-start.10 = (bf16[128,512]{1,0:T(8,128)(2,1)S(1)}, bf16[128,512]{1,0:T(8,128)(2,1)S(1)}, u32[]{:S(2)}, u32[]{:S(2)}) collective-permute-start(bf16[128,512]{1,0:T(8,128)(2,1)S(1)} %get-tuple-element.59), channel_id=1, source_target_pairs={{0,8},{8,16},{16,24},{24,0},{1,9},{9,17},{17,25},{25,1},{2,10},{10... | collective-permute-start | bytes 393224 | tf_op jit(solution)/shard_map/ppermute | solution.py:42
  43.6 5.4 %collective-permute-start.11 = (bf16[128,512]{1,0:T(8,128)(2,1)S(1)}, bf16[128,512]{1,0:T(8,128)(2,1)S(1)}, u32[]{:S(2)}, u32[]{:S(2)}) collective-permute-start(bf16[128,512]{1,0:T(8,128)(2,1)S(1)} %get-tuple-element.59), channel_id=1, source_target_pairs={{0,24},{8,0},{16,8},{24,16},{1,25},{9,1},{17,9},{25,17},{2,26},{10... | collective-permute-start | bytes 393224 | tf_op jit(solution)/shard_map/ppermute | solution.py:42
  44.2 6.5 %collective-permute-start.12 = (bf16[128,512]{1,0:T(8,128)(2,1)S(1)}, bf16[128,512]{1,0:T(8,128)(2,1)S(1)}, u32[]{:S(2)}, u32[]{:S(2)}) collective-permute-start(bf16[128,512]{1,0:T(8,128)(2,1)S(1)} %get-tuple-element.59), channel_id=1, source_target_pairs={{0,16},{8,24},{16,0},{24,8},{1,17},{9,25},{17,1},{25,9},{2,18},{10... | collective-permute-start | bytes 393224 | tf_op jit(solution)/shard_map/ppermute | solution.py:42
  46.3 24.2 %copy-start.1 = (bf16[512,512]{1,0:T(8,128)(2,1)}, bf16[512,512]{1,0:T(8,128)(2,1)S(1)}, u32[]{:S(2)}) copy-start(bf16[512,512]{1,0:T(8,128)(2,1)S(1)} %constant_dynamic-update-slice_fusion.4.refs_0_) | copy-start | bytes 1572868
  49.0 15.0 %collective-permute-start.14 = (bf16[512,512]{1,0:T(8,128)(2,1)S(1)}, bf16[512,512]{1,0:T(8,128)(2,1)}, u32[]{:S(2)}, u32[]{:S(2)}) collective-permute-start(bf16[512,512]{1,0:T(8,128)(2,1)S(1)} %constant_dynamic-update-slice_fusion.refs_0_), channel_id=1, source_target_pairs={{0,192},{64,0},{128,64},{192,128},{1,193},{65,1},{129,65},{193,129... | collective-permute-start | bytes 1572872 | tf_op jit(solution)/shard_map/ppermute | solution.py:42
  50.7 15.3 %collective-permute-start.19 = (bf16[512,512]{1,0:T(8,128)(2,1)S(1)}, bf16[512,512]{1,0:T(8,128)(2,1)}, u32[]{:S(2)}, u32[]{:S(2)}) collective-permute-start(bf16[512,512]{1,0:T(8,128)(2,1)S(1)} %pad_maximum_fusion.1.refs_3_), channel_id=1, source_target_pairs={{0,24},{8,0},{16,8},{24,16},{1,25},{9,1},{17,9},{25,17},{2,26},{10... | collective-permute-start | bytes 1572872 | tf_op jit(solution)/shard_map/ppermute | solution.py:42
  53.6 20.4 %collective-permute-start.8 = (bf16[512,512]{1,0:T(8,128)(2,1)S(1)}, bf16[512,512]{1,0:T(8,128)(2,1)S(1)}, u32[]{:S(2)}, u32[]{:S(2)}) collective-permute-start(bf16[512,512]{1,0:T(8,128)(2,1)S(1)} %constant_dynamic-update-slice_fusion.4.refs_0_), channel_id=1, source_target_pairs={{0,24},{8,0},{16,8},{24,16},{1,25},{9,1},{17,9},{25,17},{2,26},{10... | collective-permute-start | bytes 1572872 | tf_op jit(solution)/shard_map/ppermute | solution.py:42
  55.8 18.2 %collective-permute-start.13 = (bf16[512,512]{1,0:T(8,128)(2,1)S(1)}, bf16[512,512]{1,0:T(8,128)(2,1)S(1)}, u32[]{:S(2)}, u32[]{:S(2)}) collective-permute-start(bf16[512,512]{1,0:T(8,128)(2,1)S(1)} %pad_maximum_fusion.refs_4_), channel_id=1, source_target_pairs={{0,192},{64,0},{128,64},{192,128},{1,193},{65,1},{129,65},{193,129... | collective-permute-start | bytes 1572872 | tf_op jit(solution)/shard_map/ppermute | solution.py:42
  58.1 18.5 %collective-permute-start.21 = (bf16[512,512]{1,0:T(8,128)(2,1)}, bf16[512,512]{1,0:T(8,128)(2,1)}, u32[]{:S(2)}, u32[]{:S(2)}) collective-permute-start(bf16[512,512]{1,0:T(8,128)(2,1)} %collective-permute-done.18.refs_4_), channel_id=1, source_target_pairs={{0,8},{8,16},{16,24},{24,0},{1,9},{9,17},{17,25},{25,1},{2,10},{10... | collective-permute-start | bytes 1572872 | tf_op jit(solution)/shard_map/ppermute | solution.py:42
  64.0 27.0 %collective-permute-start.22 = (bf16[512,512]{1,0:T(8,128)(2,1)S(1)}, bf16[512,512]{1,0:T(8,128)(2,1)S(1)}, u32[]{:S(2)}, u32[]{:S(2)}) collective-permute-start(bf16[512,512]{1,0:T(8,128)(2,1)S(1)} %constant_dynamic-update-slice_fusion.4.refs_0_), channel_id=1, source_target_pairs={{0,8},{8,16},{16,24},{24,0},{1,9},{9,17},{17,25},{25,1},{2,10},{10... | collective-permute-start | bytes 1572872 | tf_op jit(solution)/shard_map/ppermute | solution.py:42
  66.0 25.0 %collective-permute-start.24 = (bf16[512,512]{1,0:T(8,128)(2,1)S(1)}, bf16[512,512]{1,0:T(8,128)(2,1)S(1)}, u32[]{:S(2)}, u32[]{:S(2)}) collective-permute-start(bf16[512,512]{1,0:T(8,128)(2,1)S(1)} %pad_maximum_fusion.refs_4_), channel_id=1, source_target_pairs={{0,64},{64,128},{128,192},{192,0},{1,65},{65,129},{129,193},{193,1... | collective-permute-start | bytes 1572872 | tf_op jit(solution)/shard_map/ppermute | solution.py:42
  74.0 13.7 %collective-permute-start.20 = (bf16[512,512]{1,0:T(8,128)(2,1)}, bf16[512,512]{1,0:T(8,128)(2,1)}, u32[]{:S(2)}, u32[]{:S(2)}) collective-permute-start(bf16[512,512]{1,0:T(8,128)(2,1)} %collective-permute-done.3.refs_1_), channel_id=1, source_target_pairs={{0,64},{64,128},{128,192},{192,0},{1,65},{65,129},{129,193},{193,1... | collective-permute-start | bytes 1572872 | tf_op jit(solution)/shard_map/ppermute | solution.py:42
  74.0 17.0 %copy-start.3 = (bf16[512,512]{1,0:T(8,128)(2,1)}, bf16[512,512]{1,0:T(8,128)(2,1)S(1)}, u32[]{:S(2)}) copy-start(bf16[512,512]{1,0:T(8,128)(2,1)S(1)} %collective-permute-done.13.refs_6_) | copy-start | bytes 1572868
  74.0 16.9 %collective-permute-start.23 = (bf16[512,512]{1,0:T(8,128)(2,1)S(1)}, bf16[512,512]{1,0:T(8,128)(2,1)}, u32[]{:S(2)}, u32[]{:S(2)}) collective-permute-start(bf16[512,512]{1,0:T(8,128)(2,1)S(1)} %collective-permute-done.8.refs_2_), channel_id=1, source_target_pairs={{0,24},{8,0},{16,8},{24,16},{1,25},{9,1},{17,9},{25,17},{2,26},{10... | collective-permute-start | bytes 1572872 | tf_op jit(solution)/shard_map/ppermute | solution.py:42
  76.6 14.4 %collective-permute-start.25 = (bf16[512,512]{1,0:T(8,128)(2,1)S(1)}, bf16[512,512]{1,0:T(8,128)(2,1)}, u32[]{:S(2)}, u32[]{:S(2)}) collective-permute-start(bf16[512,512]{1,0:T(8,128)(2,1)S(1)} %collective-permute-done.13.refs_6_), channel_id=1, source_target_pairs={{0,192},{64,0},{128,64},{192,128},{1,193},{65,1},{129,65},{193,129... | collective-permute-start | bytes 1572872 | tf_op jit(solution)/shard_map/ppermute | solution.py:42
  96.7 5.0 %collective-permute-start.26 = (bf16[8,16,4096]{2,1,0:T(8,128)(2,1)}, bf16[8,16,4096]{2,1,0:T(8,128)(2,1)S(1)}, u32[]{:S(2)}, u32[]{:S(2)}) collective-permute-start(bf16[8,16,4096]{2,1,0:T(8,128)(2,1)} %output_send.1.refs_8_), channel_id=1, source_target_pairs={{0,1},{1,0},{2,3},{3,2},{4,5},{5,4},{6,7},{7,6},{8,9},{9,8},{10,11... | collective-permute-start | bytes 3145736 | tf_op jit(solution)/shard_map/ppermute | solution.py:46
  103.7 10.0 %collective-permute-start.28 = (bf16[4,16,2048]{2,1,0:T(8,128)(2,1)S(1)}, bf16[4,16,2048]{2,1,0:T(8,128)(2,1)S(1)}, u32[]{:S(2)}, u32[]{:S(2)}) collective-permute-start(bf16[4,16,2048]{2,1,0:T(8,128)(2,1)S(1)} %maximum_select_fusion), channel_id=1, source_target_pairs={{0,38},{32,2},{2,32},{34,4},{4,34},{36,6},{6,36},{38,0},{1,39},{33... | collective-permute-start | bytes 786440 | tf_op jit(solution)/shard_map/ppermute | solution.py:53
  104.2 9.6 %collective-permute-start.27 = (bf16[4,16,2048]{2,1,0:T(8,128)(2,1)S(1)}, bf16[4,16,2048]{2,1,0:T(8,128)(2,1)S(1)}, u32[]{:S(2)}, u32[]{:S(2)}) collective-permute-start(bf16[4,16,2048]{2,1,0:T(8,128)(2,1)S(1)} %slice.83), channel_id=1, source_target_pairs={{0,32},{32,0},{1,33},{33,1},{2,34},{34,2},{3,35},{35,3},{4,36},{36... | collective-permute-start | bytes 786440 | tf_op jit(solution)/shard_map/ppermute | solution.py:46
  114.0 14.1 %collective-permute-start.29 = (bf16[16,4096]{1,0:T(8,128)(2,1)S(1)}, bf16[16,4096]{1,0:T(8,128)(2,1)S(1)}, u32[]{:S(2)}, u32[]{:S(2)}) collective-permute-start(bf16[16,4096]{1,0:T(8,128)(2,1)S(1)} %get-tuple-element.57), channel_id=1, source_target_pairs={{0,2},{2,4},{4,6},{6,0},{1,3},{3,5},{5,7},{7,1},{8,10},{10,12},{12... | collective-permute-start | bytes 393224 | tf_op jit(solution)/shard_map/ppermute | solution.py:42
  114.0 14.0 %collective-permute-start.30 = (bf16[16,4096]{1,0:T(8,128)(2,1)S(1)}, bf16[16,4096]{1,0:T(8,128)(2,1)S(1)}, u32[]{:S(2)}, u32[]{:S(2)}) collective-permute-start(bf16[16,4096]{1,0:T(8,128)(2,1)S(1)} %get-tuple-element.56), channel_id=1, source_target_pairs={{0,4},{2,6},{4,0},{6,2},{1,5},{3,7},{5,1},{7,3},{8,12},{10,14},{12... | collective-permute-start | bytes 393224 | tf_op jit(solution)/shard_map/ppermute | solution.py:42
  117.9 13.0 %collective-permute-start.31 = (bf16[16,4096]{1,0:T(8,128)(2,1)S(1)}, bf16[16,4096]{1,0:T(8,128)(2,1)S(1)}, u32[]{:S(2)}, u32[]{:S(2)}) collective-permute-start(bf16[16,4096]{1,0:T(8,128)(2,1)S(1)} %get-tuple-element.55), channel_id=1, source_target_pairs={{0,6},{2,0},{4,2},{6,4},{1,7},{3,1},{5,3},{7,5},{8,14},{10,8},{12,... | collective-permute-start | bytes 393224 | tf_op jit(solution)/shard_map/ppermute | solution.py:42
  133.7 10.4 %collective-permute-start.32 = (bf16[16,4096]{1,0:T(8,128)(2,1)}, bf16[16,4096]{1,0:T(8,128)(2,1)S(1)}, u32[]{:S(2)}, u32[]{:S(2)}) collective-permute-start(bf16[16,4096]{1,0:T(8,128)(2,1)} %finish.1), channel_id=1, source_target_pairs={{0,6},{2,0},{4,2},{6,4},{1,7},{3,1},{5,3},{7,5},{8,14},{10,8},{12,... | collective-permute-start | bytes 393224 | tf_op jit(solution)/shard_map/ppermute | solution.py:42
  137.1 14.0 %collective-permute-start.33 = (bf16[16,4096]{1,0:T(8,128)(2,1)}, bf16[16,4096]{1,0:T(8,128)(2,1)S(1)}, u32[]{:S(2)}, u32[]{:S(2)}) collective-permute-start(bf16[16,4096]{1,0:T(8,128)(2,1)} %finish.1), channel_id=1, source_target_pairs={{0,4},{2,6},{4,0},{6,2},{1,5},{3,7},{5,1},{7,3},{8,12},{10,14},{12... | collective-permute-start | bytes 393224 | tf_op jit(solution)/shard_map/ppermute | solution.py:42
  140.3 10.7 %collective-permute-start.34 = (bf16[16,4096]{1,0:T(8,128)(2,1)}, bf16[16,4096]{1,0:T(8,128)(2,1)S(1)}, u32[]{:S(2)}, u32[]{:S(2)}) collective-permute-start(bf16[16,4096]{1,0:T(8,128)(2,1)} %finish.1), channel_id=1, source_target_pairs={{0,2},{2,4},{4,6},{6,0},{1,3},{3,5},{5,7},{7,1},{8,10},{10,12},{12... | collective-permute-start | bytes 393224 | tf_op jit(solution)/shard_map/ppermute | solution.py:42
  152.0 12.0 %collective-permute-start.39 = (bf16[4,16,4096]{2,1,0:T(8,128)(2,1)S(1)}, bf16[4,16,4096]{2,1,0:T(8,128)(2,1)S(1)}, u32[]{:S(2)}, u32[]{:S(2)}) collective-permute-start(bf16[4,16,4096]{2,1,0:T(8,128)(2,1)S(1)} %pad_maximum_fusion.2.q_ref), channel_id=1, source_target_pairs={{0,1},{1,0},{2,3},{3,2},{4,5},{5,4},{6,7},{7,6},{8,9},{9,8},{10,11... | collective-permute-start | bytes 1572872 | tf_op jit(solution)/shard_map/ppermute | solution.py:46
  152.2 9.2 %collective-permute-start.35 = (bf16[4,16,2048]{2,1,0:T(8,128)(2,1)S(1)}, bf16[4,16,2048]{2,1,0:T(8,128)(2,1)S(1)}, u32[]{:S(2)}, u32[]{:S(2)}) collective-permute-start(bf16[4,16,2048]{2,1,0:T(8,128)(2,1)S(1)} %get-tuple-element.54), channel_id=1, source_target_pairs={{0,32},{32,0},{1,33},{33,1},{2,34},{34,2},{3,35},{35,3},{4,36},{36... | collective-permute-start | bytes 786440 | tf_op jit(solution)/shard_map/ppermute | solution.py:46
  154.4 9.6 %collective-permute-start.37 = (bf16[4,16,2048]{2,1,0:T(8,128)(2,1)S(1)}, bf16[4,16,2048]{2,1,0:T(8,128)(2,1)S(1)}, u32[]{:S(2)}, u32[]{:S(2)}) collective-permute-start(bf16[4,16,2048]{2,1,0:T(8,128)(2,1)S(1)} %get-tuple-element.53), channel_id=1, source_target_pairs={{0,38},{32,2},{2,32},{34,4},{4,34},{36,6},{6,36},{38,0},{1,39},{33... | collective-permute-start | bytes 786440 | tf_op jit(solution)/shard_map/ppermute | solution.py:53
  161.3 7.6 %collective-permute-start.36 = (bf16[4,16,2048]{2,1,0:T(8,128)(2,1)S(1)}, bf16[4,16,2048]{2,1,0:T(8,128)(2,1)S(1)}, u32[]{:S(2)}, u32[]{:S(2)}) collective-permute-start(bf16[4,16,2048]{2,1,0:T(8,128)(2,1)S(1)} %collective-permute-done.35.left_ref), channel_id=1, source_target_pairs={{0,1},{1,0},{2,3},{3,2},{4,5},{5,4},{6,7},{7,6},{8,9},{9,8},{10,11... | collective-permute-start | bytes 786440 | tf_op jit(solution)/shard_map/ppermute | solution.py:46
  164.0 5.0 %collective-permute-start.38 = (bf16[4,16,2048]{2,1,0:T(8,128)(2,1)S(1)}, bf16[4,16,2048]{2,1,0:T(8,128)(2,1)S(1)}, u32[]{:S(2)}, u32[]{:S(2)}) collective-permute-start(bf16[4,16,2048]{2,1,0:T(8,128)(2,1)S(1)} %collective-permute-done.37.right_ref), channel_id=1, source_target_pairs={{0,1},{1,0},{2,3},{3,2},{4,5},{5,4},{6,7},{7,6},{8,9},{9,8},{10,11... | collective-permute-start | bytes 786440 | tf_op jit(solution)/shard_map/ppermute | solution.py:46
  174.0 24.5 %copy-start.21 = (f32[16,512]{1,0:T(8,128)S(1)}, f32[16,512]{1,0:T(8,128)}, u32[]{:S(2)}) copy-start(f32[16,512]{1,0:T(8,128)} %get-tuple-element.44) | copy-start | bytes 98308
  174.0 40.4 %copy-start.15 = (f32[16,512]{1,0:T(8,128)S(1)}, f32[16,512]{1,0:T(8,128)}, u32[]{:S(2)}) copy-start(f32[16,512]{1,0:T(8,128)} %get-tuple-element.38.up_own_ref) | copy-start | bytes 98308
  190.5 26.8 %all-to-all-start.1 = ((bf16[32,16,1152]{2,1,0:T(8,128)(2,1)}), bf16[32,16,1152]{2,1,0:T(8,128)(2,1)S(1)}, u32[]{:S(2)}, u32[]{:S(2)}) async-start(bf16[32,16,1152]{2,1,0:T(8,128)(2,1)} %get-tuple-element.42), calls=%async_computation.1 | async-start | bytes 2359296 | tf_op jit(solution)/shard_map/all_to_all | solution.py:385
  198.5 15.9 %collective-permute-start.40 = (f32[16,512]{1,0:T(8,128)S(1)}, f32[16,512]{1,0:T(8,128)S(1)}, u32[]{:S(2)}, u32[]{:S(2)}) collective-permute-start(f32[16,512]{1,0:T(8,128)S(1)} %copy-done.21), channel_id=1, source_target_pairs={{0,32},{32,0},{1,33},{33,1},{2,34},{34,2},{3,35},{35,3},{4,36},{36... | collective-permute-start | bytes 98312 | tf_op jit(solution)/shard_map/ppermute | solution.py:46
  (16 other events, 89.3 us)

commit v4 on v2

--- a/solution.py
+++ b/solution.py
@@ -12,6 +12,7 @@
 RANK = 16
 ROWS = 16
 BLOCK = 128
+HALF = 64
 HID = 512
 SIDE = MODEL_WIDTH // 2
 REP = ("y", "l", "x")
@@ -77,9 +78,9 @@
 
 
 def token_row(i):
-    h, c = lax.axis_index("h"), lax.axis_index("c")
-    j, e = (i // 2) % 4, i % 2
-    return pl.multiple_of((((h + j) % 4) * 2 + (c + e) % 2) * ROWS, ROWS)
+    c = lax.axis_index("c")
+    h, e = (i // 2) % 4, i % 2
+    return pl.multiple_of((h * 2 + (c + e) % 2) * ROWS, ROWS)
 
 
 def column(dy, side, dx):
@@ -101,43 +102,65 @@
     b_own_ref[...] = b_ref[:, lanes(mine, HID)]
 
 
-def pack_kernel(tokens_ref, a_ref, out_ref):
-    out_ref[:TOK] = tokens_ref[...]
-    out_ref[TOK:, :TOK] = dot_nt(a_ref[...], tokens_ref[...]).astype(BF16)
-
-
-def arrange_kernel(own_ref, oth_ref, x_ref, p_ref, turned_ref):
-    l = lax.axis_index("l")
-    for k, ref in enumerate((own_ref, oth_ref)):
-        turned_ref[k] = ref[TOK:, :TOK].astype(F32).T.astype(BF16)
-    cols = [column(dy, l, dx) for dy in RING for dx in RING]
-    cols += [column(dy, 1 - l, dx) for dx in RING for dy in RING]
+def pack_kernel(tokens_ref, a_ref, out_ref, p_ref):
+    c = lax.axis_index("c")
+    p = dot_nt(a_ref[...], tokens_ref[...]).astype(BF16)
+    out_ref[:HALF] = tokens_ref[pl.ds(pl.multiple_of(c * HALF, HALF), HALF), :]
+    out_ref[HALF:, :TOK] = p
+    p_ref[...] = p
+
+
+def arrange_kernel(own_ref, oth_ref, oth_core_ref, p_own_ref, near_ref, far_ref, p_ref, pt_ref, turned_ref):
+    l, c = lax.axis_index("l"), lax.axis_index("c")
+    p_oth = oth_ref[HALF:, :TOK]
+    pt_ref[0] = p_own_ref[...]
+    pt_ref[1] = p_oth
+    turned_ref[0] = p_own_ref[...].astype(F32).T.astype(BF16)
+    turned_ref[1] = p_oth.astype(F32).T.astype(BF16)
+    near = [column(dy, l, dx) for dy in RING[:3] for dx in RING]
+    near += [column(dy, 1 - l, dx) for dx in RING[:3] for dy in RING]
+    far = [column(RING[3], l, dx) for dx in RING] + [column(dy, 1 - l, RING[3]) for dy in RING]
     p_ref[...] = jnp.zeros_like(p_ref)
     for i in range(16):
-        src = own_ref if i < 8 else oth_ref
+        here = slice(i * ROWS, (i + 1) * ROWS)
         row = token_row(i)
         lane = 0 if i < 8 else RANK
-        p_ref[i * ROWS : (i + 1) * ROWS, lane : lane + RANK] = turned_ref[
-            i // 8, pl.ds(row, ROWS), :
-        ]
-        for j in range(32):
-            x_ref[i * ROWS : (i + 1) * ROWS, j * BLOCK : (j + 1) * BLOCK] = src[
-                pl.ds(row, ROWS), lanes(cols[j], BLOCK)
-            ]
+        p_ref[here, lane : lane + RANK] = turned_ref[i // 8, pl.ds(row, ROWS), :]
+        half = ((i // 2) % 4) // 2
+        row_oth = pl.multiple_of(row - half * HALF, ROWS)
+        for ref, cols in ((near_ref, near), (far_ref, far)):
+            for j, col in enumerate(cols):
+                if i < 8:
+                    block = own_ref[pl.ds(row, ROWS), lanes(col, BLOCK)]
+                else:
+                    block = jnp.where(
+                        c == half,
+                        oth_ref[pl.ds(row_oth, ROWS), lanes(col, BLOCK)],
+                        oth_core_ref[pl.ds(row_oth, ROWS), lanes(col, BLOCK)],
+                    )
+                ref[here, j * BLOCK : (j + 1) * BLOCK] = block
+
+
+def targets_kernel(targets_ref, out_ref):
+    h, c = lax.axis_index("h"), lax.axis_index("c")
+    row = pl.multiple_of((h * 2 + c) * ROWS, ROWS)
+    cols = [column(dy, side, dx) for side in range(2) for dy in RING for dx in RING]
+    for j, col in enumerate(cols):
+        out_ref[:, j * BLOCK : (j + 1) * BLOCK] = targets_ref[pl.ds(row, ROWS), lanes(col, BLOCK)]
 
 
 def near_kernel(x_ref, p_ref, b_own_ref, b_oth_ref, *refs):
     pieces, total_ref = refs[:6], refs[6]
     b = jnp.concatenate([b_own_ref[...], b_oth_ref[...]], axis=0)
     total = ADAPTER_SCALE * dot(p_ref[...], b)
-    for k, piece in zip((0, 1, 2, 4, 5, 6), pieces):
+    for k, piece in enumerate(pieces):
         total = total + dot(x_ref[:, k * HID : (k + 1) * HID], piece[...])
     total_ref[...] = total
 
 
 def hidden_kernel(x_ref, total_ref, own_ref, oth_ref, hidden_ref, mask_ref):
     total = total_ref[...]
-    for k, piece in ((3, own_ref), (7, oth_ref)):
+    for k, piece in enumerate((own_ref, oth_ref)):
         total = total + dot(x_ref[:, k * HID : (k + 1) * HID], piece[...])
     preact = total * MODEL_WIDTH ** (-0.5)
     hidden_ref[...] = jnp.maximum(preact, 0.0).astype(BF16)
@@ -158,25 +181,8 @@
             send_ref[:, :, lanes(to, size)] = part[:, 1, :, begin : begin + size].astype(BF16)
 
 
-def finish_kernel(mine_ref, r1_ref, r2_ref, r3_ref, targets_ref, out_ref):
-    h, c = lax.axis_index("h"), lax.axis_index("c")
-    row = pl.multiple_of((h * 2 + c) * ROWS, ROWS)
-    j = 0
-    for side in range(2):
-        for dy in RING:
-            for dx in RING:
-                here = slice(j * BLOCK, (j + 1) * BLOCK)
-                total = mine_ref[:, here]
-                for ref in (r1_ref, r2_ref, r3_ref):
-                    total = total + ref[:, here].astype(F32)
-                target = targets_ref[pl.ds(row, ROWS), lanes(column(dy, side, dx), BLOCK)]
-                grad = (total * FF ** (-0.5) - target.astype(F32)) / TOK
-                out_ref[:, here] = grad.astype(BF16)
-                j += 1
-
-
-def backward_kernel(q_ref, qc_ref, left_ref, leftc_ref, right_ref, rightc_ref, mask_ref, own_pack_ref,
-                    oth_pack_ref, b_own_ref, b_oth_ref, *refs):
+def backward_kernel(q_ref, qc_ref, left_ref, leftc_ref, right_ref, rightc_ref, mask_ref, pt_ref,
+                    b_own_ref, b_oth_ref, *refs):
     pieces, (up_own_ref, up_oth_ref, wire_ref, back_ref, grad_ref, own_ref, oth_ref) = refs[:8], refs[8:]
     l = lax.axis_index("l")
     for i in range(16):
@@ -185,9 +191,8 @@
         if i < 8:
             grad_ref[here, :] = (q_ref, qc_ref)[e][j]
         else:
-            turned = (j + 1 + 2 * l) % 4
             grad_ref[here, :SIDE] = (left_ref, leftc_ref)[e][j]
-            grad_ref[here, SIDE:] = (right_ref, rightc_ref)[e][turned]
+            grad_ref[here, SIDE:] = (right_ref, rightc_ref)[e][j]
     total = None
     for k, piece in enumerate(pieces):
         if k < 4:
@@ -205,11 +210,11 @@
         ref[pl.ds(token_row(i), ROWS), :] = total[i * ROWS : (i + 1) * ROWS]
     scale = ADAPTER_SCALE * MODEL_WIDTH ** (-0.5)
     sides = (
-        (l, own_ref, own_pack_ref, up_own_ref, b_own_ref[...]),
-        (1 - l, oth_ref, oth_pack_ref, up_oth_ref, b_oth_ref[...]),
-    )
-    for side, hid_ref, p_ref, up_ref, b in sides:
-        up = b.astype(F32) - RATE_UP * (scale * dot(p_ref[...], hid_ref[...]))
+        (l, own_ref, pt_ref[0], up_own_ref, b_own_ref[...]),
+        (1 - l, oth_ref, pt_ref[1], up_oth_ref, b_oth_ref[...]),
+    )
+    for side, hid_ref, p, up_ref, b in sides:
+        up = b.astype(F32) - RATE_UP * (scale * dot(p, hid_ref[...]))
         up_ref[...] = up
         wire_ref[side] = up.astype(BF16)
         back = dot_nt(b, hid_ref[...])
@@ -284,19 +289,26 @@
         name="own",
     )
     b_oth = w_oth[2 * TOK :]
-    packed = call(pack_kernel, shape(TOK + RANK, MODEL_WIDTH), tokens, a, name="pack")
-    packed_oth = near_z(packed)
+    packed, p_own = call(
+        pack_kernel, (shape(HALF + RANK, MODEL_WIDTH), shape(RANK, TOK)), tokens, a, name="pack"
+    )
+    tokens_oth = near_z(packed)
+    tokens_oth_core = partner(tokens_oth, "c")
     in_own = jnp.concatenate(ring(in_own, "x"), axis=0)
     out_own = jnp.concatenate(ring(out_own, "y"), axis=0)
     in_oth = jnp.concatenate(ring_direct(w_oth[:TOK], "y"), axis=0)
     out_oth = jnp.concatenate(ring_direct(w_oth[TOK : 2 * TOK], "x"), axis=0)
 
-    x_rel, p_rel = call(
+    x_near, x_far, p_rel, pt = call(
         arrange_kernel,
-        (shape(2 * TOK, MODEL_WIDTH), shape(2 * TOK, 2 * RANK)),
-        packed, packed_oth,
+        (shape(2 * TOK, 3072), shape(2 * TOK, 1024), shape(2 * TOK, 2 * RANK), shape(2, RANK, TOK)),
+        tokens, tokens_oth, tokens_oth_core, p_own,
         scratch=[pltpu.VMEM((2, TOK, RANK), BF16)],
         name="arrange",
+    )
+    my_targets = call(targets_kernel, shape(ROWS, MODEL_WIDTH), targets, name="targets")
+    in_oth, x_near, p_rel, my_targets = lax.optimization_barrier(
+        (in_oth, x_near, p_rel, my_targets)
     )
 
     in_a = [in_own, shift(in_own, "y", 1), shift(in_own, "y", -1)]
@@ -312,13 +324,13 @@
     total = call(
         near_kernel,
         shape(2 * TOK, HID, dtype=F32),
-        x_rel, p_rel, b_own, b_oth, *in_a, *in_b,
+        x_near, p_rel, b_own, b_oth, *in_a, *in_b,
         name="near",
     )
     hidden, mask = call(
         hidden_kernel,
         (shape(2 * TOK, HID), shape(2 * TOK, HID)),
-        x_rel, total, in_a_far, in_b_far,
+        x_far, total, in_a_far, in_b_far,
         name="hidden",
     )
     keep, send = call(
@@ -332,14 +344,13 @@
     away = summed[4:].astype(BF16)
     left = partner(away[:, :, :SIDE], "l")
     right = away[:, :, SIDE:]
-    right = near_z(jnp.where(l == 0, jnp.roll(right, 1, 0), jnp.roll(right, -1, 0)))
+    right = near_z(right)
     summed = summed[:4] + jnp.concatenate([left, right], axis=2).astype(F32)
-    steps = [shift(summed[j].astype(BF16), "h", j) for j in (1, 2, 3)]
-    grad_rows = call(
-        finish_kernel, shape(ROWS, MODEL_WIDTH), summed[0], *steps, targets, name="finish"
-    )
-
-    q = jnp.stack([grad_rows] + [shift(grad_rows, "h", -j) for j in (1, 2, 3)])
+    shares = lax.all_to_all(summed.astype(BF16), "h", 0, 0, tiled=True)
+    share = shares.astype(F32).sum(axis=0) * FF ** (-0.5)
+    grad_rows = ((share - my_targets.astype(F32)) / TOK).astype(BF16)
+
+    q = lax.all_to_all(jnp.broadcast_to(grad_rows, (4, ROWS, MODEL_WIDTH)), "h", 0, 0, tiled=True)
     left = partner(q[:, :, :SIDE], "l")
     right = near_z(q[:, :, SIDE:])
     q_far, left_far, right_far = partner(q, "c"), partner(left, "c"), partner(right, "c")
@@ -352,8 +363,7 @@
             shape(2, RANK, HID),
             shape(16, RANK, TOK, dtype=F32),
         ),
-        q, q_far, left, left_far, right, right_far, mask, packed[TOK:, :TOK],
-        packed_oth[TOK:, :TOK], b_own, b_oth, *out_pieces,
+        q, q_far, left, left_far, right, right_far, mask, pt, b_own, b_oth, *out_pieces,
         scratch=[
             pltpu.VMEM((2 * TOK, MODEL_WIDTH), BF16),
             pltpu.VMEM((TOK, HID), BF16),

time: 218 us -> 219 us (level)
  blocking collectives: 13.7 us -> 51.2 us
  waiting for transfers between devices: 89.6 us -> 65.2 us
  starting transfers between devices: 63.3 us -> 56.8 us
  local copies, waits for them, and re-layouts: 9.51 us -> 5.32 us
    all_to_all x0 -> x2, blocking collectives: none -> 38.3 us  [the longest x1 19.2 us: shards(): shares = lax.all_to_all(summed.astype(BF16), 'h', 0, 0, tiled=True)]
    ppermute x30 -> x24, waiting for transfers between devices: 55.5 us -> 25.9 us  [shift(): return lax.ppermute(value, axis, [(i, (i + by) % n) for i in range(n)])]
    ppermute x8 -> x9, waiting for transfers between devices: 19.1 us -> 25.6 us  [partner(): return lax.ppermute(value, axis, [(0, 1), (1, 0)])]
    ppermute x30 -> x24, starting transfers between devices: 43.4 us -> 38 us  [shift(): return lax.ppermute(value, axis, [(i, (i + by) % n) for i in range(n)])]
    ppermute x8 -> x9, starting transfers between devices: 5.03 us -> 1.75 us  [partner(): return lax.ppermute(value, axis, [(0, 1), (1, 0)])]
    slice x4 -> x0, local copies, waits for them, and re-layouts: 2.59 us -> none  [the longest x1 1.28 us: shards(): packed[TOK:, :TOK]]
  transfers between devices with their start and end apart: 42 -> 37, of which waited for: 20 -> 15; matrix products, arithmetic and copies ran while one was open for 3% -> 2% of each run, Pallas kernels for 6% -> 7%
where the time goes in v4:
time: 219 us
  waiting for transfers between devices  65.2 us (30%)
  starting transfers between devices  56.8 us (26%)
  blocking collectives  51.2 us (23%)
  Pallas kernels  34.4 us (16%)
  local copies, waits for them, and re-layouts  5.32 us (2%)
  other arithmetic  4.84 us (2%)
    ppermute x24, starting transfers between devices, shift(): return lax.ppermute(value, axis, [(i, (i + by) % n) for i in range(n)])  38 us
    pallas_call x11, Pallas kernels, call(): pl.pallas_call(kernel, out_shape=out_shape, in_specs=[vmem] * len(args),...  34.4 us
    ppermute x24, waiting for transfers between devices, shift(): return lax.ppermute(value, axis, [(i, (i + by) % n) for i in range(n)])  25.9 us
    ppermute x9, waiting for transfers between devices, partner(): return lax.ppermute(value, axis, [(0, 1), (1, 0)])  25.6 us
    all_to_all x1, blocking collectives, shards(): shares = lax.all_to_all(summed.astype(BF16), 'h', 0, 0, tiled=True)  19.2 us
    all_to_all x1, blocking collectives, shards(): lax.all_to_all(jnp.broadcast_to(grad_rows, (4, ROWS, MODEL_WIDTH)), 'h',...  19.1 us
    all_to_all x1, blocking collectives, shards(): back = lax.all_to_all(back, ('l', 'h', 'c'), 0, 0, tiled=True)  12.9 us
    ppermute x3, waiting for transfers between devices, near_z(): lax.ppermute(value, Z, [(place(z), place(z + 1 if z % 2 else z - 1)) for...  11.2 us
  transfers between devices with their start and end apart: 37, of which 15 were waited for; matrix products, arithmetic and copies ran while one was open for 2% of the time, Pallas kernels for 7%

profile of v4, /device:TPU:2, one launch (start us, length us, event | category | flops | bytes accessed | tf_op | source)
XLA Modules:
  0.0 218.7 jit_solution(5636188641663175606)
XLA Ops:
  0.6 2.5 %pack.1 = (bf16[80,4096]{1,0:T(8,128)(2,1)}, bf16[16,128]{1,0:T(8,128)(2,1)}) custom-call(bf16[128,4096]{1,0:T(8,128)(2,1)} %x_ref.1, bf16[16,4096]{1,0:T(8,128)(2,1)} %bitcast.5), custom_call_target="tpu_custom_call" | custom-call | tf_op jit(solution)/shard_map/pack/pallas_call | solution.py:62
  3.1 5.9 %collective-permute-start = (bf16[80,4096]{1,0:T(8,128)(2,1)}, bf16[80,4096]{1,0:T(8,128)(2,1)S(1)}, u32[]{:S(2)}, u32[]{:S(2)}) collective-permute-start(bf16[80,4096]{1,0:T(8,128)(2,1)} %get-tuple-element.26), channel_id=1, source_target_pairs={{0,38},{32,2},{2,32},{34,4},{4,34},{36,6},{6,36},{38,0},{1,39},{33... | collective-permute-start | bytes 1966088 | tf_op jit(solution)/shard_map/ppermute | solution.py:54
  9.0 1.8 send.1.send_ref
  10.8 1.9 own.1
  12.7 1.5 collective-permute-start.6
  14.7 1.6 collective-permute-start.15
  17.3 1.9 targets.1
  19.2 1.7 collective-permute-start.16
  21.1 1.5 collective-permute-start.8
  24.0 3.3 %collective-permute-start.5 = (bf16[128,512]{1,0:T(8,128)(2,1)S(1)}, bf16[128,512]{1,0:T(8,128)(2,1)S(1)}, u32[]{:S(2)}, u32[]{:S(2)}) collective-permute-start(bf16[128,512]{1,0:T(8,128)(2,1)S(1)} %get-tuple-element.56), channel_id=1, source_target_pairs={{0,128},{64,192},{128,0},{192,64},{1,129},{65,193},{129,1},{193,65... | collective-permute-start | bytes 393224 | tf_op jit(solution)/shard_map/ppermute | solution.py:43
  28.1 2.6 %collective-permute-start.10 = (bf16[512,512]{1,0:T(8,128)(2,1)S(1)}, bf16[512,512]{1,0:T(8,128)(2,1)S(1)}, u32[]{:S(2)}, u32[]{:S(2)}) collective-permute-start(bf16[512,512]{1,0:T(8,128)(2,1)S(1)} %constant_dynamic-update-slice_fusion.refs_0_), channel_id=1, source_target_pairs={{0,192},{64,0},{128,64},{192,128},{1,193},{65,1},{129,65},{193,129... | collective-permute-start | bytes 1572872 | tf_op jit(solution)/shard_map/ppermute | solution.py:43
  30.7 1.2 collective-permute-done.5
  31.9 1.5 collective-permute-start.3
  33.5 12.4 %collective-permute-done.4 = bf16[128,512]{1,0:T(8,128)(2,1)S(1)} collective-permute-done((bf16[128,512]{1,0:T(8,128)(2,1)S(1)}, bf16[128,512]{1,0:T(8,128)(2,1)S(1)}, u32[]{:S(2)}, u32[]{:S(2)}) %collective-permute-start.4) | collective-permute-done | bytes 131104 | tf_op jit(solution)/shard_map/ppermute | solution.py:43
  45.9 2.1 collective-permute-start.23
  48.0 1.4 collective-permute-start.22
  51.0 3.8 %arrange.1 = (bf16[256,3072]{1,0:T(8,128)(2,1)}, bf16[256,1024]{1,0:T(8,128)(2,1)}, bf16[256,32]{1,0:T(8,128)(2,1)}, bf16[2,16,128]{2,1,0:T(8,128)(2,1)}) custom-call(bf16[128,4096]{1,0:T(8,128)(2,1)} %x_ref.1, bf16[80,4096]{1,0:T(8,128)(2,1)} %copy-done.9, bf16[80,4096]{1,0:T(8,128)(2,1)} %copy-done.10, bf16[16,128]{1,0:T(8,128)(2,1)} %get-tuple-element.27.p_own_ref), custom_call_target="tpu_custom_call" | custom-call | tf_op jit(solution)/shard_map/arrange/pallas_call | solution.py:62
  54.8 1.5 collective-permute-start.19
  58.1 2.9 %collective-permute-start.25 = (bf16[512,512]{1,0:T(8,128)(2,1)S(1)}, bf16[512,512]{1,0:T(8,128)(2,1)S(1)}, u32[]{:S(2)}, u32[]{:S(2)}) collective-permute-start(bf16[512,512]{1,0:T(8,128)(2,1)S(1)} %pad_maximum_fusion.1.refs_4_), channel_id=1, source_target_pairs={{0,192},{64,0},{128,64},{192,128},{1,193},{65,1},{129,65},{193,129... | collective-permute-start | bytes 1572872 | tf_op jit(solution)/shard_map/ppermute | solution.py:43
  61.0 2.4 %collective-permute-start.12 = (bf16[512,512]{1,0:T(8,128)(2,1)}, bf16[512,512]{1,0:T(8,128)(2,1)S(1)}, u32[]{:S(2)}, u32[]{:S(2)}) collective-permute-start(bf16[512,512]{1,0:T(8,128)(2,1)} %pad_maximum_fusion.refs_3_), channel_id=1, source_target_pairs={{0,24},{8,0},{16,8},{24,16},{1,25},{9,1},{17,9},{25,17},{2,26},{10... | collective-permute-start | bytes 1572872 | tf_op jit(solution)/shard_map/ppermute | solution.py:43
  63.4 6.4 %collective-permute-done.19.refs_2_ = bf16[512,512]{1,0:T(8,128)(2,1)S(1)} collective-permute-done((bf16[512,512]{1,0:T(8,128)(2,1)S(1)}, bf16[512,512]{1,0:T(8,128)(2,1)S(1)}, u32[]{:S(2)}, u32[]{:S(2)}) %collective-permute-start.19) | collective-permute-done | bytes 524320 | tf_op jit(solution)/shard_map/ppermute | solution.py:43
  71.0 3.2 %collective-permute-start.14 = (bf16[512,512]{1,0:T(8,128)(2,1)}, bf16[512,512]{1,0:T(8,128)(2,1)}, u32[]{:S(2)}, u32[]{:S(2)}) collective-permute-start(bf16[512,512]{1,0:T(8,128)(2,1)} %collective-permute-done.11.refs_4_), channel_id=1, source_target_pairs={{0,8},{8,16},{16,24},{24,0},{1,9},{9,17},{17,25},{25,1},{2,10},{10... | collective-permute-start | bytes 1572872 | tf_op jit(solution)/shard_map/ppermute | solution.py:43
  74.2 1.3 collective-permute-start.24
  75.5 2.6 %collective-permute-start.20 = (bf16[512,512]{1,0:T(8,128)(2,1)S(1)}, bf16[512,512]{1,0:T(8,128)(2,1)}, u32[]{:S(2)}, u32[]{:S(2)}) collective-permute-start(bf16[512,512]{1,0:T(8,128)(2,1)S(1)} %collective-permute-done.19.refs_2_), channel_id=1, source_target_pairs={{0,24},{8,0},{16,8},{24,16},{1,25},{9,1},{17,9},{25,17},{2,26},{10... | collective-permute-start | bytes 1572872 | tf_op jit(solution)/shard_map/ppermute | solution.py:43
  78.1 2.9 %collective-permute-done.12.refs_5_ = bf16[512,512]{1,0:T(8,128)(2,1)S(1)} collective-permute-done((bf16[512,512]{1,0:T(8,128)(2,1)}, bf16[512,512]{1,0:T(8,128)(2,1)S(1)}, u32[]{:S(2)}, u32[]{:S(2)}) %collective-permute-start.12) | collective-permute-done | bytes 524320 | tf_op jit(solution)/shard_map/ppermute | solution.py:43
  81.8 2.8 %collective-permute-start.26 = (bf16[512,512]{1,0:T(8,128)(2,1)S(1)}, bf16[512,512]{1,0:T(8,128)(2,1)}, u32[]{:S(2)}, u32[]{:S(2)}) collective-permute-start(bf16[512,512]{1,0:T(8,128)(2,1)S(1)} %collective-permute-done.25.refs_6_), channel_id=1, source_target_pairs={{0,192},{64,0},{128,64},{192,128},{1,193},{65,1},{129,65},{193,129... | collective-permute-start | bytes 1572872 | tf_op jit(solution)/shard_map/ppermute | solution.py:43
  85.2 4.2 %near.1.total_ref = f32[256,512]{1,0:T(8,128)} custom-call(bf16[256,3072]{1,0:T(8,128)(2,1)} %get-tuple-element.31.x_ref, bf16[256,32]{1,0:T(8,128)(2,1)} %get-tuple-element.32.p_ref, bf16[16,512]{1,0:T(8,128)(2,1)} %get-tuple-element.33.b_own_ref, bf16[16,512]{1,0:T(8,128)(2,1)} %slice.37.b_oth_ref, bf16[512,512]{1,0:T(8,128)(2,1)} %copy-done.8, ...), custom_call_target="tpu_custom_call" | custom-call | tf_op jit(solution)/shard_map/near/pallas_call | solution.py:62
  89.4 2.8 %collective-permute-done.14.oth_ref = bf16[512,512]{1,0:T(8,128)(2,1)} collective-permute-done((bf16[512,512]{1,0:T(8,128)(2,1)}, bf16[512,512]{1,0:T(8,128)(2,1)}, u32[]{:S(2)}, u32[]{:S(2)}) %collective-permute-start.14) | collective-permute-done | bytes 524320 | tf_op jit(solution)/shard_map/ppermute | solution.py:43
  92.2 2.8 %hidden.1 = (bf16[256,512]{1,0:T(8,128)(2,1)}, bf16[256,512]{1,0:T(8,128)(2,1)}) custom-call(bf16[256,1024]{1,0:T(8,128)(2,1)} %get-tuple-element.28.x_ref, f32[256,512]{1,0:T(8,128)} %near.1.total_ref, bf16[512,512]{1,0:T(8,128)(2,1)} %copy-done.13, bf16[512,512]{1,0:T(8,128)(2,1)} %collective-permute-done.14.oth_ref), custom_call_target="tpu_custom_call" | custom-call | tf_op jit(solution)/shard_map/hidden/pallas_call | solution.py:62
  95.9 5.1 %output.1 = (f32[8,16,4096]{2,1,0:T(8,128)}, bf16[8,16,4096]{2,1,0:T(8,128)(2,1)}) custom-call(bf16[256,512]{1,0:T(8,128)(2,1)} %get-tuple-element.36.hidden_ref, bf16[512,512]{1,0:T(8,128)(2,1)} %copy-done.3, bf16[512,512]{1,0:T(8,128)(2,1)} %copy-done.6, bf16[512,512]{1,0:T(8,128)(2,1)} %copy-done.4, bf16[512,512]{1,0:T(8,128)(2,1)} %collective-permute-done.20.refs_3_, ...), custom_call_target="tpu_custom_call" | custom-call | tf_op jit(solution)/shard_map/output/pallas_call | solution.py:62
  101.1 2.9 %collective-permute-done.27 = bf16[8,16,4096]{2,1,0:T(8,128)(2,1)S(1)} collective-permute-done((bf16[8,16,4096]{2,1,0:T(8,128)(2,1)}, bf16[8,16,4096]{2,1,0:T(8,128)(2,1)S(1)}, u32[]{:S(2)}, u32[]{:S(2)}) %collective-permute-start.27) | collective-permute-done | bytes 1048608 | tf_op jit(solution)/shard_map/ppermute | solution.py:47
  103.9 1.9 fusion.1
  105.9 3.3 %collective-permute-start.29 = (bf16[4,16,2048]{2,1,0:T(8,128)(2,1)S(1)}, bf16[4,16,2048]{2,1,0:T(8,128)(2,1)S(1)}, u32[]{:S(2)}, u32[]{:S(2)}) collective-permute-start(bf16[4,16,2048]{2,1,0:T(8,128)(2,1)S(1)} %get-tuple-element.52), channel_id=1, source_target_pairs={{0,38},{32,2},{2,32},{34,4},{4,34},{36,6},{6,36},{38,0},{1,39},{33... | collective-permute-start | bytes 786440 | tf_op jit(solution)/shard_map/ppermute | solution.py:54
  109.2 6.6 %collective-permute-done.29 = bf16[4,16,2048]{2,1,0:T(8,128)(2,1)S(1)} collective-permute-done((bf16[4,16,2048]{2,1,0:T(8,128)(2,1)S(1)}, bf16[4,16,2048]{2,1,0:T(8,128)(2,1)S(1)}, u32[]{:S(2)}, u32[]{:S(2)}) %collective-permute-start.29) | collective-permute-done | bytes 262176 | tf_op jit(solution)/shard_map/ppermute | solution.py:54
  115.8 1.5 collective-permute-done.28
  117.4 19.2 %all_to_all.20 = bf16[4,16,4096]{2,1,0:T(8,128)(2,1)S(1)} all-to-all(bf16[4,16,4096]{2,1,0:T(8,128)(2,1)S(1)} %fusion), channel_id=1, replica_groups=mesh['y'=4,'l'=2,'x'=4,'h'=4,'c'=2] {'h'}, dimensions={0} | all-to-all | bytes 1048576 | tf_op jit(solution)/shard_map/all_to_all | solution.py:349
  136.8 19.1 %all_to_all.21.q_ref = bf16[4,16,4096]{2,1,0:T(8,128)(2,1)S(1)} all-to-all(bf16[4,16,4096]{2,1,0:T(8,128)(2,1)S(1)} %broadcast_in_dim.7), channel_id=1, replica_groups=mesh['y'=4,'l'=2,'x'=4,'h'=4,'c'=2] {'h'}, dimensions={0} | all-to-all | bytes 1048576 | tf_op jit(solution)/shard_map/all_to_all | solution.py:353
  156.9 5.5 %collective-permute-done.31.left_ref = bf16[4,16,2048]{2,1,0:T(8,128)(2,1)S(1)} collective-permute-done((bf16[4,16,2048]{2,1,0:T(8,128)(2,1)S(1)}, bf16[4,16,2048]{2,1,0:T(8,128)(2,1)S(1)}, u32[]{:S(2)}, u32[]{:S(2)}) %collective-permute-start.31) | collective-permute-done | bytes 262176 | tf_op jit(solution)/shard_map/ppermute | solution.py:47
  162.4 3.7 %collective-permute-done.33.right_ref = bf16[4,16,2048]{2,1,0:T(8,128)(2,1)S(1)} collective-permute-done((bf16[4,16,2048]{2,1,0:T(8,128)(2,1)S(1)}, bf16[4,16,2048]{2,1,0:T(8,128)(2,1)S(1)}, u32[]{:S(2)}, u32[]{:S(2)}) %collective-permute-start.33) | collective-permute-done | bytes 262176 | tf_op jit(solution)/shard_map/ppermute | solution.py:54
  166.1 1.5 collective-permute-done.34.rightc_ref
  168.3 5.2 %backward.1 = (f32[16,512]{1,0:T(8,128)}, f32[16,512]{1,0:T(8,128)}, bf16[2,16,512]{2,1,0:T(8,128)(2,1)}, f32[16,16,128]{2,1,0:T(8,128)}) custom-call(bf16[4,16,4096]{2,1,0:T(8,128)(2,1)} %copy-done.1, bf16[4,16,4096]{2,1,0:T(8,128)(2,1)} %copy-done.11, bf16[4,16,2048]{2,1,0:T(8,128)(2,1)} %copy-done.16, bf16[4,16,2048]{2,1,0:T(8,128)(2,1)} %copy-done.18, ...), custom_call_target="tpu_custom_call" | custom-call | tf_op jit(solution)/shard_map/backward/pallas_call | solution.py:62
  173.6 12.9 %all_to_all.22.back_ref = f32[16,16,128]{2,1,0:T(8,128)} all-to-all(f32[16,16,128]{2,1,0:T(8,128)} %get-tuple-element.43), channel_id=1, replica_groups=mesh['y'=4,'l'=2,'x'=4,'h'=4,'c'=2] {'l','h','c'}, dimensions={0} | all-to-all | bytes 262144 | tf_op jit(solution)/shard_map/all_to_all | solution.py:374
  186.4 2.7 %down.1 = (f32[16,4096]{1,0:T(8,128)}, bf16[32,16,1152]{2,1,0:T(8,128)(2,1)}) custom-call(f32[16,16,128]{2,1,0:T(8,128)} %all_to_all.22.back_ref, bf16[128,4096]{1,0:T(8,128)(2,1)} %x_ref.1, bf16[16,4096]{1,0:T(8,128)(2,1)} %bitcast.6, bf16[2,16,512]{2,1,0:T(8,128)(2,1)} %get-tuple-element.44.up_ref), custom_call_target="tpu_custom_call" | custom-call | tf_op jit(solution)/shard_map/down/pallas_call | solution.py:62
  189.1 7.1 %all-to-all-start.3 = ((bf16[32,16,1152]{2,1,0:T(8,128)(2,1)}), bf16[32,16,1152]{2,1,0:T(8,128)(2,1)S(1)}, u32[]{:S(2)}, u32[]{:S(2)}) async-start(bf16[32,16,1152]{2,1,0:T(8,128)(2,1)} %get-tuple-element.45), calls=%async_computation.3 | async-start | bytes 2359296 | tf_op jit(solution)/shard_map/all_to_all | solution.py:381
  196.3 1.6 collective-permute-start.35
  197.8 14.3 %collective-permute-done.35 = f32[16,512]{1,0:T(8,128)S(1)} collective-permute-done((f32[16,512]{1,0:T(8,128)S(1)}, f32[16,512]{1,0:T(8,128)S(1)}, u32[]{:S(2)}, u32[]{:S(2)}) %collective-permute-start.35) | collective-permute-done | bytes 32800 | tf_op jit(solution)/shard_map/ppermute | solution.py:47
  212.7 2.5 %all-to-all-done.3.wire_ref = bf16[32,16,1152]{2,1,0:T(8,128)(2,1)S(1)} async-done(((bf16[32,16,1152]{2,1,0:T(8,128)(2,1)}), bf16[32,16,1152]{2,1,0:T(8,128)(2,1)S(1)}, u32[]{:S(2)}, u32[]{:S(2)}) %all-to-all-start.3) | async-done | bytes 1179680 | tf_op jit(solution)/shard_map/all_to_all | solution.py:381
  216.2 2.4 %merge.1 = f32[128,1024]{1,0:T(8,128)} custom-call(bf16[32,16,1152]{2,1,0:T(8,128)(2,1)} %copy-done.2, bf16[128,1024]{1,0:T(8,128)(2,1)} %w_ref.1), custom_call_target="tpu_custom_call" | custom-call | tf_op jit(solution)/shard_map/merge/pallas_call | solution.py:62
  (107 shorter events, 14.5 us)
Async XLA Ops:
  3.1 20.8 %collective-permute-start = (bf16[80,4096]{1,0:T(8,128)(2,1)}, bf16[80,4096]{1,0:T(8,128)(2,1)S(1)}, u32[]{:S(2)}, u32[]{:S(2)}) collective-permute-start(bf16[80,4096]{1,0:T(8,128)(2,1)} %get-tuple-element.26), channel_id=1, source_target_pairs={{0,38},{32,2},{2,32},{34,4},{4,34},{36,6},{6,36},{38,0},{1,39},{33... | collective-permute-start | bytes 1966088 | tf_op jit(solution)/shard_map/ppermute | solution.py:54
  10.8 11.8 %collective-permute-start.2 = (bf16[272,512]{1,0:T(8,128)(2,1)}, bf16[272,512]{1,0:T(8,128)(2,1)S(1)}, u32[]{:S(2)}, u32[]{:S(2)}) collective-permute-start(bf16[272,512]{1,0:T(8,128)(2,1)} %send.1.send_ref), channel_id=1, source_target_pairs={{0,32},{32,0},{1,33},{33,1},{2,34},{34,2},{3,35},{35,3},{4,36},{36... | collective-permute-start | bytes 835592 | tf_op jit(solution)/shard_map/ppermute | solution.py:47
  12.7 6.5 %collective-permute-start.6 = (bf16[128,512]{1,0:T(8,128)(2,1)}, bf16[128,512]{1,0:T(8,128)(2,1)S(1)}, u32[]{:S(2)}, u32[]{:S(2)}) collective-permute-start(bf16[128,512]{1,0:T(8,128)(2,1)} %get-tuple-element.34), channel_id=1, source_target_pairs={{0,8},{8,16},{16,24},{24,0},{1,9},{9,17},{17,25},{25,1},{2,10},{10... | collective-permute-start | bytes 393224 | tf_op jit(solution)/shard_map/ppermute | solution.py:43
  14.2 9.8 %collective-permute-start.7 = (bf16[128,512]{1,0:T(8,128)(2,1)}, bf16[128,512]{1,0:T(8,128)(2,1)S(1)}, u32[]{:S(2)}, u32[]{:S(2)}) collective-permute-start(bf16[128,512]{1,0:T(8,128)(2,1)} %get-tuple-element.34), channel_id=1, source_target_pairs={{0,24},{8,0},{16,8},{24,16},{1,25},{9,1},{17,9},{25,17},{2,26},{10... | collective-permute-start | bytes 393224 | tf_op jit(solution)/shard_map/ppermute | solution.py:43
  14.7 6.4 %collective-permute-start.15 = (bf16[128,512]{1,0:T(8,128)(2,1)}, bf16[128,512]{1,0:T(8,128)(2,1)S(1)}, u32[]{:S(2)}, u32[]{:S(2)}) collective-permute-start(bf16[128,512]{1,0:T(8,128)(2,1)} %get-tuple-element.37), channel_id=1, source_target_pairs={{0,64},{64,128},{128,192},{192,0},{1,65},{65,129},{129,193},{193,1... | collective-permute-start | bytes 393224 | tf_op jit(solution)/shard_map/ppermute | solution.py:43
  19.2 8.8 %collective-permute-start.16 = (bf16[128,512]{1,0:T(8,128)(2,1)}, bf16[128,512]{1,0:T(8,128)(2,1)S(1)}, u32[]{:S(2)}, u32[]{:S(2)}) collective-permute-start(bf16[128,512]{1,0:T(8,128)(2,1)} %get-tuple-element.37), channel_id=1, source_target_pairs={{0,192},{64,0},{128,64},{192,128},{1,193},{65,1},{129,65},{193,129... | collective-permute-start | bytes 393224 | tf_op jit(solution)/shard_map/ppermute | solution.py:43
  21.1 6.2 %collective-permute-start.8 = (bf16[128,512]{1,0:T(8,128)(2,1)S(1)}, bf16[128,512]{1,0:T(8,128)(2,1)S(1)}, u32[]{:S(2)}, u32[]{:S(2)}) collective-permute-start(bf16[128,512]{1,0:T(8,128)(2,1)S(1)} %collective-permute-done.6), channel_id=1, source_target_pairs={{0,8},{8,16},{16,24},{24,0},{1,9},{9,17},{17,25},{25,1},{2,10},{10... | collective-permute-start | bytes 393224 | tf_op jit(solution)/shard_map/ppermute | solution.py:43
  22.6 8.0 %collective-permute-start.17 = (bf16[128,512]{1,0:T(8,128)(2,1)S(1)}, bf16[128,512]{1,0:T(8,128)(2,1)S(1)}, u32[]{:S(2)}, u32[]{:S(2)}) collective-permute-start(bf16[128,512]{1,0:T(8,128)(2,1)S(1)} %collective-permute-done.15), channel_id=1, source_target_pairs={{0,64},{64,128},{128,192},{192,0},{1,65},{65,129},{129,193},{193,1... | collective-permute-start | bytes 393224 | tf_op jit(solution)/shard_map/ppermute | solution.py:43
  23.9 27.1 %copy-start.9 = (bf16[80,4096]{1,0:T(8,128)(2,1)}, bf16[80,4096]{1,0:T(8,128)(2,1)S(1)}, u32[]{:S(2)}) copy-start(bf16[80,4096]{1,0:T(8,128)(2,1)S(1)} %collective-permute-done.oth_ref) | copy-start | bytes 1966084
  23.9 25.5 %collective-permute-start.1 = (bf16[80,4096]{1,0:T(8,128)(2,1)S(1)}, bf16[80,4096]{1,0:T(8,128)(2,1)S(1)}, u32[]{:S(2)}, u32[]{:S(2)}) collective-permute-start(bf16[80,4096]{1,0:T(8,128)(2,1)S(1)} %collective-permute-done.oth_ref), channel_id=1, source_target_pairs={{0,1},{1,0},{2,3},{3,2},{4,5},{5,4},{6,7},{7,6},{8,9},{9,8},{10,11... | collective-permute-start | bytes 1966088 | tf_op jit(solution)/shard_map/ppermute | solution.py:47
  24.0 8.0 %collective-permute-start.5 = (bf16[128,512]{1,0:T(8,128)(2,1)S(1)}, bf16[128,512]{1,0:T(8,128)(2,1)S(1)}, u32[]{:S(2)}, u32[]{:S(2)}) collective-permute-start(bf16[128,512]{1,0:T(8,128)(2,1)S(1)} %get-tuple-element.56), channel_id=1, source_target_pairs={{0,128},{64,192},{128,0},{192,64},{1,129},{65,193},{129,1},{193,65... | collective-permute-start | bytes 393224 | tf_op jit(solution)/shard_map/ppermute | solution.py:43
  27.3 27.5 %copy-start.8 = (bf16[512,512]{1,0:T(8,128)(2,1)}, bf16[512,512]{1,0:T(8,128)(2,1)S(1)}, u32[]{:S(2)}) copy-start(bf16[512,512]{1,0:T(8,128)(2,1)S(1)} %constant_dynamic-update-slice_fusion.refs_0_) | copy-start | bytes 1572868
  27.3 33.7 %collective-permute-start.9 = (bf16[512,512]{1,0:T(8,128)(2,1)S(1)}, bf16[512,512]{1,0:T(8,128)(2,1)}, u32[]{:S(2)}, u32[]{:S(2)}) collective-permute-start(bf16[512,512]{1,0:T(8,128)(2,1)S(1)} %constant_dynamic-update-slice_fusion.refs_0_), channel_id=1, source_target_pairs={{0,64},{64,128},{128,192},{192,0},{1,65},{65,129},{129,193},{193,1... | collective-permute-start | bytes 1572872 | tf_op jit(solution)/shard_map/ppermute | solution.py:43
  28.1 32.9 %collective-permute-start.10 = (bf16[512,512]{1,0:T(8,128)(2,1)S(1)}, bf16[512,512]{1,0:T(8,128)(2,1)S(1)}, u32[]{:S(2)}, u32[]{:S(2)}) collective-permute-start(bf16[512,512]{1,0:T(8,128)(2,1)S(1)} %constant_dynamic-update-slice_fusion.refs_0_), channel_id=1, source_target_pairs={{0,192},{64,0},{128,64},{192,128},{1,193},{65,1},{129,65},{193,129... | collective-permute-start | bytes 1572872 | tf_op jit(solution)/shard_map/ppermute | solution.py:43
  30.6 15.2 %collective-permute-start.4 = (bf16[128,512]{1,0:T(8,128)(2,1)S(1)}, bf16[128,512]{1,0:T(8,128)(2,1)S(1)}, u32[]{:S(2)}, u32[]{:S(2)}) collective-permute-start(bf16[128,512]{1,0:T(8,128)(2,1)S(1)} %get-tuple-element.56), channel_id=1, source_target_pairs={{0,192},{64,0},{128,64},{192,128},{1,193},{65,1},{129,65},{193,129... | collective-permute-start | bytes 393224 | tf_op jit(solution)/shard_map/ppermute | solution.py:43
  31.9 16.1 %collective-permute-start.3 = (bf16[128,512]{1,0:T(8,128)(2,1)S(1)}, bf16[128,512]{1,0:T(8,128)(2,1)S(1)}, u32[]{:S(2)}, u32[]{:S(2)}) collective-permute-start(bf16[128,512]{1,0:T(8,128)(2,1)S(1)} %get-tuple-element.56), channel_id=1, source_target_pairs={{0,64},{64,128},{128,192},{192,0},{1,65},{65,129},{129,193},{193,1... | collective-permute-start | bytes 393224 | tf_op jit(solution)/shard_map/ppermute | solution.py:43
  45.9 9.0 %collective-permute-start.23 = (bf16[128,512]{1,0:T(8,128)(2,1)S(1)}, bf16[128,512]{1,0:T(8,128)(2,1)S(1)}, u32[]{:S(2)}, u32[]{:S(2)}) collective-permute-start(bf16[128,512]{1,0:T(8,128)(2,1)S(1)} %get-tuple-element.55), channel_id=1, source_target_pairs={{0,16},{8,24},{16,0},{24,8},{1,17},{9,25},{17,1},{25,9},{2,18},{10... | collective-permute-start | bytes 393224 | tf_op jit(solution)/shard_map/ppermute | solution.py:43
  48.0 8.4 %collective-permute-start.22 = (bf16[128,512]{1,0:T(8,128)(2,1)S(1)}, bf16[128,512]{1,0:T(8,128)(2,1)S(1)}, u32[]{:S(2)}, u32[]{:S(2)}) collective-permute-start(bf16[128,512]{1,0:T(8,128)(2,1)S(1)} %get-tuple-element.55), channel_id=1, source_target_pairs={{0,24},{8,0},{16,8},{24,16},{1,25},{9,1},{17,9},{25,17},{2,26},{10... | collective-permute-start | bytes 393224 | tf_op jit(solution)/shard_map/ppermute | solution.py:43
  49.4 7.6 %collective-permute-start.21 = (bf16[128,512]{1,0:T(8,128)(2,1)S(1)}, bf16[128,512]{1,0:T(8,128)(2,1)}, u32[]{:S(2)}, u32[]{:S(2)}) collective-permute-start(bf16[128,512]{1,0:T(8,128)(2,1)S(1)} %get-tuple-element.55), channel_id=1, source_target_pairs={{0,8},{8,16},{16,24},{24,0},{1,9},{9,17},{17,25},{25,1},{2,10},{10... | collective-permute-start | bytes 393224 | tf_op jit(solution)/shard_map/ppermute | solution.py:43
  50.0 19.7 %copy-start.3 = (bf16[512,512]{1,0:T(8,128)(2,1)}, bf16[512,512]{1,0:T(8,128)(2,1)S(1)}, u32[]{:S(2)}) copy-start(bf16[512,512]{1,0:T(8,128)(2,1)S(1)} %constant_dynamic-update-slice_fusion.4.refs_0_) | copy-start | bytes 1572868
  54.8 14.9 %collective-permute-start.19 = (bf16[512,512]{1,0:T(8,128)(2,1)S(1)}, bf16[512,512]{1,0:T(8,128)(2,1)S(1)}, u32[]{:S(2)}, u32[]{:S(2)}) collective-permute-start(bf16[512,512]{1,0:T(8,128)(2,1)S(1)} %constant_dynamic-update-slice_fusion.4.refs_0_), channel_id=1, source_target_pairs={{0,24},{8,0},{16,8},{24,16},{1,25},{9,1},{17,9},{25,17},{2,26},{10... | collective-permute-start | bytes 1572872 | tf_op jit(solution)/shard_map/ppermute | solution.py:43
  56.4 14.6 %collective-permute-start.11 = (bf16[512,512]{1,0:T(8,128)(2,1)}, bf16[512,512]{1,0:T(8,128)(2,1)}, u32[]{:S(2)}, u32[]{:S(2)}) collective-permute-start(bf16[512,512]{1,0:T(8,128)(2,1)} %pad_maximum_fusion.refs_3_), channel_id=1, source_target_pairs={{0,8},{8,16},{16,24},{24,0},{1,9},{9,17},{17,25},{25,1},{2,10},{10... | collective-permute-start | bytes 1572872 | tf_op jit(solution)/shard_map/ppermute | solution.py:43
  58.1 31.3 %copy-start = (bf16[512,512]{1,0:T(8,128)(2,1)}, bf16[512,512]{1,0:T(8,128)(2,1)S(1)}, u32[]{:S(2)}) copy-start(bf16[512,512]{1,0:T(8,128)(2,1)S(1)} %pad_maximum_fusion.1.refs_4_) | copy-start | bytes 1572868
  58.1 16.1 %collective-permute-start.25 = (bf16[512,512]{1,0:T(8,128)(2,1)S(1)}, bf16[512,512]{1,0:T(8,128)(2,1)S(1)}, u32[]{:S(2)}, u32[]{:S(2)}) collective-permute-start(bf16[512,512]{1,0:T(8,128)(2,1)S(1)} %pad_maximum_fusion.1.refs_4_), channel_id=1, source_target_pairs={{0,192},{64,0},{128,64},{192,128},{1,193},{65,1},{129,65},{193,129... | collective-permute-start | bytes 1572872 | tf_op jit(solution)/shard_map/ppermute | solution.py:43
  61.0 14.5 %collective-permute-start.13 = (bf16[512,512]{1,0:T(8,128)(2,1)}, bf16[512,512]{1,0:T(8,128)(2,1)S(1)}, u32[]{:S(2)}, u32[]{:S(2)}) collective-permute-start(bf16[512,512]{1,0:T(8,128)(2,1)} %collective-permute-done.9.refs_1_), channel_id=1, source_target_pairs={{0,64},{64,128},{128,192},{192,0},{1,65},{65,129},{129,193},{193,1... | collective-permute-start | bytes 1572872 | tf_op jit(solution)/shard_map/ppermute | solution.py:43
  61.0 13.2 %copy-start.14 = (bf16[512,512]{1,0:T(8,128)(2,1)}, bf16[512,512]{1,0:T(8,128)(2,1)S(1)}, u32[]{:S(2)}) copy-start(bf16[512,512]{1,0:T(8,128)(2,1)S(1)} %collective-permute-done.10.refs_2_) | copy-start | bytes 1572868
  61.0 20.0 %collective-permute-start.12 = (bf16[512,512]{1,0:T(8,128)(2,1)}, bf16[512,512]{1,0:T(8,128)(2,1)S(1)}, u32[]{:S(2)}, u32[]{:S(2)}) collective-permute-start(bf16[512,512]{1,0:T(8,128)(2,1)} %pad_maximum_fusion.refs_3_), channel_id=1, source_target_pairs={{0,24},{8,0},{16,8},{24,16},{1,25},{9,1},{17,9},{25,17},{2,26},{10... | collective-permute-start | bytes 1572872 | tf_op jit(solution)/shard_map/ppermute | solution.py:43
  69.8 19.6 %copy-start.4 = (bf16[512,512]{1,0:T(8,128)(2,1)}, bf16[512,512]{1,0:T(8,128)(2,1)S(1)}, u32[]{:S(2)}) copy-start(bf16[512,512]{1,0:T(8,128)(2,1)S(1)} %collective-permute-done.19.refs_2_) | copy-start | bytes 1572868
  69.8 25.2 %collective-permute-start.18 = (bf16[512,512]{1,0:T(8,128)(2,1)S(1)}, bf16[512,512]{1,0:T(8,128)(2,1)S(1)}, u32[]{:S(2)}, u32[]{:S(2)}) collective-permute-start(bf16[512,512]{1,0:T(8,128)(2,1)S(1)} %constant_dynamic-update-slice_fusion.4.refs_0_), channel_id=1, source_target_pairs={{0,8},{8,16},{16,24},{24,0},{1,9},{9,17},{17,25},{25,1},{2,10},{10... | collective-permute-start | bytes 1572872 | tf_op jit(solution)/shard_map/ppermute | solution.py:43
  71.0 21.2 %collective-permute-start.14 = (bf16[512,512]{1,0:T(8,128)(2,1)}, bf16[512,512]{1,0:T(8,128)(2,1)}, u32[]{:S(2)}, u32[]{:S(2)}) collective-permute-start(bf16[512,512]{1,0:T(8,128)(2,1)} %collective-permute-done.11.refs_4_), channel_id=1, source_target_pairs={{0,8},{8,16},{16,24},{24,0},{1,9},{9,17},{17,25},{25,1},{2,10},{10... | collective-permute-start | bytes 1572872 | tf_op jit(solution)/shard_map/ppermute | solution.py:43
  74.2 15.2 %copy-start.5 = (bf16[512,512]{1,0:T(8,128)(2,1)}, bf16[512,512]{1,0:T(8,128)(2,1)S(1)}, u32[]{:S(2)}) copy-start(bf16[512,512]{1,0:T(8,128)(2,1)S(1)} %collective-permute-done.25.refs_6_) | copy-start | bytes 1572868
  74.2 20.8 %collective-permute-start.24 = (bf16[512,512]{1,0:T(8,128)(2,1)S(1)}, bf16[512,512]{1,0:T(8,128)(2,1)S(1)}, u32[]{:S(2)}, u32[]{:S(2)}) collective-permute-start(bf16[512,512]{1,0:T(8,128)(2,1)S(1)} %pad_maximum_fusion.1.refs_4_), channel_id=1, source_target_pairs={{0,64},{64,128},{128,192},{192,0},{1,65},{65,129},{129,193},{193,1... | collective-permute-start | bytes 1572872 | tf_op jit(solution)/shard_map/ppermute | solution.py:43
  75.5 19.5 %collective-permute-start.20 = (bf16[512,512]{1,0:T(8,128)(2,1)S(1)}, bf16[512,512]{1,0:T(8,128)(2,1)}, u32[]{:S(2)}, u32[]{:S(2)}) collective-permute-start(bf16[512,512]{1,0:T(8,128)(2,1)S(1)} %collective-permute-done.19.refs_2_), channel_id=1, source_target_pairs={{0,24},{8,0},{16,8},{24,16},{1,25},{9,1},{17,9},{25,17},{2,26},{10... | collective-permute-start | bytes 1572872 | tf_op jit(solution)/shard_map/ppermute | solution.py:43
  81.8 13.2 %collective-permute-start.26 = (bf16[512,512]{1,0:T(8,128)(2,1)S(1)}, bf16[512,512]{1,0:T(8,128)(2,1)}, u32[]{:S(2)}, u32[]{:S(2)}) collective-permute-start(bf16[512,512]{1,0:T(8,128)(2,1)S(1)} %collective-permute-done.25.refs_6_), channel_id=1, source_target_pairs={{0,192},{64,0},{128,64},{192,128},{1,193},{65,1},{129,65},{193,129... | collective-permute-start | bytes 1572872 | tf_op jit(solution)/shard_map/ppermute | solution.py:43
  101.1 2.9 %collective-permute-start.27 = (bf16[8,16,4096]{2,1,0:T(8,128)(2,1)}, bf16[8,16,4096]{2,1,0:T(8,128)(2,1)S(1)}, u32[]{:S(2)}, u32[]{:S(2)}) collective-permute-start(bf16[8,16,4096]{2,1,0:T(8,128)(2,1)} %get-tuple-element.39), channel_id=1, source_target_pairs={{0,1},{1,0},{2,3},{3,2},{4,5},{5,4},{6,7},{7,6},{8,9},{9,8},{10,11... | collective-permute-start | bytes 3145736 | tf_op jit(solution)/shard_map/ppermute | solution.py:47
  105.9 30.8 %copy-start.12 = (bf16[16,4096]{1,0:T(8,128)(2,1)S(1)}, bf16[16,4096]{1,0:T(8,128)(2,1)}, u32[]{:S(2)}) copy-start(bf16[16,4096]{1,0:T(8,128)(2,1)} %targets.1) | copy-start | bytes 393220
  105.9 9.9 %collective-permute-start.29 = (bf16[4,16,2048]{2,1,0:T(8,128)(2,1)S(1)}, bf16[4,16,2048]{2,1,0:T(8,128)(2,1)S(1)}, u32[]{:S(2)}, u32[]{:S(2)}) collective-permute-start(bf16[4,16,2048]{2,1,0:T(8,128)(2,1)S(1)} %get-tuple-element.52), channel_id=1, source_target_pairs={{0,38},{32,2},{2,32},{34,4},{4,34},{36,6},{6,36},{38,0},{1,39},{33... | collective-permute-start | bytes 786440 | tf_op jit(solution)/shard_map/ppermute | solution.py:54
  109.2 8.1 %collective-permute-start.28 = (bf16[4,16,2048]{2,1,0:T(8,128)(2,1)S(1)}, bf16[4,16,2048]{2,1,0:T(8,128)(2,1)S(1)}, u32[]{:S(2)}, u32[]{:S(2)}) collective-permute-start(bf16[4,16,2048]{2,1,0:T(8,128)(2,1)S(1)} %get-tuple-element.51), channel_id=1, source_target_pairs={{0,32},{32,0},{1,33},{33,1},{2,34},{34,2},{3,35},{35,3},{4,36},{36... | collective-permute-start | bytes 786440 | tf_op jit(solution)/shard_map/ppermute | solution.py:47
  155.9 11.7 %copy-start.1 = (bf16[4,16,4096]{2,1,0:T(8,128)(2,1)}, bf16[4,16,4096]{2,1,0:T(8,128)(2,1)S(1)}, u32[]{:S(2)}) copy-start(bf16[4,16,4096]{2,1,0:T(8,128)(2,1)S(1)} %all_to_all.21.q_ref) | copy-start | bytes 1572868
  155.9 6.5 %collective-permute-start.31 = (bf16[4,16,2048]{2,1,0:T(8,128)(2,1)S(1)}, bf16[4,16,2048]{2,1,0:T(8,128)(2,1)S(1)}, u32[]{:S(2)}, u32[]{:S(2)}) collective-permute-start(bf16[4,16,2048]{2,1,0:T(8,128)(2,1)S(1)} %get-tuple-element.54), channel_id=1, source_target_pairs={{0,32},{32,0},{1,33},{33,1},{2,34},{34,2},{3,35},{35,3},{4,36},{36... | collective-permute-start | bytes 786440 | tf_op jit(solution)/shard_map/ppermute | solution.py:47
  156.0 10.0 %collective-permute-start.30 = (bf16[4,16,4096]{2,1,0:T(8,128)(2,1)S(1)}, bf16[4,16,4096]{2,1,0:T(8,128)(2,1)S(1)}, u32[]{:S(2)}, u32[]{:S(2)}) collective-permute-start(bf16[4,16,4096]{2,1,0:T(8,128)(2,1)S(1)} %all_to_all.21.q_ref), channel_id=1, source_target_pairs={{0,1},{1,0},{2,3},{3,2},{4,5},{5,4},{6,7},{7,6},{8,9},{9,8},{10,11... | collective-permute-start | bytes 1572872 | tf_op jit(solution)/shard_map/ppermute | solution.py:47
  156.1 9.9 %collective-permute-start.33 = (bf16[4,16,2048]{2,1,0:T(8,128)(2,1)S(1)}, bf16[4,16,2048]{2,1,0:T(8,128)(2,1)S(1)}, u32[]{:S(2)}, u32[]{:S(2)}) collective-permute-start(bf16[4,16,2048]{2,1,0:T(8,128)(2,1)S(1)} %get-tuple-element.53), channel_id=1, source_target_pairs={{0,38},{32,2},{2,32},{34,4},{4,34},{36,6},{6,36},{38,0},{1,39},{33... | collective-permute-start | bytes 786440 | tf_op jit(solution)/shard_map/ppermute | solution.py:54
  162.4 3.7 %collective-permute-start.32 = (bf16[4,16,2048]{2,1,0:T(8,128)(2,1)S(1)}, bf16[4,16,2048]{2,1,0:T(8,128)(2,1)S(1)}, u32[]{:S(2)}, u32[]{:S(2)}) collective-permute-start(bf16[4,16,2048]{2,1,0:T(8,128)(2,1)S(1)} %collective-permute-done.31.left_ref), channel_id=1, source_target_pairs={{0,1},{1,0},{2,3},{3,2},{4,5},{5,4},{6,7},{7,6},{8,9},{9,8},{10,11... | collective-permute-start | bytes 786440 | tf_op jit(solution)/shard_map/ppermute | solution.py:47
  166.1 1.5 collective-permute-start.34
  173.6 22.7 %copy-start.23 = (f32[16,512]{1,0:T(8,128)S(1)}, f32[16,512]{1,0:T(8,128)}, u32[]{:S(2)}) copy-start(f32[16,512]{1,0:T(8,128)} %get-tuple-element.48) | copy-start | bytes 98308
  173.6 38.5 %copy-start.22 = (f32[16,512]{1,0:T(8,128)S(1)}, f32[16,512]{1,0:T(8,128)}, u32[]{:S(2)}) copy-start(f32[16,512]{1,0:T(8,128)} %get-tuple-element.47) | copy-start | bytes 98308
  189.1 26.1 %all-to-all-start.3 = ((bf16[32,16,1152]{2,1,0:T(8,128)(2,1)}), bf16[32,16,1152]{2,1,0:T(8,128)(2,1)S(1)}, u32[]{:S(2)}, u32[]{:S(2)}) async-start(bf16[32,16,1152]{2,1,0:T(8,128)(2,1)} %get-tuple-element.45), calls=%async_computation.3 | async-start | bytes 2359296 | tf_op jit(solution)/shard_map/all_to_all | solution.py:381
  196.3 15.8 %collective-permute-start.35 = (f32[16,512]{1,0:T(8,128)S(1)}, f32[16,512]{1,0:T(8,128)S(1)}, u32[]{:S(2)}, u32[]{:S(2)}) collective-permute-start(f32[16,512]{1,0:T(8,128)S(1)} %copy-done.23), channel_id=1, source_target_pairs={{0,32},{32,0},{1,33},{33,1},{2,34},{34,2},{3,35},{35,3},{4,36},{36... | collective-permute-start | bytes 98312 | tf_op jit(solution)/shard_map/ppermute | solution.py:47
  (13 other events, 21.1 us)

commit v5 on v4

--- a/solution.py
+++ b/solution.py
@@ -56,17 +56,18 @@
     )
 
 
-def call(kernel, out_shape, *args, scratch=(), name):
+def call(kernel, out_shape, *args, scratch=(), after=(), name):
     vmem = pl.BlockSpec(memory_space=pltpu.VMEM)
+    wait = pl.BlockSpec(memory_space=pl.ANY)
     many = isinstance(out_shape, tuple)
     return pl.pallas_call(
         kernel,
         out_shape=out_shape,
-        in_specs=[vmem] * len(args),
+        in_specs=[vmem] * len(args) + [wait] * len(after),
         out_specs=(vmem,) * len(out_shape) if many else vmem,
         scratch_shapes=scratch,
         name=name,
-    )(*args)
+    )(*args, *after)
 
 
 def shape(*dims, dtype=BF16):
@@ -102,7 +103,7 @@
     b_own_ref[...] = b_ref[:, lanes(mine, HID)]
 
 
-def pack_kernel(tokens_ref, a_ref, out_ref, p_ref):
+def pack_kernel(tokens_ref, a_ref, after_ref, out_ref, p_ref):
     c = lax.axis_index("c")
     p = dot_nt(a_ref[...], tokens_ref[...]).astype(BF16)
     out_ref[:HALF] = tokens_ref[pl.ds(pl.multiple_of(c * HALF, HALF), HALF), :]
@@ -111,15 +112,14 @@
 
 
 def arrange_kernel(own_ref, oth_ref, oth_core_ref, p_own_ref, near_ref, far_ref, p_ref, pt_ref, turned_ref):
-    l, c = lax.axis_index("l"), lax.axis_index("c")
+    c = lax.axis_index("c")
     p_oth = oth_ref[HALF:, :TOK]
     pt_ref[0] = p_own_ref[...]
     pt_ref[1] = p_oth
     turned_ref[0] = p_own_ref[...].astype(F32).T.astype(BF16)
     turned_ref[1] = p_oth.astype(F32).T.astype(BF16)
-    near = [column(dy, l, dx) for dy in RING[:3] for dx in RING]
-    near += [column(dy, 1 - l, dx) for dx in RING[:3] for dy in RING]
-    far = [column(RING[3], l, dx) for dx in RING] + [column(dy, 1 - l, RING[3]) for dy in RING]
+    near = [column(dy, side, dx) for dy in RING[:3] for dx in RING for side in range(2)]
+    far = [column(RING[3], side, dx) for dx in RING for side in range(2)]
     p_ref[...] = jnp.zeros_like(p_ref)
     for i in range(16):
         here = slice(i * ROWS, (i + 1) * ROWS)
@@ -141,49 +141,50 @@
                 ref[here, j * BLOCK : (j + 1) * BLOCK] = block
 
 
-def targets_kernel(targets_ref, out_ref):
+def targets_kernel(targets_ref, after_ref, out_ref):
     h, c = lax.axis_index("h"), lax.axis_index("c")
     row = pl.multiple_of((h * 2 + c) * ROWS, ROWS)
-    cols = [column(dy, side, dx) for side in range(2) for dy in RING for dx in RING]
+    cols = [column(dy, side, dx) for dx in RING for dy in RING for side in range(2)]
     for j, col in enumerate(cols):
         out_ref[:, j * BLOCK : (j + 1) * BLOCK] = targets_ref[pl.ds(row, ROWS), lanes(col, BLOCK)]
 
 
 def near_kernel(x_ref, p_ref, b_own_ref, b_oth_ref, *refs):
-    pieces, total_ref = refs[:6], refs[6]
+    pieces, total_ref = refs[:3], refs[3]
     b = jnp.concatenate([b_own_ref[...], b_oth_ref[...]], axis=0)
     total = ADAPTER_SCALE * dot(p_ref[...], b)
     for k, piece in enumerate(pieces):
-        total = total + dot(x_ref[:, k * HID : (k + 1) * HID], piece[...])
+        total = total + dot(x_ref[:, k * 1024 : (k + 1) * 1024], piece[...])
     total_ref[...] = total
 
 
-def hidden_kernel(x_ref, total_ref, own_ref, oth_ref, hidden_ref, mask_ref):
+def hidden_kernel(x_ref, total_ref, low_ref, high_ref, hidden_ref, mask_ref):
     total = total_ref[...]
-    for k, piece in enumerate((own_ref, oth_ref)):
+    for k, piece in enumerate((low_ref, high_ref)):
         total = total + dot(x_ref[:, k * HID : (k + 1) * HID], piece[...])
     preact = total * MODEL_WIDTH ** (-0.5)
     hidden_ref[...] = jnp.maximum(preact, 0.0).astype(BF16)
     mask_ref[...] = jnp.where(preact > 0, 1.0, 0.0).astype(BF16)
 
 
+def spans(pieces):
+    begin = 0
+    for piece in pieces:
+        yield slice(begin, begin + piece.shape[0]), piece
+        begin += piece.shape[0]
+
+
 def output_kernel(hidden_ref, *refs):
-    pieces, (keep_ref, send_ref) = refs[:8], refs[8:]
-    l = lax.axis_index("l")
-    for k, piece in enumerate(pieces):
-        part = dot_nt(hidden_ref[...], piece[...]).reshape(8, 2, ROWS, HID)
-        if k < 4:
-            places = [(l * SIDE + (j * 4 + k) * BLOCK, j * BLOCK, BLOCK) for j in range(4)]
-        else:
-            places = [((1 - l) * SIDE + (k - 4) * HID, 0, HID)]
-        for to, begin, size in places:
-            keep_ref[:, :, lanes(to, size)] = part[:, 0, :, begin : begin + size]
-            send_ref[:, :, lanes(to, size)] = part[:, 1, :, begin : begin + size].astype(BF16)
+    pieces, (keep_ref, send_ref) = refs[:5], refs[5:]
+    for cols, piece in spans(pieces):
+        part = dot_nt(hidden_ref[...], piece[...]).reshape(8, 2, ROWS, piece.shape[0])
+        keep_ref[:, :, cols] = part[:, 0]
+        send_ref[:, :, cols] = part[:, 1].astype(BF16)
 
 
 def backward_kernel(q_ref, qc_ref, left_ref, leftc_ref, right_ref, rightc_ref, mask_ref, pt_ref,
                     b_own_ref, b_oth_ref, *refs):
-    pieces, (up_own_ref, up_oth_ref, wire_ref, back_ref, grad_ref, own_ref, oth_ref) = refs[:8], refs[8:]
+    pieces, (up_own_ref, up_oth_ref, wire_ref, back_ref, grad_ref, own_ref, oth_ref) = refs[:5], refs[5:]
     l = lax.axis_index("l")
     for i in range(16):
         j, e = (i // 2) % 4, i % 2
@@ -194,15 +195,8 @@
             grad_ref[here, :SIDE] = (left_ref, leftc_ref)[e][j]
             grad_ref[here, SIDE:] = (right_ref, rightc_ref)[e][j]
     total = None
-    for k, piece in enumerate(pieces):
-        if k < 4:
-            part = jnp.concatenate(
-                [grad_ref[:, lanes(l * SIDE + (j * 4 + k) * BLOCK, BLOCK)] for j in range(4)],
-                axis=1,
-            )
-        else:
-            part = grad_ref[:, lanes((1 - l) * SIDE + (k - 4) * HID, HID)]
-        term = dot(part, piece[...])
+    for cols, piece in spans(pieces):
+        term = dot(grad_ref[:, cols], piece[...])
         total = term if total is None else total + term
     total = jnp.where(mask_ref[...].astype(F32) > 0, total * FF ** (-0.5), 0.0).astype(BF16)
     for i in range(16):
@@ -271,8 +265,9 @@
     return [value, below, above, shift(below, axis, 1)]
 
 
-def ring_direct(value, axis):
-    return [value, shift(value, axis, 1), shift(value, axis, -1), shift(value, axis, 2)]
+def far_halves(below, above, axis):
+    half = below.shape[0] // 2
+    return [shift(below[:half], axis, 1), shift(above[half:], axis, -1)]
 
 
 def shards(tokens, targets, w_in, w_out, factor_down, factor_up):
@@ -290,14 +285,24 @@
     )
     b_oth = w_oth[2 * TOK :]
     packed, p_own = call(
-        pack_kernel, (shape(HALF + RANK, MODEL_WIDTH), shape(RANK, TOK)), tokens, a, name="pack"
+        pack_kernel,
+        (shape(HALF + RANK, MODEL_WIDTH), shape(RANK, TOK)),
+        tokens, a,
+        after=[in_own],
+        name="pack",
     )
     tokens_oth = near_z(packed)
     tokens_oth_core = partner(tokens_oth, "c")
-    in_own = jnp.concatenate(ring(in_own, "x"), axis=0)
-    out_own = jnp.concatenate(ring(out_own, "y"), axis=0)
-    in_oth = jnp.concatenate(ring_direct(w_oth[:TOK], "y"), axis=0)
-    out_oth = jnp.concatenate(ring_direct(w_oth[TOK : 2 * TOK], "x"), axis=0)
+
+    def joined(own, oth):
+        return jnp.where(
+            l == 0, jnp.concatenate([own, oth], axis=0), jnp.concatenate([oth, own], axis=0)
+        )
+
+    in_line = jnp.concatenate(ring(joined(in_own, w_oth[:TOK]), "x"), axis=0)
+    out_line = jnp.concatenate(ring(joined(out_own, w_oth[TOK : 2 * TOK]), "y"), axis=0)
+    in_near = [in_line, shift(in_line, "y", 1), shift(in_line, "y", -1)]
+    out_near = [out_line, shift(out_line, "x", 1), shift(out_line, "x", -1)]
 
     x_near, x_far, p_rel, pt = call(
         arrange_kernel,
@@ -306,31 +311,25 @@
         scratch=[pltpu.VMEM((2, TOK, RANK), BF16)],
         name="arrange",
     )
-    my_targets = call(targets_kernel, shape(ROWS, MODEL_WIDTH), targets, name="targets")
-    in_oth, x_near, p_rel, my_targets = lax.optimization_barrier(
-        (in_oth, x_near, p_rel, my_targets)
-    )
-
-    in_a = [in_own, shift(in_own, "y", 1), shift(in_own, "y", -1)]
-    in_b = [in_oth, shift(in_oth, "x", 1), shift(in_oth, "x", -1)]
-    out_a = [out_own, shift(out_own, "x", 1), shift(out_own, "x", -1)]
-    out_b = [out_oth, shift(out_oth, "y", 1), shift(out_oth, "y", -1)]
-    in_a_far = shift(in_a[1], "y", 1)
-    in_b_far = shift(in_b[1], "x", 1)
-    out_a_far = shift(out_a[2], "x", -1)
-    out_b_far = shift(out_b[2], "y", -1)
-    out_pieces = out_a + [out_a_far] + out_b + [out_b_far]
-
+    my_targets = call(
+        targets_kernel, shape(ROWS, MODEL_WIDTH), targets, after=[p_rel], name="targets"
+    )
+    in_near[1], in_near[2], x_near, p_rel, my_targets = lax.optimization_barrier(
+        (in_near[1], in_near[2], x_near, p_rel, my_targets)
+    )
+    in_far = far_halves(in_near[1], in_near[2], "y")
+    out_far = far_halves(out_near[1], out_near[2], "x")
+    out_pieces = out_near + out_far
     total = call(
         near_kernel,
         shape(2 * TOK, HID, dtype=F32),
-        x_near, p_rel, b_own, b_oth, *in_a, *in_b,
+        x_near, p_rel, b_own, b_oth, *in_near,
         name="near",
     )
     hidden, mask = call(
         hidden_kernel,
         (shape(2 * TOK, HID), shape(2 * TOK, HID)),
-        x_far, total, in_a_far, in_b_far,
+        x_far, total, *in_far,
         name="hidden",
     )
     keep, send = call(

time: 219 us -> 201 us (0.918)
  starting transfers between devices: 56.8 us -> 37.3 us
  waiting for transfers between devices: 65.2 us -> 60 us
  local copies, waits for them, and re-layouts: 5.32 us -> 9.64 us
    ppermute x24 -> x14, starting transfers between devices: 38 us -> 18.9 us  [shift(): return lax.ppermute(value, axis, [(i, (i + by) % n) for i in range(n)])]
    ppermute x24 -> x14, waiting for transfers between devices: 25.9 us -> 9.11 us  [shift(): return lax.ppermute(value, axis, [(i, (i + by) % n) for i in range(n)])]
    ppermute x9, waiting for transfers between devices: 25.6 us -> 34.3 us  [partner(): return lax.ppermute(value, axis, [(0, 1), (1, 0)])]
    slice x1 -> x5, local copies, waits for them, and re-layouts: 0.02 us -> 4.68 us  [the longest x4 4.66 us: far_halves(): return [shift(below[:half], axis, 1), shift(above[half:], axis, -1)]]
    ppermute x3, waiting for transfers between devices: 11.2 us -> 14.4 us  [near_z(): lax.ppermute(value, Z, [(place(z), place(z + 1 if z % 2 else z - 1)) for...]
    unnamed x53 -> x32, local copies, waits for them, and re-layouts: 4.57 us -> 4.25 us
  transfers between devices with their start and end apart: 37 -> 27, of which waited for: 15 -> 15; matrix products, arithmetic and copies ran while one was open for 2% -> 4% of each run, Pallas kernels for 7% -> 9%
where the time goes in v5:
time: 201 us; the launch traced here: 199 us
  waiting for transfers between devices  60 us (30%)
  blocking collectives  51 us (25%)
  starting transfers between devices  37.3 us (19%)
  Pallas kernels  34.2 us (17%)
  local copies, waits for them, and re-layouts  9.64 us (5%)
  other arithmetic  6.03 us (3%)
    ppermute x9, waiting for transfers between devices, partner(): return lax.ppermute(value, axis, [(0, 1), (1, 0)])  34.3 us
    pallas_call x11, Pallas kernels, call(): pl.pallas_call(kernel, out_shape=out_shape, in_specs=[vmem] * len(args) +...  34.2 us
    all_to_all x1, blocking collectives, shards(): shares = lax.all_to_all(summed.astype(BF16), 'h', 0, 0, tiled=True)  19.4 us
    ppermute x14, starting transfers between devices, shift(): return lax.ppermute(value, axis, [(i, (i + by) % n) for i in range(n)])  18.9 us
    all_to_all x1, blocking collectives, shards(): lax.all_to_all(jnp.broadcast_to(grad_rows, (4, ROWS, MODEL_WIDTH)), 'h',...  18.5 us
    ppermute x3, waiting for transfers between devices, near_z(): lax.ppermute(value, Z, [(place(z), place(z + 1 if z % 2 else z - 1)) for...  14.4 us
    all_to_all x1, blocking collectives, shards(): back = lax.all_to_all(back, ('l', 'h', 'c'), 0, 0, tiled=True)  13.1 us
    ppermute x14, waiting for transfers between devices, shift(): return lax.ppermute(value, axis, [(i, (i + by) % n) for i in range(n)])  9.11 us
  transfers between devices with their start and end apart: 27, of which 15 were waited for; matrix products, arithmetic and copies ran while one was open for 4% of the time, Pallas kernels for 9%

profile of v5, /device:TPU:2, one launch (start us, length us, event | category | flops | bytes accessed | tf_op | source)
XLA Modules:
  0.0 199.1 jit_solution(10588188994686483839)
XLA Ops:
  0.6 1.8 send.1.send_ref
  2.5 1.9 collective-permute-start.2
  4.4 1.9 own.1
  6.3 5.0 %collective-permute-done.2 = bf16[272,512]{1,0:T(8,128)(2,1)S(1)} collective-permute-done((bf16[272,512]{1,0:T(8,128)(2,1)}, bf16[272,512]{1,0:T(8,128)(2,1)S(1)}, u32[]{:S(2)}, u32[]{:S(2)}) %collective-permute-start.2) | collective-permute-done | bytes 278560 | tf_op jit(solution)/shard_map/ppermute | solution.py:47
  11.3 1.1 maximum_select_fusion
  12.3 1.6 collective-permute-start.3
  13.9 1.0 maximum_select_fusion.1
  14.9 1.7 collective-permute-start.10
  17.1 2.6 %collective-permute-done.3 = bf16[256,512]{1,0:T(8,128)(2,1)S(1)} collective-permute-done((bf16[256,512]{1,0:T(8,128)(2,1)S(1)}, bf16[256,512]{1,0:T(8,128)(2,1)S(1)}, u32[]{:S(2)}, u32[]{:S(2)}) %collective-permute-start.3) | collective-permute-done | bytes 262176 | tf_op jit(solution)/shard_map/ppermute | solution.py:43
  19.8 1.5 collective-permute-start.5
  21.3 3.0 %collective-permute-start.11 = (bf16[256,512]{1,0:T(8,128)(2,1)S(1)}, bf16[256,512]{1,0:T(8,128)(2,1)S(1)}, u32[]{:S(2)}, u32[]{:S(2)}) collective-permute-start(bf16[256,512]{1,0:T(8,128)(2,1)S(1)} %maximum_select_fusion.1), channel_id=1, source_target_pairs={{0,192},{64,0},{128,64},{192,128},{1,193},{65,1},{129,65},{193,129... | collective-permute-start | bytes 786440 | tf_op jit(solution)/shard_map/ppermute | solution.py:43
  24.3 2.5 %pack.1 = (bf16[80,4096]{1,0:T(8,128)(2,1)}, bf16[16,128]{1,0:T(8,128)(2,1)}) custom-call(bf16[128,4096]{1,0:T(8,128)(2,1)} %x_ref.1, bf16[16,4096]{1,0:T(8,128)(2,1)} %bitcast.5, bf16[128,512]{1,0:T(8,128)(2,1)} %get-tuple-element.27.after_ref), custom_call_target="tpu_custom_call" | custom-call | tf_op jit(solution)/shard_map/pack/pallas_call | solution.py:63
  26.8 5.5 %collective-permute-start = (bf16[80,4096]{1,0:T(8,128)(2,1)}, bf16[80,4096]{1,0:T(8,128)(2,1)S(1)}, u32[]{:S(2)}, u32[]{:S(2)}) collective-permute-start(bf16[80,4096]{1,0:T(8,128)(2,1)} %get-tuple-element.28), channel_id=1, source_target_pairs={{0,38},{32,2},{2,32},{34,4},{4,34},{36,6},{6,36},{38,0},{1,39},{33... | collective-permute-start | bytes 1966088 | tf_op jit(solution)/shard_map/ppermute | solution.py:54
  32.3 1.1 pad_maximum_fusion.refs_0_
  33.3 3.2 %collective-permute-start.7 = (bf16[1024,512]{1,0:T(8,128)(2,1)}, bf16[1024,512]{1,0:T(8,128)(2,1)}, u32[]{:S(2)}, u32[]{:S(2)}) collective-permute-start(bf16[1024,512]{1,0:T(8,128)(2,1)} %pad_maximum_fusion.refs_0_), channel_id=1, source_target_pairs={{0,192},{64,0},{128,64},{192,128},{1,193},{65,1},{129,65},{193,129... | collective-permute-start | bytes 3145736 | tf_op jit(solution)/shard_map/ppermute | solution.py:43
  37.3 1.5 collective-permute-start.13
  38.7 6.1 %collective-permute-done.oth_ref = bf16[80,4096]{1,0:T(8,128)(2,1)S(1)} collective-permute-done((bf16[80,4096]{1,0:T(8,128)(2,1)}, bf16[80,4096]{1,0:T(8,128)(2,1)S(1)}, u32[]{:S(2)}, u32[]{:S(2)}) %collective-permute-start) | collective-permute-done | bytes 655392 | tf_op jit(solution)/shard_map/ppermute | solution.py:54
  45.7 2.1 %collective-permute-done.1.oth_core_ref = bf16[80,4096]{1,0:T(8,128)(2,1)S(1)} collective-permute-done((bf16[80,4096]{1,0:T(8,128)(2,1)S(1)}, bf16[80,4096]{1,0:T(8,128)(2,1)S(1)}, u32[]{:S(2)}, u32[]{:S(2)}) %collective-permute-start.1) | collective-permute-done | bytes 655392 | tf_op jit(solution)/shard_map/ppermute | solution.py:47
  48.6 3.8 %arrange.1 = (bf16[256,3072]{1,0:T(8,128)(2,1)}, bf16[256,1024]{1,0:T(8,128)(2,1)}, bf16[256,32]{1,0:T(8,128)(2,1)}, bf16[2,16,128]{2,1,0:T(8,128)(2,1)}) custom-call(bf16[128,4096]{1,0:T(8,128)(2,1)} %x_ref.1, bf16[80,4096]{1,0:T(8,128)(2,1)} %copy-done.6, bf16[80,4096]{1,0:T(8,128)(2,1)} %copy-done.7, bf16[16,128]{1,0:T(8,128)(2,1)} %get-tuple-element.29.p_own_ref), custom_call_target="tpu_custom_call" | custom-call | tf_op jit(solution)/shard_map/arrange/pallas_call | solution.py:63
  52.4 1.9 targets.1
  54.3 2.0 %collective-permute-done.7.refs_2_ = bf16[1024,512]{1,0:T(8,128)(2,1)} collective-permute-done((bf16[1024,512]{1,0:T(8,128)(2,1)}, bf16[1024,512]{1,0:T(8,128)(2,1)}, u32[]{:S(2)}, u32[]{:S(2)}) %collective-permute-start.7) | collective-permute-done | bytes 1048608 | tf_op jit(solution)/shard_map/ppermute | solution.py:43
  56.4 3.4 %collective-permute-done.6.refs_1_ = bf16[1024,512]{1,0:T(8,128)(2,1)} collective-permute-done((bf16[1024,512]{1,0:T(8,128)(2,1)}, bf16[1024,512]{1,0:T(8,128)(2,1)}, u32[]{:S(2)}, u32[]{:S(2)}) %collective-permute-start.6) | collective-permute-done | bytes 1048608 | tf_op jit(solution)/shard_map/ppermute | solution.py:43
  59.8 1.9 slice.43
  61.6 1.9 slice.42
  63.5 3.2 %collective-permute-start.9 = (bf16[512,512]{1,0:T(8,128)(2,1)}, bf16[512,512]{1,0:T(8,128)(2,1)}, u32[]{:S(2)}, u32[]{:S(2)}) collective-permute-start(bf16[512,512]{1,0:T(8,128)(2,1)} %slice.43), channel_id=1, source_target_pairs={{0,192},{64,0},{128,64},{192,128},{1,193},{65,1},{129,65},{193,129... | collective-permute-start | bytes 1572872 | tf_op jit(solution)/shard_map/ppermute | solution.py:43
  68.2 1.6 collective-permute-start.15
  70.4 4.2 %near.1.total_ref = f32[256,512]{1,0:T(8,128)} custom-call(bf16[256,3072]{1,0:T(8,128)(2,1)} %get-tuple-element.33.x_ref, bf16[256,32]{1,0:T(8,128)(2,1)} %get-tuple-element.34.after_ref.p_ref, bf16[16,512]{1,0:T(8,128)(2,1)} %get-tuple-element.35.b_own_ref, bf16[16,512]{1,0:T(8,128)(2,1)} %slice.53.b_oth_ref, bf16[1024,512]{1,0:T(8,128)(2,1)} %pad_maximum_fusion.refs_0_, ...), custom_call_target="tpu_custom_call" | custom-call | tf_op jit(solution)/shard_map/near/pallas_call | solution.py:63
  74.6 2.8 %hidden.1 = (bf16[256,512]{1,0:T(8,128)(2,1)}, bf16[256,512]{1,0:T(8,128)(2,1)}) custom-call(bf16[256,1024]{1,0:T(8,128)(2,1)} %get-tuple-element.30.x_ref, f32[256,512]{1,0:T(8,128)} %near.1.total_ref, bf16[512,512]{1,0:T(8,128)(2,1)} %collective-permute-done.8.low_ref, bf16[512,512]{1,0:T(8,128)(2,1)} %collective-permute-done.9.high_ref), custom_call_target="tpu_custom_call" | custom-call | tf_op jit(solution)/shard_map/hidden/pallas_call | solution.py:63
  79.2 5.1 %output.1 = (f32[8,16,4096]{2,1,0:T(8,128)}, bf16[8,16,4096]{2,1,0:T(8,128)(2,1)}) custom-call(bf16[256,512]{1,0:T(8,128)(2,1)} %get-tuple-element.38.hidden_ref, bf16[1024,512]{1,0:T(8,128)(2,1)} %copy-done, bf16[1024,512]{1,0:T(8,128)(2,1)} %copy-done.2, bf16[1024,512]{1,0:T(8,128)(2,1)} %copy-done.1, bf16[512,512]{1,0:T(8,128)(2,1)} %copy-done.5, ...), custom_call_target="tpu_custom_call" | custom-call | tf_op jit(solution)/shard_map/output/pallas_call | solution.py:63
  84.4 2.9 %collective-permute-done.17 = bf16[8,16,4096]{2,1,0:T(8,128)(2,1)S(1)} collective-permute-done((bf16[8,16,4096]{2,1,0:T(8,128)(2,1)}, bf16[8,16,4096]{2,1,0:T(8,128)(2,1)S(1)}, u32[]{:S(2)}, u32[]{:S(2)}) %collective-permute-start.17) | collective-permute-done | bytes 1048608 | tf_op jit(solution)/shard_map/ppermute | solution.py:47
  87.2 1.9 fusion.1
  89.3 2.0 %collective-permute-start.19 = (bf16[4,16,2048]{2,1,0:T(8,128)(2,1)S(1)}, bf16[4,16,2048]{2,1,0:T(8,128)(2,1)S(1)}, u32[]{:S(2)}, u32[]{:S(2)}) collective-permute-start(bf16[4,16,2048]{2,1,0:T(8,128)(2,1)S(1)} %get-tuple-element.54), channel_id=1, source_target_pairs={{0,38},{32,2},{2,32},{34,4},{4,34},{36,6},{6,36},{38,0},{1,39},{33... | collective-permute-start | bytes 786440 | tf_op jit(solution)/shard_map/ppermute | solution.py:54
  91.3 6.3 %collective-permute-done.18 = bf16[4,16,2048]{2,1,0:T(8,128)(2,1)S(1)} collective-permute-done((bf16[4,16,2048]{2,1,0:T(8,128)(2,1)S(1)}, bf16[4,16,2048]{2,1,0:T(8,128)(2,1)S(1)}, u32[]{:S(2)}, u32[]{:S(2)}) %collective-permute-start.18) | collective-permute-done | bytes 262176 | tf_op jit(solution)/shard_map/ppermute | solution.py:47
  97.7 1.3 collective-permute-done.19
  99.1 19.4 %all_to_all.20 = bf16[4,16,4096]{2,1,0:T(8,128)(2,1)S(1)} all-to-all(bf16[4,16,4096]{2,1,0:T(8,128)(2,1)S(1)} %fusion), channel_id=1, replica_groups=mesh['y'=4,'l'=2,'x'=4,'h'=4,'c'=2] {'h'}, dimensions={0} | all-to-all | bytes 1048576 | tf_op jit(solution)/shard_map/all_to_all | solution.py:348
  118.6 18.5 %all_to_all.21.q_ref = bf16[4,16,4096]{2,1,0:T(8,128)(2,1)S(1)} all-to-all(bf16[4,16,4096]{2,1,0:T(8,128)(2,1)S(1)} %broadcast_in_dim.7), channel_id=1, replica_groups=mesh['y'=4,'l'=2,'x'=4,'h'=4,'c'=2] {'h'}, dimensions={0} | all-to-all | bytes 1048576 | tf_op jit(solution)/shard_map/all_to_all | solution.py:352
  137.9 7.0 %collective-permute-done.23.right_ref = bf16[4,16,2048]{2,1,0:T(8,128)(2,1)S(1)} collective-permute-done((bf16[4,16,2048]{2,1,0:T(8,128)(2,1)S(1)}, bf16[4,16,2048]{2,1,0:T(8,128)(2,1)S(1)}, u32[]{:S(2)}, u32[]{:S(2)}) %collective-permute-start.23) | collective-permute-done | bytes 262176 | tf_op jit(solution)/shard_map/ppermute | solution.py:54
  144.9 1.8 collective-permute-done.21.left_ref
  146.7 1.5 collective-permute-done.22.leftc_ref
  148.9 5.1 %backward.1 = (f32[16,512]{1,0:T(8,128)}, f32[16,512]{1,0:T(8,128)}, bf16[2,16,512]{2,1,0:T(8,128)(2,1)}, f32[16,16,128]{2,1,0:T(8,128)}) custom-call(bf16[4,16,4096]{2,1,0:T(8,128)(2,1)} %copy-done.3, bf16[4,16,4096]{2,1,0:T(8,128)(2,1)} %copy-done.8, bf16[4,16,2048]{2,1,0:T(8,128)(2,1)} %copy-done.11, bf16[4,16,2048]{2,1,0:T(8,128)(2,1)} %copy-done.13, ...), custom_call_target="tpu_custom_call" | custom-call | tf_op jit(solution)/shard_map/backward/pallas_call | solution.py:63
  154.0 13.1 %all_to_all.22.back_ref = f32[16,16,128]{2,1,0:T(8,128)} all-to-all(f32[16,16,128]{2,1,0:T(8,128)} %get-tuple-element.45), channel_id=1, replica_groups=mesh['y'=4,'l'=2,'x'=4,'h'=4,'c'=2] {'l','h','c'}, dimensions={0} | all-to-all | bytes 262144 | tf_op jit(solution)/shard_map/all_to_all | solution.py:373
  167.1 2.7 %down.1 = (f32[16,4096]{1,0:T(8,128)}, bf16[32,16,1152]{2,1,0:T(8,128)(2,1)}) custom-call(f32[16,16,128]{2,1,0:T(8,128)} %all_to_all.22.back_ref, bf16[128,4096]{1,0:T(8,128)(2,1)} %x_ref.1, bf16[16,4096]{1,0:T(8,128)(2,1)} %bitcast.6, bf16[2,16,512]{2,1,0:T(8,128)(2,1)} %get-tuple-element.46.up_ref), custom_call_target="tpu_custom_call" | custom-call | tf_op jit(solution)/shard_map/down/pallas_call | solution.py:63
  169.8 6.6 %all-to-all-start.3 = ((bf16[32,16,1152]{2,1,0:T(8,128)(2,1)}), bf16[32,16,1152]{2,1,0:T(8,128)(2,1)S(1)}, u32[]{:S(2)}, u32[]{:S(2)}) async-start(bf16[32,16,1152]{2,1,0:T(8,128)(2,1)} %get-tuple-element.47), calls=%async_computation.3 | async-start | bytes 2359296 | tf_op jit(solution)/shard_map/all_to_all | solution.py:380
  176.4 1.6 collective-permute-start.25
  177.9 14.8 %collective-permute-done.25 = f32[16,512]{1,0:T(8,128)S(1)} collective-permute-done((f32[16,512]{1,0:T(8,128)S(1)}, f32[16,512]{1,0:T(8,128)S(1)}, u32[]{:S(2)}, u32[]{:S(2)}) %collective-permute-start.25) | collective-permute-done | bytes 32800 | tf_op jit(solution)/shard_map/ppermute | solution.py:47
  193.3 2.3 %all-to-all-done.3.wire_ref = bf16[32,16,1152]{2,1,0:T(8,128)(2,1)S(1)} async-done(((bf16[32,16,1152]{2,1,0:T(8,128)(2,1)}), bf16[32,16,1152]{2,1,0:T(8,128)(2,1)S(1)}, u32[]{:S(2)}, u32[]{:S(2)}) %all-to-all-start.3) | async-done | bytes 1179680 | tf_op jit(solution)/shard_map/all_to_all | solution.py:380
  195.6 1.1 copy-done.4
  196.7 2.4 %merge.1 = f32[128,1024]{1,0:T(8,128)} custom-call(bf16[32,16,1152]{2,1,0:T(8,128)(2,1)} %copy-done.4, bf16[128,1024]{1,0:T(8,128)(2,1)} %w_ref.1), custom_call_target="tpu_custom_call" | custom-call | tf_op jit(solution)/shard_map/merge/pallas_call | solution.py:63
  (70 shorter events, 9.3 us)
Async XLA Ops:
  2.5 8.8 %collective-permute-start.2 = (bf16[272,512]{1,0:T(8,128)(2,1)}, bf16[272,512]{1,0:T(8,128)(2,1)S(1)}, u32[]{:S(2)}, u32[]{:S(2)}) collective-permute-start(bf16[272,512]{1,0:T(8,128)(2,1)} %send.1.send_ref), channel_id=1, source_target_pairs={{0,32},{32,0},{1,33},{33,1},{2,34},{34,2},{3,35},{35,3},{4,36},{36... | collective-permute-start | bytes 835592 | tf_op jit(solution)/shard_map/ppermute | solution.py:47
  12.3 7.4 %collective-permute-start.3 = (bf16[256,512]{1,0:T(8,128)(2,1)S(1)}, bf16[256,512]{1,0:T(8,128)(2,1)S(1)}, u32[]{:S(2)}, u32[]{:S(2)}) collective-permute-start(bf16[256,512]{1,0:T(8,128)(2,1)S(1)} %maximum_select_fusion), channel_id=1, source_target_pairs={{0,8},{8,16},{16,24},{24,0},{1,9},{9,17},{17,25},{25,1},{2,10},{10... | collective-permute-start | bytes 786440 | tf_op jit(solution)/shard_map/ppermute | solution.py:43
  14.9 9.3 %collective-permute-start.10 = (bf16[256,512]{1,0:T(8,128)(2,1)S(1)}, bf16[256,512]{1,0:T(8,128)(2,1)S(1)}, u32[]{:S(2)}, u32[]{:S(2)}) collective-permute-start(bf16[256,512]{1,0:T(8,128)(2,1)S(1)} %maximum_select_fusion.1), channel_id=1, source_target_pairs={{0,64},{64,128},{128,192},{192,0},{1,65},{65,129},{129,193},{193,1... | collective-permute-start | bytes 786440 | tf_op jit(solution)/shard_map/ppermute | solution.py:43
  16.6 15.7 %collective-permute-start.4 = (bf16[256,512]{1,0:T(8,128)(2,1)S(1)}, bf16[256,512]{1,0:T(8,128)(2,1)S(1)}, u32[]{:S(2)}, u32[]{:S(2)}) collective-permute-start(bf16[256,512]{1,0:T(8,128)(2,1)S(1)} %maximum_select_fusion), channel_id=1, source_target_pairs={{0,24},{8,0},{16,8},{24,16},{1,25},{9,1},{17,9},{25,17},{2,26},{10... | collective-permute-start | bytes 786440 | tf_op jit(solution)/shard_map/ppermute | solution.py:43
  19.8 12.5 %collective-permute-start.5 = (bf16[256,512]{1,0:T(8,128)(2,1)S(1)}, bf16[256,512]{1,0:T(8,128)(2,1)S(1)}, u32[]{:S(2)}, u32[]{:S(2)}) collective-permute-start(bf16[256,512]{1,0:T(8,128)(2,1)S(1)} %collective-permute-done.3), channel_id=1, source_target_pairs={{0,8},{8,16},{16,24},{24,0},{1,9},{9,17},{17,25},{25,1},{2,10},{10... | collective-permute-start | bytes 786440 | tf_op jit(solution)/shard_map/ppermute | solution.py:43
  21.3 15.3 %collective-permute-start.11 = (bf16[256,512]{1,0:T(8,128)(2,1)S(1)}, bf16[256,512]{1,0:T(8,128)(2,1)S(1)}, u32[]{:S(2)}, u32[]{:S(2)}) collective-permute-start(bf16[256,512]{1,0:T(8,128)(2,1)S(1)} %maximum_select_fusion.1), channel_id=1, source_target_pairs={{0,192},{64,0},{128,64},{192,128},{1,193},{65,1},{129,65},{193,129... | collective-permute-start | bytes 786440 | tf_op jit(solution)/shard_map/ppermute | solution.py:43
  24.3 12.3 %collective-permute-start.12 = (bf16[256,512]{1,0:T(8,128)(2,1)S(1)}, bf16[256,512]{1,0:T(8,128)(2,1)S(1)}, u32[]{:S(2)}, u32[]{:S(2)}) collective-permute-start(bf16[256,512]{1,0:T(8,128)(2,1)S(1)} %collective-permute-done.10), channel_id=1, source_target_pairs={{0,64},{64,128},{128,192},{192,0},{1,65},{65,129},{129,193},{193,1... | collective-permute-start | bytes 786440 | tf_op jit(solution)/shard_map/ppermute | solution.py:43
  26.8 18.1 %collective-permute-start = (bf16[80,4096]{1,0:T(8,128)(2,1)}, bf16[80,4096]{1,0:T(8,128)(2,1)S(1)}, u32[]{:S(2)}, u32[]{:S(2)}) collective-permute-start(bf16[80,4096]{1,0:T(8,128)(2,1)} %get-tuple-element.28), channel_id=1, source_target_pairs={{0,38},{32,2},{2,32},{34,4},{4,34},{36,6},{6,36},{38,0},{1,39},{33... | collective-permute-start | bytes 1966088 | tf_op jit(solution)/shard_map/ppermute | solution.py:54
  33.3 23.1 %collective-permute-start.7 = (bf16[1024,512]{1,0:T(8,128)(2,1)}, bf16[1024,512]{1,0:T(8,128)(2,1)}, u32[]{:S(2)}, u32[]{:S(2)}) collective-permute-start(bf16[1024,512]{1,0:T(8,128)(2,1)} %pad_maximum_fusion.refs_0_), channel_id=1, source_target_pairs={{0,192},{64,0},{128,64},{192,128},{1,193},{65,1},{129,65},{193,129... | collective-permute-start | bytes 3145736 | tf_op jit(solution)/shard_map/ppermute | solution.py:43
  36.5 23.2 %collective-permute-start.6 = (bf16[1024,512]{1,0:T(8,128)(2,1)}, bf16[1024,512]{1,0:T(8,128)(2,1)}, u32[]{:S(2)}, u32[]{:S(2)}) collective-permute-start(bf16[1024,512]{1,0:T(8,128)(2,1)} %pad_maximum_fusion.refs_0_), channel_id=1, source_target_pairs={{0,64},{64,128},{128,192},{192,0},{1,65},{65,129},{129,193},{193,1... | collective-permute-start | bytes 3145736 | tf_op jit(solution)/shard_map/ppermute | solution.py:43
  36.6 25.0 %copy-start = (bf16[1024,512]{1,0:T(8,128)(2,1)}, bf16[1024,512]{1,0:T(8,128)(2,1)S(1)}, u32[]{:S(2)}) copy-start(bf16[1024,512]{1,0:T(8,128)(2,1)S(1)} %pad_maximum_fusion.1.refs_0_) | copy-start | bytes 3145732
  36.6 30.1 %collective-permute-start.14 = (bf16[1024,512]{1,0:T(8,128)(2,1)S(1)}, bf16[1024,512]{1,0:T(8,128)(2,1)S(1)}, u32[]{:S(2)}, u32[]{:S(2)}) collective-permute-start(bf16[1024,512]{1,0:T(8,128)(2,1)S(1)} %pad_maximum_fusion.1.refs_0_), channel_id=1, source_target_pairs={{0,24},{8,0},{16,8},{24,16},{1,25},{9,1},{17,9},{25,17},{2,26},{10... | collective-permute-start | bytes 3145736 | tf_op jit(solution)/shard_map/ppermute | solution.py:43
  37.3 30.9 %collective-permute-start.13 = (bf16[1024,512]{1,0:T(8,128)(2,1)S(1)}, bf16[1024,512]{1,0:T(8,128)(2,1)S(1)}, u32[]{:S(2)}, u32[]{:S(2)}) collective-permute-start(bf16[1024,512]{1,0:T(8,128)(2,1)S(1)} %pad_maximum_fusion.1.refs_0_), channel_id=1, source_target_pairs={{0,8},{8,16},{16,24},{24,0},{1,9},{9,17},{17,25},{25,1},{2,10},{10... | collective-permute-start | bytes 3145736 | tf_op jit(solution)/shard_map/ppermute | solution.py:43
  44.8 0.8 copy-start.6
  45.7 2.1 %collective-permute-start.1 = (bf16[80,4096]{1,0:T(8,128)(2,1)S(1)}, bf16[80,4096]{1,0:T(8,128)(2,1)S(1)}, u32[]{:S(2)}, u32[]{:S(2)}) collective-permute-start(bf16[80,4096]{1,0:T(8,128)(2,1)S(1)} %collective-permute-done.oth_ref), channel_id=1, source_target_pairs={{0,1},{1,0},{2,3},{3,2},{4,5},{5,4},{6,7},{7,6},{8,9},{9,8},{10,11... | collective-permute-start | bytes 1966088 | tf_op jit(solution)/shard_map/ppermute | solution.py:47
  47.8 0.9 copy-start.7
  63.5 11.1 %collective-permute-start.8 = (bf16[512,512]{1,0:T(8,128)(2,1)}, bf16[512,512]{1,0:T(8,128)(2,1)}, u32[]{:S(2)}, u32[]{:S(2)}) collective-permute-start(bf16[512,512]{1,0:T(8,128)(2,1)} %slice.42), channel_id=1, source_target_pairs={{0,64},{64,128},{128,192},{192,0},{1,65},{65,129},{129,193},{193,1... | collective-permute-start | bytes 1572872 | tf_op jit(solution)/shard_map/ppermute | solution.py:43
  63.5 11.1 %collective-permute-start.9 = (bf16[512,512]{1,0:T(8,128)(2,1)}, bf16[512,512]{1,0:T(8,128)(2,1)}, u32[]{:S(2)}, u32[]{:S(2)}) collective-permute-start(bf16[512,512]{1,0:T(8,128)(2,1)} %slice.43), channel_id=1, source_target_pairs={{0,192},{64,0},{128,64},{192,128},{1,193},{65,1},{129,65},{193,129... | collective-permute-start | bytes 1572872 | tf_op jit(solution)/shard_map/ppermute | solution.py:43
  66.8 7.9 %copy-start.1 = (bf16[1024,512]{1,0:T(8,128)(2,1)}, bf16[1024,512]{1,0:T(8,128)(2,1)S(1)}, u32[]{:S(2)}) copy-start(bf16[1024,512]{1,0:T(8,128)(2,1)S(1)} %collective-permute-done.14.refs_2_) | copy-start | bytes 3145732
  67.6 9.8 %collective-permute-start.16 = (bf16[512,512]{1,0:T(8,128)(2,1)}, bf16[512,512]{1,0:T(8,128)(2,1)}, u32[]{:S(2)}, u32[]{:S(2)}) collective-permute-start(bf16[512,512]{1,0:T(8,128)(2,1)} %slice.56), channel_id=1, source_target_pairs={{0,24},{8,0},{16,8},{24,16},{1,25},{9,1},{17,9},{25,17},{2,26},{10... | collective-permute-start | bytes 1572872 | tf_op jit(solution)/shard_map/ppermute | solution.py:43
  68.2 6.4 %copy-start.2 = (bf16[1024,512]{1,0:T(8,128)(2,1)}, bf16[1024,512]{1,0:T(8,128)(2,1)S(1)}, u32[]{:S(2)}) copy-start(bf16[1024,512]{1,0:T(8,128)(2,1)S(1)} %collective-permute-done.13.refs_1_) | copy-start | bytes 3145732
  68.2 10.2 %collective-permute-start.15 = (bf16[512,512]{1,0:T(8,128)(2,1)S(1)}, bf16[512,512]{1,0:T(8,128)(2,1)S(1)}, u32[]{:S(2)}, u32[]{:S(2)}) collective-permute-start(bf16[512,512]{1,0:T(8,128)(2,1)S(1)} %slice.55), channel_id=1, source_target_pairs={{0,8},{8,16},{16,24},{24,0},{1,9},{9,17},{17,25},{25,1},{2,10},{10... | collective-permute-start | bytes 1572872 | tf_op jit(solution)/shard_map/ppermute | solution.py:43
  78.4 0.8 copy-start.5
  84.4 2.9 %collective-permute-start.17 = (bf16[8,16,4096]{2,1,0:T(8,128)(2,1)}, bf16[8,16,4096]{2,1,0:T(8,128)(2,1)S(1)}, u32[]{:S(2)}, u32[]{:S(2)}) collective-permute-start(bf16[8,16,4096]{2,1,0:T(8,128)(2,1)} %get-tuple-element.41), channel_id=1, source_target_pairs={{0,1},{1,0},{2,3},{3,2},{4,5},{5,4},{6,7},{7,6},{8,9},{9,8},{10,11... | collective-permute-start | bytes 3145736 | tf_op jit(solution)/shard_map/ppermute | solution.py:47
  89.2 29.3 %copy-start.9 = (bf16[16,4096]{1,0:T(8,128)(2,1)S(1)}, bf16[16,4096]{1,0:T(8,128)(2,1)}, u32[]{:S(2)}) copy-start(bf16[16,4096]{1,0:T(8,128)(2,1)} %targets.1) | copy-start | bytes 393220
  89.2 8.4 %collective-permute-start.18 = (bf16[4,16,2048]{2,1,0:T(8,128)(2,1)S(1)}, bf16[4,16,2048]{2,1,0:T(8,128)(2,1)S(1)}, u32[]{:S(2)}, u32[]{:S(2)}) collective-permute-start(bf16[4,16,2048]{2,1,0:T(8,128)(2,1)S(1)} %get-tuple-element.53), channel_id=1, source_target_pairs={{0,32},{32,0},{1,33},{33,1},{2,34},{34,2},{3,35},{35,3},{4,36},{36... | collective-permute-start | bytes 786440 | tf_op jit(solution)/shard_map/ppermute | solution.py:47
  89.3 9.6 %collective-permute-start.19 = (bf16[4,16,2048]{2,1,0:T(8,128)(2,1)S(1)}, bf16[4,16,2048]{2,1,0:T(8,128)(2,1)S(1)}, u32[]{:S(2)}, u32[]{:S(2)}) collective-permute-start(bf16[4,16,2048]{2,1,0:T(8,128)(2,1)S(1)} %get-tuple-element.54), channel_id=1, source_target_pairs={{0,38},{32,2},{2,32},{34,4},{4,34},{36,6},{6,36},{38,0},{1,39},{33... | collective-permute-start | bytes 786440 | tf_op jit(solution)/shard_map/ppermute | solution.py:54
  137.2 11.0 %copy-start.3 = (bf16[4,16,4096]{2,1,0:T(8,128)(2,1)}, bf16[4,16,4096]{2,1,0:T(8,128)(2,1)S(1)}, u32[]{:S(2)}) copy-start(bf16[4,16,4096]{2,1,0:T(8,128)(2,1)S(1)} %all_to_all.21.q_ref) | copy-start | bytes 1572868
  137.2 7.7 %collective-permute-start.23 = (bf16[4,16,2048]{2,1,0:T(8,128)(2,1)S(1)}, bf16[4,16,2048]{2,1,0:T(8,128)(2,1)S(1)}, u32[]{:S(2)}, u32[]{:S(2)}) collective-permute-start(bf16[4,16,2048]{2,1,0:T(8,128)(2,1)S(1)} %get-tuple-element.55), channel_id=1, source_target_pairs={{0,38},{32,2},{2,32},{34,4},{4,34},{36,6},{6,36},{38,0},{1,39},{33... | collective-permute-start | bytes 786440 | tf_op jit(solution)/shard_map/ppermute | solution.py:54
  137.9 8.7 %collective-permute-start.20 = (bf16[4,16,4096]{2,1,0:T(8,128)(2,1)S(1)}, bf16[4,16,4096]{2,1,0:T(8,128)(2,1)S(1)}, u32[]{:S(2)}, u32[]{:S(2)}) collective-permute-start(bf16[4,16,4096]{2,1,0:T(8,128)(2,1)S(1)} %all_to_all.21.q_ref), channel_id=1, source_target_pairs={{0,1},{1,0},{2,3},{3,2},{4,5},{5,4},{6,7},{7,6},{8,9},{9,8},{10,11... | collective-permute-start | bytes 1572872 | tf_op jit(solution)/shard_map/ppermute | solution.py:47
  137.9 8.7 %collective-permute-start.21 = (bf16[4,16,2048]{2,1,0:T(8,128)(2,1)S(1)}, bf16[4,16,2048]{2,1,0:T(8,128)(2,1)S(1)}, u32[]{:S(2)}, u32[]{:S(2)}) collective-permute-start(bf16[4,16,2048]{2,1,0:T(8,128)(2,1)S(1)} %get-tuple-element.56), channel_id=1, source_target_pairs={{0,32},{32,0},{1,33},{33,1},{2,34},{34,2},{3,35},{35,3},{4,36},{36... | collective-permute-start | bytes 786440 | tf_op jit(solution)/shard_map/ppermute | solution.py:47
  144.9 3.3 %copy-start.10 = (bf16[4,16,2048]{2,1,0:T(8,128)(2,1)}, bf16[4,16,2048]{2,1,0:T(8,128)(2,1)S(1)}, u32[]{:S(2)}) copy-start(bf16[4,16,2048]{2,1,0:T(8,128)(2,1)S(1)} %collective-permute-done.23.right_ref) | copy-start | bytes 786436
  144.9 1.8 collective-permute-start.24
  146.6 1.5 copy-start.11
  146.6 1.5 collective-permute-start.22
  146.7 1.5 copy-start.8
  146.7 1.5 copy-start.12
  148.2 0.7 copy-start.13
  154.0 22.4 %copy-start.15 = (f32[16,512]{1,0:T(8,128)S(1)}, f32[16,512]{1,0:T(8,128)}, u32[]{:S(2)}) copy-start(f32[16,512]{1,0:T(8,128)} %get-tuple-element.50) | copy-start | bytes 98308
  154.0 38.8 %copy-start.14 = (f32[16,512]{1,0:T(8,128)S(1)}, f32[16,512]{1,0:T(8,128)}, u32[]{:S(2)}) copy-start(f32[16,512]{1,0:T(8,128)} %get-tuple-element.49) | copy-start | bytes 98308
  169.8 25.8 %all-to-all-start.3 = ((bf16[32,16,1152]{2,1,0:T(8,128)(2,1)}), bf16[32,16,1152]{2,1,0:T(8,128)(2,1)S(1)}, u32[]{:S(2)}, u32[]{:S(2)}) async-start(bf16[32,16,1152]{2,1,0:T(8,128)(2,1)} %get-tuple-element.47), calls=%async_computation.3 | async-start | bytes 2359296 | tf_op jit(solution)/shard_map/all_to_all | solution.py:380
  176.4 16.4 %collective-permute-start.25 = (f32[16,512]{1,0:T(8,128)S(1)}, f32[16,512]{1,0:T(8,128)S(1)}, u32[]{:S(2)}, u32[]{:S(2)}) collective-permute-start(f32[16,512]{1,0:T(8,128)S(1)} %copy-done.15), channel_id=1, source_target_pairs={{0,32},{32,0},{1,33},{33,1},{2,34},{34,2},{3,35},{35,3},{4,36},{36... | collective-permute-start | bytes 98312 | tf_op jit(solution)/shard_map/ppermute | solution.py:47
  195.6 1.1 copy-start.4

commit v6 on v5

--- a/solution.py
+++ b/solution.py
@@ -150,18 +150,18 @@
 
 
 def near_kernel(x_ref, p_ref, b_own_ref, b_oth_ref, *refs):
-    pieces, total_ref = refs[:3], refs[3]
+    pieces, total_ref = refs[:6], refs[6]
     b = jnp.concatenate([b_own_ref[...], b_oth_ref[...]], axis=0)
     total = ADAPTER_SCALE * dot(p_ref[...], b)
-    for k, piece in enumerate(pieces):
-        total = total + dot(x_ref[:, k * 1024 : (k + 1) * 1024], piece[...])
+    for cols, piece in spans(pieces):
+        total = total + dot(x_ref[:, cols], piece[...])
     total_ref[...] = total
 
 
 def hidden_kernel(x_ref, total_ref, low_ref, high_ref, hidden_ref, mask_ref):
     total = total_ref[...]
-    for k, piece in enumerate((low_ref, high_ref)):
-        total = total + dot(x_ref[:, k * HID : (k + 1) * HID], piece[...])
+    for cols, piece in spans((low_ref, high_ref)):
+        total = total + dot(x_ref[:, cols], piece[...])
     preact = total * MODEL_WIDTH ** (-0.5)
     hidden_ref[...] = jnp.maximum(preact, 0.0).astype(BF16)
     mask_ref[...] = jnp.where(preact > 0, 1.0, 0.0).astype(BF16)
@@ -175,7 +175,7 @@
 
 
 def output_kernel(hidden_ref, *refs):
-    pieces, (keep_ref, send_ref) = refs[:5], refs[5:]
+    pieces, (keep_ref, send_ref) = refs[:8], refs[8:]
     for cols, piece in spans(pieces):
         part = dot_nt(hidden_ref[...], piece[...]).reshape(8, 2, ROWS, piece.shape[0])
         keep_ref[:, :, cols] = part[:, 0]
@@ -184,8 +184,7 @@
 
 def backward_kernel(q_ref, qc_ref, left_ref, leftc_ref, right_ref, rightc_ref, mask_ref, pt_ref,
                     b_own_ref, b_oth_ref, *refs):
-    pieces, (up_own_ref, up_oth_ref, wire_ref, back_ref, grad_ref, own_ref, oth_ref) = refs[:5], refs[5:]
-    l = lax.axis_index("l")
+    pieces, (up_ref, back_ref, grad_ref, own_ref, oth_ref) = refs[:8], refs[8:]
     for i in range(16):
         j, e = (i // 2) % 4, i % 2
         here = slice(i * ROWS, (i + 1) * ROWS)
@@ -203,24 +202,23 @@
         ref = own_ref if i < 8 else oth_ref
         ref[pl.ds(token_row(i), ROWS), :] = total[i * ROWS : (i + 1) * ROWS]
     scale = ADAPTER_SCALE * MODEL_WIDTH ** (-0.5)
-    sides = (
-        (l, own_ref, pt_ref[0], up_own_ref, b_own_ref[...]),
-        (1 - l, oth_ref, pt_ref[1], up_oth_ref, b_oth_ref[...]),
-    )
-    for side, hid_ref, p, up_ref, b in sides:
-        up = b.astype(F32) - RATE_UP * (scale * dot(p, hid_ref[...]))
-        up_ref[...] = up
-        wire_ref[side] = up.astype(BF16)
-        back = dot_nt(b, hid_ref[...])
-        for k in range(8):
-            back_ref[side * 8 + k] = back
-
-
-def down_kernel(back_ref, x_ref, a_ref, up_ref, new_ref, wire_ref):
-    terms = [back_ref[k] for k in range(16)]
-    while len(terms) > 1:
-        terms = [terms[k] + terms[k + 1] for k in range(0, len(terms), 2)]
-    rest = terms[0]
+    for side, (hid_ref, b_ref) in enumerate(((own_ref, b_own_ref), (oth_ref, b_oth_ref))):
+        grad = dot(pt_ref[side], hid_ref[...])
+        up_ref[side] = b_ref[...].astype(F32) - RATE_UP * (scale * grad)
+        back_ref[side] = dot_nt(b_ref[...], hid_ref[...])
+
+
+def ups_kernel(mine_ref, arrived_ref, new_ref, wire_ref):
+    l = lax.axis_index("l")
+    for ref, half in ((mine_ref, l), (arrived_ref, 1 - l)):
+        new_ref[:, lanes(half * HID, HID)] = ref[0]
+        for side, row in ((0, l * RANK), (1, (1 - l) * RANK)):
+            rows = pl.ds(pl.multiple_of(row, RANK), RANK)
+            wire_ref[rows, lanes(half * HID, HID)] = ref[side].astype(BF16)
+
+
+def down_kernel(t0_ref, t1_ref, t2_ref, t3_ref, x_ref, a_ref, new_ref, wire_ref):
+    rest = (t0_ref[...] + t1_ref[...]) + (t2_ref[...] + t3_ref[...])
     parts = []
     for _ in range(3):
         parts.append(rest.astype(BF16))
@@ -234,40 +232,38 @@
         new = a_ref[:, here].astype(F32) - RATE_DOWN * (scale * grad)
         new_ref[:, here] = new
         for j in range(4):
-            wire_ref[k * 4 + j, :, :BLOCK] = new[:, j * BLOCK : (j + 1) * BLOCK].astype(BF16)
+            wire_ref[k * 4 + j] = new[:, j * BLOCK : (j + 1) * BLOCK].astype(BF16)
+
+
+def merge_kernel(wire_ref, u0_ref, u1_ref, u2_ref, u3_ref, w_ref, out_ref, d_ref):
+    y, x = lax.axis_index("y"), lax.axis_index("x")
+    total = None
+    for k, (dy, u_ref) in enumerate(zip(RING, (u0_ref, u1_ref, u2_ref, u3_ref))):
+        for j, dx in enumerate(RING):
             for l in range(2):
-                begin = BLOCK + l * HID
-                wire_ref[k * 4 + j, :, begin : begin + HID] = up_ref[l]
-
-
-def merge_kernel(wire_ref, w_ref, out_ref, d_ref, u_ref):
-    for y in range(4):
-        for x in range(4):
-            for l in range(2):
-                at = ((y * 4 + x) * 2 + l) * RANK
-                d_ref[at : at + RANK, :] = wire_ref[y * 8 + l * 4 + x, :, :BLOCK]
-    for side in range(2):
-        for y in range(4):
-            for x in range(4):
-                for l in range(2):
-                    at = ((y * 4 + x) * 2 + l) * RANK
-                    begin = BLOCK + l * HID
-                    u_ref[at : at + RANK, :] = wire_ref[
-                        y * 8 + side * 4 + x, :, begin : begin + HID
-                    ]
-        here = slice(side * HID, (side + 1) * HID)
-        delta = dot_tn(d_ref[...], u_ref[...])
-        out_ref[:, here] = w_ref[:, here].astype(F32) + ADAPTER_SCALE / 32 * delta
-
-
-def ring(value, axis):
-    below, above = shift(value, axis, 1), shift(value, axis, -1)
-    return [value, below, above, shift(below, axis, 1)]
-
-
-def far_halves(below, above, axis):
-    half = below.shape[0] // 2
-    return [shift(below[:half], axis, 1), shift(above[half:], axis, -1)]
+                at = ((k * 4 + j) * 2 + l) * RANK
+                d_ref[at : at + RANK, :] = wire_ref[((y + dy) % 4) * 8 + l * 4 + (x + dx) % 4]
+        term = dot_tn(d_ref[k * TOK : (k + 1) * TOK, :], u_ref[...])
+        total = term if total is None else total + term
+    out_ref[...] = w_ref[...].astype(F32) + ADAPTER_SCALE / 32 * total
+
+
+def gather_grid(value, first, second):
+    below, above = shift(value, first, 1), shift(value, first, -1)
+    low = jnp.concatenate([value, below], axis=0)
+    high = jnp.concatenate([above, shift(below, first, 1)], axis=0)
+    near = [low, high]
+    for by in (1, -1):
+        near += [shift(low, second, by), shift(high, second, by)]
+    return near, [shift(near[2], second, 1), shift(near[5], second, -1)]
+
+
+def ring_direct(value, axis):
+    return [value, shift(value, axis, 1), shift(value, axis, -1), shift(value, axis, 2)]
+
+
+def swap(value, mask):
+    return lax.ppermute(value, "h", [(i, i ^ mask) for i in range(4)])
 
 
 def shards(tokens, targets, w_in, w_out, factor_down, factor_up):
@@ -299,10 +295,9 @@
             l == 0, jnp.concatenate([own, oth], axis=0), jnp.concatenate([oth, own], axis=0)
         )
 
-    in_line = jnp.concatenate(ring(joined(in_own, w_oth[:TOK]), "x"), axis=0)
-    out_line = jnp.concatenate(ring(joined(out_own, w_oth[TOK : 2 * TOK]), "y"), axis=0)
-    in_near = [in_line, shift(in_line, "y", 1), shift(in_line, "y", -1)]
-    out_near = [out_line, shift(out_line, "x", 1), shift(out_line, "x", -1)]
+    in_near, in_far = gather_grid(joined(in_own, w_oth[:TOK]), "x", "y")
+    out_near, out_far = gather_grid(joined(out_own, w_oth[TOK : 2 * TOK]), "y", "x")
+    out_pieces = out_near + out_far
 
     x_near, x_far, p_rel, pt = call(
         arrange_kernel,
@@ -311,15 +306,6 @@
         scratch=[pltpu.VMEM((2, TOK, RANK), BF16)],
         name="arrange",
     )
-    my_targets = call(
-        targets_kernel, shape(ROWS, MODEL_WIDTH), targets, after=[p_rel], name="targets"
-    )
-    in_near[1], in_near[2], x_near, p_rel, my_targets = lax.optimization_barrier(
-        (in_near[1], in_near[2], x_near, p_rel, my_targets)
-    )
-    in_far = far_halves(in_near[1], in_near[2], "y")
-    out_far = far_halves(out_near[1], out_near[2], "x")
-    out_pieces = out_near + out_far
     total = call(
         near_kernel,
         shape(2 * TOK, HID, dtype=F32),
@@ -337,6 +323,10 @@
         (shape(8, ROWS, MODEL_WIDTH, dtype=F32), shape(8, ROWS, MODEL_WIDTH)),
         hidden, *out_pieces,
         name="output",
+    )
+
+    my_targets = call(
+        targets_kernel, shape(ROWS, MODEL_WIDTH), targets, after=[send], name="targets"
     )
 
     summed = keep + partner(send, "c").astype(F32)
@@ -354,14 +344,9 @@
     right = near_z(q[:, :, SIDE:])
     q_far, left_far, right_far = partner(q, "c"), partner(left, "c"), partner(right, "c")
 
-    up_own, up_oth, up_wire, back = call(
+    ups, back = call(
         backward_kernel,
-        (
-            shape(RANK, HID, dtype=F32),
-            shape(RANK, HID, dtype=F32),
-            shape(2, RANK, HID),
-            shape(16, RANK, TOK, dtype=F32),
-        ),
+        (shape(2, RANK, HID, dtype=F32), shape(2, RANK, TOK, dtype=F32)),
         q, q_far, left, left_far, right, right_far, mask, pt, b_own, b_oth, *out_pieces,
         scratch=[
             pltpu.VMEM((2 * TOK, MODEL_WIDTH), BF16),
@@ -370,25 +355,30 @@
         ],
         name="backward",
     )
-    back = lax.all_to_all(back, ("l", "h", "c"), 0, 0, tiled=True)
+    back = back + partner(back, "c")
+    ups_arrived = partner(ups[::-1], "l")
+    back = back[0] + partner(back[1], "l")
+    back = [back] + [swap(back, mask) for mask in (1, 2, 3)]
+    new_b, up_wire = call(
+        ups_kernel,
+        (shape(RANK, 2 * HID, dtype=F32), shape(2 * RANK, 2 * HID)),
+        ups, ups_arrived,
+        name="ups",
+    )
+    up_line = jnp.concatenate(ring_direct(up_wire, "x"), axis=0)
+    up_grid = ring_direct(up_line, "y")
     new_a, wire = call(
         down_kernel,
-        (shape(RANK, MODEL_WIDTH, dtype=F32), shape(32, RANK, BLOCK + 2 * HID)),
-        back, tokens, a, up_wire,
+        (shape(RANK, MODEL_WIDTH, dtype=F32), shape(32, RANK, BLOCK)),
+        *back, tokens, a,
         name="down",
     )
     wires = lax.all_to_all(wire, REP, 0, 0, tiled=True)
-    up_arrived = partner(up_oth, "l")
-    new_b = jnp.where(
-        l == 0,
-        jnp.concatenate([up_own, up_arrived], axis=1),
-        jnp.concatenate([up_arrived, up_own], axis=1),
-    )
     merged = call(
         merge_kernel,
         shape(TOK, 2 * HID, dtype=F32),
-        wires, w_in,
-        scratch=[pltpu.VMEM((32 * RANK, BLOCK), BF16), pltpu.VMEM((32 * RANK, HID), BF16)],
+        wires, *up_grid, w_in,
+        scratch=[pltpu.VMEM((32 * RANK, BLOCK), BF16)],
         name="merge",
     )
     return merged, new_a[None], new_b[None]

time: 201 us -> 219 us (1.090)
  starting transfers between devices: 37.3 us -> 55.9 us
  waiting for transfers between devices: 60 us -> 76.6 us
  blocking collectives: 51 us -> 36.2 us
  local copies, waits for them, and re-layouts: 9.64 us -> 7.08 us
    ppermute x14 -> x24, waiting for transfers between devices: 9.11 us -> 40.8 us  [shift(): return lax.ppermute(value, axis, [(i, (i + by) % n) for i in range(n)])]
    ppermute x9 -> x11, waiting for transfers between devices: 34.3 us -> 12.9 us  [partner(): return lax.ppermute(value, axis, [(0, 1), (1, 0)])]
    all_to_all x2 -> x1, blocking collectives: 32.5 us -> 16 us  [shards(): wires = lax.all_to_all(wire, REP, 0, 0, tiled=True)]
    ppermute x14 -> x24, starting transfers between devices: 18.9 us -> 32.5 us  [shift(): return lax.ppermute(value, axis, [(i, (i + by) % n) for i in range(n)])]
    all_to_all x1, waiting for transfers between devices: 2.26 us -> 12.4 us  [shards(): shares = lax.all_to_all(summed.astype(BF16), 'h', 0, 0, tiled=True)]
    ppermute x0 -> x3, starting transfers between devices: none -> 6.5 us  [swap(): return lax.ppermute(value, 'h', [(i, i ^ mask) for i in range(4)])]
    slice x4 -> x0, local copies, waits for them, and re-layouts: 4.66 us -> none  [far_halves(): return [shift(below[:half], axis, 1), shift(above[half:], axis, -1)]]
    ppermute x3, waiting for transfers between devices: 14.4 us -> 10.6 us  [near_z(): lax.ppermute(value, Z, [(place(z), place(z + 1 if z % 2 else z - 1)) for...]
  transfers between devices with their start and end apart: 27 -> 42, of which waited for: 15 -> 18; matrix products, arithmetic and copies ran while one was open for 4% -> 2% of each run, Pallas kernels for 9% -> 10%
where the time goes in v6:
time: 219 us; the launch traced here: 218 us
  waiting for transfers between devices  76.6 us (35%)
  starting transfers between devices  55.9 us (26%)
  blocking collectives  36.2 us (17%)
  Pallas kernels  35.6 us (16%)
  local copies, waits for them, and re-layouts  7.08 us (3%)
  other arithmetic  5.79 us (3%)
    ppermute x24, waiting for transfers between devices, shift(): return lax.ppermute(value, axis, [(i, (i + by) % n) for i in range(n)])  40.8 us
    pallas_call x12, Pallas kernels, call(): pl.pallas_call(kernel, out_shape=out_shape, in_specs=[vmem] * len(args) +...  35.6 us
    ppermute x24, starting transfers between devices, shift(): return lax.ppermute(value, axis, [(i, (i + by) % n) for i in range(n)])  32.5 us
    all_to_all x1, blocking collectives, shards(): lax.all_to_all(jnp.broadcast_to(grad_rows, (4, ROWS, MODEL_WIDTH)), 'h',...  20.2 us
    all_to_all x1, blocking collectives, shards(): wires = lax.all_to_all(wire, REP, 0, 0, tiled=True)  16 us
    ppermute x11, waiting for transfers between devices, partner(): return lax.ppermute(value, axis, [(0, 1), (1, 0)])  12.9 us
    all_to_all x1, waiting for transfers between devices, shards(): shares = lax.all_to_all(summed.astype(BF16), 'h', 0, 0, tiled=True)  12.4 us
    ppermute x3, waiting for transfers between devices, near_z(): lax.ppermute(value, Z, [(place(z), place(z + 1 if z % 2 else z - 1)) for...  10.6 us
  transfers between devices with their start and end apart: 42, of which 18 were waited for; matrix products, arithmetic and copies ran while one was open for 2% of the time, Pallas kernels for 10%

profile of v6, /device:TPU:2, one launch (start us, length us, event | category | flops | bytes accessed | tf_op | source)
XLA Modules:
  0.0 218.3 jit_solution(3928993675621228479)
XLA Ops:
  0.6 1.8 send.1.send_ref
  2.5 1.9 collective-permute-start.2
  4.4 1.9 own.1
  6.3 2.5 %pack.1 = (bf16[80,4096]{1,0:T(8,128)(2,1)}, bf16[16,128]{1,0:T(8,128)(2,1)}) custom-call(bf16[128,4096]{1,0:T(8,128)(2,1)} %x_ref.1, bf16[16,4096]{1,0:T(8,128)(2,1)} %bitcast.10, bf16[128,512]{1,0:T(8,128)(2,1)} %get-tuple-element.22.after_ref), custom_call_target="tpu_custom_call" | custom-call | tf_op jit(solution)/shard_map/pack/pallas_call | solution.py:63
  8.8 5.0 %collective-permute-start = (bf16[80,4096]{1,0:T(8,128)(2,1)}, bf16[80,4096]{1,0:T(8,128)(2,1)S(1)}, u32[]{:S(2)}, u32[]{:S(2)}) collective-permute-start(bf16[80,4096]{1,0:T(8,128)(2,1)} %get-tuple-element.23), channel_id=1, source_target_pairs={{0,38},{32,2},{2,32},{34,4},{4,34},{36,6},{6,36},{38,0},{1,39},{33... | collective-permute-start | bytes 1966088 | tf_op jit(solution)/shard_map/ppermute | solution.py:54
  14.8 1.6 collective-permute-start.3
  16.4 1.7 collective-permute-start.12
  18.6 1.7 collective-permute-start.13
  20.3 2.1 collective-permute-done.3
  22.4 1.7 collective-permute-start.6
  25.2 1.7 collective-permute-start.8
  28.6 1.4 collective-permute-start.14
  30.0 14.1 %collective-permute-done.5 = bf16[256,512]{1,0:T(8,128)(2,1)S(1)} collective-permute-done((bf16[256,512]{1,0:T(8,128)(2,1)S(1)}, bf16[256,512]{1,0:T(8,128)(2,1)S(1)}, u32[]{:S(2)}, u32[]{:S(2)}) %collective-permute-start.5) | collective-permute-done | bytes 262176 | tf_op jit(solution)/shard_map/ppermute | solution.py:43
  45.1 1.3 collective-permute-start.7
  46.4 2.1 collective-permute-start.18
  49.7 9.0 %collective-permute-done.9.refs_5_ = bf16[512,512]{1,0:T(8,128)(2,1)} collective-permute-done((bf16[512,512]{1,0:T(8,128)(2,1)S(1)}, bf16[512,512]{1,0:T(8,128)(2,1)}, u32[]{:S(2)}, u32[]{:S(2)}) %collective-permute-start.9) | collective-permute-done | bytes 524320 | tf_op jit(solution)/shard_map/ppermute | solution.py:43
  58.7 2.0 collective-permute-start.11
  61.1 1.5 collective-permute-start.16
  63.8 7.8 %collective-permute-done.10.low_ref = bf16[512,512]{1,0:T(8,128)(2,1)S(1)} collective-permute-done((bf16[512,512]{1,0:T(8,128)(2,1)S(1)}, bf16[512,512]{1,0:T(8,128)(2,1)S(1)}, u32[]{:S(2)}, u32[]{:S(2)}) %collective-permute-start.10) | collective-permute-done | bytes 524320 | tf_op jit(solution)/shard_map/ppermute | solution.py:43
  71.7 3.0 %collective-permute-start.20 = (bf16[512,512]{1,0:T(8,128)(2,1)S(1)}, bf16[512,512]{1,0:T(8,128)(2,1)}, u32[]{:S(2)}, u32[]{:S(2)}) collective-permute-start(bf16[512,512]{1,0:T(8,128)(2,1)S(1)} %collective-permute-done.18.refs_5_), channel_id=1, source_target_pairs={{0,24},{8,0},{16,8},{24,16},{1,25},{9,1},{17,9},{25,17},{2,26},{10... | collective-permute-start | bytes 1572872 | tf_op jit(solution)/shard_map/ppermute | solution.py:43
  75.2 3.7 %arrange.1 = (bf16[256,3072]{1,0:T(8,128)(2,1)}, bf16[256,1024]{1,0:T(8,128)(2,1)}, bf16[256,32]{1,0:T(8,128)(2,1)}, bf16[2,16,128]{2,1,0:T(8,128)(2,1)}) custom-call(bf16[128,4096]{1,0:T(8,128)(2,1)} %x_ref.1, bf16[80,4096]{1,0:T(8,128)(2,1)} %copy-done.9, bf16[80,4096]{1,0:T(8,128)(2,1)} %copy-done.10, bf16[16,128]{1,0:T(8,128)(2,1)} %get-tuple-element.24.p_own_ref), custom_call_target="tpu_custom_call" | custom-call | tf_op jit(solution)/shard_map/arrange/pallas_call | solution.py:63
  79.0 4.2 %near.1.total_ref = f32[256,512]{1,0:T(8,128)} custom-call(bf16[256,3072]{1,0:T(8,128)(2,1)} %get-tuple-element.26.x_ref, bf16[256,32]{1,0:T(8,128)(2,1)} %get-tuple-element.27.p_ref, bf16[16,512]{1,0:T(8,128)(2,1)} %get-tuple-element.28.b_own_ref, bf16[16,512]{1,0:T(8,128)(2,1)} %slice.44.b_oth_ref, bf16[512,512]{1,0:T(8,128)(2,1)} %copy-done.7, ...), custom_call_target="tpu_custom_call" | custom-call | tf_op jit(solution)/shard_map/near/pallas_call | solution.py:63
  83.2 2.8 %hidden.1 = (bf16[256,512]{1,0:T(8,128)(2,1)}, bf16[256,512]{1,0:T(8,128)(2,1)}) custom-call(bf16[256,1024]{1,0:T(8,128)(2,1)} %get-tuple-element.25.x_ref, f32[256,512]{1,0:T(8,128)} %near.1.total_ref, bf16[512,512]{1,0:T(8,128)(2,1)} %copy-done.12, bf16[512,512]{1,0:T(8,128)(2,1)} %collective-permute-done.11.high_ref), custom_call_target="tpu_custom_call" | custom-call | tf_op jit(solution)/shard_map/hidden/pallas_call | solution.py:63
  87.0 5.2 %output.1 = (f32[8,16,4096]{2,1,0:T(8,128)}, bf16[8,16,4096]{2,1,0:T(8,128)(2,1)}) custom-call(bf16[256,512]{1,0:T(8,128)(2,1)} %get-tuple-element.29.hidden_ref, bf16[512,512]{1,0:T(8,128)(2,1)} %copy-done, bf16[512,512]{1,0:T(8,128)(2,1)} %copy-done.2, bf16[512,512]{1,0:T(8,128)(2,1)} %copy-done.3, bf16[512,512]{1,0:T(8,128)(2,1)} %copy-done.6, ...), custom_call_target="tpu_custom_call" | custom-call | tf_op jit(solution)/shard_map/output/pallas_call | solution.py:63
  92.2 2.9 %collective-permute-done.21 = bf16[8,16,4096]{2,1,0:T(8,128)(2,1)S(1)} collective-permute-done((bf16[8,16,4096]{2,1,0:T(8,128)(2,1)}, bf16[8,16,4096]{2,1,0:T(8,128)(2,1)S(1)}, u32[]{:S(2)}, u32[]{:S(2)}) %collective-permute-start.21) | collective-permute-done | bytes 1048608 | tf_op jit(solution)/shard_map/ppermute | solution.py:47
  95.1 1.9 fusion.2
  97.1 2.7 %collective-permute-start.23 = (bf16[4,16,2048]{2,1,0:T(8,128)(2,1)S(1)}, bf16[4,16,2048]{2,1,0:T(8,128)(2,1)S(1)}, u32[]{:S(2)}, u32[]{:S(2)}) collective-permute-start(bf16[4,16,2048]{2,1,0:T(8,128)(2,1)S(1)} %get-tuple-element.44), channel_id=1, source_target_pairs={{0,38},{32,2},{2,32},{34,4},{4,34},{36,6},{6,36},{38,0},{1,39},{33... | collective-permute-start | bytes 786440 | tf_op jit(solution)/shard_map/ppermute | solution.py:54
  99.7 7.0 %collective-permute-done.23 = bf16[4,16,2048]{2,1,0:T(8,128)(2,1)S(1)} collective-permute-done((bf16[4,16,2048]{2,1,0:T(8,128)(2,1)S(1)}, bf16[4,16,2048]{2,1,0:T(8,128)(2,1)S(1)}, u32[]{:S(2)}, u32[]{:S(2)}) %collective-permute-start.23) | collective-permute-done | bytes 262176 | tf_op jit(solution)/shard_map/ppermute | solution.py:54
  108.7 4.1 %all-to-all-start = ((bf16[4,16,4096]{2,1,0:T(8,128)(2,1)}), bf16[4,16,4096]{2,1,0:T(8,128)(2,1)S(1)}, u32[]{:S(2)}, u32[]{:S(2)}) async-start(bf16[4,16,4096]{2,1,0:T(8,128)(2,1)} %fusion), calls=%async_computation | async-start | bytes 1048576 | tf_op jit(solution)/shard_map/all_to_all | solution.py:338
  112.8 1.9 targets.1
  114.8 12.4 %all-to-all-done = bf16[4,16,4096]{2,1,0:T(8,128)(2,1)S(1)} async-done(((bf16[4,16,4096]{2,1,0:T(8,128)(2,1)}), bf16[4,16,4096]{2,1,0:T(8,128)(2,1)S(1)}, u32[]{:S(2)}, u32[]{:S(2)}) %all-to-all-start) | async-done | bytes 524320 | tf_op jit(solution)/shard_map/all_to_all | solution.py:338
  128.2 20.2 %all_to_all.15.q_ref = bf16[4,16,4096]{2,1,0:T(8,128)(2,1)S(1)} all-to-all(bf16[4,16,4096]{2,1,0:T(8,128)(2,1)S(1)} %broadcast_in_dim.9), channel_id=1, replica_groups=mesh['y'=4,'l'=2,'x'=4,'h'=4,'c'=2] {'h'}, dimensions={0} | all-to-all | bytes 1048576 | tf_op jit(solution)/shard_map/all_to_all | solution.py:342
  149.6 5.4 %collective-permute-done.25.left_ref = bf16[4,16,2048]{2,1,0:T(8,128)(2,1)S(1)} collective-permute-done((bf16[4,16,2048]{2,1,0:T(8,128)(2,1)S(1)}, bf16[4,16,2048]{2,1,0:T(8,128)(2,1)S(1)}, u32[]{:S(2)}, u32[]{:S(2)}) %collective-permute-start.25) | collective-permute-done | bytes 262176 | tf_op jit(solution)/shard_map/ppermute | solution.py:47
  155.0 3.7 %collective-permute-done.27.right_ref = bf16[4,16,2048]{2,1,0:T(8,128)(2,1)S(1)} collective-permute-done((bf16[4,16,2048]{2,1,0:T(8,128)(2,1)S(1)}, bf16[4,16,2048]{2,1,0:T(8,128)(2,1)S(1)}, u32[]{:S(2)}, u32[]{:S(2)}) %collective-permute-start.27) | collective-permute-done | bytes 262176 | tf_op jit(solution)/shard_map/ppermute | solution.py:54
  158.7 1.5 collective-permute-done.28.rightc_ref
  160.9 5.0 %backward.1 = (f32[2,16,512]{2,1,0:T(8,128)}, f32[2,16,128]{2,1,0:T(8,128)}) custom-call(bf16[4,16,4096]{2,1,0:T(8,128)(2,1)} %copy-done.1, bf16[4,16,4096]{2,1,0:T(8,128)(2,1)} %copy-done.11, bf16[4,16,2048]{2,1,0:T(8,128)(2,1)} %copy-done.16, bf16[4,16,2048]{2,1,0:T(8,128)(2,1)} %copy-done.18, bf16[4,16,2048]{2,1,0:T(8,128)(2,1)} %copy-done.17, ...), custom_call_target="tpu_custom_call" | custom-call | tf_op jit(solution)/shard_map/backward/pallas_call | solution.py:63
  169.6 1.3 collective-permute-start.34
  172.1 2.2 %collective-permute-start.32 = (f32[16,128]{1,0:T(8,128)S(1)}, f32[16,128]{1,0:T(8,128)S(1)}, u32[]{:S(2)}, u32[]{:S(2)}) collective-permute-start(f32[16,128]{1,0:T(8,128)S(1)} %fusion.1.t0_ref), channel_id=1, source_target_pairs={{0,4},{2,6},{4,0},{6,2},{1,5},{3,7},{5,1},{7,3},{8,12},{10,14},{12... | collective-permute-start | bytes 24584 | tf_op jit(solution)/shard_map/ppermute | solution.py:266
  174.4 3.8 %collective-permute-start.33 = (f32[16,128]{1,0:T(8,128)S(1)}, f32[16,128]{1,0:T(8,128)S(1)}, u32[]{:S(2)}, u32[]{:S(2)}) collective-permute-start(f32[16,128]{1,0:T(8,128)S(1)} %fusion.1.t0_ref), channel_id=1, source_target_pairs={{0,6},{2,4},{4,2},{6,0},{1,7},{3,5},{5,3},{7,1},{8,14},{10,12},{12... | collective-permute-start | bytes 24584 | tf_op jit(solution)/shard_map/ppermute | solution.py:266
  178.8 1.5 ups.1
  180.3 2.5 %collective-permute-start.36 = (bf16[32,1024]{1,0:T(8,128)(2,1)}, bf16[32,1024]{1,0:T(8,128)(2,1)S(1)}, u32[]{:S(2)}, u32[]{:S(2)}) collective-permute-start(bf16[32,1024]{1,0:T(8,128)(2,1)} %get-tuple-element.38), channel_id=1, source_target_pairs={{0,24},{8,0},{16,8},{24,16},{1,25},{9,1},{17,9},{25,17},{2,26},{10... | collective-permute-start | bytes 196616 | tf_op jit(solution)/shard_map/ppermute | solution.py:43
  183.7 1.6 collective-permute-done.35
  185.3 1.8 collective-permute-start.37
  187.1 4.1 %collective-permute-done.37 = bf16[32,1024]{1,0:T(8,128)(2,1)S(1)} collective-permute-done((bf16[32,1024]{1,0:T(8,128)(2,1)}, bf16[32,1024]{1,0:T(8,128)(2,1)S(1)}, u32[]{:S(2)}, u32[]{:S(2)}) %collective-permute-start.37) | collective-permute-done | bytes 65568 | tf_op jit(solution)/shard_map/ppermute | solution.py:43
  191.3 3.2 %collective-permute-start.39 = (bf16[128,1024]{1,0:T(8,128)(2,1)S(1)}, bf16[128,1024]{1,0:T(8,128)(2,1)S(1)}, u32[]{:S(2)}, u32[]{:S(2)}) collective-permute-start(bf16[128,1024]{1,0:T(8,128)(2,1)S(1)} %constant_dynamic-update-slice_fusion.4.u0_ref), channel_id=1, source_target_pairs={{0,192},{64,0},{128,64},{192,128},{1,193},{65,1},{129,65},{193,129... | collective-permute-start | bytes 786440 | tf_op jit(solution)/shard_map/ppermute | solution.py:43
  195.8 2.3 %down.1 = (f32[16,4096]{1,0:T(8,128)}, bf16[32,16,128]{2,1,0:T(8,128)(2,1)}) custom-call(f32[16,128]{1,0:T(8,128)} %copy-done.25, f32[16,128]{1,0:T(8,128)} %copy-done.26, f32[16,128]{1,0:T(8,128)} %copy-done.27, f32[16,128]{1,0:T(8,128)} %copy-done.28, bf16[128,4096]{1,0:T(8,128)(2,1)} %x_ref.1, bf16[16,4096]{1,0:T(8,128)(2,1)} %bitcast.11), custom_call_target="tpu_custom_call" | custom-call | tf_op jit(solution)/shard_map/down/pallas_call | solution.py:63
  198.1 16.0 %all_to_all.16.wire_ref = bf16[32,16,128]{2,1,0:T(8,128)(2,1)} all-to-all(bf16[32,16,128]{2,1,0:T(8,128)(2,1)} %get-tuple-element.36), channel_id=1, replica_groups=mesh['y'=4,'l'=2,'x'=4,'h'=4,'c'=2] {'y','l','x'}, dimensions={0} | all-to-all | bytes 262144 | tf_op jit(solution)/shard_map/all_to_all | solution.py:376
  215.7 2.6 %merge.1 = f32[128,1024]{1,0:T(8,128)} custom-call(bf16[32,16,128]{2,1,0:T(8,128)(2,1)} %all_to_all.16.wire_ref, bf16[128,1024]{1,0:T(8,128)(2,1)} %copy-done.15, bf16[128,1024]{1,0:T(8,128)(2,1)} %copy-done.19, bf16[128,1024]{1,0:T(8,128)(2,1)} %copy-done.20, bf16[128,1024]{1,0:T(8,128)(2,1)} %copy-done.22, bf16[128,1024]{1,0:T(8,128)(2,1)} %w_ref.1), custom_call_target="tpu_custom_call" | custom-call | tf_op jit(solution)/shard_map/merge/pallas_call | solution.py:63
  (133 shorter events, 24.0 us)
Async XLA Ops:
  2.5 11.2 %collective-permute-start.2 = (bf16[272,512]{1,0:T(8,128)(2,1)}, bf16[272,512]{1,0:T(8,128)(2,1)S(1)}, u32[]{:S(2)}, u32[]{:S(2)}) collective-permute-start(bf16[272,512]{1,0:T(8,128)(2,1)} %send.1.send_ref), channel_id=1, source_target_pairs={{0,32},{32,0},{1,33},{33,1},{2,34},{34,2},{3,35},{35,3},{4,36},{36... | collective-permute-start | bytes 835592 | tf_op jit(solution)/shard_map/ppermute | solution.py:47
  8.8 19.8 %collective-permute-start = (bf16[80,4096]{1,0:T(8,128)(2,1)}, bf16[80,4096]{1,0:T(8,128)(2,1)S(1)}, u32[]{:S(2)}, u32[]{:S(2)}) collective-permute-start(bf16[80,4096]{1,0:T(8,128)(2,1)} %get-tuple-element.23), channel_id=1, source_target_pairs={{0,38},{32,2},{2,32},{34,4},{4,34},{36,6},{6,36},{38,0},{1,39},{33... | collective-permute-start | bytes 1966088 | tf_op jit(solution)/shard_map/ppermute | solution.py:54
  14.8 7.6 %collective-permute-start.3 = (bf16[256,512]{1,0:T(8,128)(2,1)S(1)}, bf16[256,512]{1,0:T(8,128)(2,1)S(1)}, u32[]{:S(2)}, u32[]{:S(2)}) collective-permute-start(bf16[256,512]{1,0:T(8,128)(2,1)S(1)} %maximum_select_fusion), channel_id=1, source_target_pairs={{0,8},{8,16},{16,24},{24,0},{1,9},{9,17},{17,25},{25,1},{2,10},{10... | collective-permute-start | bytes 786440 | tf_op jit(solution)/shard_map/ppermute | solution.py:43
  16.4 8.8 %collective-permute-start.12 = (bf16[256,512]{1,0:T(8,128)(2,1)S(1)}, bf16[256,512]{1,0:T(8,128)(2,1)S(1)}, u32[]{:S(2)}, u32[]{:S(2)}) collective-permute-start(bf16[256,512]{1,0:T(8,128)(2,1)S(1)} %maximum_select_fusion.1), channel_id=1, source_target_pairs={{0,64},{64,128},{128,192},{192,0},{1,65},{65,129},{129,193},{193,1... | collective-permute-start | bytes 786440 | tf_op jit(solution)/shard_map/ppermute | solution.py:43
  18.1 8.9 %collective-permute-start.4 = (bf16[256,512]{1,0:T(8,128)(2,1)S(1)}, bf16[256,512]{1,0:T(8,128)(2,1)S(1)}, u32[]{:S(2)}, u32[]{:S(2)}) collective-permute-start(bf16[256,512]{1,0:T(8,128)(2,1)S(1)} %maximum_select_fusion), channel_id=1, source_target_pairs={{0,24},{8,0},{16,8},{24,16},{1,25},{9,1},{17,9},{25,17},{2,26},{10... | collective-permute-start | bytes 786440 | tf_op jit(solution)/shard_map/ppermute | solution.py:43
  18.6 9.4 %collective-permute-start.13 = (bf16[256,512]{1,0:T(8,128)(2,1)S(1)}, bf16[256,512]{1,0:T(8,128)(2,1)S(1)}, u32[]{:S(2)}, u32[]{:S(2)}) collective-permute-start(bf16[256,512]{1,0:T(8,128)(2,1)S(1)} %maximum_select_fusion.1), channel_id=1, source_target_pairs={{0,192},{64,0},{128,64},{192,128},{1,193},{65,1},{129,65},{193,129... | collective-permute-start | bytes 786440 | tf_op jit(solution)/shard_map/ppermute | solution.py:43
  22.4 41.4 %copy-start.7 = (bf16[512,512]{1,0:T(8,128)(2,1)}, bf16[512,512]{1,0:T(8,128)(2,1)S(1)}, u32[]{:S(2)}) copy-start(bf16[512,512]{1,0:T(8,128)(2,1)S(1)} %pad_maximum_fusion.refs_0_) | copy-start | bytes 1572868
  22.4 22.7 %collective-permute-start.6 = (bf16[512,512]{1,0:T(8,128)(2,1)S(1)}, bf16[512,512]{1,0:T(8,128)(2,1)S(1)}, u32[]{:S(2)}, u32[]{:S(2)}) collective-permute-start(bf16[512,512]{1,0:T(8,128)(2,1)S(1)} %pad_maximum_fusion.refs_0_), channel_id=1, source_target_pairs={{0,64},{64,128},{128,192},{192,0},{1,65},{65,129},{129,193},{193,1... | collective-permute-start | bytes 1572872 | tf_op jit(solution)/shard_map/ppermute | solution.py:43
  25.2 21.2 %collective-permute-start.8 = (bf16[512,512]{1,0:T(8,128)(2,1)S(1)}, bf16[512,512]{1,0:T(8,128)(2,1)}, u32[]{:S(2)}, u32[]{:S(2)}) collective-permute-start(bf16[512,512]{1,0:T(8,128)(2,1)S(1)} %pad_maximum_fusion.refs_0_), channel_id=1, source_target_pairs={{0,192},{64,0},{128,64},{192,128},{1,193},{65,1},{129,65},{193,129... | collective-permute-start | bytes 1572872 | tf_op jit(solution)/shard_map/ppermute | solution.py:43
  27.0 52.0 %copy-start = (bf16[512,512]{1,0:T(8,128)(2,1)}, bf16[512,512]{1,0:T(8,128)(2,1)S(1)}, u32[]{:S(2)}) copy-start(bf16[512,512]{1,0:T(8,128)(2,1)S(1)} %pad_maximum_fusion.1.refs_0_) | copy-start | bytes 1572868
  27.0 21.5 %collective-permute-start.15 = (bf16[512,512]{1,0:T(8,128)(2,1)S(1)}, bf16[512,512]{1,0:T(8,128)(2,1)S(1)}, u32[]{:S(2)}, u32[]{:S(2)}) collective-permute-start(bf16[512,512]{1,0:T(8,128)(2,1)S(1)} %pad_maximum_fusion.1.refs_0_), channel_id=1, source_target_pairs={{0,8},{8,16},{16,24},{24,0},{1,9},{9,17},{17,25},{25,1},{2,10},{10... | collective-permute-start | bytes 1572872 | tf_op jit(solution)/shard_map/ppermute | solution.py:43
  28.1 16.0 %collective-permute-start.5 = (bf16[256,512]{1,0:T(8,128)(2,1)S(1)}, bf16[256,512]{1,0:T(8,128)(2,1)S(1)}, u32[]{:S(2)}, u32[]{:S(2)}) collective-permute-start(bf16[256,512]{1,0:T(8,128)(2,1)S(1)} %collective-permute-done.3), channel_id=1, source_target_pairs={{0,8},{8,16},{16,24},{24,0},{1,9},{9,17},{17,25},{25,1},{2,10},{10... | collective-permute-start | bytes 786440 | tf_op jit(solution)/shard_map/ppermute | solution.py:43
  28.6 15.6 %collective-permute-start.14 = (bf16[256,512]{1,0:T(8,128)(2,1)S(1)}, bf16[256,512]{1,0:T(8,128)(2,1)S(1)}, u32[]{:S(2)}, u32[]{:S(2)}) collective-permute-start(bf16[256,512]{1,0:T(8,128)(2,1)S(1)} %collective-permute-done.12), channel_id=1, source_target_pairs={{0,64},{64,128},{128,192},{192,0},{1,65},{65,129},{129,193},{193,1... | collective-permute-start | bytes 786440 | tf_op jit(solution)/shard_map/ppermute | solution.py:43
  44.1 4.6 %collective-permute-start.1 = (bf16[80,4096]{1,0:T(8,128)(2,1)S(1)}, bf16[80,4096]{1,0:T(8,128)(2,1)S(1)}, u32[]{:S(2)}, u32[]{:S(2)}) collective-permute-start(bf16[80,4096]{1,0:T(8,128)(2,1)S(1)} %collective-permute-done.oth_ref), channel_id=1, source_target_pairs={{0,1},{1,0},{2,3},{3,2},{4,5},{5,4},{6,7},{7,6},{8,9},{9,8},{10,11... | collective-permute-start | bytes 1966088 | tf_op jit(solution)/shard_map/ppermute | solution.py:47
  44.1 27.5 %copy-start.8 = (bf16[512,512]{1,0:T(8,128)(2,1)}, bf16[512,512]{1,0:T(8,128)(2,1)S(1)}, u32[]{:S(2)}) copy-start(bf16[512,512]{1,0:T(8,128)(2,1)S(1)} %constant_dynamic-update-slice_fusion.refs_1_) | copy-start | bytes 1572868
  44.1 14.5 %collective-permute-start.9 = (bf16[512,512]{1,0:T(8,128)(2,1)S(1)}, bf16[512,512]{1,0:T(8,128)(2,1)}, u32[]{:S(2)}, u32[]{:S(2)}) collective-permute-start(bf16[512,512]{1,0:T(8,128)(2,1)S(1)} %constant_dynamic-update-slice_fusion.refs_1_), channel_id=1, source_target_pairs={{0,192},{64,0},{128,64},{192,128},{1,193},{65,1},{129,65},{193,129... | collective-permute-start | bytes 1572872 | tf_op jit(solution)/shard_map/ppermute | solution.py:43
  45.0 38.2 %copy-start.2 = (bf16[512,512]{1,0:T(8,128)(2,1)}, bf16[512,512]{1,0:T(8,128)(2,1)S(1)}, u32[]{:S(2)}) copy-start(bf16[512,512]{1,0:T(8,128)(2,1)S(1)} %constant_dynamic-update-slice_fusion.2.refs_1_) | copy-start | bytes 1572868
  45.1 30.2 %copy-start.13 = (bf16[512,512]{1,0:T(8,128)(2,1)}, bf16[512,512]{1,0:T(8,128)(2,1)S(1)}, u32[]{:S(2)}) copy-start(bf16[512,512]{1,0:T(8,128)(2,1)S(1)} %collective-permute-done.6.refs_2_) | copy-start | bytes 1572868
  45.1 16.0 %collective-permute-start.7 = (bf16[512,512]{1,0:T(8,128)(2,1)S(1)}, bf16[512,512]{1,0:T(8,128)(2,1)S(1)}, u32[]{:S(2)}, u32[]{:S(2)}) collective-permute-start(bf16[512,512]{1,0:T(8,128)(2,1)S(1)} %constant_dynamic-update-slice_fusion.refs_1_), channel_id=1, source_target_pairs={{0,64},{64,128},{128,192},{192,0},{1,65},{65,129},{129,193},{193,1... | collective-permute-start | bytes 1572872 | tf_op jit(solution)/shard_map/ppermute | solution.py:43
  46.4 16.2 %collective-permute-start.18 = (bf16[512,512]{1,0:T(8,128)(2,1)S(1)}, bf16[512,512]{1,0:T(8,128)(2,1)S(1)}, u32[]{:S(2)}, u32[]{:S(2)}) collective-permute-start(bf16[512,512]{1,0:T(8,128)(2,1)S(1)} %constant_dynamic-update-slice_fusion.2.refs_1_), channel_id=1, source_target_pairs={{0,24},{8,0},{16,8},{24,16},{1,25},{9,1},{17,9},{25,17},{2,26},{10... | collective-permute-start | bytes 1572872 | tf_op jit(solution)/shard_map/ppermute | solution.py:43
  48.5 34.7 %copy-start.3 = (bf16[512,512]{1,0:T(8,128)(2,1)}, bf16[512,512]{1,0:T(8,128)(2,1)S(1)}, u32[]{:S(2)}) copy-start(bf16[512,512]{1,0:T(8,128)(2,1)S(1)} %collective-permute-done.15.refs_2_) | copy-start | bytes 1572868
  48.5 23.2 %collective-permute-start.10 = (bf16[512,512]{1,0:T(8,128)(2,1)S(1)}, bf16[512,512]{1,0:T(8,128)(2,1)S(1)}, u32[]{:S(2)}, u32[]{:S(2)}) collective-permute-start(bf16[512,512]{1,0:T(8,128)(2,1)S(1)} %collective-permute-done.6.refs_2_), channel_id=1, source_target_pairs={{0,64},{64,128},{128,192},{192,0},{1,65},{65,129},{129,193},{193,1... | collective-permute-start | bytes 1572872 | tf_op jit(solution)/shard_map/ppermute | solution.py:43
  48.7 37.3 %collective-permute-start.17 = (bf16[512,512]{1,0:T(8,128)(2,1)S(1)}, bf16[512,512]{1,0:T(8,128)(2,1)S(1)}, u32[]{:S(2)}, u32[]{:S(2)}) collective-permute-start(bf16[512,512]{1,0:T(8,128)(2,1)S(1)} %pad_maximum_fusion.1.refs_0_), channel_id=1, source_target_pairs={{0,24},{8,0},{16,8},{24,16},{1,25},{9,1},{17,9},{25,17},{2,26},{10... | collective-permute-start | bytes 1572872 | tf_op jit(solution)/shard_map/ppermute | solution.py:43
  58.7 24.6 %collective-permute-start.11 = (bf16[512,512]{1,0:T(8,128)(2,1)}, bf16[512,512]{1,0:T(8,128)(2,1)}, u32[]{:S(2)}, u32[]{:S(2)}) collective-permute-start(bf16[512,512]{1,0:T(8,128)(2,1)} %collective-permute-done.9.refs_5_), channel_id=1, source_target_pairs={{0,192},{64,0},{128,64},{192,128},{1,193},{65,1},{129,65},{193,129... | collective-permute-start | bytes 1572872 | tf_op jit(solution)/shard_map/ppermute | solution.py:43
  61.1 24.9 %collective-permute-start.16 = (bf16[512,512]{1,0:T(8,128)(2,1)S(1)}, bf16[512,512]{1,0:T(8,128)(2,1)S(1)}, u32[]{:S(2)}, u32[]{:S(2)}) collective-permute-start(bf16[512,512]{1,0:T(8,128)(2,1)S(1)} %constant_dynamic-update-slice_fusion.2.refs_1_), channel_id=1, source_target_pairs={{0,8},{8,16},{16,24},{24,0},{1,9},{9,17},{17,25},{25,1},{2,10},{10... | collective-permute-start | bytes 1572872 | tf_op jit(solution)/shard_map/ppermute | solution.py:43
  62.6 23.9 %collective-permute-start.19 = (bf16[512,512]{1,0:T(8,128)(2,1)S(1)}, bf16[512,512]{1,0:T(8,128)(2,1)}, u32[]{:S(2)}, u32[]{:S(2)}) collective-permute-start(bf16[512,512]{1,0:T(8,128)(2,1)S(1)} %collective-permute-done.15.refs_2_), channel_id=1, source_target_pairs={{0,8},{8,16},{16,24},{24,0},{1,9},{9,17},{17,25},{25,1},{2,10},{10... | collective-permute-start | bytes 1572872 | tf_op jit(solution)/shard_map/ppermute | solution.py:43
  71.7 14.8 %collective-permute-start.20 = (bf16[512,512]{1,0:T(8,128)(2,1)S(1)}, bf16[512,512]{1,0:T(8,128)(2,1)}, u32[]{:S(2)}, u32[]{:S(2)}) collective-permute-start(bf16[512,512]{1,0:T(8,128)(2,1)S(1)} %collective-permute-done.18.refs_5_), channel_id=1, source_target_pairs={{0,24},{8,0},{16,8},{24,16},{1,25},{9,1},{17,9},{25,17},{2,26},{10... | collective-permute-start | bytes 1572872 | tf_op jit(solution)/shard_map/ppermute | solution.py:43
  92.2 2.9 %collective-permute-start.21 = (bf16[8,16,4096]{2,1,0:T(8,128)(2,1)}, bf16[8,16,4096]{2,1,0:T(8,128)(2,1)S(1)}, u32[]{:S(2)}, u32[]{:S(2)}) collective-permute-start(bf16[8,16,4096]{2,1,0:T(8,128)(2,1)} %get-tuple-element.32.after_ref), channel_id=1, source_target_pairs={{0,1},{1,0},{2,3},{3,2},{4,5},{5,4},{6,7},{7,6},{8,9},{9,8},{10,11... | collective-permute-start | bytes 3145736 | tf_op jit(solution)/shard_map/ppermute | solution.py:47
  97.1 9.6 %collective-permute-start.23 = (bf16[4,16,2048]{2,1,0:T(8,128)(2,1)S(1)}, bf16[4,16,2048]{2,1,0:T(8,128)(2,1)S(1)}, u32[]{:S(2)}, u32[]{:S(2)}) collective-permute-start(bf16[4,16,2048]{2,1,0:T(8,128)(2,1)S(1)} %get-tuple-element.44), channel_id=1, source_target_pairs={{0,38},{32,2},{2,32},{34,4},{4,34},{36,6},{6,36},{38,0},{1,39},{33... | collective-permute-start | bytes 786440 | tf_op jit(solution)/shard_map/ppermute | solution.py:54
  99.7 8.1 %collective-permute-start.22 = (bf16[4,16,2048]{2,1,0:T(8,128)(2,1)S(1)}, bf16[4,16,2048]{2,1,0:T(8,128)(2,1)S(1)}, u32[]{:S(2)}, u32[]{:S(2)}) collective-permute-start(bf16[4,16,2048]{2,1,0:T(8,128)(2,1)S(1)} %get-tuple-element.43), channel_id=1, source_target_pairs={{0,32},{32,0},{1,33},{33,1},{2,34},{34,2},{3,35},{35,3},{4,36},{36... | collective-permute-start | bytes 786440 | tf_op jit(solution)/shard_map/ppermute | solution.py:47
  108.7 18.4 %all-to-all-start = ((bf16[4,16,4096]{2,1,0:T(8,128)(2,1)}), bf16[4,16,4096]{2,1,0:T(8,128)(2,1)S(1)}, u32[]{:S(2)}, u32[]{:S(2)}) async-start(bf16[4,16,4096]{2,1,0:T(8,128)(2,1)} %fusion), calls=%async_computation | async-start | bytes 1048576 | tf_op jit(solution)/shard_map/all_to_all | solution.py:338
  148.5 6.5 %collective-permute-start.25 = (bf16[4,16,2048]{2,1,0:T(8,128)(2,1)S(1)}, bf16[4,16,2048]{2,1,0:T(8,128)(2,1)S(1)}, u32[]{:S(2)}, u32[]{:S(2)}) collective-permute-start(bf16[4,16,2048]{2,1,0:T(8,128)(2,1)S(1)} %get-tuple-element.46), channel_id=1, source_target_pairs={{0,32},{32,0},{1,33},{33,1},{2,34},{34,2},{3,35},{35,3},{4,36},{36... | collective-permute-start | bytes 786440 | tf_op jit(solution)/shard_map/ppermute | solution.py:47
  148.6 10.0 %collective-permute-start.24 = (bf16[4,16,4096]{2,1,0:T(8,128)(2,1)S(1)}, bf16[4,16,4096]{2,1,0:T(8,128)(2,1)S(1)}, u32[]{:S(2)}, u32[]{:S(2)}) collective-permute-start(bf16[4,16,4096]{2,1,0:T(8,128)(2,1)S(1)} %all_to_all.15.q_ref), channel_id=1, source_target_pairs={{0,1},{1,0},{2,3},{3,2},{4,5},{5,4},{6,7},{7,6},{8,9},{9,8},{10,11... | collective-permute-start | bytes 1572872 | tf_op jit(solution)/shard_map/ppermute | solution.py:47
  148.7 9.9 %collective-permute-start.27 = (bf16[4,16,2048]{2,1,0:T(8,128)(2,1)S(1)}, bf16[4,16,2048]{2,1,0:T(8,128)(2,1)S(1)}, u32[]{:S(2)}, u32[]{:S(2)}) collective-permute-start(bf16[4,16,2048]{2,1,0:T(8,128)(2,1)S(1)} %get-tuple-element.45), channel_id=1, source_target_pairs={{0,38},{32,2},{2,32},{34,4},{4,34},{36,6},{6,36},{38,0},{1,39},{33... | collective-permute-start | bytes 786440 | tf_op jit(solution)/shard_map/ppermute | solution.py:54
  154.9 3.7 %collective-permute-start.26 = (bf16[4,16,2048]{2,1,0:T(8,128)(2,1)S(1)}, bf16[4,16,2048]{2,1,0:T(8,128)(2,1)S(1)}, u32[]{:S(2)}, u32[]{:S(2)}) collective-permute-start(bf16[4,16,2048]{2,1,0:T(8,128)(2,1)S(1)} %collective-permute-done.25.left_ref), channel_id=1, source_target_pairs={{0,1},{1,0},{2,3},{3,2},{4,5},{5,4},{6,7},{7,6},{8,9},{9,8},{10,11... | collective-permute-start | bytes 786440 | tf_op jit(solution)/shard_map/ppermute | solution.py:47
  158.6 1.5 collective-permute-start.28
  165.9 1.4 collective-permute-start.29
  168.0 3.7 %collective-permute-start.30 = (f32[16,128]{1,0:T(8,128)S(1)}, f32[16,128]{1,0:T(8,128)S(1)}, u32[]{:S(2)}, u32[]{:S(2)}) collective-permute-start(f32[16,128]{1,0:T(8,128)S(1)} %slice_bitcast_fusion), channel_id=1, source_target_pairs={{0,32},{32,0},{1,33},{33,1},{2,34},{34,2},{3,35},{35,3},{4,36},{36... | collective-permute-start | bytes 24584 | tf_op jit(solution)/shard_map/ppermute | solution.py:47
  169.6 8.6 %collective-permute-start.34 = (f32[2,16,512]{2,1,0:T(8,128)S(1)}, f32[2,16,512]{2,1,0:T(8,128)S(1)}, u32[]{:S(2)}, u32[]{:S(2)}) collective-permute-start(f32[2,16,512]{2,1,0:T(8,128)S(1)} %rev.3), channel_id=1, source_target_pairs={{0,32},{32,0},{1,33},{33,1},{2,34},{34,2},{3,35},{35,3},{4,36},{36... | collective-permute-start | bytes 196616 | tf_op jit(solution)/shard_map/ppermute | solution.py:47
  171.7 22.9 %collective-permute-start.31 = (f32[16,128]{1,0:T(8,128)S(1)}, f32[16,128]{1,0:T(8,128)S(1)}, u32[]{:S(2)}, u32[]{:S(2)}) collective-permute-start(f32[16,128]{1,0:T(8,128)S(1)} %fusion.1.t0_ref), channel_id=1, source_target_pairs={{0,2},{2,0},{4,6},{6,4},{1,3},{3,1},{5,7},{7,5},{8,10},{10,8},{12,... | collective-permute-start | bytes 24584 | tf_op jit(solution)/shard_map/ppermute | solution.py:266
  172.1 22.4 %collective-permute-start.32 = (f32[16,128]{1,0:T(8,128)S(1)}, f32[16,128]{1,0:T(8,128)S(1)}, u32[]{:S(2)}, u32[]{:S(2)}) collective-permute-start(f32[16,128]{1,0:T(8,128)S(1)} %fusion.1.t0_ref), channel_id=1, source_target_pairs={{0,4},{2,6},{4,0},{6,2},{1,5},{3,7},{5,1},{7,3},{8,12},{10,14},{12... | collective-permute-start | bytes 24584 | tf_op jit(solution)/shard_map/ppermute | solution.py:266
  174.4 20.2 %collective-permute-start.33 = (f32[16,128]{1,0:T(8,128)S(1)}, f32[16,128]{1,0:T(8,128)S(1)}, u32[]{:S(2)}, u32[]{:S(2)}) collective-permute-start(f32[16,128]{1,0:T(8,128)S(1)} %fusion.1.t0_ref), channel_id=1, source_target_pairs={{0,6},{2,4},{4,2},{6,0},{1,7},{3,5},{5,3},{7,1},{8,14},{10,12},{12... | collective-permute-start | bytes 24584 | tf_op jit(solution)/shard_map/ppermute | solution.py:266
  180.3 4.9 %collective-permute-start.35 = (bf16[32,1024]{1,0:T(8,128)(2,1)}, bf16[32,1024]{1,0:T(8,128)(2,1)S(1)}, u32[]{:S(2)}, u32[]{:S(2)}) collective-permute-start(bf16[32,1024]{1,0:T(8,128)(2,1)} %get-tuple-element.38), channel_id=1, source_target_pairs={{0,8},{8,16},{16,24},{24,0},{1,9},{9,17},{17,25},{25,1},{2,10},{10... | collective-permute-start | bytes 196616 | tf_op jit(solution)/shard_map/ppermute | solution.py:43
  180.3 6.8 %collective-permute-start.36 = (bf16[32,1024]{1,0:T(8,128)(2,1)}, bf16[32,1024]{1,0:T(8,128)(2,1)S(1)}, u32[]{:S(2)}, u32[]{:S(2)}) collective-permute-start(bf16[32,1024]{1,0:T(8,128)(2,1)} %get-tuple-element.38), channel_id=1, source_target_pairs={{0,24},{8,0},{16,8},{24,16},{1,25},{9,1},{17,9},{25,17},{2,26},{10... | collective-permute-start | bytes 196616 | tf_op jit(solution)/shard_map/ppermute | solution.py:43
  185.3 6.0 %collective-permute-start.37 = (bf16[32,1024]{1,0:T(8,128)(2,1)}, bf16[32,1024]{1,0:T(8,128)(2,1)S(1)}, u32[]{:S(2)}, u32[]{:S(2)}) collective-permute-start(bf16[32,1024]{1,0:T(8,128)(2,1)} %get-tuple-element.38), channel_id=1, source_target_pairs={{0,16},{8,24},{16,0},{24,8},{1,17},{9,25},{17,1},{25,9},{2,18},{10... | collective-permute-start | bytes 196616 | tf_op jit(solution)/shard_map/ppermute | solution.py:43
  191.2 22.9 %collective-permute-start.38 = (bf16[128,1024]{1,0:T(8,128)(2,1)S(1)}, bf16[128,1024]{1,0:T(8,128)(2,1)S(1)}, u32[]{:S(2)}, u32[]{:S(2)}) collective-permute-start(bf16[128,1024]{1,0:T(8,128)(2,1)S(1)} %constant_dynamic-update-slice_fusion.4.u0_ref), channel_id=1, source_target_pairs={{0,64},{64,128},{128,192},{192,0},{1,65},{65,129},{129,193},{193,1... | collective-permute-start | bytes 786440 | tf_op jit(solution)/shard_map/ppermute | solution.py:43
  191.3 22.8 %collective-permute-start.39 = (bf16[128,1024]{1,0:T(8,128)(2,1)S(1)}, bf16[128,1024]{1,0:T(8,128)(2,1)S(1)}, u32[]{:S(2)}, u32[]{:S(2)}) collective-permute-start(bf16[128,1024]{1,0:T(8,128)(2,1)S(1)} %constant_dynamic-update-slice_fusion.4.u0_ref), channel_id=1, source_target_pairs={{0,192},{64,0},{128,64},{192,128},{1,193},{65,1},{129,65},{193,129... | collective-permute-start | bytes 786440 | tf_op jit(solution)/shard_map/ppermute | solution.py:43
  194.6 19.6 %collective-permute-start.40 = (bf16[128,1024]{1,0:T(8,128)(2,1)S(1)}, bf16[128,1024]{1,0:T(8,128)(2,1)S(1)}, u32[]{:S(2)}, u32[]{:S(2)}) collective-permute-start(bf16[128,1024]{1,0:T(8,128)(2,1)S(1)} %constant_dynamic-update-slice_fusion.4.u0_ref), channel_id=1, source_target_pairs={{0,128},{64,192},{128,0},{192,64},{1,129},{65,193},{129,1},{193,65... | collective-permute-start | bytes 786440 | tf_op jit(solution)/shard_map/ppermute | solution.py:43
  (23 other events, 169.0 us)

commit v7 on v5

--- a/solution.py
+++ b/solution.py
@@ -56,18 +56,30 @@
     )
 
 
-def call(kernel, out_shape, *args, scratch=(), after=(), name):
+def call(kernel, out_shape, *args, scratch=(), after=(), stage=(), name):
     vmem = pl.BlockSpec(memory_space=pltpu.VMEM)
     wait = pl.BlockSpec(memory_space=pl.ANY)
     many = isinstance(out_shape, tuple)
     return pl.pallas_call(
         kernel,
         out_shape=out_shape,
-        in_specs=[vmem] * len(args) + [wait] * len(after),
+        in_specs=[vmem] * len(args) + [wait] * (len(stage) + len(after)),
         out_specs=(vmem,) * len(out_shape) if many else vmem,
-        scratch_shapes=scratch,
+        scratch_shapes=[pltpu.VMEM(block.shape, block.dtype) for block in stage]
+        + ([pltpu.SemaphoreType.DMA((len(stage),))] if stage else [])
+        + list(scratch),
         name=name,
-    )(*args, *after)
+    )(*args, *stage, *after)
+
+
+def staged(refs, buffers, sems):
+    copies = [
+        pltpu.make_async_copy(ref, buffer, sems.at[k])
+        for k, (ref, buffer) in enumerate(zip(refs, buffers))
+    ]
+    for copy in copies:
+        copy.start()
+    return copies
 
 
 def shape(*dims, dtype=BF16):
@@ -150,10 +162,12 @@
 
 
 def near_kernel(x_ref, p_ref, b_own_ref, b_oth_ref, *refs):
-    pieces, total_ref = refs[:3], refs[3]
+    pieces, total_ref, buffers, sems = refs[:3], refs[3], refs[4:7], refs[7]
+    copies = staged(pieces, buffers, sems)
     b = jnp.concatenate([b_own_ref[...], b_oth_ref[...]], axis=0)
     total = ADAPTER_SCALE * dot(p_ref[...], b)
-    for k, piece in enumerate(pieces):
+    for k, piece in enumerate(buffers):
+        copies[k].wait()
         total = total + dot(x_ref[:, k * 1024 : (k + 1) * 1024], piece[...])
     total_ref[...] = total
 
@@ -175,8 +189,10 @@
 
 
 def output_kernel(hidden_ref, *refs):
-    pieces, (keep_ref, send_ref) = refs[:5], refs[5:]
-    for cols, piece in spans(pieces):
+    pieces, (keep_ref, send_ref), buffers, sems = refs[:5], refs[5:7], refs[7:12], refs[12]
+    copies = staged(pieces, buffers, sems)
+    for copy, (cols, piece) in zip(copies, spans(buffers)):
+        copy.wait()
         part = dot_nt(hidden_ref[...], piece[...]).reshape(8, 2, ROWS, piece.shape[0])
         keep_ref[:, :, cols] = part[:, 0]
         send_ref[:, :, cols] = part[:, 1].astype(BF16)
@@ -184,7 +200,9 @@
 
 def backward_kernel(q_ref, qc_ref, left_ref, leftc_ref, right_ref, rightc_ref, mask_ref, pt_ref,
                     b_own_ref, b_oth_ref, *refs):
-    pieces, (up_own_ref, up_oth_ref, wire_ref, back_ref, grad_ref, own_ref, oth_ref) = refs[:5], refs[5:]
+    pieces, (up_own_ref, up_oth_ref, wire_ref, back_ref) = refs[:5], refs[5:9]
+    buffers, sems, (grad_ref, own_ref, oth_ref) = refs[9:14], refs[14], refs[15:]
+    copies = staged(pieces, buffers, sems)
     l = lax.axis_index("l")
     for i in range(16):
         j, e = (i // 2) % 4, i % 2
@@ -195,7 +213,8 @@
             grad_ref[here, :SIDE] = (left_ref, leftc_ref)[e][j]
             grad_ref[here, SIDE:] = (right_ref, rightc_ref)[e][j]
     total = None
-    for cols, piece in spans(pieces):
+    for copy, (cols, piece) in zip(copies, spans(buffers)):
+        copy.wait()
         term = dot(grad_ref[:, cols], piece[...])
         total = term if total is None else total + term
     total = jnp.where(mask_ref[...].astype(F32) > 0, total * FF ** (-0.5), 0.0).astype(BF16)
@@ -207,20 +226,15 @@
         (l, own_ref, pt_ref[0], up_own_ref, b_own_ref[...]),
         (1 - l, oth_ref, pt_ref[1], up_oth_ref, b_oth_ref[...]),
     )
-    for side, hid_ref, p, up_ref, b in sides:
+    for order, (side, hid_ref, p, up_ref, b) in enumerate(sides):
         up = b.astype(F32) - RATE_UP * (scale * dot(p, hid_ref[...]))
         up_ref[...] = up
         wire_ref[side] = up.astype(BF16)
-        back = dot_nt(b, hid_ref[...])
-        for k in range(8):
-            back_ref[side * 8 + k] = back
-
-
-def down_kernel(back_ref, x_ref, a_ref, up_ref, new_ref, wire_ref):
-    terms = [back_ref[k] for k in range(16)]
-    while len(terms) > 1:
-        terms = [terms[k] + terms[k + 1] for k in range(0, len(terms), 2)]
-    rest = terms[0]
+        back_ref[order] = dot_nt(b, hid_ref[...])
+
+
+def down_kernel(t0_ref, t1_ref, t2_ref, t3_ref, x_ref, a_ref, new_ref, wire_ref):
+    rest = (t0_ref[...] + t1_ref[...]) + (t2_ref[...] + t3_ref[...])
     parts = []
     for _ in range(3):
         parts.append(rest.astype(BF16))
@@ -234,27 +248,21 @@
         new = a_ref[:, here].astype(F32) - RATE_DOWN * (scale * grad)
         new_ref[:, here] = new
         for j in range(4):
-            wire_ref[k * 4 + j, :, :BLOCK] = new[:, j * BLOCK : (j + 1) * BLOCK].astype(BF16)
-            for l in range(2):
-                begin = BLOCK + l * HID
-                wire_ref[k * 4 + j, :, begin : begin + HID] = up_ref[l]
-
-
-def merge_kernel(wire_ref, w_ref, out_ref, d_ref, u_ref):
+            wire_ref[k * 4 + j] = new[:, j * BLOCK : (j + 1) * BLOCK].astype(BF16)
+
+
+def merge_kernel(down_ref, up_ref, w_ref, out_ref, d_ref, u_ref):
     for y in range(4):
         for x in range(4):
             for l in range(2):
                 at = ((y * 4 + x) * 2 + l) * RANK
-                d_ref[at : at + RANK, :] = wire_ref[y * 8 + l * 4 + x, :, :BLOCK]
+                d_ref[at : at + RANK, :] = down_ref[y * 8 + l * 4 + x]
     for side in range(2):
         for y in range(4):
             for x in range(4):
                 for l in range(2):
                     at = ((y * 4 + x) * 2 + l) * RANK
-                    begin = BLOCK + l * HID
-                    u_ref[at : at + RANK, :] = wire_ref[
-                        y * 8 + side * 4 + x, :, begin : begin + HID
-                    ]
+                    u_ref[at : at + RANK, :] = up_ref[y * 8 + side * 4 + x, l]
         here = slice(side * HID, (side + 1) * HID)
         delta = dot_tn(d_ref[...], u_ref[...])
         out_ref[:, here] = w_ref[:, here].astype(F32) + ADAPTER_SCALE / 32 * delta
@@ -265,9 +273,32 @@
     return [value, below, above, shift(below, axis, 1)]
 
 
+def halves_kernel(below_ref, above_ref, low_ref, high_ref, sems):
+    copies = [
+        pltpu.make_async_copy(below_ref.at[:HID], low_ref, sems.at[0]),
+        pltpu.make_async_copy(above_ref.at[HID:], high_ref, sems.at[1]),
+    ]
+    for copy in copies:
+        copy.start()
+    for copy in copies:
+        copy.wait()
+
+
 def far_halves(below, above, axis):
-    half = below.shape[0] // 2
-    return [shift(below[:half], axis, 1), shift(above[half:], axis, -1)]
+    anywhere = pl.BlockSpec(memory_space=pl.ANY)
+    low, high = pl.pallas_call(
+        halves_kernel,
+        out_shape=(shape(HID, HID), shape(HID, HID)),
+        in_specs=[anywhere] * 2,
+        out_specs=(anywhere,) * 2,
+        scratch_shapes=[pltpu.SemaphoreType.DMA((2,))],
+        name="halves",
+    )(below, above)
+    return [shift(low, axis, 1), shift(high, axis, -1)]
+
+
+def swap(value, mask):
+    return lax.ppermute(value, "h", [(i, i ^ mask) for i in range(4)])
 
 
 def shards(tokens, targets, w_in, w_out, factor_down, factor_up):
@@ -311,11 +342,8 @@
         scratch=[pltpu.VMEM((2, TOK, RANK), BF16)],
         name="arrange",
     )
-    my_targets = call(
-        targets_kernel, shape(ROWS, MODEL_WIDTH), targets, after=[p_rel], name="targets"
-    )
-    in_near[1], in_near[2], x_near, p_rel, my_targets = lax.optimization_barrier(
-        (in_near[1], in_near[2], x_near, p_rel, my_targets)
+    in_near[1], in_near[2], x_near, p_rel = lax.optimization_barrier(
+        (in_near[1], in_near[2], x_near, p_rel)
     )
     in_far = far_halves(in_near[1], in_near[2], "y")
     out_far = far_halves(out_near[1], out_near[2], "x")
@@ -323,7 +351,8 @@
     total = call(
         near_kernel,
         shape(2 * TOK, HID, dtype=F32),
-        x_near, p_rel, b_own, b_oth, *in_near,
+        x_near, p_rel, b_own, b_oth,
+        stage=in_near,
         name="near",
     )
     hidden, mask = call(
@@ -335,8 +364,13 @@
     keep, send = call(
         output_kernel,
         (shape(8, ROWS, MODEL_WIDTH, dtype=F32), shape(8, ROWS, MODEL_WIDTH)),
-        hidden, *out_pieces,
+        hidden,
+        stage=out_pieces,
         name="output",
+    )
+
+    my_targets = call(
+        targets_kernel, shape(ROWS, MODEL_WIDTH), targets, after=[send], name="targets"
     )
 
     summed = keep + partner(send, "c").astype(F32)
@@ -360,9 +394,10 @@
             shape(RANK, HID, dtype=F32),
             shape(RANK, HID, dtype=F32),
             shape(2, RANK, HID),
-            shape(16, RANK, TOK, dtype=F32),
+            shape(2, RANK, TOK, dtype=F32),
         ),
-        q, q_far, left, left_far, right, right_far, mask, pt, b_own, b_oth, *out_pieces,
+        q, q_far, left, left_far, right, right_far, mask, pt, b_own, b_oth,
+        stage=out_pieces,
         scratch=[
             pltpu.VMEM((2 * TOK, MODEL_WIDTH), BF16),
             pltpu.VMEM((TOK, HID), BF16),
@@ -370,14 +405,20 @@
         ],
         name="backward",
     )
-    back = lax.all_to_all(back, ("l", "h", "c"), 0, 0, tiled=True)
+    ups = lax.all_to_all(
+        jnp.broadcast_to(up_wire, (32, 2, RANK, HID)), REP, 0, 0, tiled=True
+    )
+    back = back + partner(back, "c")
+    back = back[0] + partner(back[1], "l")
+    back = [back] + [swap(back, mask) for mask in (1, 2, 3)]
     new_a, wire = call(
         down_kernel,
-        (shape(RANK, MODEL_WIDTH, dtype=F32), shape(32, RANK, BLOCK + 2 * HID)),
-        back, tokens, a, up_wire,
+        (shape(RANK, MODEL_WIDTH, dtype=F32), shape(32, RANK, BLOCK)),
+        *back, tokens, a,
         name="down",
     )
-    wires = lax.all_to_all(wire, REP, 0, 0, tiled=True)
+    wire, ups = lax.optimization_barrier((wire, ups))
+    downs = lax.all_to_all(wire, REP, 0, 0, tiled=True)
     up_arrived = partner(up_oth, "l")
     new_b = jnp.where(
         l == 0,
@@ -387,7 +428,7 @@
     merged = call(
         merge_kernel,
         shape(TOK, 2 * HID, dtype=F32),
-        wires, w_in,
+        downs, ups, w_in,
         scratch=[pltpu.VMEM((32 * RANK, BLOCK), BF16), pltpu.VMEM((32 * RANK, HID), BF16)],
         name="merge",
     )

time: 201 us -> 275 us (1.37)
  Pallas kernels: 34.2 us -> 101 us
  blocking collectives: 51 us -> 19.5 us
  starting transfers between devices: 37.3 us -> 56.5 us
  waiting for transfers between devices: 60 us -> 78.2 us
    pallas_call x0 -> x2, Pallas kernels: none -> 65.8 us  [far_halves(): pl.pallas_call(halves_kernel, out_shape=(shape(HID, HID), shape(HID, HID)...]
    all_to_all x2 -> x0, blocking collectives: 32.5 us -> none  [the longest x1 19.4 us: shards(): shares = lax.all_to_all(summed.astype(BF16), 'h', 0, 0, tiled=True)]
    all_to_all x1 -> x3, waiting for transfers between devices: 2.26 us -> 14.8 us  [the longest x1 12 us: shards(): shares = lax.all_to_all(summed.astype(BF16), 'h', 0, 0, tiled=True)]
    all_to_all x1 -> x3, starting transfers between devices: 6.56 us -> 17.5 us  [the longest x1 7.4 us: shards(): downs = lax.all_to_all(wire, REP, 0, 0, tiled=True)]
    ppermute x0 -> x3, starting transfers between devices: none -> 6.5 us  [swap(): return lax.ppermute(value, 'h', [(i, i ^ mask) for i in range(4)])]
    slice x4 -> x0, local copies, waits for them, and re-layouts: 4.66 us -> none  [far_halves(): return [shift(below[:half], axis, 1), shift(above[half:], axis, -1)]]
    ppermute x0 -> x3, waiting for transfers between devices: none -> 4.53 us  [swap(): return lax.ppermute(value, 'h', [(i, i ^ mask) for i in range(4)])]
    unnamed x32 -> x44, local copies, waits for them, and re-layouts: 4.25 us -> 6.95 us
  transfers between devices with their start and end apart: 27 -> 34, of which waited for: 15 -> 19; matrix products, arithmetic and copies ran while one was open for 4% -> 1% of each run, Pallas kernels for 9% -> 31%
where the time goes in v7:
time: 275 us; the launch traced here: 274 us
  Pallas kernels  101 us (37%)
  waiting for transfers between devices  78.2 us (28%)
  starting transfers between devices  56.5 us (21%)
  blocking collectives  19.5 us (7%)
  local copies, waits for them, and re-layouts  9.59 us (3%)
  other arithmetic  7.75 us (3%)
    pallas_call x2, Pallas kernels, far_halves(): pl.pallas_call(halves_kernel, out_shape=(shape(HID, HID), shape(HID, HID)...  65.8 us
    pallas_call x11, Pallas kernels, call(): pl.pallas_call(kernel, out_shape=out_shape, in_specs=[vmem] * len(args) +...  35.5 us
    ppermute x11, waiting for transfers between devices, partner(): return lax.ppermute(value, axis, [(0, 1), (1, 0)])  34 us
    all_to_all x1, blocking collectives, shards(): lax.all_to_all(jnp.broadcast_to(grad_rows, (4, ROWS, MODEL_WIDTH)), 'h',...  19.5 us
    ppermute x14, starting transfers between devices, shift(): return lax.ppermute(value, axis, [(i, (i + by) % n) for i in range(n)])  19 us
    ppermute x3, waiting for transfers between devices, near_z(): lax.ppermute(value, Z, [(place(z), place(z + 1 if z % 2 else z - 1)) for...  14.3 us
    all_to_all x1, waiting for transfers between devices, shards(): shares = lax.all_to_all(summed.astype(BF16), 'h', 0, 0, tiled=True)  12 us
    ppermute x14, waiting for transfers between devices, shift(): return lax.ppermute(value, axis, [(i, (i + by) % n) for i in range(n)])  10.6 us
  transfers between devices with their start and end apart: 34, of which 19 were waited for; matrix products, arithmetic and copies ran while one was open for 1% of the time, Pallas kernels for 31%

profile of v7, /device:TPU:2, one launch (start us, length us, event | category | flops | bytes accessed | tf_op | source)
XLA Modules:
  0.0 273.8 jit_solution(8997169112571274674)
XLA Ops:
  0.6 1.8 send.1.send_ref
  2.5 1.9 collective-permute-start.2
  4.4 1.9 own.1
  6.2 5.0 %collective-permute-done.2 = bf16[272,512]{1,0:T(8,128)(2,1)S(1)} collective-permute-done((bf16[272,512]{1,0:T(8,128)(2,1)}, bf16[272,512]{1,0:T(8,128)(2,1)S(1)}, u32[]{:S(2)}, u32[]{:S(2)}) %collective-permute-start.2) | collective-permute-done | bytes 278560 | tf_op jit(solution)/shard_map/ppermute | solution.py:47
  12.3 1.6 collective-permute-start.3
  14.9 1.7 collective-permute-start.10
  17.1 2.6 collective-permute-done.3
  19.8 1.5 collective-permute-start.5
  21.3 3.0 %collective-permute-start.11 = (bf16[256,512]{1,0:T(8,128)(2,1)S(1)}, bf16[256,512]{1,0:T(8,128)(2,1)S(1)}, u32[]{:S(2)}, u32[]{:S(2)}) collective-permute-start(bf16[256,512]{1,0:T(8,128)(2,1)S(1)} %maximum_select_fusion.1), channel_id=1, source_target_pairs={{0,192},{64,0},{128,64},{192,128},{1,193},{65,1},{129,65},{193,129... | collective-permute-start | bytes 786440 | tf_op jit(solution)/shard_map/ppermute | solution.py:43
  24.3 2.5 pack.1
  26.8 5.5 %collective-permute-start = (bf16[80,4096]{1,0:T(8,128)(2,1)}, bf16[80,4096]{1,0:T(8,128)(2,1)S(1)}, u32[]{:S(2)}, u32[]{:S(2)}) collective-permute-start(bf16[80,4096]{1,0:T(8,128)(2,1)} %get-tuple-element.33), channel_id=1, source_target_pairs={{0,38},{32,2},{2,32},{34,4},{4,34},{36,6},{6,36},{38,0},{1,39},{33... | collective-permute-start | bytes 1966088 | tf_op jit(solution)/shard_map/ppermute | solution.py:54
  33.3 3.2 %collective-permute-start.7 = (bf16[1024,512]{1,0:T(8,128)(2,1)}, bf16[1024,512]{1,0:T(8,128)(2,1)}, u32[]{:S(2)}, u32[]{:S(2)}) collective-permute-start(bf16[1024,512]{1,0:T(8,128)(2,1)} %pad_maximum_fusion.refs_0_), channel_id=1, source_target_pairs={{0,192},{64,0},{128,64},{192,128},{1,193},{65,1},{129,65},{193,129... | collective-permute-start | bytes 3145736 | tf_op jit(solution)/shard_map/ppermute | solution.py:43
  37.3 1.5 collective-permute-start.13
  38.8 6.1 %collective-permute-done.oth_ref = bf16[80,4096]{1,0:T(8,128)(2,1)S(1)} collective-permute-done((bf16[80,4096]{1,0:T(8,128)(2,1)}, bf16[80,4096]{1,0:T(8,128)(2,1)S(1)}, u32[]{:S(2)}, u32[]{:S(2)}) %collective-permute-start) | collective-permute-done | bytes 655392 | tf_op jit(solution)/shard_map/ppermute | solution.py:54
  45.7 2.1 collective-permute-done.1.oth_core_ref
  48.6 3.8 %arrange.1 = (bf16[256,3072]{1,0:T(8,128)(2,1)}, bf16[256,1024]{1,0:T(8,128)(2,1)}, bf16[256,32]{1,0:T(8,128)(2,1)}, bf16[2,16,128]{2,1,0:T(8,128)(2,1)}) custom-call(bf16[128,4096]{1,0:T(8,128)(2,1)} %x_ref.1, bf16[80,4096]{1,0:T(8,128)(2,1)} %copy-done.7, bf16[80,4096]{1,0:T(8,128)(2,1)} %copy-done.8, bf16[16,128]{1,0:T(8,128)(2,1)} %get-tuple-element.34.p_own_ref), custom_call_target="tpu_custom_call" | custom-call | tf_op jit(solution)/shard_map/arrange/pallas_call | solution.py:63
  52.4 4.0 %collective-permute-done.7.refs_2_.above_ref = bf16[1024,512]{1,0:T(8,128)(2,1)} collective-permute-done((bf16[1024,512]{1,0:T(8,128)(2,1)}, bf16[1024,512]{1,0:T(8,128)(2,1)}, u32[]{:S(2)}, u32[]{:S(2)}) %collective-permute-start.7) | collective-permute-done | bytes 1048608 | tf_op jit(solution)/shard_map/ppermute | solution.py:43
  56.4 3.4 %collective-permute-done.6.refs_1_.below_ref = bf16[1024,512]{1,0:T(8,128)(2,1)} collective-permute-done((bf16[1024,512]{1,0:T(8,128)(2,1)}, bf16[1024,512]{1,0:T(8,128)(2,1)}, u32[]{:S(2)}, u32[]{:S(2)}) %collective-permute-start.6) | collective-permute-done | bytes 1048608 | tf_op jit(solution)/shard_map/ppermute | solution.py:43
  59.8 32.9 %halves.2 = (bf16[512,512]{1,0:T(8,128)(2,1)}, bf16[512,512]{1,0:T(8,128)(2,1)}) custom-call(bf16[1024,512]{1,0:T(8,128)(2,1)} %collective-permute-done.6.refs_1_.below_ref, bf16[1024,512]{1,0:T(8,128)(2,1)} %collective-permute-done.7.refs_2_.above_ref), custom_call_target="tpu_custom_call" | custom-call | tf_op jit(solution)/shard_map/halves/pallas_call | solution.py:289
  92.8 3.2 %collective-permute-start.9 = (bf16[512,512]{1,0:T(8,128)(2,1)}, bf16[512,512]{1,0:T(8,128)(2,1)}, u32[]{:S(2)}, u32[]{:S(2)}) collective-permute-start(bf16[512,512]{1,0:T(8,128)(2,1)} %get-tuple-element.44), channel_id=1, source_target_pairs={{0,192},{64,0},{128,64},{192,128},{1,193},{65,1},{129,65},{193,129... | collective-permute-start | bytes 1572872 | tf_op jit(solution)/shard_map/ppermute | solution.py:43
  98.0 32.9 %halves.3 = (bf16[512,512]{1,0:T(8,128)(2,1)}, bf16[512,512]{1,0:T(8,128)(2,1)}) custom-call(bf16[1024,512]{1,0:T(8,128)(2,1)} %copy-done.2, bf16[1024,512]{1,0:T(8,128)(2,1)} %copy-done.1), custom_call_target="tpu_custom_call" | custom-call | tf_op jit(solution)/shard_map/halves/pallas_call | solution.py:289
  133.6 4.6 %near.1.total_ref = f32[256,512]{1,0:T(8,128)} custom-call(bf16[256,3072]{1,0:T(8,128)(2,1)} %get-tuple-element.38.x_ref, bf16[256,32]{1,0:T(8,128)(2,1)} %get-tuple-element.39.p_ref, bf16[16,512]{1,0:T(8,128)(2,1)} %get-tuple-element.40.b_own_ref, bf16[16,512]{1,0:T(8,128)(2,1)} %slice.45.b_oth_ref, bf16[1024,512]{1,0:T(8,128)(2,1)} %pad_maximum_fusion.refs_0_, ...), custom_call_target="tpu_custom_call" | custom-call | tf_op jit(solution)/shard_map/near/pallas_call | solution.py:63
  138.2 2.8 %hidden.1 = (bf16[256,512]{1,0:T(8,128)(2,1)}, bf16[256,512]{1,0:T(8,128)(2,1)}) custom-call(bf16[256,1024]{1,0:T(8,128)(2,1)} %get-tuple-element.35.x_ref, f32[256,512]{1,0:T(8,128)} %near.1.total_ref, bf16[512,512]{1,0:T(8,128)(2,1)} %collective-permute-done.8.low_ref, bf16[512,512]{1,0:T(8,128)(2,1)} %collective-permute-done.9.high_ref), custom_call_target="tpu_custom_call" | custom-call | tf_op jit(solution)/shard_map/hidden/pallas_call | solution.py:63
  142.3 5.9 %output.1 = (f32[8,16,4096]{2,1,0:T(8,128)}, bf16[8,16,4096]{2,1,0:T(8,128)(2,1)}) custom-call(bf16[256,512]{1,0:T(8,128)(2,1)} %get-tuple-element.45.hidden_ref, bf16[1024,512]{1,0:T(8,128)(2,1)} %copy-done, bf16[1024,512]{1,0:T(8,128)(2,1)} %copy-done.2, bf16[1024,512]{1,0:T(8,128)(2,1)} %copy-done.1, bf16[512,512]{1,0:T(8,128)(2,1)} %copy-done.5, ...), custom_call_target="tpu_custom_call" | custom-call | tf_op jit(solution)/shard_map/output/pallas_call | solution.py:63
  148.4 2.9 %collective-permute-done.17 = bf16[8,16,4096]{2,1,0:T(8,128)(2,1)S(1)} collective-permute-done((bf16[8,16,4096]{2,1,0:T(8,128)(2,1)}, bf16[8,16,4096]{2,1,0:T(8,128)(2,1)S(1)}, u32[]{:S(2)}, u32[]{:S(2)}) %collective-permute-start.17) | collective-permute-done | bytes 1048608 | tf_op jit(solution)/shard_map/ppermute | solution.py:47
  151.2 1.9 fusion.2
  153.3 2.0 collective-permute-start.19
  155.3 6.3 %collective-permute-done.18 = bf16[4,16,2048]{2,1,0:T(8,128)(2,1)S(1)} collective-permute-done((bf16[4,16,2048]{2,1,0:T(8,128)(2,1)S(1)}, bf16[4,16,2048]{2,1,0:T(8,128)(2,1)S(1)}, u32[]{:S(2)}, u32[]{:S(2)}) %collective-permute-start.18) | collective-permute-done | bytes 262176 | tf_op jit(solution)/shard_map/ppermute | solution.py:47
  163.9 4.3 %all-to-all-start = ((bf16[4,16,4096]{2,1,0:T(8,128)(2,1)}), bf16[4,16,4096]{2,1,0:T(8,128)(2,1)S(1)}, u32[]{:S(2)}, u32[]{:S(2)}) async-start(bf16[4,16,4096]{2,1,0:T(8,128)(2,1)} %fusion), calls=%async_computation | async-start | bytes 1048576 | tf_op jit(solution)/shard_map/all_to_all | solution.py:382
  168.1 1.9 targets.1
  170.1 12.0 %all-to-all-done = bf16[4,16,4096]{2,1,0:T(8,128)(2,1)S(1)} async-done(((bf16[4,16,4096]{2,1,0:T(8,128)(2,1)}), bf16[4,16,4096]{2,1,0:T(8,128)(2,1)S(1)}, u32[]{:S(2)}, u32[]{:S(2)}) %all-to-all-start) | async-done | bytes 524320 | tf_op jit(solution)/shard_map/all_to_all | solution.py:382
  183.1 19.5 %all_to_all.20.q_ref = bf16[4,16,4096]{2,1,0:T(8,128)(2,1)S(1)} all-to-all(bf16[4,16,4096]{2,1,0:T(8,128)(2,1)S(1)} %broadcast_in_dim.10), channel_id=1, replica_groups=mesh['y'=4,'l'=2,'x'=4,'h'=4,'c'=2] {'h'}, dimensions={0} | all-to-all | bytes 1048576 | tf_op jit(solution)/shard_map/all_to_all | solution.py:386
  203.4 6.9 %collective-permute-done.23.right_ref = bf16[4,16,2048]{2,1,0:T(8,128)(2,1)S(1)} collective-permute-done((bf16[4,16,2048]{2,1,0:T(8,128)(2,1)S(1)}, bf16[4,16,2048]{2,1,0:T(8,128)(2,1)S(1)}, u32[]{:S(2)}, u32[]{:S(2)}) %collective-permute-start.23) | collective-permute-done | bytes 262176 | tf_op jit(solution)/shard_map/ppermute | solution.py:54
  210.4 1.8 collective-permute-done.21.left_ref
  212.2 1.5 collective-permute-done.22.leftc_ref
  214.4 5.5 %backward.1 = (f32[16,512]{1,0:T(8,128)}, f32[16,512]{1,0:T(8,128)}, bf16[2,16,512]{2,1,0:T(8,128)(2,1)}, f32[2,16,128]{2,1,0:T(8,128)}) custom-call(bf16[4,16,4096]{2,1,0:T(8,128)(2,1)} %copy-done.3, bf16[4,16,4096]{2,1,0:T(8,128)(2,1)} %copy-done.9, bf16[4,16,2048]{2,1,0:T(8,128)(2,1)} %copy-done.12, bf16[4,16,2048]{2,1,0:T(8,128)(2,1)} %copy-done.14, ...), custom_call_target="tpu_custom_call" | custom-call | tf_op jit(solution)/shard_map/backward/pallas_call | solution.py:63
  219.9 1.9 broadcast_in_dim.11
  221.8 5.8 %all-to-all-start.2 = ((bf16[32,2,16,512]{3,2,1,0:T(8,128)(2,1)}), bf16[32,2,16,512]{3,2,1,0:T(8,128)(2,1)S(1)}, u32[]{:S(2)}, u32[]{:S(2)}) async-start(bf16[32,2,16,512]{3,2,1,0:T(8,128)(2,1)} %broadcast_in_dim.11), calls=%async_computation.2 | async-start | bytes 2097152 | tf_op jit(solution)/shard_map/all_to_all | solution.py:408
  230.4 10.6 %collective-permute-done.26 = f32[16,128]{1,0:T(8,128)S(1)} collective-permute-done((f32[16,128]{1,0:T(8,128)S(1)}, f32[16,128]{1,0:T(8,128)S(1)}, u32[]{:S(2)}, u32[]{:S(2)}) %collective-permute-start.26) | collective-permute-done | bytes 8224 | tf_op jit(solution)/shard_map/ppermute | solution.py:47
  241.1 3.5 %collective-permute-start.29 = (f32[16,128]{1,0:T(8,128)S(1)}, f32[16,128]{1,0:T(8,128)S(1)}, u32[]{:S(2)}, u32[]{:S(2)}) collective-permute-start(f32[16,128]{1,0:T(8,128)S(1)} %fusion.1.t0_ref), channel_id=1, source_target_pairs={{0,6},{2,4},{4,2},{6,0},{1,7},{3,5},{5,3},{7,1},{8,14},{10,12},{12... | collective-permute-start | bytes 24584 | tf_op jit(solution)/shard_map/ppermute | solution.py:301
  245.3 2.3 collective-permute-start.27
  247.6 4.5 %collective-permute-done.28.t2_ref = f32[16,128]{1,0:T(8,128)S(1)} collective-permute-done((f32[16,128]{1,0:T(8,128)S(1)}, f32[16,128]{1,0:T(8,128)S(1)}, u32[]{:S(2)}, u32[]{:S(2)}) %collective-permute-start.28) | collective-permute-done | bytes 8224 | tf_op jit(solution)/shard_map/ppermute | solution.py:301
  253.3 2.3 down.1
  255.7 7.4 %all-to-all-start.3 = ((bf16[32,16,128]{2,1,0:T(8,128)(2,1)}), bf16[32,16,128]{2,1,0:T(8,128)(2,1)S(1)}, u32[]{:S(2)}, u32[]{:S(2)}) async-start(bf16[32,16,128]{2,1,0:T(8,128)(2,1)} %get-tuple-element.56), calls=%async_computation.3 | async-start | bytes 262144 | tf_op jit(solution)/shard_map/all_to_all | solution.py:421
  263.1 1.6 collective-permute-start.30
  264.6 2.6 collective-permute-done.30
  267.9 2.8 %all-to-all-done.3.down_ref = bf16[32,16,128]{2,1,0:T(8,128)(2,1)S(1)} async-done(((bf16[32,16,128]{2,1,0:T(8,128)(2,1)}), bf16[32,16,128]{2,1,0:T(8,128)(2,1)S(1)}, u32[]{:S(2)}, u32[]{:S(2)}) %all-to-all-start.3) | async-done | bytes 131104 | tf_op jit(solution)/shard_map/all_to_all | solution.py:421
  271.3 2.4 merge.1
  (96 shorter events, 23.1 us)
Async XLA Ops:
  2.5 8.8 %collective-permute-start.2 = (bf16[272,512]{1,0:T(8,128)(2,1)}, bf16[272,512]{1,0:T(8,128)(2,1)S(1)}, u32[]{:S(2)}, u32[]{:S(2)}) collective-permute-start(bf16[272,512]{1,0:T(8,128)(2,1)} %send.1.send_ref), channel_id=1, source_target_pairs={{0,32},{32,0},{1,33},{33,1},{2,34},{34,2},{3,35},{35,3},{4,36},{36... | collective-permute-start | bytes 835592 | tf_op jit(solution)/shard_map/ppermute | solution.py:47
  12.3 7.4 %collective-permute-start.3 = (bf16[256,512]{1,0:T(8,128)(2,1)S(1)}, bf16[256,512]{1,0:T(8,128)(2,1)S(1)}, u32[]{:S(2)}, u32[]{:S(2)}) collective-permute-start(bf16[256,512]{1,0:T(8,128)(2,1)S(1)} %maximum_select_fusion), channel_id=1, source_target_pairs={{0,8},{8,16},{16,24},{24,0},{1,9},{9,17},{17,25},{25,1},{2,10},{10... | collective-permute-start | bytes 786440 | tf_op jit(solution)/shard_map/ppermute | solution.py:43
  14.9 9.3 %collective-permute-start.10 = (bf16[256,512]{1,0:T(8,128)(2,1)S(1)}, bf16[256,512]{1,0:T(8,128)(2,1)S(1)}, u32[]{:S(2)}, u32[]{:S(2)}) collective-permute-start(bf16[256,512]{1,0:T(8,128)(2,1)S(1)} %maximum_select_fusion.1), channel_id=1, source_target_pairs={{0,64},{64,128},{128,192},{192,0},{1,65},{65,129},{129,193},{193,1... | collective-permute-start | bytes 786440 | tf_op jit(solution)/shard_map/ppermute | solution.py:43
  16.6 15.7 %collective-permute-start.4 = (bf16[256,512]{1,0:T(8,128)(2,1)S(1)}, bf16[256,512]{1,0:T(8,128)(2,1)S(1)}, u32[]{:S(2)}, u32[]{:S(2)}) collective-permute-start(bf16[256,512]{1,0:T(8,128)(2,1)S(1)} %maximum_select_fusion), channel_id=1, source_target_pairs={{0,24},{8,0},{16,8},{24,16},{1,25},{9,1},{17,9},{25,17},{2,26},{10... | collective-permute-start | bytes 786440 | tf_op jit(solution)/shard_map/ppermute | solution.py:43
  19.8 12.5 %collective-permute-start.5 = (bf16[256,512]{1,0:T(8,128)(2,1)S(1)}, bf16[256,512]{1,0:T(8,128)(2,1)S(1)}, u32[]{:S(2)}, u32[]{:S(2)}) collective-permute-start(bf16[256,512]{1,0:T(8,128)(2,1)S(1)} %collective-permute-done.3), channel_id=1, source_target_pairs={{0,8},{8,16},{16,24},{24,0},{1,9},{9,17},{17,25},{25,1},{2,10},{10... | collective-permute-start | bytes 786440 | tf_op jit(solution)/shard_map/ppermute | solution.py:43
  21.3 15.3 %collective-permute-start.11 = (bf16[256,512]{1,0:T(8,128)(2,1)S(1)}, bf16[256,512]{1,0:T(8,128)(2,1)S(1)}, u32[]{:S(2)}, u32[]{:S(2)}) collective-permute-start(bf16[256,512]{1,0:T(8,128)(2,1)S(1)} %maximum_select_fusion.1), channel_id=1, source_target_pairs={{0,192},{64,0},{128,64},{192,128},{1,193},{65,1},{129,65},{193,129... | collective-permute-start | bytes 786440 | tf_op jit(solution)/shard_map/ppermute | solution.py:43
  24.3 12.3 %collective-permute-start.12 = (bf16[256,512]{1,0:T(8,128)(2,1)S(1)}, bf16[256,512]{1,0:T(8,128)(2,1)S(1)}, u32[]{:S(2)}, u32[]{:S(2)}) collective-permute-start(bf16[256,512]{1,0:T(8,128)(2,1)S(1)} %collective-permute-done.10), channel_id=1, source_target_pairs={{0,64},{64,128},{128,192},{192,0},{1,65},{65,129},{129,193},{193,1... | collective-permute-start | bytes 786440 | tf_op jit(solution)/shard_map/ppermute | solution.py:43
  26.8 18.1 %collective-permute-start = (bf16[80,4096]{1,0:T(8,128)(2,1)}, bf16[80,4096]{1,0:T(8,128)(2,1)S(1)}, u32[]{:S(2)}, u32[]{:S(2)}) collective-permute-start(bf16[80,4096]{1,0:T(8,128)(2,1)} %get-tuple-element.33), channel_id=1, source_target_pairs={{0,38},{32,2},{2,32},{34,4},{4,34},{36,6},{6,36},{38,0},{1,39},{33... | collective-permute-start | bytes 1966088 | tf_op jit(solution)/shard_map/ppermute | solution.py:54
  33.3 23.1 %collective-permute-start.7 = (bf16[1024,512]{1,0:T(8,128)(2,1)}, bf16[1024,512]{1,0:T(8,128)(2,1)}, u32[]{:S(2)}, u32[]{:S(2)}) collective-permute-start(bf16[1024,512]{1,0:T(8,128)(2,1)} %pad_maximum_fusion.refs_0_), channel_id=1, source_target_pairs={{0,192},{64,0},{128,64},{192,128},{1,193},{65,1},{129,65},{193,129... | collective-permute-start | bytes 3145736 | tf_op jit(solution)/shard_map/ppermute | solution.py:43
  36.6 23.2 %collective-permute-start.6 = (bf16[1024,512]{1,0:T(8,128)(2,1)}, bf16[1024,512]{1,0:T(8,128)(2,1)}, u32[]{:S(2)}, u32[]{:S(2)}) collective-permute-start(bf16[1024,512]{1,0:T(8,128)(2,1)} %pad_maximum_fusion.refs_0_), channel_id=1, source_target_pairs={{0,64},{64,128},{128,192},{192,0},{1,65},{65,129},{129,193},{193,1... | collective-permute-start | bytes 3145736 | tf_op jit(solution)/shard_map/ppermute | solution.py:43
  36.7 56.0 %copy-start = (bf16[1024,512]{1,0:T(8,128)(2,1)}, bf16[1024,512]{1,0:T(8,128)(2,1)S(1)}, u32[]{:S(2)}) copy-start(bf16[1024,512]{1,0:T(8,128)(2,1)S(1)} %pad_maximum_fusion.1.refs_0_) | copy-start | bytes 3145732
  36.7 59.3 %collective-permute-start.14 = (bf16[1024,512]{1,0:T(8,128)(2,1)S(1)}, bf16[1024,512]{1,0:T(8,128)(2,1)S(1)}, u32[]{:S(2)}, u32[]{:S(2)}) collective-permute-start(bf16[1024,512]{1,0:T(8,128)(2,1)S(1)} %pad_maximum_fusion.1.refs_0_), channel_id=1, source_target_pairs={{0,24},{8,0},{16,8},{24,16},{1,25},{9,1},{17,9},{25,17},{2,26},{10... | collective-permute-start | bytes 3145736 | tf_op jit(solution)/shard_map/ppermute | solution.py:43
  37.3 58.7 %collective-permute-start.13 = (bf16[1024,512]{1,0:T(8,128)(2,1)S(1)}, bf16[1024,512]{1,0:T(8,128)(2,1)S(1)}, u32[]{:S(2)}, u32[]{:S(2)}) collective-permute-start(bf16[1024,512]{1,0:T(8,128)(2,1)S(1)} %pad_maximum_fusion.1.refs_0_), channel_id=1, source_target_pairs={{0,8},{8,16},{16,24},{24,0},{1,9},{9,17},{17,25},{25,1},{2,10},{10... | collective-permute-start | bytes 3145736 | tf_op jit(solution)/shard_map/ppermute | solution.py:43
  45.7 2.1 collective-permute-start.1
  92.7 45.5 %collective-permute-start.8 = (bf16[512,512]{1,0:T(8,128)(2,1)}, bf16[512,512]{1,0:T(8,128)(2,1)}, u32[]{:S(2)}, u32[]{:S(2)}) collective-permute-start(bf16[512,512]{1,0:T(8,128)(2,1)} %get-tuple-element.43), channel_id=1, source_target_pairs={{0,64},{64,128},{128,192},{192,0},{1,65},{65,129},{129,193},{193,1... | collective-permute-start | bytes 1572872 | tf_op jit(solution)/shard_map/ppermute | solution.py:43
  92.8 45.4 %collective-permute-start.9 = (bf16[512,512]{1,0:T(8,128)(2,1)}, bf16[512,512]{1,0:T(8,128)(2,1)}, u32[]{:S(2)}, u32[]{:S(2)}) collective-permute-start(bf16[512,512]{1,0:T(8,128)(2,1)} %get-tuple-element.44), channel_id=1, source_target_pairs={{0,192},{64,0},{128,64},{192,128},{1,193},{65,1},{129,65},{193,129... | collective-permute-start | bytes 1572872 | tf_op jit(solution)/shard_map/ppermute | solution.py:43
  96.0 1.0 copy-start.1
  97.0 1.0 copy-start.2
  130.9 10.1 %collective-permute-start.15 = (bf16[512,512]{1,0:T(8,128)(2,1)}, bf16[512,512]{1,0:T(8,128)(2,1)S(1)}, u32[]{:S(2)}, u32[]{:S(2)}) collective-permute-start(bf16[512,512]{1,0:T(8,128)(2,1)} %get-tuple-element.47), channel_id=1, source_target_pairs={{0,8},{8,16},{16,24},{24,0},{1,9},{9,17},{17,25},{25,1},{2,10},{10... | collective-permute-start | bytes 1572872 | tf_op jit(solution)/shard_map/ppermute | solution.py:43
  132.2 9.4 %collective-permute-start.16 = (bf16[512,512]{1,0:T(8,128)(2,1)}, bf16[512,512]{1,0:T(8,128)(2,1)S(1)}, u32[]{:S(2)}, u32[]{:S(2)}) collective-permute-start(bf16[512,512]{1,0:T(8,128)(2,1)} %get-tuple-element.48), channel_id=1, source_target_pairs={{0,24},{8,0},{16,8},{24,16},{1,25},{9,1},{17,9},{25,17},{2,26},{10... | collective-permute-start | bytes 1572872 | tf_op jit(solution)/shard_map/ppermute | solution.py:43
  148.3 3.0 %collective-permute-start.17 = (bf16[8,16,4096]{2,1,0:T(8,128)(2,1)}, bf16[8,16,4096]{2,1,0:T(8,128)(2,1)S(1)}, u32[]{:S(2)}, u32[]{:S(2)}) collective-permute-start(bf16[8,16,4096]{2,1,0:T(8,128)(2,1)} %get-tuple-element.50.after_ref), channel_id=1, source_target_pairs={{0,1},{1,0},{2,3},{3,2},{4,5},{5,4},{6,7},{7,6},{8,9},{9,8},{10,11... | collective-permute-start | bytes 3145736 | tf_op jit(solution)/shard_map/ppermute | solution.py:47
  153.2 8.4 %collective-permute-start.18 = (bf16[4,16,2048]{2,1,0:T(8,128)(2,1)S(1)}, bf16[4,16,2048]{2,1,0:T(8,128)(2,1)S(1)}, u32[]{:S(2)}, u32[]{:S(2)}) collective-permute-start(bf16[4,16,2048]{2,1,0:T(8,128)(2,1)S(1)} %get-tuple-element.63), channel_id=1, source_target_pairs={{0,32},{32,0},{1,33},{33,1},{2,34},{34,2},{3,35},{35,3},{4,36},{36... | collective-permute-start | bytes 786440 | tf_op jit(solution)/shard_map/ppermute | solution.py:47
  153.3 9.6 %collective-permute-start.19 = (bf16[4,16,2048]{2,1,0:T(8,128)(2,1)S(1)}, bf16[4,16,2048]{2,1,0:T(8,128)(2,1)S(1)}, u32[]{:S(2)}, u32[]{:S(2)}) collective-permute-start(bf16[4,16,2048]{2,1,0:T(8,128)(2,1)S(1)} %get-tuple-element.64), channel_id=1, source_target_pairs={{0,38},{32,2},{2,32},{34,4},{4,34},{36,6},{6,36},{38,0},{1,39},{33... | collective-permute-start | bytes 786440 | tf_op jit(solution)/shard_map/ppermute | solution.py:54
  163.9 18.2 %all-to-all-start = ((bf16[4,16,4096]{2,1,0:T(8,128)(2,1)}), bf16[4,16,4096]{2,1,0:T(8,128)(2,1)S(1)}, u32[]{:S(2)}, u32[]{:S(2)}) async-start(bf16[4,16,4096]{2,1,0:T(8,128)(2,1)} %fusion), calls=%async_computation | async-start | bytes 1048576 | tf_op jit(solution)/shard_map/all_to_all | solution.py:382
  202.6 11.1 %copy-start.3 = (bf16[4,16,4096]{2,1,0:T(8,128)(2,1)}, bf16[4,16,4096]{2,1,0:T(8,128)(2,1)S(1)}, u32[]{:S(2)}) copy-start(bf16[4,16,4096]{2,1,0:T(8,128)(2,1)S(1)} %all_to_all.20.q_ref) | copy-start | bytes 1572868
  202.7 7.7 %collective-permute-start.23 = (bf16[4,16,2048]{2,1,0:T(8,128)(2,1)S(1)}, bf16[4,16,2048]{2,1,0:T(8,128)(2,1)S(1)}, u32[]{:S(2)}, u32[]{:S(2)}) collective-permute-start(bf16[4,16,2048]{2,1,0:T(8,128)(2,1)S(1)} %get-tuple-element.65), channel_id=1, source_target_pairs={{0,38},{32,2},{2,32},{34,4},{4,34},{36,6},{6,36},{38,0},{1,39},{33... | collective-permute-start | bytes 786440 | tf_op jit(solution)/shard_map/ppermute | solution.py:54
  203.4 8.7 %collective-permute-start.20 = (bf16[4,16,4096]{2,1,0:T(8,128)(2,1)S(1)}, bf16[4,16,4096]{2,1,0:T(8,128)(2,1)S(1)}, u32[]{:S(2)}, u32[]{:S(2)}) collective-permute-start(bf16[4,16,4096]{2,1,0:T(8,128)(2,1)S(1)} %all_to_all.20.q_ref), channel_id=1, source_target_pairs={{0,1},{1,0},{2,3},{3,2},{4,5},{5,4},{6,7},{7,6},{8,9},{9,8},{10,11... | collective-permute-start | bytes 1572872 | tf_op jit(solution)/shard_map/ppermute | solution.py:47
  203.4 8.7 %collective-permute-start.21 = (bf16[4,16,2048]{2,1,0:T(8,128)(2,1)S(1)}, bf16[4,16,2048]{2,1,0:T(8,128)(2,1)S(1)}, u32[]{:S(2)}, u32[]{:S(2)}) collective-permute-start(bf16[4,16,2048]{2,1,0:T(8,128)(2,1)S(1)} %get-tuple-element.66), channel_id=1, source_target_pairs={{0,32},{32,0},{1,33},{33,1},{2,34},{34,2},{3,35},{35,3},{4,36},{36... | collective-permute-start | bytes 786440 | tf_op jit(solution)/shard_map/ppermute | solution.py:47
  210.3 3.3 %copy-start.11 = (bf16[4,16,2048]{2,1,0:T(8,128)(2,1)}, bf16[4,16,2048]{2,1,0:T(8,128)(2,1)S(1)}, u32[]{:S(2)}) copy-start(bf16[4,16,2048]{2,1,0:T(8,128)(2,1)S(1)} %collective-permute-done.23.right_ref) | copy-start | bytes 786436
  210.4 1.8 collective-permute-start.24
  212.1 1.5 copy-start.12
  212.1 1.5 collective-permute-start.22
  212.2 1.5 copy-start.9
  212.2 1.5 copy-start.13
  219.9 7.8 %copy-start.17 = (f32[2,16,128]{2,1,0:T(8,128)S(1)}, f32[2,16,128]{2,1,0:T(8,128)}, u32[]{:S(2)}) copy-start(f32[2,16,128]{2,1,0:T(8,128)} %get-tuple-element.53) | copy-start | bytes 49156
  221.8 41.2 %copy-start.21 = (f32[16,512]{1,0:T(8,128)S(1)}, f32[16,512]{1,0:T(8,128)}, u32[]{:S(2)}) copy-start(f32[16,512]{1,0:T(8,128)} %get-tuple-element.60) | copy-start | bytes 98308
  221.8 45.4 %copy-start.16 = (f32[16,512]{1,0:T(8,128)S(1)}, f32[16,512]{1,0:T(8,128)}, u32[]{:S(2)}) copy-start(f32[16,512]{1,0:T(8,128)} %get-tuple-element.59) | copy-start | bytes 98308
  221.8 33.8 %all-to-all-start.2 = ((bf16[32,2,16,512]{3,2,1,0:T(8,128)(2,1)}), bf16[32,2,16,512]{3,2,1,0:T(8,128)(2,1)S(1)}, u32[]{:S(2)}, u32[]{:S(2)}) async-start(bf16[32,2,16,512]{3,2,1,0:T(8,128)(2,1)} %broadcast_in_dim.11), calls=%async_computation.2 | async-start | bytes 2097152 | tf_op jit(solution)/shard_map/all_to_all | solution.py:408
  227.7 1.3 collective-permute-start.25
  229.0 12.1 %collective-permute-start.26 = (f32[16,128]{1,0:T(8,128)S(1)}, f32[16,128]{1,0:T(8,128)S(1)}, u32[]{:S(2)}, u32[]{:S(2)}) collective-permute-start(f32[16,128]{1,0:T(8,128)S(1)} %slice_bitcast_fusion), channel_id=1, source_target_pairs={{0,32},{32,0},{1,33},{33,1},{2,34},{34,2},{3,35},{35,3},{4,36},{36... | collective-permute-start | bytes 24584 | tf_op jit(solution)/shard_map/ppermute | solution.py:47
  241.1 11.0 %copy-start.15 = (f32[16,128]{1,0:T(8,128)}, f32[16,128]{1,0:T(8,128)S(1)}, u32[]{:S(2)}) copy-start(f32[16,128]{1,0:T(8,128)S(1)} %fusion.1.t0_ref) | copy-start | bytes 24580
  241.1 6.5 %collective-permute-start.29 = (f32[16,128]{1,0:T(8,128)S(1)}, f32[16,128]{1,0:T(8,128)S(1)}, u32[]{:S(2)}, u32[]{:S(2)}) collective-permute-start(f32[16,128]{1,0:T(8,128)S(1)} %fusion.1.t0_ref), channel_id=1, source_target_pairs={{0,6},{2,4},{4,2},{6,0},{1,7},{3,5},{5,3},{7,1},{8,14},{10,12},{12... | collective-permute-start | bytes 24584 | tf_op jit(solution)/shard_map/ppermute | solution.py:301
  244.6 7.6 %collective-permute-start.28 = (f32[16,128]{1,0:T(8,128)S(1)}, f32[16,128]{1,0:T(8,128)S(1)}, u32[]{:S(2)}, u32[]{:S(2)}) collective-permute-start(f32[16,128]{1,0:T(8,128)S(1)} %fusion.1.t0_ref), channel_id=1, source_target_pairs={{0,4},{2,6},{4,0},{6,2},{1,5},{3,7},{5,1},{7,3},{8,12},{10,14},{12... | collective-permute-start | bytes 24584 | tf_op jit(solution)/shard_map/ppermute | solution.py:301
  245.3 6.9 %collective-permute-start.27 = (f32[16,128]{1,0:T(8,128)S(1)}, f32[16,128]{1,0:T(8,128)S(1)}, u32[]{:S(2)}, u32[]{:S(2)}) collective-permute-start(f32[16,128]{1,0:T(8,128)S(1)} %fusion.1.t0_ref), channel_id=1, source_target_pairs={{0,2},{2,0},{4,6},{6,4},{1,3},{3,1},{5,7},{7,5},{8,10},{10,8},{12,... | collective-permute-start | bytes 24584 | tf_op jit(solution)/shard_map/ppermute | solution.py:301
  247.6 4.5 %copy-start.18 = (f32[16,128]{1,0:T(8,128)}, f32[16,128]{1,0:T(8,128)S(1)}, u32[]{:S(2)}) copy-start(f32[16,128]{1,0:T(8,128)S(1)} %collective-permute-done.29.t3_ref) | copy-start | bytes 24580
  255.7 15.0 %copy-start.4 = (bf16[32,2,16,512]{3,2,1,0:T(8,128)(2,1)}, bf16[32,2,16,512]{3,2,1,0:T(8,128)(2,1)S(1)}, u32[]{:S(2)}) copy-start(bf16[32,2,16,512]{3,2,1,0:T(8,128)(2,1)S(1)} %all-to-all-done.2.up_ref) | copy-start | bytes 3145732
  255.7 15.0 %all-to-all-start.3 = ((bf16[32,16,128]{2,1,0:T(8,128)(2,1)}), bf16[32,16,128]{2,1,0:T(8,128)(2,1)S(1)}, u32[]{:S(2)}, u32[]{:S(2)}) async-start(bf16[32,16,128]{2,1,0:T(8,128)(2,1)} %get-tuple-element.56), calls=%async_computation.3 | async-start | bytes 262144 | tf_op jit(solution)/shard_map/all_to_all | solution.py:421
  263.1 4.1 %collective-permute-start.30 = (f32[16,512]{1,0:T(8,128)S(1)}, f32[16,512]{1,0:T(8,128)S(1)}, u32[]{:S(2)}, u32[]{:S(2)}) collective-permute-start(f32[16,512]{1,0:T(8,128)S(1)} %copy-done.21), channel_id=1, source_target_pairs={{0,32},{32,0},{1,33},{33,1},{2,34},{34,2},{3,35},{35,3},{4,36},{36... | collective-permute-start | bytes 98312 | tf_op jit(solution)/shard_map/ppermute | solution.py:47
  (8 other events, 5.8 us)

commit v8 on v5

--- a/solution.py
+++ b/solution.py
@@ -12,6 +12,7 @@
 RANK = 16
 ROWS = 16
 BLOCK = 128
+VMEM_LIMIT = 16 * 2**20
 HALF = 64
 HID = 512
 SIDE = MODEL_WIDTH // 2
@@ -66,6 +67,7 @@
         in_specs=[vmem] * len(args) + [wait] * len(after),
         out_specs=(vmem,) * len(out_shape) if many else vmem,
         scratch_shapes=scratch,
+        compiler_params=pltpu.CompilerParams(vmem_limit_bytes=VMEM_LIMIT),
         name=name,
     )(*args, *after)
 
@@ -207,20 +209,15 @@
         (l, own_ref, pt_ref[0], up_own_ref, b_own_ref[...]),
         (1 - l, oth_ref, pt_ref[1], up_oth_ref, b_oth_ref[...]),
     )
-    for side, hid_ref, p, up_ref, b in sides:
+    for order, (side, hid_ref, p, up_ref, b) in enumerate(sides):
         up = b.astype(F32) - RATE_UP * (scale * dot(p, hid_ref[...]))
         up_ref[...] = up
         wire_ref[side] = up.astype(BF16)
-        back = dot_nt(b, hid_ref[...])
-        for k in range(8):
-            back_ref[side * 8 + k] = back
-
-
-def down_kernel(back_ref, x_ref, a_ref, up_ref, new_ref, wire_ref):
-    terms = [back_ref[k] for k in range(16)]
-    while len(terms) > 1:
-        terms = [terms[k] + terms[k + 1] for k in range(0, len(terms), 2)]
-    rest = terms[0]
+        back_ref[order] = dot_nt(b, hid_ref[...])
+
+
+def down_kernel(t0_ref, t1_ref, t2_ref, t3_ref, x_ref, a_ref, up_ref, new_ref, wire_ref):
+    rest = (t0_ref[...] + t1_ref[...]) + (t2_ref[...] + t3_ref[...])
     parts = []
     for _ in range(3):
         parts.append(rest.astype(BF16))
@@ -265,9 +262,28 @@
     return [value, below, above, shift(below, axis, 1)]
 
 
+def halves_kernel(below_ref, above_ref, low_ref, high_ref):
+    low_ref[...] = below_ref[...]
+    high_ref[...] = above_ref[...]
+
+
 def far_halves(below, above, axis):
-    half = below.shape[0] // 2
-    return [shift(below[:half], axis, 1), shift(above[half:], axis, -1)]
+    block = (HID, HID)
+    first, second = pl.BlockSpec(block, lambda i: (0, 0)), pl.BlockSpec(block, lambda i: (1, 0))
+    low, high = pl.pallas_call(
+        halves_kernel,
+        grid=(1,),
+        out_shape=(shape(*block), shape(*block)),
+        in_specs=[first, second],
+        out_specs=(first, first),
+        compiler_params=pltpu.CompilerParams(vmem_limit_bytes=VMEM_LIMIT),
+        name="halves",
+    )(below, above)
+    return [shift(low, axis, 1), shift(high, axis, -1)]
+
+
+def swap(value, mask):
+    return lax.ppermute(value, "h", [(i, i ^ mask) for i in range(4)])
 
 
 def shards(tokens, targets, w_in, w_out, factor_down, factor_up):
@@ -311,11 +327,8 @@
         scratch=[pltpu.VMEM((2, TOK, RANK), BF16)],
         name="arrange",
     )
-    my_targets = call(
-        targets_kernel, shape(ROWS, MODEL_WIDTH), targets, after=[p_rel], name="targets"
-    )
-    in_near[1], in_near[2], x_near, p_rel, my_targets = lax.optimization_barrier(
-        (in_near[1], in_near[2], x_near, p_rel, my_targets)
+    in_near[1], in_near[2], x_near, p_rel = lax.optimization_barrier(
+        (in_near[1], in_near[2], x_near, p_rel)
     )
     in_far = far_halves(in_near[1], in_near[2], "y")
     out_far = far_halves(out_near[1], out_near[2], "x")
@@ -337,6 +350,10 @@
         (shape(8, ROWS, MODEL_WIDTH, dtype=F32), shape(8, ROWS, MODEL_WIDTH)),
         hidden, *out_pieces,
         name="output",
+    )
+
+    my_targets = call(
+        targets_kernel, shape(ROWS, MODEL_WIDTH), targets, after=[p_rel], name="targets"
     )
 
     summed = keep + partner(send, "c").astype(F32)
@@ -360,7 +377,7 @@
             shape(RANK, HID, dtype=F32),
             shape(RANK, HID, dtype=F32),
             shape(2, RANK, HID),
-            shape(16, RANK, TOK, dtype=F32),
+            shape(2, RANK, TOK, dtype=F32),
         ),
         q, q_far, left, left_far, right, right_far, mask, pt, b_own, b_oth, *out_pieces,
         scratch=[
@@ -370,11 +387,13 @@
         ],
         name="backward",
     )
-    back = lax.all_to_all(back, ("l", "h", "c"), 0, 0, tiled=True)
+    back = back + partner(back, "c")
+    back = back[0] + partner(back[1], "l")
+    back = [back] + [swap(back, mask) for mask in (1, 2, 3)]
     new_a, wire = call(
         down_kernel,
         (shape(RANK, MODEL_WIDTH, dtype=F32), shape(32, RANK, BLOCK + 2 * HID)),
-        back, tokens, a, up_wire,
+        *back, tokens, a, up_wire,
         name="down",
     )
     wires = lax.all_to_all(wire, REP, 0, 0, tiled=True)

time: 201 us -> 182 us (0.905)
  blocking collectives: 51 us -> 20.1 us
  waiting for transfers between devices: 60 us -> 85.9 us
  Pallas kernels: 34.2 us -> 8.74 us
  starting transfers between devices: 37.3 us -> 56.3 us
  local copies, waits for them, and re-layouts: 9.64 us -> 5.63 us
  other arithmetic: 6.03 us -> 3.39 us
    all_to_all x2 -> x0, blocking collectives: 32.5 us -> none  [the longest x1 19.4 us: shards(): shares = lax.all_to_all(summed.astype(BF16), 'h', 0, 0, tiled=True)]
    pallas_call x11, Pallas kernels: 34.2 us -> 8.6 us  [call(): pl.pallas_call(kernel, out_shape=out_shape, in_specs=[vmem] * len(args) +...]
    all_to_all x0 -> x1, waiting for transfers between devices: none -> 12.8 us  [shards(): shares = lax.all_to_all(summed.astype(BF16), 'h', 0, 0, tiled=True)]
    ppermute x14, waiting for transfers between devices: 9.11 us -> 19 us  [shift(): return lax.ppermute(value, axis, [(i, (i + by) % n) for i in range(n)])]
    ppermute x0 -> x3, starting transfers between devices: none -> 6.5 us  [swap(): return lax.ppermute(value, 'h', [(i, i ^ mask) for i in range(4)])]
    all_to_all x0 -> x1, starting transfers between devices: none -> 5.56 us  [shards(): shares = lax.all_to_all(summed.astype(BF16), 'h', 0, 0, tiled=True)]
    slice x4 -> x0, local copies, waits for them, and re-layouts: 4.66 us -> none  [far_halves(): return [shift(below[:half], axis, 1), shift(above[half:], axis, -1)]]
    ppermute x3, starting transfers between devices: 8.19 us -> 11.2 us  [near_z(): lax.ppermute(value, Z, [(place(z), place(z + 1 if z % 2 else z - 1)) for...]
  transfers between devices with their start and end apart: 27 -> 33, of which waited for: 15 -> 21; matrix products, arithmetic and copies ran while one was open for 4% -> 1% of each run, Pallas kernels for 9% -> 2%
where the time goes in v8:
time: 182 us; the launch traced here: 181 us
  waiting for transfers between devices  85.9 us (47%)
  starting transfers between devices  56.3 us (31%)
  blocking collectives  20.1 us (11%)
  Pallas kernels  8.74 us (5%)
  local copies, waits for them, and re-layouts  5.63 us (3%)
  other arithmetic  3.39 us (2%)
    ppermute x11, waiting for transfers between devices, partner(): return lax.ppermute(value, axis, [(0, 1), (1, 0)])  35.6 us
    all_to_all x1, blocking collectives, shards(): lax.all_to_all(jnp.broadcast_to(grad_rows, (4, ROWS, MODEL_WIDTH)), 'h',...  20.1 us
    ppermute x14, starting transfers between devices, shift(): return lax.ppermute(value, axis, [(i, (i + by) % n) for i in range(n)])  19.2 us
    ppermute x14, waiting for transfers between devices, shift(): return lax.ppermute(value, axis, [(i, (i + by) % n) for i in range(n)])  19 us
    ppermute x3, waiting for transfers between devices, near_z(): lax.ppermute(value, Z, [(place(z), place(z + 1 if z % 2 else z - 1)) for...  13.9 us
    all_to_all x1, waiting for transfers between devices, shards(): shares = lax.all_to_all(summed.astype(BF16), 'h', 0, 0, tiled=True)  12.8 us
    ppermute x3, starting transfers between devices, near_z(): lax.ppermute(value, Z, [(place(z), place(z + 1 if z % 2 else z - 1)) for...  11.2 us
    pallas_call x11, Pallas kernels, call(): pl.pallas_call(kernel, out_shape=out_shape, in_specs=[vmem] * len(args) +...  8.6 us
  transfers between devices with their start and end apart: 33, of which 21 were waited for; matrix products, arithmetic and copies ran while one was open for 1% of the time, Pallas kernels for 2%

profile of v8, /device:TPU:2, one launch (start us, length us, event | category | flops | bytes accessed | tf_op | source)
XLA Modules:
  0.0 181.0 jit_solution(6741917656197586697)
XLA Ops:
  0.7 1.0 copy-done.3
  1.7 0.9 copy-done.9
  3.5 2.0 %collective-permute-start.2 = (bf16[272,512]{1,0:T(8,128)(2,1)S(1)}, bf16[272,512]{1,0:T(8,128)(2,1)S(1)}, u32[]{:S(2)}, u32[]{:S(2)}) collective-permute-start(bf16[272,512]{1,0:T(8,128)(2,1)S(1)} %send.1.send_ref), channel_id=1, source_target_pairs={{0,32},{32,0},{1,33},{33,1},{2,34},{34,2},{3,35},{35,3},{4,36},{36... | collective-permute-start | bytes 835592 | tf_op jit(solution)/shard_map/ppermute | solution.py:48
  6.4 5.8 %collective-permute-done.2 = bf16[272,512]{1,0:T(8,128)(2,1)S(1)} collective-permute-done((bf16[272,512]{1,0:T(8,128)(2,1)S(1)}, bf16[272,512]{1,0:T(8,128)(2,1)S(1)}, u32[]{:S(2)}, u32[]{:S(2)}) %collective-permute-start.2) | collective-permute-done | bytes 278560 | tf_op jit(solution)/shard_map/ppermute | solution.py:48
  12.2 1.6 collective-permute-start.3
  13.9 1.7 collective-permute-start.10
  16.1 3.6 %collective-permute-done.3 = bf16[256,512]{1,0:T(8,128)(2,1)S(1)} collective-permute-done((bf16[256,512]{1,0:T(8,128)(2,1)S(1)}, bf16[256,512]{1,0:T(8,128)(2,1)S(1)}, u32[]{:S(2)}, u32[]{:S(2)}) %collective-permute-start.3) | collective-permute-done | bytes 262176 | tf_op jit(solution)/shard_map/ppermute | solution.py:44
  19.7 1.5 collective-permute-start.5
  21.2 3.0 %collective-permute-start.11 = (bf16[256,512]{1,0:T(8,128)(2,1)S(1)}, bf16[256,512]{1,0:T(8,128)(2,1)S(1)}, u32[]{:S(2)}, u32[]{:S(2)}) collective-permute-start(bf16[256,512]{1,0:T(8,128)(2,1)S(1)} %maximum_select_fusion.1), channel_id=1, source_target_pairs={{0,192},{64,0},{128,64},{192,128},{1,193},{65,1},{129,65},{193,129... | collective-permute-start | bytes 786440 | tf_op jit(solution)/shard_map/ppermute | solution.py:44
  24.6 5.5 %collective-permute-start = (bf16[80,4096]{1,0:T(8,128)(2,1)S(1)}, bf16[80,4096]{1,0:T(8,128)(2,1)S(1)}, u32[]{:S(2)}, u32[]{:S(2)}) collective-permute-start(bf16[80,4096]{1,0:T(8,128)(2,1)S(1)} %get-tuple-element.31), channel_id=1, source_target_pairs={{0,38},{32,2},{2,32},{34,4},{4,34},{36,6},{6,36},{38,0},{1,39},{33... | collective-permute-start | bytes 1966088 | tf_op jit(solution)/shard_map/ppermute | solution.py:55
  30.8 2.7 %collective-permute-start.7 = (bf16[1024,512]{1,0:T(8,128)(2,1)S(1)}, bf16[1024,512]{1,0:T(8,128)(2,1)S(1)}, u32[]{:S(2)}, u32[]{:S(2)}) collective-permute-start(bf16[1024,512]{1,0:T(8,128)(2,1)S(1)} %pad_maximum_fusion.refs_0_), channel_id=1, source_target_pairs={{0,192},{64,0},{128,64},{192,128},{1,193},{65,1},{129,65},{193,129... | collective-permute-start | bytes 3145736 | tf_op jit(solution)/shard_map/ppermute | solution.py:44
  33.7 1.3 collective-permute-start.13
  35.8 6.7 %collective-permute-done.oth_ref = bf16[80,4096]{1,0:T(8,128)(2,1)S(1)} collective-permute-done((bf16[80,4096]{1,0:T(8,128)(2,1)S(1)}, bf16[80,4096]{1,0:T(8,128)(2,1)S(1)}, u32[]{:S(2)}, u32[]{:S(2)}) %collective-permute-start) | collective-permute-done | bytes 655392 | tf_op jit(solution)/shard_map/ppermute | solution.py:55
  42.5 2.1 %collective-permute-done.1.oth_core_ref = bf16[80,4096]{1,0:T(8,128)(2,1)S(1)} collective-permute-done((bf16[80,4096]{1,0:T(8,128)(2,1)S(1)}, bf16[80,4096]{1,0:T(8,128)(2,1)S(1)}, u32[]{:S(2)}, u32[]{:S(2)}) %collective-permute-start.1) | collective-permute-done | bytes 655392 | tf_op jit(solution)/shard_map/ppermute | solution.py:48
  44.6 1.0 arrange.1
  45.6 8.7 %collective-permute-done.6.refs_1_.below_ref = bf16[1024,512]{1,0:T(8,128)(2,1)S(1)} collective-permute-done((bf16[1024,512]{1,0:T(8,128)(2,1)S(1)}, bf16[1024,512]{1,0:T(8,128)(2,1)S(1)}, u32[]{:S(2)}, u32[]{:S(2)}) %collective-permute-start.6) | collective-permute-done | bytes 1048608 | tf_op jit(solution)/shard_map/ppermute | solution.py:44
  55.0 2.6 %collective-permute-start.9 = (bf16[512,512]{1,0:T(8,128)(2,1)S(1)}, bf16[512,512]{1,0:T(8,128)(2,1)S(1)}, u32[]{:S(2)}, u32[]{:S(2)}) collective-permute-start(bf16[512,512]{1,0:T(8,128)(2,1)S(1)} %get-tuple-element.42), channel_id=1, source_target_pairs={{0,192},{64,0},{128,64},{192,128},{1,193},{65,1},{129,65},{193,129... | collective-permute-start | bytes 1572872 | tf_op jit(solution)/shard_map/ppermute | solution.py:44
  57.7 1.3 collective-permute-start.15
  60.5 1.0 near.1.total_ref
  61.6 4.7 %collective-permute-done.8.low_ref = bf16[512,512]{1,0:T(8,128)(2,1)S(1)} collective-permute-done((bf16[512,512]{1,0:T(8,128)(2,1)S(1)}, bf16[512,512]{1,0:T(8,128)(2,1)S(1)}, u32[]{:S(2)}, u32[]{:S(2)}) %collective-permute-start.8) | collective-permute-done | bytes 524320 | tf_op jit(solution)/shard_map/ppermute | solution.py:44
  66.7 1.1 collective-permute-done.15.refs_3_
  67.9 0.9 collective-permute-done.16.refs_4_
  68.8 1.4 output.1
  70.3 2.6 %collective-permute-done.17 = bf16[8,16,4096]{2,1,0:T(8,128)(2,1)S(1)} collective-permute-done((bf16[8,16,4096]{2,1,0:T(8,128)(2,1)S(1)}, bf16[8,16,4096]{2,1,0:T(8,128)(2,1)S(1)}, u32[]{:S(2)}, u32[]{:S(2)}) %collective-permute-start.17) | collective-permute-done | bytes 1048608 | tf_op jit(solution)/shard_map/ppermute | solution.py:48
  74.0 5.0 %collective-permute-start.19 = (bf16[4,16,2048]{2,1,0:T(8,128)(2,1)S(1)}, bf16[4,16,2048]{2,1,0:T(8,128)(2,1)S(1)}, u32[]{:S(2)}, u32[]{:S(2)}) collective-permute-start(bf16[4,16,2048]{2,1,0:T(8,128)(2,1)S(1)} %get-tuple-element.60), channel_id=1, source_target_pairs={{0,38},{32,2},{2,32},{34,4},{4,34},{36,6},{6,36},{38,0},{1,39},{33... | collective-permute-start | bytes 786440 | tf_op jit(solution)/shard_map/ppermute | solution.py:55
  78.9 2.8 %collective-permute-done.18 = bf16[4,16,2048]{2,1,0:T(8,128)(2,1)S(1)} collective-permute-done((bf16[4,16,2048]{2,1,0:T(8,128)(2,1)S(1)}, bf16[4,16,2048]{2,1,0:T(8,128)(2,1)S(1)}, u32[]{:S(2)}, u32[]{:S(2)}) %collective-permute-start.18) | collective-permute-done | bytes 262176 | tf_op jit(solution)/shard_map/ppermute | solution.py:48
  81.7 3.6 %collective-permute-done.19 = bf16[4,16,2048]{2,1,0:T(8,128)(2,1)S(1)} collective-permute-done((bf16[4,16,2048]{2,1,0:T(8,128)(2,1)S(1)}, bf16[4,16,2048]{2,1,0:T(8,128)(2,1)S(1)}, u32[]{:S(2)}, u32[]{:S(2)}) %collective-permute-start.19) | collective-permute-done | bytes 262176 | tf_op jit(solution)/shard_map/ppermute | solution.py:55
  85.3 0.9 fusion
  86.2 5.6 %all-to-all-start = ((bf16[4,16,4096]{2,1,0:T(8,128)(2,1)}), bf16[4,16,4096]{2,1,0:T(8,128)(2,1)}, u32[]{:S(2)}, u32[]{:S(2)}) async-start(bf16[4,16,4096]{2,1,0:T(8,128)(2,1)} %fusion), calls=%async_computation | async-start | bytes 1048576 | tf_op jit(solution)/shard_map/all_to_all | solution.py:365
  91.7 1.2 copy-done.10
  93.0 12.8 %all-to-all-done = bf16[4,16,4096]{2,1,0:T(8,128)(2,1)} async-done(((bf16[4,16,4096]{2,1,0:T(8,128)(2,1)}), bf16[4,16,4096]{2,1,0:T(8,128)(2,1)}, u32[]{:S(2)}, u32[]{:S(2)}) %all-to-all-start) | async-done | bytes 524320 | tf_op jit(solution)/shard_map/all_to_all | solution.py:365
  105.8 1.2 convert_reduce_fusion
  107.2 20.1 %all_to_all.15.q_ref = bf16[4,16,4096]{2,1,0:T(8,128)(2,1)S(1)} all-to-all(bf16[4,16,4096]{2,1,0:T(8,128)(2,1)S(1)} %broadcast_in_dim.7), channel_id=1, replica_groups=mesh['y'=4,'l'=2,'x'=4,'h'=4,'c'=2] {'h'}, dimensions={0} | all-to-all | bytes 1048576 | tf_op jit(solution)/shard_map/all_to_all | solution.py:369
  128.3 5.5 %collective-permute-done.21.left_ref = bf16[4,16,2048]{2,1,0:T(8,128)(2,1)S(1)} collective-permute-done((bf16[4,16,2048]{2,1,0:T(8,128)(2,1)S(1)}, bf16[4,16,2048]{2,1,0:T(8,128)(2,1)S(1)}, u32[]{:S(2)}, u32[]{:S(2)}) %collective-permute-start.21) | collective-permute-done | bytes 262176 | tf_op jit(solution)/shard_map/ppermute | solution.py:48
  133.8 3.7 %collective-permute-done.23.right_ref = bf16[4,16,2048]{2,1,0:T(8,128)(2,1)S(1)} collective-permute-done((bf16[4,16,2048]{2,1,0:T(8,128)(2,1)S(1)}, bf16[4,16,2048]{2,1,0:T(8,128)(2,1)S(1)}, u32[]{:S(2)}, u32[]{:S(2)}) %collective-permute-start.23) | collective-permute-done | bytes 262176 | tf_op jit(solution)/shard_map/ppermute | solution.py:55
  137.5 1.5 collective-permute-done.24.rightc_ref
  139.0 1.5 backward.1
  140.7 1.1 collective-permute-done.25
  142.5 3.0 %collective-permute-done.26 = f32[16,128]{1,0:T(8,128)S(1)} collective-permute-done((f32[16,128]{1,0:T(8,128)S(1)}, f32[16,128]{1,0:T(8,128)S(1)}, u32[]{:S(2)}, u32[]{:S(2)}) %collective-permute-start.26) | collective-permute-done | bytes 8224 | tf_op jit(solution)/shard_map/ppermute | solution.py:48
  145.8 2.2 %collective-permute-start.28 = (f32[16,128]{1,0:T(8,128)S(1)}, f32[16,128]{1,0:T(8,128)S(1)}, u32[]{:S(2)}, u32[]{:S(2)}) collective-permute-start(f32[16,128]{1,0:T(8,128)S(1)} %fusion.1.t0_ref), channel_id=1, source_target_pairs={{0,4},{2,6},{4,0},{6,2},{1,5},{3,7},{5,1},{7,3},{8,12},{10,14},{12... | collective-permute-start | bytes 24584 | tf_op jit(solution)/shard_map/ppermute | solution.py:286
  148.0 3.9 %collective-permute-start.29 = (f32[16,128]{1,0:T(8,128)S(1)}, f32[16,128]{1,0:T(8,128)S(1)}, u32[]{:S(2)}, u32[]{:S(2)}) collective-permute-start(f32[16,128]{1,0:T(8,128)S(1)} %fusion.1.t0_ref), channel_id=1, source_target_pairs={{0,6},{2,4},{4,2},{6,0},{1,7},{3,5},{5,3},{7,1},{8,14},{10,12},{12... | collective-permute-start | bytes 24584 | tf_op jit(solution)/shard_map/ppermute | solution.py:286
  151.9 1.5 collective-permute-done.28.t2_ref
  153.8 1.5 down.1
  155.2 8.4 %all-to-all-start.2 = ((bf16[32,16,1152]{2,1,0:T(8,128)(2,1)}), bf16[32,16,1152]{2,1,0:T(8,128)(2,1)S(1)}, u32[]{:S(2)}, u32[]{:S(2)}) async-start(bf16[32,16,1152]{2,1,0:T(8,128)(2,1)} %get-tuple-element.53), calls=%async_computation.2 | async-start | bytes 2359296 | tf_op jit(solution)/shard_map/all_to_all | solution.py:399
  163.7 1.6 collective-permute-start.30
  165.2 11.3 %collective-permute-done.30 = f32[16,512]{1,0:T(8,128)S(1)} collective-permute-done((f32[16,512]{1,0:T(8,128)S(1)}, f32[16,512]{1,0:T(8,128)S(1)}, u32[]{:S(2)}, u32[]{:S(2)}) %collective-permute-start.30) | collective-permute-done | bytes 32800 | tf_op jit(solution)/shard_map/ppermute | solution.py:48
  177.2 2.7 %all-to-all-done.2.wire_ref = bf16[32,16,1152]{2,1,0:T(8,128)(2,1)S(1)} async-done(((bf16[32,16,1152]{2,1,0:T(8,128)(2,1)}), bf16[32,16,1152]{2,1,0:T(8,128)(2,1)S(1)}, u32[]{:S(2)}, u32[]{:S(2)}) %all-to-all-start.2) | async-done | bytes 1179680 | tf_op jit(solution)/shard_map/all_to_all | solution.py:399
  179.8 1.1 merge.1
  (83 shorter events, 11.9 us)
Async XLA Ops:
  0.6 23.6 %copy-start = (bf16[128,4096]{1,0:T(8,128)(2,1)S(1)}, bf16[128,4096]{1,0:T(8,128)(2,1)}, u32[]{:S(2)}) copy-start(bf16[128,4096]{1,0:T(8,128)(2,1)} %x_ref.1) | copy-start | bytes 3145732
  0.6 1.0 copy-start.3
  1.7 0.9 copy-start.9
  3.4 20.8 %copy-start.11 = (bf16[1,16,4096]{2,1,0:T(8,128)(2,1)S(1)}, bf16[1,16,4096]{2,1,0:T(8,128)(2,1)}, u32[]{:S(2)}) copy-start(bf16[1,16,4096]{2,1,0:T(8,128)(2,1)} %param.10) | copy-start | bytes 393220
  3.5 8.7 %collective-permute-start.2 = (bf16[272,512]{1,0:T(8,128)(2,1)S(1)}, bf16[272,512]{1,0:T(8,128)(2,1)S(1)}, u32[]{:S(2)}, u32[]{:S(2)}) collective-permute-start(bf16[272,512]{1,0:T(8,128)(2,1)S(1)} %send.1.send_ref), channel_id=1, source_target_pairs={{0,32},{32,0},{1,33},{33,1},{2,34},{34,2},{3,35},{35,3},{4,36},{36... | collective-permute-start | bytes 835592 | tf_op jit(solution)/shard_map/ppermute | solution.py:48
  12.2 18.0 %copy-start.16 = (bf16[272,512]{1,0:T(8,128)(2,1)}, bf16[272,512]{1,0:T(8,128)(2,1)S(1)}, u32[]{:S(2)}) copy-start(bf16[272,512]{1,0:T(8,128)(2,1)S(1)} %collective-permute-done.2) | copy-start | bytes 835588
  12.2 7.4 %collective-permute-start.3 = (bf16[256,512]{1,0:T(8,128)(2,1)S(1)}, bf16[256,512]{1,0:T(8,128)(2,1)S(1)}, u32[]{:S(2)}, u32[]{:S(2)}) collective-permute-start(bf16[256,512]{1,0:T(8,128)(2,1)S(1)} %maximum_select_fusion), channel_id=1, source_target_pairs={{0,8},{8,16},{16,24},{24,0},{1,9},{9,17},{17,25},{25,1},{2,10},{10... | collective-permute-start | bytes 786440 | tf_op jit(solution)/shard_map/ppermute | solution.py:44
  13.9 10.3 %collective-permute-start.10 = (bf16[256,512]{1,0:T(8,128)(2,1)S(1)}, bf16[256,512]{1,0:T(8,128)(2,1)S(1)}, u32[]{:S(2)}, u32[]{:S(2)}) collective-permute-start(bf16[256,512]{1,0:T(8,128)(2,1)S(1)} %maximum_select_fusion.1), channel_id=1, source_target_pairs={{0,64},{64,128},{128,192},{192,0},{1,65},{65,129},{129,193},{193,1... | collective-permute-start | bytes 786440 | tf_op jit(solution)/shard_map/ppermute | solution.py:44
  15.5 14.6 %collective-permute-start.4 = (bf16[256,512]{1,0:T(8,128)(2,1)S(1)}, bf16[256,512]{1,0:T(8,128)(2,1)S(1)}, u32[]{:S(2)}, u32[]{:S(2)}) collective-permute-start(bf16[256,512]{1,0:T(8,128)(2,1)S(1)} %maximum_select_fusion), channel_id=1, source_target_pairs={{0,24},{8,0},{16,8},{24,16},{1,25},{9,1},{17,9},{25,17},{2,26},{10... | collective-permute-start | bytes 786440 | tf_op jit(solution)/shard_map/ppermute | solution.py:44
  19.7 10.4 %collective-permute-start.5 = (bf16[256,512]{1,0:T(8,128)(2,1)S(1)}, bf16[256,512]{1,0:T(8,128)(2,1)S(1)}, u32[]{:S(2)}, u32[]{:S(2)}) collective-permute-start(bf16[256,512]{1,0:T(8,128)(2,1)S(1)} %collective-permute-done.3), channel_id=1, source_target_pairs={{0,8},{8,16},{16,24},{24,0},{1,9},{9,17},{17,25},{25,1},{2,10},{10... | collective-permute-start | bytes 786440 | tf_op jit(solution)/shard_map/ppermute | solution.py:44
  21.2 12.4 %collective-permute-start.11 = (bf16[256,512]{1,0:T(8,128)(2,1)S(1)}, bf16[256,512]{1,0:T(8,128)(2,1)S(1)}, u32[]{:S(2)}, u32[]{:S(2)}) collective-permute-start(bf16[256,512]{1,0:T(8,128)(2,1)S(1)} %maximum_select_fusion.1), channel_id=1, source_target_pairs={{0,192},{64,0},{128,64},{192,128},{1,193},{65,1},{129,65},{193,129... | collective-permute-start | bytes 786440 | tf_op jit(solution)/shard_map/ppermute | solution.py:44
  24.2 9.4 %collective-permute-start.12 = (bf16[256,512]{1,0:T(8,128)(2,1)S(1)}, bf16[256,512]{1,0:T(8,128)(2,1)S(1)}, u32[]{:S(2)}, u32[]{:S(2)}) collective-permute-start(bf16[256,512]{1,0:T(8,128)(2,1)S(1)} %collective-permute-done.10), channel_id=1, source_target_pairs={{0,64},{64,128},{128,192},{192,0},{1,65},{65,129},{129,193},{193,1... | collective-permute-start | bytes 786440 | tf_op jit(solution)/shard_map/ppermute | solution.py:44
  24.6 20.0 %copy-start.1 = (bf16[128,4096]{1,0:T(8,128)(2,1)S(1)}, bf16[128,4096]{1,0:T(8,128)(2,1)}, u32[]{:S(2)}) copy-start(bf16[128,4096]{1,0:T(8,128)(2,1)} %x_ref.1) | copy-start | bytes 3145732
  24.6 17.9 %collective-permute-start = (bf16[80,4096]{1,0:T(8,128)(2,1)S(1)}, bf16[80,4096]{1,0:T(8,128)(2,1)S(1)}, u32[]{:S(2)}, u32[]{:S(2)}) collective-permute-start(bf16[80,4096]{1,0:T(8,128)(2,1)S(1)} %get-tuple-element.31), channel_id=1, source_target_pairs={{0,38},{32,2},{2,32},{34,4},{4,34},{36,6},{6,36},{38,0},{1,39},{33... | collective-permute-start | bytes 1966088 | tf_op jit(solution)/shard_map/ppermute | solution.py:55
  30.2 24.1 %collective-permute-start.6 = (bf16[1024,512]{1,0:T(8,128)(2,1)S(1)}, bf16[1024,512]{1,0:T(8,128)(2,1)S(1)}, u32[]{:S(2)}, u32[]{:S(2)}) collective-permute-start(bf16[1024,512]{1,0:T(8,128)(2,1)S(1)} %pad_maximum_fusion.refs_0_), channel_id=1, source_target_pairs={{0,64},{64,128},{128,192},{192,0},{1,65},{65,129},{129,193},{193,1... | collective-permute-start | bytes 3145736 | tf_op jit(solution)/shard_map/ppermute | solution.py:44
  30.8 23.4 %collective-permute-start.7 = (bf16[1024,512]{1,0:T(8,128)(2,1)S(1)}, bf16[1024,512]{1,0:T(8,128)(2,1)S(1)}, u32[]{:S(2)}, u32[]{:S(2)}) collective-permute-start(bf16[1024,512]{1,0:T(8,128)(2,1)S(1)} %pad_maximum_fusion.refs_0_), channel_id=1, source_target_pairs={{0,192},{64,0},{128,64},{192,128},{1,193},{65,1},{129,65},{193,129... | collective-permute-start | bytes 3145736 | tf_op jit(solution)/shard_map/ppermute | solution.py:44
  33.7 24.0 %collective-permute-start.13 = (bf16[1024,512]{1,0:T(8,128)(2,1)S(1)}, bf16[1024,512]{1,0:T(8,128)(2,1)S(1)}, u32[]{:S(2)}, u32[]{:S(2)}) collective-permute-start(bf16[1024,512]{1,0:T(8,128)(2,1)S(1)} %pad_maximum_fusion.1.refs_0_), channel_id=1, source_target_pairs={{0,8},{8,16},{16,24},{24,0},{1,9},{9,17},{17,25},{25,1},{2,10},{10... | collective-permute-start | bytes 3145736 | tf_op jit(solution)/shard_map/ppermute | solution.py:44
  34.9 22.7 %collective-permute-start.14 = (bf16[1024,512]{1,0:T(8,128)(2,1)S(1)}, bf16[1024,512]{1,0:T(8,128)(2,1)S(1)}, u32[]{:S(2)}, u32[]{:S(2)}) collective-permute-start(bf16[1024,512]{1,0:T(8,128)(2,1)S(1)} %pad_maximum_fusion.1.refs_0_), channel_id=1, source_target_pairs={{0,24},{8,0},{16,8},{24,16},{1,25},{9,1},{17,9},{25,17},{2,26},{10... | collective-permute-start | bytes 3145736 | tf_op jit(solution)/shard_map/ppermute | solution.py:44
  42.5 2.1 %collective-permute-start.1 = (bf16[80,4096]{1,0:T(8,128)(2,1)S(1)}, bf16[80,4096]{1,0:T(8,128)(2,1)S(1)}, u32[]{:S(2)}, u32[]{:S(2)}) collective-permute-start(bf16[80,4096]{1,0:T(8,128)(2,1)S(1)} %collective-permute-done.oth_ref), channel_id=1, source_target_pairs={{0,1},{1,0},{2,3},{3,2},{4,5},{5,4},{6,7},{7,6},{8,9},{9,8},{10,11... | collective-permute-start | bytes 1966088 | tf_op jit(solution)/shard_map/ppermute | solution.py:48
  54.3 11.9 %collective-permute-start.8 = (bf16[512,512]{1,0:T(8,128)(2,1)S(1)}, bf16[512,512]{1,0:T(8,128)(2,1)S(1)}, u32[]{:S(2)}, u32[]{:S(2)}) collective-permute-start(bf16[512,512]{1,0:T(8,128)(2,1)S(1)} %get-tuple-element.41), channel_id=1, source_target_pairs={{0,64},{64,128},{128,192},{192,0},{1,65},{65,129},{129,193},{193,1... | collective-permute-start | bytes 1572872 | tf_op jit(solution)/shard_map/ppermute | solution.py:44
  55.0 11.2 %collective-permute-start.9 = (bf16[512,512]{1,0:T(8,128)(2,1)S(1)}, bf16[512,512]{1,0:T(8,128)(2,1)S(1)}, u32[]{:S(2)}, u32[]{:S(2)}) collective-permute-start(bf16[512,512]{1,0:T(8,128)(2,1)S(1)} %get-tuple-element.42), channel_id=1, source_target_pairs={{0,192},{64,0},{128,64},{192,128},{1,193},{65,1},{129,65},{193,129... | collective-permute-start | bytes 1572872 | tf_op jit(solution)/shard_map/ppermute | solution.py:44
  57.7 10.1 %collective-permute-start.15 = (bf16[512,512]{1,0:T(8,128)(2,1)S(1)}, bf16[512,512]{1,0:T(8,128)(2,1)S(1)}, u32[]{:S(2)}, u32[]{:S(2)}) collective-permute-start(bf16[512,512]{1,0:T(8,128)(2,1)S(1)} %get-tuple-element.45), channel_id=1, source_target_pairs={{0,8},{8,16},{16,24},{24,0},{1,9},{9,17},{17,25},{25,1},{2,10},{10... | collective-permute-start | bytes 1572872 | tf_op jit(solution)/shard_map/ppermute | solution.py:44
  59.0 9.8 %collective-permute-start.16 = (bf16[512,512]{1,0:T(8,128)(2,1)S(1)}, bf16[512,512]{1,0:T(8,128)(2,1)S(1)}, u32[]{:S(2)}, u32[]{:S(2)}) collective-permute-start(bf16[512,512]{1,0:T(8,128)(2,1)S(1)} %get-tuple-element.46), channel_id=1, source_target_pairs={{0,24},{8,0},{16,8},{24,16},{1,25},{9,1},{17,9},{25,17},{2,26},{10... | collective-permute-start | bytes 1572872 | tf_op jit(solution)/shard_map/ppermute | solution.py:44
  66.7 3.4 %copy-start.12 = (bf16[256,512]{1,0:T(8,128)(2,1)}, bf16[256,512]{1,0:T(8,128)(2,1)S(1)}, u32[]{:S(2)}) copy-start(bf16[256,512]{1,0:T(8,128)(2,1)S(1)} %get-tuple-element.49.mask_ref) | copy-start | bytes 786436
  67.9 2.3 %copy-start.5 = (bf16[512,512]{1,0:T(8,128)(2,1)}, bf16[512,512]{1,0:T(8,128)(2,1)S(1)}, u32[]{:S(2)}) copy-start(bf16[512,512]{1,0:T(8,128)(2,1)S(1)} %collective-permute-done.15.refs_3_) | copy-start | bytes 1572868
  68.8 1.4 copy-start.7
  70.2 2.7 %collective-permute-start.17 = (bf16[8,16,4096]{2,1,0:T(8,128)(2,1)S(1)}, bf16[8,16,4096]{2,1,0:T(8,128)(2,1)S(1)}, u32[]{:S(2)}, u32[]{:S(2)}) collective-permute-start(bf16[8,16,4096]{2,1,0:T(8,128)(2,1)S(1)} %get-tuple-element.48), channel_id=1, source_target_pairs={{0,1},{1,0},{2,3},{3,2},{4,5},{5,4},{6,7},{7,6},{8,9},{9,8},{10,11... | collective-permute-start | bytes 3145736 | tf_op jit(solution)/shard_map/ppermute | solution.py:48
  73.3 8.4 %collective-permute-start.18 = (bf16[4,16,2048]{2,1,0:T(8,128)(2,1)S(1)}, bf16[4,16,2048]{2,1,0:T(8,128)(2,1)S(1)}, u32[]{:S(2)}, u32[]{:S(2)}) collective-permute-start(bf16[4,16,2048]{2,1,0:T(8,128)(2,1)S(1)} %get-tuple-element.59), channel_id=1, source_target_pairs={{0,32},{32,0},{1,33},{33,1},{2,34},{34,2},{3,35},{35,3},{4,36},{36... | collective-permute-start | bytes 786440 | tf_op jit(solution)/shard_map/ppermute | solution.py:48
  74.0 11.3 %collective-permute-start.19 = (bf16[4,16,2048]{2,1,0:T(8,128)(2,1)S(1)}, bf16[4,16,2048]{2,1,0:T(8,128)(2,1)S(1)}, u32[]{:S(2)}, u32[]{:S(2)}) collective-permute-start(bf16[4,16,2048]{2,1,0:T(8,128)(2,1)S(1)} %get-tuple-element.60), channel_id=1, source_target_pairs={{0,38},{32,2},{2,32},{34,4},{4,34},{36,6},{6,36},{38,0},{1,39},{33... | collective-permute-start | bytes 786440 | tf_op jit(solution)/shard_map/ppermute | solution.py:55
  86.2 19.6 %all-to-all-start = ((bf16[4,16,4096]{2,1,0:T(8,128)(2,1)}), bf16[4,16,4096]{2,1,0:T(8,128)(2,1)}, u32[]{:S(2)}, u32[]{:S(2)}) async-start(bf16[4,16,4096]{2,1,0:T(8,128)(2,1)} %fusion), calls=%async_computation | async-start | bytes 1048576 | tf_op jit(solution)/shard_map/all_to_all | solution.py:365
  91.7 1.2 copy-start.10
  105.8 33.2 %copy-start.6 = (bf16[512,512]{1,0:T(8,128)(2,1)S(1)}, bf16[512,512]{1,0:T(8,128)(2,1)}, u32[]{:S(2)}) copy-start(bf16[512,512]{1,0:T(8,128)(2,1)} %copy-done.5) | copy-start | bytes 1572868
  105.8 33.2 %copy-start.8 = (bf16[512,512]{1,0:T(8,128)(2,1)S(1)}, bf16[512,512]{1,0:T(8,128)(2,1)}, u32[]{:S(2)}) copy-start(bf16[512,512]{1,0:T(8,128)(2,1)} %copy-done.7) | copy-start | bytes 1572868
  105.8 33.2 %copy-start.13 = (bf16[256,512]{1,0:T(8,128)(2,1)S(1)}, bf16[256,512]{1,0:T(8,128)(2,1)}, u32[]{:S(2)}) copy-start(bf16[256,512]{1,0:T(8,128)(2,1)} %copy-done.12) | copy-start | bytes 786436
  127.3 6.5 %collective-permute-start.21 = (bf16[4,16,2048]{2,1,0:T(8,128)(2,1)S(1)}, bf16[4,16,2048]{2,1,0:T(8,128)(2,1)S(1)}, u32[]{:S(2)}, u32[]{:S(2)}) collective-permute-start(bf16[4,16,2048]{2,1,0:T(8,128)(2,1)S(1)} %get-tuple-element.62), channel_id=1, source_target_pairs={{0,32},{32,0},{1,33},{33,1},{2,34},{34,2},{3,35},{35,3},{4,36},{36... | collective-permute-start | bytes 786440 | tf_op jit(solution)/shard_map/ppermute | solution.py:48
  127.4 10.0 %collective-permute-start.20 = (bf16[4,16,4096]{2,1,0:T(8,128)(2,1)S(1)}, bf16[4,16,4096]{2,1,0:T(8,128)(2,1)S(1)}, u32[]{:S(2)}, u32[]{:S(2)}) collective-permute-start(bf16[4,16,4096]{2,1,0:T(8,128)(2,1)S(1)} %all_to_all.15.q_ref), channel_id=1, source_target_pairs={{0,1},{1,0},{2,3},{3,2},{4,5},{5,4},{6,7},{7,6},{8,9},{9,8},{10,11... | collective-permute-start | bytes 1572872 | tf_op jit(solution)/shard_map/ppermute | solution.py:48
  127.5 9.9 %collective-permute-start.23 = (bf16[4,16,2048]{2,1,0:T(8,128)(2,1)S(1)}, bf16[4,16,2048]{2,1,0:T(8,128)(2,1)S(1)}, u32[]{:S(2)}, u32[]{:S(2)}) collective-permute-start(bf16[4,16,2048]{2,1,0:T(8,128)(2,1)S(1)} %get-tuple-element.61), channel_id=1, source_target_pairs={{0,38},{32,2},{2,32},{34,4},{4,34},{36,6},{6,36},{38,0},{1,39},{33... | collective-permute-start | bytes 786440 | tf_op jit(solution)/shard_map/ppermute | solution.py:55
  133.8 3.7 %collective-permute-start.22 = (bf16[4,16,2048]{2,1,0:T(8,128)(2,1)S(1)}, bf16[4,16,2048]{2,1,0:T(8,128)(2,1)S(1)}, u32[]{:S(2)}, u32[]{:S(2)}) collective-permute-start(bf16[4,16,2048]{2,1,0:T(8,128)(2,1)S(1)} %collective-permute-done.21.left_ref), channel_id=1, source_target_pairs={{0,1},{1,0},{2,3},{3,2},{4,5},{5,4},{6,7},{7,6},{8,9},{9,8},{10,11... | collective-permute-start | bytes 786440 | tf_op jit(solution)/shard_map/ppermute | solution.py:48
  137.5 1.5 collective-permute-start.24
  139.0 14.7 %copy-start.2 = (bf16[128,4096]{1,0:T(8,128)(2,1)S(1)}, bf16[128,4096]{1,0:T(8,128)(2,1)}, u32[]{:S(2)}) copy-start(bf16[128,4096]{1,0:T(8,128)(2,1)} %x_ref.1) | copy-start | bytes 3145732
  140.5 39.3 %copy-start.4 = (bf16[128,1024]{1,0:T(8,128)(2,1)S(1)}, bf16[128,1024]{1,0:T(8,128)(2,1)}, u32[]{:S(2)}) copy-start(bf16[128,1024]{1,0:T(8,128)(2,1)} %w_ref.1) | copy-start | bytes 786436
  140.5 1.2 collective-permute-start.25
  141.8 3.7 %collective-permute-start.26 = (f32[16,128]{1,0:T(8,128)S(1)}, f32[16,128]{1,0:T(8,128)S(1)}, u32[]{:S(2)}, u32[]{:S(2)}) collective-permute-start(f32[16,128]{1,0:T(8,128)S(1)} %slice_bitcast_fusion), channel_id=1, source_target_pairs={{0,32},{32,0},{1,33},{33,1},{2,34},{34,2},{3,35},{35,3},{4,36},{36... | collective-permute-start | bytes 24584 | tf_op jit(solution)/shard_map/ppermute | solution.py:48
  145.4 6.5 %collective-permute-start.27 = (f32[16,128]{1,0:T(8,128)S(1)}, f32[16,128]{1,0:T(8,128)S(1)}, u32[]{:S(2)}, u32[]{:S(2)}) collective-permute-start(f32[16,128]{1,0:T(8,128)S(1)} %fusion.1.t0_ref), channel_id=1, source_target_pairs={{0,2},{2,0},{4,6},{6,4},{1,3},{3,1},{5,7},{7,5},{8,10},{10,8},{12,... | collective-permute-start | bytes 24584 | tf_op jit(solution)/shard_map/ppermute | solution.py:286
  145.8 7.6 %collective-permute-start.28 = (f32[16,128]{1,0:T(8,128)S(1)}, f32[16,128]{1,0:T(8,128)S(1)}, u32[]{:S(2)}, u32[]{:S(2)}) collective-permute-start(f32[16,128]{1,0:T(8,128)S(1)} %fusion.1.t0_ref), channel_id=1, source_target_pairs={{0,4},{2,6},{4,0},{6,2},{1,5},{3,7},{5,1},{7,3},{8,12},{10,14},{12... | collective-permute-start | bytes 24584 | tf_op jit(solution)/shard_map/ppermute | solution.py:286
  148.0 5.8 %collective-permute-start.29 = (f32[16,128]{1,0:T(8,128)S(1)}, f32[16,128]{1,0:T(8,128)S(1)}, u32[]{:S(2)}, u32[]{:S(2)}) collective-permute-start(f32[16,128]{1,0:T(8,128)S(1)} %fusion.1.t0_ref), channel_id=1, source_target_pairs={{0,6},{2,4},{4,2},{6,0},{1,7},{3,5},{5,3},{7,1},{8,14},{10,12},{12... | collective-permute-start | bytes 24584 | tf_op jit(solution)/shard_map/ppermute | solution.py:286
  155.2 24.6 %all-to-all-start.2 = ((bf16[32,16,1152]{2,1,0:T(8,128)(2,1)}), bf16[32,16,1152]{2,1,0:T(8,128)(2,1)S(1)}, u32[]{:S(2)}, u32[]{:S(2)}) async-start(bf16[32,16,1152]{2,1,0:T(8,128)(2,1)} %get-tuple-element.53), calls=%async_computation.2 | async-start | bytes 2359296 | tf_op jit(solution)/shard_map/all_to_all | solution.py:399
  163.7 12.8 %collective-permute-start.30 = (f32[16,512]{1,0:T(8,128)S(1)}, f32[16,512]{1,0:T(8,128)S(1)}, u32[]{:S(2)}, u32[]{:S(2)}) collective-permute-start(f32[16,512]{1,0:T(8,128)S(1)} %get-tuple-element.56), channel_id=1, source_target_pairs={{0,32},{32,0},{1,33},{33,1},{2,34},{34,2},{3,35},{35,3},{4,36},{36... | collective-permute-start | bytes 98312 | tf_op jit(solution)/shard_map/ppermute | solution.py:48
  (2 other events, 1.5 us)

commit v9 on v8

--- a/solution.py
+++ b/solution.py
@@ -105,7 +105,7 @@
     b_own_ref[...] = b_ref[:, lanes(mine, HID)]
 
 
-def pack_kernel(tokens_ref, a_ref, after_ref, out_ref, p_ref):
+def pack_kernel(tokens_ref, a_ref, out_ref, p_ref):
     c = lax.axis_index("c")
     p = dot_nt(a_ref[...], tokens_ref[...]).astype(BF16)
     out_ref[:HALF] = tokens_ref[pl.ds(pl.multiple_of(c * HALF, HALF), HALF), :]
@@ -216,6 +216,14 @@
         back_ref[order] = dot_nt(b, hid_ref[...])
 
 
+def route_kernel(near_ref, left_ref, right_ref, mine_ref, s1_ref, s2_ref, s3_ref):
+    h = lax.axis_index("h")
+    for j, ref in enumerate((mine_ref, s1_ref, s2_ref, s3_ref)):
+        k = (h + j) % 4
+        ref[:, :SIDE] = (near_ref[k, :, :SIDE] + left_ref[k].astype(F32)).astype(ref.dtype)
+        ref[:, SIDE:] = (near_ref[k, :, SIDE:] + right_ref[k].astype(F32)).astype(ref.dtype)
+
+
 def down_kernel(t0_ref, t1_ref, t2_ref, t3_ref, x_ref, a_ref, up_ref, new_ref, wire_ref):
     rest = (t0_ref[...] + t1_ref[...]) + (t2_ref[...] + t3_ref[...])
     parts = []
@@ -300,23 +308,26 @@
         name="own",
     )
     b_oth = w_oth[2 * TOK :]
+    def line(own, oth, axis):
+        pairs = list(zip(ring(own, axis), ring(oth, axis)))
+        return jnp.where(
+            l == 0,
+            jnp.concatenate([block for o, t in pairs for block in (o, t)], axis=0),
+            jnp.concatenate([block for o, t in pairs for block in (t, o)], axis=0),
+        )
+
+    in_line = line(in_own, w_oth[:TOK], "x")
+    out_line = line(out_own, w_oth[TOK : 2 * TOK], "y")
+    late_tokens, in_line = lax.optimization_barrier((tokens, in_line))
     packed, p_own = call(
         pack_kernel,
         (shape(HALF + RANK, MODEL_WIDTH), shape(RANK, TOK)),
-        tokens, a,
-        after=[in_own],
+        late_tokens, a,
         name="pack",
     )
     tokens_oth = near_z(packed)
     tokens_oth_core = partner(tokens_oth, "c")
 
-    def joined(own, oth):
-        return jnp.where(
-            l == 0, jnp.concatenate([own, oth], axis=0), jnp.concatenate([oth, own], axis=0)
-        )
-
-    in_line = jnp.concatenate(ring(joined(in_own, w_oth[:TOK]), "x"), axis=0)
-    out_line = jnp.concatenate(ring(joined(out_own, w_oth[TOK : 2 * TOK]), "y"), axis=0)
     in_near = [in_line, shift(in_line, "y", 1), shift(in_line, "y", -1)]
     out_near = [out_line, shift(out_line, "x", 1), shift(out_line, "x", -1)]
 
@@ -361,9 +372,14 @@
     left = partner(away[:, :, :SIDE], "l")
     right = away[:, :, SIDE:]
     right = near_z(right)
-    summed = summed[:4] + jnp.concatenate([left, right], axis=2).astype(F32)
-    shares = lax.all_to_all(summed.astype(BF16), "h", 0, 0, tiled=True)
-    share = shares.astype(F32).sum(axis=0) * FF ** (-0.5)
+    mine, *steps = call(
+        route_kernel,
+        (shape(ROWS, MODEL_WIDTH, dtype=F32),) + (shape(ROWS, MODEL_WIDTH),) * 3,
+        summed[:4], left, right,
+        name="route",
+    )
+    steps = [shift(step, "h", j + 1).astype(F32) for j, step in enumerate(steps)]
+    share = ((mine + steps[0]) + (steps[1] + steps[2])) * FF ** (-0.5)
     grad_rows = ((share - my_targets.astype(F32)) / TOK).astype(BF16)
 
     q = lax.all_to_all(jnp.broadcast_to(grad_rows, (4, ROWS, MODEL_WIDTH)), "h", 0, 0, tiled=True)

time: 182 us -> 187 us (1.027)
  waiting for transfers between devices: 85.9 us -> 92.4 us
  starting transfers between devices: 56.3 us -> 60.2 us
  local copies, waits for them, and re-layouts: 5.63 us -> 3.19 us
  other arithmetic: 3.39 us -> 1.28 us
    ppermute x14 -> x23, waiting for transfers between devices: 19 us -> 44.2 us  [shift(): return lax.ppermute(value, axis, [(i, (i + by) % n) for i in range(n)])]
    ppermute x14 -> x23, starting transfers between devices: 19.2 us -> 34.8 us  [shift(): return lax.ppermute(value, axis, [(i, (i + by) % n) for i in range(n)])]
    ppermute x11, waiting for transfers between devices: 35.6 us -> 20.9 us  [partner(): return lax.ppermute(value, axis, [(0, 1), (1, 0)])]
    all_to_all x1 -> x0, waiting for transfers between devices: 12.8 us -> none  [shards(): shares = lax.all_to_all(summed.astype(BF16), 'h', 0, 0, tiled=True)]
    ppermute x3, waiting for transfers between devices: 13.9 us -> 20.8 us  [near_z(): lax.ppermute(value, Z, [(place(z), place(z + 1 if z % 2 else z - 1)) for...]
    all_to_all x1 -> x0, starting transfers between devices: 5.56 us -> none  [shards(): shares = lax.all_to_all(summed.astype(BF16), 'h', 0, 0, tiled=True)]
    ppermute x3, starting transfers between devices: 11.2 us -> 6.07 us  [near_z(): lax.ppermute(value, Z, [(place(z), place(z + 1 if z % 2 else z - 1)) for...]
    ppermute x3, waiting for transfers between devices: 1.83 us -> 3.9 us  [swap(): return lax.ppermute(value, 'h', [(i, i ^ mask) for i in range(4)])]
  transfers between devices with their start and end apart: 33 -> 41, of which waited for: 21 -> 26; matrix products, arithmetic and copies ran while one was open for 1% -> 1% of each run, Pallas kernels for 2% -> 2%
where the time goes in v9:
time: 187 us
  waiting for transfers between devices  92.4 us (49%)
  starting transfers between devices  60.2 us (32%)
  blocking collectives  19.7 us (11%)
  Pallas kernels  8.71 us (5%)
  local copies, waits for them, and re-layouts  3.19 us (2%)
    ppermute x23, waiting for transfers between devices, shift(): return lax.ppermute(value, axis, [(i, (i + by) % n) for i in range(n)])  44.2 us
    ppermute x23, starting transfers between devices, shift(): return lax.ppermute(value, axis, [(i, (i + by) % n) for i in range(n)])  34.8 us
    ppermute x11, waiting for transfers between devices, partner(): return lax.ppermute(value, axis, [(0, 1), (1, 0)])  20.9 us
    ppermute x3, waiting for transfers between devices, near_z(): lax.ppermute(value, Z, [(place(z), place(z + 1 if z % 2 else z - 1)) for...  20.8 us
    all_to_all x1, blocking collectives, shards(): lax.all_to_all(jnp.broadcast_to(grad_rows, (4, ROWS, MODEL_WIDTH)), 'h',...  19.7 us
    pallas_call x12, Pallas kernels, call(): pl.pallas_call(kernel, out_shape=out_shape, in_specs=[vmem] * len(args) +...  8.57 us
    all_to_all x1, starting transfers between devices, shards(): wires = lax.all_to_all(wire, REP, 0, 0, tiled=True)  6.7 us
    ppermute x3, starting transfers between devices, swap(): return lax.ppermute(value, 'h', [(i, i ^ mask) for i in range(4)])  6.5 us
  transfers between devices with their start and end apart: 41, of which 26 were waited for; matrix products, arithmetic and copies ran while one was open for 1% of the time, Pallas kernels for 2%

profile of v9, /device:TPU:2, one launch (start us, length us, event | category | flops | bytes accessed | tf_op | source)
XLA Modules:
  0.0 186.6 jit_solution(9549471507725302595)
XLA Ops:
  3.4 2.0 %collective-permute-start = (bf16[272,512]{1,0:T(8,128)(2,1)S(1)}, bf16[272,512]{1,0:T(8,128)(2,1)S(1)}, u32[]{:S(2)}, u32[]{:S(2)}) collective-permute-start(bf16[272,512]{1,0:T(8,128)(2,1)S(1)} %send.1.send_ref), channel_id=1, source_target_pairs={{0,32},{32,0},{1,33},{33,1},{2,34},{34,2},{3,35},{35,3},{4,36},{36... | collective-permute-start | bytes 835592 | tf_op jit(solution)/shard_map/ppermute | solution.py:48
  6.1 1.5 collective-permute-start.1
  7.6 3.0 %collective-permute-start.15 = (bf16[128,512]{1,0:T(8,128)(2,1)S(1)}, bf16[128,512]{1,0:T(8,128)(2,1)S(1)}, u32[]{:S(2)}, u32[]{:S(2)}) collective-permute-start(bf16[128,512]{1,0:T(8,128)(2,1)S(1)} %get-tuple-element.52), channel_id=1, source_target_pairs={{0,192},{64,0},{128,64},{192,128},{1,193},{65,1},{129,65},{193,129... | collective-permute-start | bytes 393224 | tf_op jit(solution)/shard_map/ppermute | solution.py:44
  10.6 1.4 collective-permute-done
  12.1 1.7 collective-permute-start.14
  13.8 1.6 collective-permute-start.2
  15.4 1.7 collective-permute-start.13
  17.0 1.9 %collective-permute-done.14 = bf16[128,512]{1,0:T(8,128)(2,1)S(1)} collective-permute-done((bf16[128,512]{1,0:T(8,128)(2,1)S(1)}, bf16[128,512]{1,0:T(8,128)(2,1)S(1)}, u32[]{:S(2)}, u32[]{:S(2)}) %collective-permute-start.14) | collective-permute-done | bytes 131104 | tf_op jit(solution)/shard_map/ppermute | solution.py:44
  18.9 1.8 collective-permute-start.5
  20.7 2.0 %collective-permute-start.16 = (bf16[128,512]{1,0:T(8,128)(2,1)S(1)}, bf16[128,512]{1,0:T(8,128)(2,1)S(1)}, u32[]{:S(2)}, u32[]{:S(2)}) collective-permute-start(bf16[128,512]{1,0:T(8,128)(2,1)S(1)} %get-tuple-element.79), channel_id=1, source_target_pairs={{0,192},{64,0},{128,64},{192,128},{1,193},{65,1},{129,65},{193,129... | collective-permute-start | bytes 393224 | tf_op jit(solution)/shard_map/ppermute | solution.py:44
  23.5 2.3 %collective-permute-done.16 = bf16[128,512]{1,0:T(8,128)(2,1)S(1)} collective-permute-done((bf16[128,512]{1,0:T(8,128)(2,1)S(1)}, bf16[128,512]{1,0:T(8,128)(2,1)S(1)}, u32[]{:S(2)}, u32[]{:S(2)}) %collective-permute-start.16) | collective-permute-done | bytes 131104 | tf_op jit(solution)/shard_map/ppermute | solution.py:44
  26.4 1.4 collective-permute-done.4
  28.1 1.6 collective-permute-start.6
  29.8 3.4 %collective-permute-done.6 = bf16[128,512]{1,0:T(8,128)(2,1)S(1)} collective-permute-done((bf16[128,512]{1,0:T(8,128)(2,1)S(1)}, bf16[128,512]{1,0:T(8,128)(2,1)S(1)}, u32[]{:S(2)}, u32[]{:S(2)}) %collective-permute-start.6) | collective-permute-done | bytes 131104 | tf_op jit(solution)/shard_map/ppermute | solution.py:44
  33.7 5.9 %collective-permute-start.7 = (bf16[80,4096]{1,0:T(8,128)(2,1)S(1)}, bf16[80,4096]{1,0:T(8,128)(2,1)S(1)}, u32[]{:S(2)}, u32[]{:S(2)}) collective-permute-start(bf16[80,4096]{1,0:T(8,128)(2,1)S(1)} %get-tuple-element.38), channel_id=1, source_target_pairs={{0,38},{32,2},{2,32},{34,4},{4,34},{36,6},{6,36},{38,0},{1,39},{33... | collective-permute-start | bytes 1966088 | tf_op jit(solution)/shard_map/ppermute | solution.py:55
  39.8 2.6 %collective-permute-start.20 = (bf16[1024,512]{1,0:T(8,128)(2,1)S(1)}, bf16[1024,512]{1,0:T(8,128)(2,1)S(1)}, u32[]{:S(2)}, u32[]{:S(2)}) collective-permute-start(bf16[1024,512]{1,0:T(8,128)(2,1)S(1)} %broadcast_select_fusion.refs_0_), channel_id=1, source_target_pairs={{0,24},{8,0},{16,8},{24,16},{1,25},{9,1},{17,9},{25,17},{2,26},{10... | collective-permute-start | bytes 3145736 | tf_op jit(solution)/shard_map/ppermute | solution.py:44
  42.4 2.6 %collective-permute-start.10 = (bf16[1024,512]{1,0:T(8,128)(2,1)S(1)}, bf16[1024,512]{1,0:T(8,128)(2,1)S(1)}, u32[]{:S(2)}, u32[]{:S(2)}) collective-permute-start(bf16[1024,512]{1,0:T(8,128)(2,1)S(1)} %broadcast_select_fusion.1.refs_0_), channel_id=1, source_target_pairs={{0,192},{64,0},{128,64},{192,128},{1,193},{65,1},{129,65},{193,129... | collective-permute-start | bytes 3145736 | tf_op jit(solution)/shard_map/ppermute | solution.py:44
  45.1 4.1 %collective-permute-done.7.oth_ref = bf16[80,4096]{1,0:T(8,128)(2,1)S(1)} collective-permute-done((bf16[80,4096]{1,0:T(8,128)(2,1)S(1)}, bf16[80,4096]{1,0:T(8,128)(2,1)S(1)}, u32[]{:S(2)}, u32[]{:S(2)}) %collective-permute-start.7) | collective-permute-done | bytes 655392 | tf_op jit(solution)/shard_map/ppermute | solution.py:55
  49.2 10.2 %collective-permute-done.20.above_ref.refs_2_ = bf16[1024,512]{1,0:T(8,128)(2,1)S(1)} collective-permute-done((bf16[1024,512]{1,0:T(8,128)(2,1)S(1)}, bf16[1024,512]{1,0:T(8,128)(2,1)S(1)}, u32[]{:S(2)}, u32[]{:S(2)}) %collective-permute-start.20) | collective-permute-done | bytes 1048608 | tf_op jit(solution)/shard_map/ppermute | solution.py:44
  59.3 1.5 collective-permute-done.19.below_ref.refs_1_
  62.1 6.1 %collective-permute-done.9.refs_1_.below_ref = bf16[1024,512]{1,0:T(8,128)(2,1)S(1)} collective-permute-done((bf16[1024,512]{1,0:T(8,128)(2,1)S(1)}, bf16[1024,512]{1,0:T(8,128)(2,1)S(1)}, u32[]{:S(2)}, u32[]{:S(2)}) %collective-permute-start.9) | collective-permute-done | bytes 1048608 | tf_op jit(solution)/shard_map/ppermute | solution.py:44
  68.4 3.2 %collective-permute-start.12 = (bf16[512,512]{1,0:T(8,128)(2,1)S(1)}, bf16[512,512]{1,0:T(8,128)(2,1)S(1)}, u32[]{:S(2)}, u32[]{:S(2)}) collective-permute-start(bf16[512,512]{1,0:T(8,128)(2,1)S(1)} %get-tuple-element.50), channel_id=1, source_target_pairs={{0,192},{64,0},{128,64},{192,128},{1,193},{65,1},{129,65},{193,129... | collective-permute-start | bytes 1572872 | tf_op jit(solution)/shard_map/ppermute | solution.py:44
  71.6 1.8 collective-permute-start.21
  74.7 4.1 %collective-permute-done.11.low_ref = bf16[512,512]{1,0:T(8,128)(2,1)S(1)} collective-permute-done((bf16[512,512]{1,0:T(8,128)(2,1)S(1)}, bf16[512,512]{1,0:T(8,128)(2,1)S(1)}, u32[]{:S(2)}, u32[]{:S(2)}) %collective-permute-start.11) | collective-permute-done | bytes 524320 | tf_op jit(solution)/shard_map/ppermute | solution.py:44
  79.2 1.6 collective-permute-done.21.refs_3_
  80.8 2.6 %collective-permute-done.22.refs_4_ = bf16[512,512]{1,0:T(8,128)(2,1)S(1)} collective-permute-done((bf16[512,512]{1,0:T(8,128)(2,1)S(1)}, bf16[512,512]{1,0:T(8,128)(2,1)S(1)}, u32[]{:S(2)}, u32[]{:S(2)}) %collective-permute-start.22) | collective-permute-done | bytes 524320 | tf_op jit(solution)/shard_map/ppermute | solution.py:44
  83.4 1.3 output.1
  84.8 2.6 %collective-permute-done.23 = bf16[8,16,4096]{2,1,0:T(8,128)(2,1)S(1)} collective-permute-done((bf16[8,16,4096]{2,1,0:T(8,128)(2,1)S(1)}, bf16[8,16,4096]{2,1,0:T(8,128)(2,1)S(1)}, u32[]{:S(2)}, u32[]{:S(2)}) %collective-permute-start.23) | collective-permute-done | bytes 1048608 | tf_op jit(solution)/shard_map/ppermute | solution.py:48
  88.1 9.4 %collective-permute-done.25.right_ref = bf16[4,16,2048]{2,1,0:T(8,128)(2,1)S(1)} collective-permute-done((bf16[4,16,2048]{2,1,0:T(8,128)(2,1)S(1)}, bf16[4,16,2048]{2,1,0:T(8,128)(2,1)S(1)}, u32[]{:S(2)}, u32[]{:S(2)}) %collective-permute-start.25) | collective-permute-done | bytes 262176 | tf_op jit(solution)/shard_map/ppermute | solution.py:55
  97.7 3.8 %collective-permute-start.27 = (bf16[16,4096]{1,0:T(8,128)(2,1)S(1)}, bf16[16,4096]{1,0:T(8,128)(2,1)S(1)}, u32[]{:S(2)}, u32[]{:S(2)}) collective-permute-start(bf16[16,4096]{1,0:T(8,128)(2,1)S(1)} %get-tuple-element.59), channel_id=1, source_target_pairs={{0,4},{2,6},{4,0},{6,2},{1,5},{3,7},{5,1},{7,3},{8,12},{10,14},{12... | collective-permute-start | bytes 393224 | tf_op jit(solution)/shard_map/ppermute | solution.py:44
  101.5 3.4 %collective-permute-start.28 = (bf16[16,4096]{1,0:T(8,128)(2,1)S(1)}, bf16[16,4096]{1,0:T(8,128)(2,1)S(1)}, u32[]{:S(2)}, u32[]{:S(2)}) collective-permute-start(bf16[16,4096]{1,0:T(8,128)(2,1)S(1)} %get-tuple-element.60), channel_id=1, source_target_pairs={{0,6},{2,0},{4,2},{6,4},{1,7},{3,1},{5,3},{7,5},{8,14},{10,8},{12,... | collective-permute-start | bytes 393224 | tf_op jit(solution)/shard_map/ppermute | solution.py:44
  105.0 6.4 %collective-permute-done.26 = bf16[16,4096]{1,0:T(8,128)(2,1)S(1)} collective-permute-done((bf16[16,4096]{1,0:T(8,128)(2,1)S(1)}, bf16[16,4096]{1,0:T(8,128)(2,1)S(1)}, u32[]{:S(2)}, u32[]{:S(2)}) %collective-permute-start.26) | collective-permute-done | bytes 131104 | tf_op jit(solution)/shard_map/ppermute | solution.py:44
  111.3 2.7 %collective-permute-done.28 = bf16[16,4096]{1,0:T(8,128)(2,1)S(1)} collective-permute-done((bf16[16,4096]{1,0:T(8,128)(2,1)S(1)}, bf16[16,4096]{1,0:T(8,128)(2,1)S(1)}, u32[]{:S(2)}, u32[]{:S(2)}) %collective-permute-start.28) | collective-permute-done | bytes 131104 | tf_op jit(solution)/shard_map/ppermute | solution.py:44
  114.1 19.7 %all_to_all.10.q_ref = bf16[4,16,4096]{2,1,0:T(8,128)(2,1)S(1)} all-to-all(bf16[4,16,4096]{2,1,0:T(8,128)(2,1)S(1)} %broadcast_in_dim.7), channel_id=1, replica_groups=mesh['y'=4,'l'=2,'x'=4,'h'=4,'c'=2] {'h'}, dimensions={0} | all-to-all | bytes 1048576 | tf_op jit(solution)/shard_map/all_to_all | solution.py:385
  135.1 7.3 %collective-permute-done.32.right_ref = bf16[4,16,2048]{2,1,0:T(8,128)(2,1)S(1)} collective-permute-done((bf16[4,16,2048]{2,1,0:T(8,128)(2,1)S(1)}, bf16[4,16,2048]{2,1,0:T(8,128)(2,1)S(1)}, u32[]{:S(2)}, u32[]{:S(2)}) %collective-permute-start.32) | collective-permute-done | bytes 262176 | tf_op jit(solution)/shard_map/ppermute | solution.py:55
  144.4 1.5 backward.1
  146.0 1.0 collective-permute-done.34
  148.1 2.6 %collective-permute-done.35 = f32[16,128]{1,0:T(8,128)S(1)} collective-permute-done((f32[16,128]{1,0:T(8,128)S(1)}, f32[16,128]{1,0:T(8,128)S(1)}, u32[]{:S(2)}, u32[]{:S(2)}) %collective-permute-start.35) | collective-permute-done | bytes 8224 | tf_op jit(solution)/shard_map/ppermute | solution.py:48
  150.8 2.8 %collective-permute-start.38 = (f32[16,128]{1,0:T(8,128)S(1)}, f32[16,128]{1,0:T(8,128)S(1)}, u32[]{:S(2)}, u32[]{:S(2)}) collective-permute-start(f32[16,128]{1,0:T(8,128)S(1)} %fusion.t0_ref), channel_id=1, source_target_pairs={{0,6},{2,4},{4,2},{6,0},{1,7},{3,5},{5,3},{7,1},{8,14},{10,12},{12... | collective-permute-start | bytes 24584 | tf_op jit(solution)/shard_map/ppermute | solution.py:294
  153.6 1.4 collective-permute-start.37
  155.0 2.2 %collective-permute-start.36 = (f32[16,128]{1,0:T(8,128)S(1)}, f32[16,128]{1,0:T(8,128)S(1)}, u32[]{:S(2)}, u32[]{:S(2)}) collective-permute-start(f32[16,128]{1,0:T(8,128)S(1)} %fusion.t0_ref), channel_id=1, source_target_pairs={{0,2},{2,0},{4,6},{6,4},{1,3},{3,1},{5,7},{7,5},{8,10},{10,8},{12,... | collective-permute-start | bytes 24584 | tf_op jit(solution)/shard_map/ppermute | solution.py:294
  157.3 3.9 %collective-permute-done.37.t2_ref = f32[16,128]{1,0:T(8,128)S(1)} collective-permute-done((f32[16,128]{1,0:T(8,128)S(1)}, f32[16,128]{1,0:T(8,128)S(1)}, u32[]{:S(2)}, u32[]{:S(2)}) %collective-permute-start.37) | collective-permute-done | bytes 8224 | tf_op jit(solution)/shard_map/ppermute | solution.py:294
  161.2 1.4 down.1
  162.6 6.7 %all-to-all-start.1 = ((bf16[32,16,1152]{2,1,0:T(8,128)(2,1)}), bf16[32,16,1152]{2,1,0:T(8,128)(2,1)S(1)}, u32[]{:S(2)}, u32[]{:S(2)}) async-start(bf16[32,16,1152]{2,1,0:T(8,128)(2,1)} %get-tuple-element.65), calls=%async_computation.1 | async-start | bytes 2359296 | tf_op jit(solution)/shard_map/all_to_all | solution.py:415
  169.3 1.6 collective-permute-start.39
  170.9 11.3 %collective-permute-done.39 = f32[16,512]{1,0:T(8,128)S(1)} collective-permute-done((f32[16,512]{1,0:T(8,128)S(1)}, f32[16,512]{1,0:T(8,128)S(1)}, u32[]{:S(2)}, u32[]{:S(2)}) %collective-permute-start.39) | collective-permute-done | bytes 32800 | tf_op jit(solution)/shard_map/ppermute | solution.py:48
  182.8 2.7 %all-to-all-done.1.wire_ref = bf16[32,16,1152]{2,1,0:T(8,128)(2,1)S(1)} async-done(((bf16[32,16,1152]{2,1,0:T(8,128)(2,1)}), bf16[32,16,1152]{2,1,0:T(8,128)(2,1)S(1)}, u32[]{:S(2)}, u32[]{:S(2)}) %all-to-all-start.1) | async-done | bytes 1179680 | tf_op jit(solution)/shard_map/all_to_all | solution.py:415
  185.4 1.1 merge.1
  (98 shorter events, 15.2 us)
Async XLA Ops:
  0.6 1.0 copy-start.1
  1.6 0.9 copy-start.3
  2.5 0.8 copy-start.6
  3.4 8.7 %collective-permute-start = (bf16[272,512]{1,0:T(8,128)(2,1)S(1)}, bf16[272,512]{1,0:T(8,128)(2,1)S(1)}, u32[]{:S(2)}, u32[]{:S(2)}) collective-permute-start(bf16[272,512]{1,0:T(8,128)(2,1)S(1)} %send.1.send_ref), channel_id=1, source_target_pairs={{0,32},{32,0},{1,33},{33,1},{2,34},{34,2},{3,35},{35,3},{4,36},{36... | collective-permute-start | bytes 835592 | tf_op jit(solution)/shard_map/ppermute | solution.py:48
  5.5 22.6 %collective-permute-start.3 = (bf16[128,512]{1,0:T(8,128)(2,1)S(1)}, bf16[128,512]{1,0:T(8,128)(2,1)S(1)}, u32[]{:S(2)}, u32[]{:S(2)}) collective-permute-start(bf16[128,512]{1,0:T(8,128)(2,1)S(1)} %get-tuple-element.36), channel_id=1, source_target_pairs={{0,24},{8,0},{16,8},{24,16},{1,25},{9,1},{17,9},{25,17},{2,26},{10... | collective-permute-start | bytes 393224 | tf_op jit(solution)/shard_map/ppermute | solution.py:44
  6.1 9.3 %collective-permute-start.1 = (bf16[128,512]{1,0:T(8,128)(2,1)S(1)}, bf16[128,512]{1,0:T(8,128)(2,1)S(1)}, u32[]{:S(2)}, u32[]{:S(2)}) collective-permute-start(bf16[128,512]{1,0:T(8,128)(2,1)S(1)} %get-tuple-element.36), channel_id=1, source_target_pairs={{0,8},{8,16},{16,24},{24,0},{1,9},{9,17},{17,25},{25,1},{2,10},{10... | collective-permute-start | bytes 393224 | tf_op jit(solution)/shard_map/ppermute | solution.py:44
  7.6 22.1 %collective-permute-start.15 = (bf16[128,512]{1,0:T(8,128)(2,1)S(1)}, bf16[128,512]{1,0:T(8,128)(2,1)S(1)}, u32[]{:S(2)}, u32[]{:S(2)}) collective-permute-start(bf16[128,512]{1,0:T(8,128)(2,1)S(1)} %get-tuple-element.52), channel_id=1, source_target_pairs={{0,192},{64,0},{128,64},{192,128},{1,193},{65,1},{129,65},{193,129... | collective-permute-start | bytes 393224 | tf_op jit(solution)/shard_map/ppermute | solution.py:44
  12.1 6.8 %collective-permute-start.14 = (bf16[128,512]{1,0:T(8,128)(2,1)S(1)}, bf16[128,512]{1,0:T(8,128)(2,1)S(1)}, u32[]{:S(2)}, u32[]{:S(2)}) collective-permute-start(bf16[128,512]{1,0:T(8,128)(2,1)S(1)} %get-tuple-element.79), channel_id=1, source_target_pairs={{0,64},{64,128},{128,192},{192,0},{1,65},{65,129},{129,193},{193,1... | collective-permute-start | bytes 393224 | tf_op jit(solution)/shard_map/ppermute | solution.py:44
  13.8 7.0 %collective-permute-start.2 = (bf16[128,512]{1,0:T(8,128)(2,1)S(1)}, bf16[128,512]{1,0:T(8,128)(2,1)S(1)}, u32[]{:S(2)}, u32[]{:S(2)}) collective-permute-start(bf16[128,512]{1,0:T(8,128)(2,1)S(1)} %get-tuple-element.80), channel_id=1, source_target_pairs={{0,8},{8,16},{16,24},{24,0},{1,9},{9,17},{17,25},{25,1},{2,10},{10... | collective-permute-start | bytes 393224 | tf_op jit(solution)/shard_map/ppermute | solution.py:44
  15.4 7.4 %collective-permute-start.13 = (bf16[128,512]{1,0:T(8,128)(2,1)S(1)}, bf16[128,512]{1,0:T(8,128)(2,1)S(1)}, u32[]{:S(2)}, u32[]{:S(2)}) collective-permute-start(bf16[128,512]{1,0:T(8,128)(2,1)S(1)} %get-tuple-element.52), channel_id=1, source_target_pairs={{0,64},{64,128},{128,192},{192,0},{1,65},{65,129},{129,193},{193,1... | collective-permute-start | bytes 393224 | tf_op jit(solution)/shard_map/ppermute | solution.py:44
  18.9 14.3 %collective-permute-start.5 = (bf16[128,512]{1,0:T(8,128)(2,1)S(1)}, bf16[128,512]{1,0:T(8,128)(2,1)S(1)}, u32[]{:S(2)}, u32[]{:S(2)}) collective-permute-start(bf16[128,512]{1,0:T(8,128)(2,1)S(1)} %collective-permute-done.1), channel_id=1, source_target_pairs={{0,8},{8,16},{16,24},{24,0},{1,9},{9,17},{17,25},{25,1},{2,10},{10... | collective-permute-start | bytes 393224 | tf_op jit(solution)/shard_map/ppermute | solution.py:44
  20.7 5.0 %collective-permute-start.16 = (bf16[128,512]{1,0:T(8,128)(2,1)S(1)}, bf16[128,512]{1,0:T(8,128)(2,1)S(1)}, u32[]{:S(2)}, u32[]{:S(2)}) collective-permute-start(bf16[128,512]{1,0:T(8,128)(2,1)S(1)} %get-tuple-element.79), channel_id=1, source_target_pairs={{0,192},{64,0},{128,64},{192,128},{1,193},{65,1},{129,65},{193,129... | collective-permute-start | bytes 393224 | tf_op jit(solution)/shard_map/ppermute | solution.py:44
  22.8 5.0 %collective-permute-start.4 = (bf16[128,512]{1,0:T(8,128)(2,1)S(1)}, bf16[128,512]{1,0:T(8,128)(2,1)S(1)}, u32[]{:S(2)}, u32[]{:S(2)}) collective-permute-start(bf16[128,512]{1,0:T(8,128)(2,1)S(1)} %get-tuple-element.80), channel_id=1, source_target_pairs={{0,24},{8,0},{16,8},{24,16},{1,25},{9,1},{17,9},{25,17},{2,26},{10... | collective-permute-start | bytes 393224 | tf_op jit(solution)/shard_map/ppermute | solution.py:44
  25.8 13.8 %collective-permute-start.17 = (bf16[128,512]{1,0:T(8,128)(2,1)S(1)}, bf16[128,512]{1,0:T(8,128)(2,1)S(1)}, u32[]{:S(2)}, u32[]{:S(2)}) collective-permute-start(bf16[128,512]{1,0:T(8,128)(2,1)S(1)} %collective-permute-done.13), channel_id=1, source_target_pairs={{0,64},{64,128},{128,192},{192,0},{1,65},{65,129},{129,193},{193,1... | collective-permute-start | bytes 393224 | tf_op jit(solution)/shard_map/ppermute | solution.py:44
  27.9 11.8 %collective-permute-start.18 = (bf16[128,512]{1,0:T(8,128)(2,1)S(1)}, bf16[128,512]{1,0:T(8,128)(2,1)S(1)}, u32[]{:S(2)}, u32[]{:S(2)}) collective-permute-start(bf16[128,512]{1,0:T(8,128)(2,1)S(1)} %collective-permute-done.14), channel_id=1, source_target_pairs={{0,64},{64,128},{128,192},{192,0},{1,65},{65,129},{129,193},{193,1... | collective-permute-start | bytes 393224 | tf_op jit(solution)/shard_map/ppermute | solution.py:44
  28.1 5.0 %collective-permute-start.6 = (bf16[128,512]{1,0:T(8,128)(2,1)S(1)}, bf16[128,512]{1,0:T(8,128)(2,1)S(1)}, u32[]{:S(2)}, u32[]{:S(2)}) collective-permute-start(bf16[128,512]{1,0:T(8,128)(2,1)S(1)} %collective-permute-done.2), channel_id=1, source_target_pairs={{0,8},{8,16},{16,24},{24,0},{1,9},{9,17},{17,25},{25,1},{2,10},{10... | collective-permute-start | bytes 393224 | tf_op jit(solution)/shard_map/ppermute | solution.py:44
  29.8 3.6 %copy-start = (bf16[128,4096]{1,0:T(8,128)(2,1)S(1)}, bf16[128,4096]{1,0:T(8,128)(2,1)}, u32[]{:S(2)}) copy-start(bf16[128,4096]{1,0:T(8,128)(2,1)} %x_ref.1) | copy-start | bytes 3145732
  29.8 3.6 %copy-start.5 = (bf16[1,16,4096]{2,1,0:T(8,128)(2,1)S(1)}, bf16[1,16,4096]{2,1,0:T(8,128)(2,1)}, u32[]{:S(2)}) copy-start(bf16[1,16,4096]{2,1,0:T(8,128)(2,1)} %param.10) | copy-start | bytes 393220
  33.7 15.4 %collective-permute-start.7 = (bf16[80,4096]{1,0:T(8,128)(2,1)S(1)}, bf16[80,4096]{1,0:T(8,128)(2,1)S(1)}, u32[]{:S(2)}, u32[]{:S(2)}) collective-permute-start(bf16[80,4096]{1,0:T(8,128)(2,1)S(1)} %get-tuple-element.38), channel_id=1, source_target_pairs={{0,38},{32,2},{2,32},{34,4},{4,34},{36,6},{6,36},{38,0},{1,39},{33... | collective-permute-start | bytes 1966088 | tf_op jit(solution)/shard_map/ppermute | solution.py:55
  39.8 19.5 %collective-permute-start.20 = (bf16[1024,512]{1,0:T(8,128)(2,1)S(1)}, bf16[1024,512]{1,0:T(8,128)(2,1)S(1)}, u32[]{:S(2)}, u32[]{:S(2)}) collective-permute-start(bf16[1024,512]{1,0:T(8,128)(2,1)S(1)} %broadcast_select_fusion.refs_0_), channel_id=1, source_target_pairs={{0,24},{8,0},{16,8},{24,16},{1,25},{9,1},{17,9},{25,17},{2,26},{10... | collective-permute-start | bytes 3145736 | tf_op jit(solution)/shard_map/ppermute | solution.py:44
  42.4 18.5 %collective-permute-start.19 = (bf16[1024,512]{1,0:T(8,128)(2,1)S(1)}, bf16[1024,512]{1,0:T(8,128)(2,1)S(1)}, u32[]{:S(2)}, u32[]{:S(2)}) collective-permute-start(bf16[1024,512]{1,0:T(8,128)(2,1)S(1)} %broadcast_select_fusion.refs_0_), channel_id=1, source_target_pairs={{0,8},{8,16},{16,24},{24,0},{1,9},{9,17},{17,25},{25,1},{2,10},{10... | collective-permute-start | bytes 3145736 | tf_op jit(solution)/shard_map/ppermute | solution.py:44
  42.4 19.7 %collective-permute-start.10 = (bf16[1024,512]{1,0:T(8,128)(2,1)S(1)}, bf16[1024,512]{1,0:T(8,128)(2,1)S(1)}, u32[]{:S(2)}, u32[]{:S(2)}) collective-permute-start(bf16[1024,512]{1,0:T(8,128)(2,1)S(1)} %broadcast_select_fusion.1.refs_0_), channel_id=1, source_target_pairs={{0,192},{64,0},{128,64},{192,128},{1,193},{65,1},{129,65},{193,129... | collective-permute-start | bytes 3145736 | tf_op jit(solution)/shard_map/ppermute | solution.py:44
  45.0 23.2 %collective-permute-start.9 = (bf16[1024,512]{1,0:T(8,128)(2,1)S(1)}, bf16[1024,512]{1,0:T(8,128)(2,1)S(1)}, u32[]{:S(2)}, u32[]{:S(2)}) collective-permute-start(bf16[1024,512]{1,0:T(8,128)(2,1)S(1)} %broadcast_select_fusion.1.refs_0_), channel_id=1, source_target_pairs={{0,64},{64,128},{128,192},{192,0},{1,65},{65,129},{129,193},{193,1... | collective-permute-start | bytes 3145736 | tf_op jit(solution)/shard_map/ppermute | solution.py:44
  49.2 11.8 %collective-permute-start.8 = (bf16[80,4096]{1,0:T(8,128)(2,1)S(1)}, bf16[80,4096]{1,0:T(8,128)(2,1)S(1)}, u32[]{:S(2)}, u32[]{:S(2)}) collective-permute-start(bf16[80,4096]{1,0:T(8,128)(2,1)S(1)} %collective-permute-done.7.oth_ref), channel_id=1, source_target_pairs={{0,1},{1,0},{2,3},{3,2},{4,5},{5,4},{6,7},{7,6},{8,9},{9,8},{10,11... | collective-permute-start | bytes 1966088 | tf_op jit(solution)/shard_map/ppermute | solution.py:48
  68.3 10.5 %collective-permute-start.11 = (bf16[512,512]{1,0:T(8,128)(2,1)S(1)}, bf16[512,512]{1,0:T(8,128)(2,1)S(1)}, u32[]{:S(2)}, u32[]{:S(2)}) collective-permute-start(bf16[512,512]{1,0:T(8,128)(2,1)S(1)} %get-tuple-element.49), channel_id=1, source_target_pairs={{0,64},{64,128},{128,192},{192,0},{1,65},{65,129},{129,193},{193,1... | collective-permute-start | bytes 1572872 | tf_op jit(solution)/shard_map/ppermute | solution.py:44
  68.4 10.4 %collective-permute-start.12 = (bf16[512,512]{1,0:T(8,128)(2,1)S(1)}, bf16[512,512]{1,0:T(8,128)(2,1)S(1)}, u32[]{:S(2)}, u32[]{:S(2)}) collective-permute-start(bf16[512,512]{1,0:T(8,128)(2,1)S(1)} %get-tuple-element.50), channel_id=1, source_target_pairs={{0,192},{64,0},{128,64},{192,128},{1,193},{65,1},{129,65},{193,129... | collective-permute-start | bytes 1572872 | tf_op jit(solution)/shard_map/ppermute | solution.py:44
  71.6 9.2 %collective-permute-start.21 = (bf16[512,512]{1,0:T(8,128)(2,1)S(1)}, bf16[512,512]{1,0:T(8,128)(2,1)S(1)}, u32[]{:S(2)}, u32[]{:S(2)}) collective-permute-start(bf16[512,512]{1,0:T(8,128)(2,1)S(1)} %get-tuple-element.53), channel_id=1, source_target_pairs={{0,8},{8,16},{16,24},{24,0},{1,9},{9,17},{17,25},{25,1},{2,10},{10... | collective-permute-start | bytes 1572872 | tf_op jit(solution)/shard_map/ppermute | solution.py:44
  73.4 10.1 %collective-permute-start.22 = (bf16[512,512]{1,0:T(8,128)(2,1)S(1)}, bf16[512,512]{1,0:T(8,128)(2,1)S(1)}, u32[]{:S(2)}, u32[]{:S(2)}) collective-permute-start(bf16[512,512]{1,0:T(8,128)(2,1)S(1)} %get-tuple-element.54), channel_id=1, source_target_pairs={{0,24},{8,0},{16,8},{24,16},{1,25},{9,1},{17,9},{25,17},{2,26},{10... | collective-permute-start | bytes 1572872 | tf_op jit(solution)/shard_map/ppermute | solution.py:44
  84.7 2.7 %collective-permute-start.23 = (bf16[8,16,4096]{2,1,0:T(8,128)(2,1)S(1)}, bf16[8,16,4096]{2,1,0:T(8,128)(2,1)S(1)}, u32[]{:S(2)}, u32[]{:S(2)}) collective-permute-start(bf16[8,16,4096]{2,1,0:T(8,128)(2,1)S(1)} %get-tuple-element.56), channel_id=1, source_target_pairs={{0,1},{1,0},{2,3},{3,2},{4,5},{5,4},{6,7},{7,6},{8,9},{9,8},{10,11... | collective-permute-start | bytes 3145736 | tf_op jit(solution)/shard_map/ppermute | solution.py:48
  87.9 17.1 %copy-start.4 = (bf16[128,4096]{1,0:T(8,128)(2,1)S(1)}, bf16[128,4096]{1,0:T(8,128)(2,1)}, u32[]{:S(2)}) copy-start(bf16[128,4096]{1,0:T(8,128)(2,1)} %targets_ref.1) | copy-start | bytes 3145732
  87.9 9.6 %collective-permute-start.25 = (bf16[4,16,2048]{2,1,0:T(8,128)(2,1)S(1)}, bf16[4,16,2048]{2,1,0:T(8,128)(2,1)S(1)}, u32[]{:S(2)}, u32[]{:S(2)}) collective-permute-start(bf16[4,16,2048]{2,1,0:T(8,128)(2,1)S(1)} %get-tuple-element.71), channel_id=1, source_target_pairs={{0,38},{32,2},{2,32},{34,4},{4,34},{36,6},{6,36},{38,0},{1,39},{33... | collective-permute-start | bytes 786440 | tf_op jit(solution)/shard_map/ppermute | solution.py:55
  88.0 9.5 %collective-permute-start.24 = (bf16[4,16,2048]{2,1,0:T(8,128)(2,1)S(1)}, bf16[4,16,2048]{2,1,0:T(8,128)(2,1)S(1)}, u32[]{:S(2)}, u32[]{:S(2)}) collective-permute-start(bf16[4,16,2048]{2,1,0:T(8,128)(2,1)S(1)} %get-tuple-element.72), channel_id=1, source_target_pairs={{0,32},{32,0},{1,33},{33,1},{2,34},{34,2},{3,35},{35,3},{4,36},{36... | collective-permute-start | bytes 786440 | tf_op jit(solution)/shard_map/ppermute | solution.py:48
  97.6 13.7 %collective-permute-start.26 = (bf16[16,4096]{1,0:T(8,128)(2,1)S(1)}, bf16[16,4096]{1,0:T(8,128)(2,1)S(1)}, u32[]{:S(2)}, u32[]{:S(2)}) collective-permute-start(bf16[16,4096]{1,0:T(8,128)(2,1)S(1)} %get-tuple-element.58), channel_id=1, source_target_pairs={{0,2},{2,4},{4,6},{6,0},{1,3},{3,5},{5,7},{7,1},{8,10},{10,12},{12... | collective-permute-start | bytes 393224 | tf_op jit(solution)/shard_map/ppermute | solution.py:44
  97.7 13.6 %collective-permute-start.27 = (bf16[16,4096]{1,0:T(8,128)(2,1)S(1)}, bf16[16,4096]{1,0:T(8,128)(2,1)S(1)}, u32[]{:S(2)}, u32[]{:S(2)}) collective-permute-start(bf16[16,4096]{1,0:T(8,128)(2,1)S(1)} %get-tuple-element.59), channel_id=1, source_target_pairs={{0,4},{2,6},{4,0},{6,2},{1,5},{3,7},{5,1},{7,3},{8,12},{10,14},{12... | collective-permute-start | bytes 393224 | tf_op jit(solution)/shard_map/ppermute | solution.py:44
  101.5 12.5 %collective-permute-start.28 = (bf16[16,4096]{1,0:T(8,128)(2,1)S(1)}, bf16[16,4096]{1,0:T(8,128)(2,1)S(1)}, u32[]{:S(2)}, u32[]{:S(2)}) collective-permute-start(bf16[16,4096]{1,0:T(8,128)(2,1)S(1)} %get-tuple-element.60), channel_id=1, source_target_pairs={{0,6},{2,0},{4,2},{6,4},{1,7},{3,1},{5,3},{7,5},{8,14},{10,8},{12,... | collective-permute-start | bytes 393224 | tf_op jit(solution)/shard_map/ppermute | solution.py:44
  133.9 8.5 %collective-permute-start.32 = (bf16[4,16,2048]{2,1,0:T(8,128)(2,1)S(1)}, bf16[4,16,2048]{2,1,0:T(8,128)(2,1)S(1)}, u32[]{:S(2)}, u32[]{:S(2)}) collective-permute-start(bf16[4,16,2048]{2,1,0:T(8,128)(2,1)S(1)} %get-tuple-element.73), channel_id=1, source_target_pairs={{0,38},{32,2},{2,32},{34,4},{4,34},{36,6},{6,36},{38,0},{1,39},{33... | collective-permute-start | bytes 786440 | tf_op jit(solution)/shard_map/ppermute | solution.py:55
  134.0 8.9 %collective-permute-start.29 = (bf16[4,16,4096]{2,1,0:T(8,128)(2,1)S(1)}, bf16[4,16,4096]{2,1,0:T(8,128)(2,1)S(1)}, u32[]{:S(2)}, u32[]{:S(2)}) collective-permute-start(bf16[4,16,4096]{2,1,0:T(8,128)(2,1)S(1)} %all_to_all.10.q_ref), channel_id=1, source_target_pairs={{0,1},{1,0},{2,3},{3,2},{4,5},{5,4},{6,7},{7,6},{8,9},{9,8},{10,11... | collective-permute-start | bytes 1572872 | tf_op jit(solution)/shard_map/ppermute | solution.py:48
  134.1 8.7 %collective-permute-start.30 = (bf16[4,16,2048]{2,1,0:T(8,128)(2,1)S(1)}, bf16[4,16,2048]{2,1,0:T(8,128)(2,1)S(1)}, u32[]{:S(2)}, u32[]{:S(2)}) collective-permute-start(bf16[4,16,2048]{2,1,0:T(8,128)(2,1)S(1)} %get-tuple-element.74), channel_id=1, source_target_pairs={{0,32},{32,0},{1,33},{33,1},{2,34},{34,2},{3,35},{35,3},{4,36},{36... | collective-permute-start | bytes 786440 | tf_op jit(solution)/shard_map/ppermute | solution.py:48
  142.4 1.5 collective-permute-start.33
  142.8 1.5 collective-permute-start.31
  145.9 39.6 %copy-start.2 = (bf16[128,1024]{1,0:T(8,128)(2,1)S(1)}, bf16[128,1024]{1,0:T(8,128)(2,1)}, u32[]{:S(2)}) copy-start(bf16[128,1024]{1,0:T(8,128)(2,1)} %w_ref.1) | copy-start | bytes 786436
  145.9 1.2 collective-permute-start.34
  147.1 3.7 %collective-permute-start.35 = (f32[16,128]{1,0:T(8,128)S(1)}, f32[16,128]{1,0:T(8,128)S(1)}, u32[]{:S(2)}, u32[]{:S(2)}) collective-permute-start(f32[16,128]{1,0:T(8,128)S(1)} %slice_bitcast_fusion), channel_id=1, source_target_pairs={{0,32},{32,0},{1,33},{33,1},{2,34},{34,2},{3,35},{35,3},{4,36},{36... | collective-permute-start | bytes 24584 | tf_op jit(solution)/shard_map/ppermute | solution.py:48
  150.8 6.5 %collective-permute-start.38 = (f32[16,128]{1,0:T(8,128)S(1)}, f32[16,128]{1,0:T(8,128)S(1)}, u32[]{:S(2)}, u32[]{:S(2)}) collective-permute-start(f32[16,128]{1,0:T(8,128)S(1)} %fusion.t0_ref), channel_id=1, source_target_pairs={{0,6},{2,4},{4,2},{6,0},{1,7},{3,5},{5,3},{7,1},{8,14},{10,12},{12... | collective-permute-start | bytes 24584 | tf_op jit(solution)/shard_map/ppermute | solution.py:294
  153.6 7.6 %collective-permute-start.37 = (f32[16,128]{1,0:T(8,128)S(1)}, f32[16,128]{1,0:T(8,128)S(1)}, u32[]{:S(2)}, u32[]{:S(2)}) collective-permute-start(f32[16,128]{1,0:T(8,128)S(1)} %fusion.t0_ref), channel_id=1, source_target_pairs={{0,4},{2,6},{4,0},{6,2},{1,5},{3,7},{5,1},{7,3},{8,12},{10,14},{12... | collective-permute-start | bytes 24584 | tf_op jit(solution)/shard_map/ppermute | solution.py:294
  155.0 6.2 %collective-permute-start.36 = (f32[16,128]{1,0:T(8,128)S(1)}, f32[16,128]{1,0:T(8,128)S(1)}, u32[]{:S(2)}, u32[]{:S(2)}) collective-permute-start(f32[16,128]{1,0:T(8,128)S(1)} %fusion.t0_ref), channel_id=1, source_target_pairs={{0,2},{2,0},{4,6},{6,4},{1,3},{3,1},{5,7},{7,5},{8,10},{10,8},{12,... | collective-permute-start | bytes 24584 | tf_op jit(solution)/shard_map/ppermute | solution.py:294
  162.6 22.8 %all-to-all-start.1 = ((bf16[32,16,1152]{2,1,0:T(8,128)(2,1)}), bf16[32,16,1152]{2,1,0:T(8,128)(2,1)S(1)}, u32[]{:S(2)}, u32[]{:S(2)}) async-start(bf16[32,16,1152]{2,1,0:T(8,128)(2,1)} %get-tuple-element.65), calls=%async_computation.1 | async-start | bytes 2359296 | tf_op jit(solution)/shard_map/all_to_all | solution.py:415
  169.3 12.8 %collective-permute-start.39 = (f32[16,512]{1,0:T(8,128)S(1)}, f32[16,512]{1,0:T(8,128)S(1)}, u32[]{:S(2)}, u32[]{:S(2)}) collective-permute-start(f32[16,512]{1,0:T(8,128)S(1)} %get-tuple-element.68), channel_id=1, source_target_pairs={{0,32},{32,0},{1,33},{33,1},{2,34},{34,2},{3,35},{35,3},{4,36},{36... | collective-permute-start | bytes 98312 | tf_op jit(solution)/shard_map/ppermute | solution.py:48

commit v10 on v8

--- a/solution.py
+++ b/solution.py
@@ -216,6 +216,14 @@
         back_ref[order] = dot_nt(b, hid_ref[...])
 
 
+def route_kernel(near_ref, left_ref, right_ref, mine_ref, s1_ref, s2_ref, s3_ref):
+    h = lax.axis_index("h")
+    for j, ref in enumerate((mine_ref, s1_ref, s2_ref, s3_ref)):
+        k = (h + j) % 4
+        ref[:, :SIDE] = (near_ref[k, :, :SIDE] + left_ref[k].astype(F32)).astype(ref.dtype)
+        ref[:, SIDE:] = (near_ref[k, :, SIDE:] + right_ref[k].astype(F32)).astype(ref.dtype)
+
+
 def down_kernel(t0_ref, t1_ref, t2_ref, t3_ref, x_ref, a_ref, up_ref, new_ref, wire_ref):
     rest = (t0_ref[...] + t1_ref[...]) + (t2_ref[...] + t3_ref[...])
     parts = []
@@ -361,9 +369,14 @@
     left = partner(away[:, :, :SIDE], "l")
     right = away[:, :, SIDE:]
     right = near_z(right)
-    summed = summed[:4] + jnp.concatenate([left, right], axis=2).astype(F32)
-    shares = lax.all_to_all(summed.astype(BF16), "h", 0, 0, tiled=True)
-    share = shares.astype(F32).sum(axis=0) * FF ** (-0.5)
+    mine, *steps = call(
+        route_kernel,
+        (shape(ROWS, MODEL_WIDTH, dtype=F32),) + (shape(ROWS, MODEL_WIDTH),) * 3,
+        summed[:4], left, right,
+        name="route",
+    )
+    steps = [shift(step, "h", j + 1).astype(F32) for j, step in enumerate(steps)]
+    share = ((mine + steps[0]) + (steps[1] + steps[2])) * FF ** (-0.5)
     grad_rows = ((share - my_targets.astype(F32)) / TOK).astype(BF16)
 
     q = lax.all_to_all(jnp.broadcast_to(grad_rows, (4, ROWS, MODEL_WIDTH)), "h", 0, 0, tiled=True)

time: 182 us -> 176 us (0.967)
  waiting for transfers between devices: 85.9 us -> 82.9 us
  starting transfers between devices: 56.3 us -> 59 us
  local copies, waits for them, and re-layouts: 5.63 us -> 2.96 us
  other arithmetic: 3.39 us -> 1.31 us
    all_to_all x1 -> x0, waiting for transfers between devices: 12.8 us -> none  [shards(): shares = lax.all_to_all(summed.astype(BF16), 'h', 0, 0, tiled=True)]
    ppermute x14 -> x17, waiting for transfers between devices: 19 us -> 28.4 us  [shift(): return lax.ppermute(value, axis, [(i, (i + by) % n) for i in range(n)])]
    ppermute x14 -> x17, starting transfers between devices: 19.2 us -> 27.7 us  [shift(): return lax.ppermute(value, axis, [(i, (i + by) % n) for i in range(n)])]
    all_to_all x1 -> x0, starting transfers between devices: 5.56 us -> none  [shards(): shares = lax.all_to_all(summed.astype(BF16), 'h', 0, 0, tiled=True)]
    unnamed x34 -> x14, local copies, waits for them, and re-layouts: 4.77 us -> 2.76 us
    pallas_call x11 -> x12, Pallas kernels: 8.6 us -> 8.59 us  [call(): pl.pallas_call(kernel, out_shape=out_shape, in_specs=[vmem] * len(args) +...]
  transfers between devices with their start and end apart: 33 -> 35, of which waited for: 21 -> 22; matrix products, arithmetic and copies ran while one was open for 1% -> 1% of each run, Pallas kernels for 2% -> 2%
where the time goes in v10:
time: 176 us
  waiting for transfers between devices  82.9 us (47%)
  starting transfers between devices  59 us (34%)
  blocking collectives  20 us (11%)
  Pallas kernels  8.73 us (5%)
  local copies, waits for them, and re-layouts  2.96 us (2%)
    ppermute x11, waiting for transfers between devices, partner(): return lax.ppermute(value, axis, [(0, 1), (1, 0)])  37.3 us
    ppermute x17, waiting for transfers between devices, shift(): return lax.ppermute(value, axis, [(i, (i + by) % n) for i in range(n)])  28.4 us
    ppermute x17, starting transfers between devices, shift(): return lax.ppermute(value, axis, [(i, (i + by) % n) for i in range(n)])  27.7 us
    all_to_all x1, blocking collectives, shards(): lax.all_to_all(jnp.broadcast_to(grad_rows, (4, ROWS, MODEL_WIDTH)), 'h',...  20 us
    ppermute x3, waiting for transfers between devices, near_z(): lax.ppermute(value, Z, [(place(z), place(z + 1 if z % 2 else z - 1)) for...  12.7 us
    ppermute x3, starting transfers between devices, near_z(): lax.ppermute(value, Z, [(place(z), place(z + 1 if z % 2 else z - 1)) for...  11.1 us
    pallas_call x12, Pallas kernels, call(): pl.pallas_call(kernel, out_shape=out_shape, in_specs=[vmem] * len(args) +...  8.59 us
    all_to_all x1, starting transfers between devices, shards(): wires = lax.all_to_all(wire, REP, 0, 0, tiled=True)  8.13 us
  transfers between devices with their start and end apart: 35, of which 22 were waited for; matrix products, arithmetic and copies ran while one was open for 1% of the time, Pallas kernels for 2%

profile of v10, /device:TPU:2, one launch (start us, length us, event | category | flops | bytes accessed | tf_op | source)
XLA Modules:
  0.0 175.8 jit_solution(4859227537234249750)
XLA Ops:
  0.7 1.0 copy-done.1
  1.7 0.9 copy-done.3
  3.5 2.0 %collective-permute-start.2 = (bf16[272,512]{1,0:T(8,128)(2,1)S(1)}, bf16[272,512]{1,0:T(8,128)(2,1)S(1)}, u32[]{:S(2)}, u32[]{:S(2)}) collective-permute-start(bf16[272,512]{1,0:T(8,128)(2,1)S(1)} %send.1.send_ref), channel_id=1, source_target_pairs={{0,32},{32,0},{1,33},{33,1},{2,34},{34,2},{3,35},{35,3},{4,36},{36... | collective-permute-start | bytes 835592 | tf_op jit(solution)/shard_map/ppermute | solution.py:48
  5.6 6.6 %collective-permute-done.2 = bf16[272,512]{1,0:T(8,128)(2,1)S(1)} collective-permute-done((bf16[272,512]{1,0:T(8,128)(2,1)S(1)}, bf16[272,512]{1,0:T(8,128)(2,1)S(1)}, u32[]{:S(2)}, u32[]{:S(2)}) %collective-permute-start.2) | collective-permute-done | bytes 278560 | tf_op jit(solution)/shard_map/ppermute | solution.py:48
  12.2 1.6 collective-permute-start.3
  13.9 1.7 collective-permute-start.10
  16.1 3.6 %collective-permute-done.3 = bf16[256,512]{1,0:T(8,128)(2,1)S(1)} collective-permute-done((bf16[256,512]{1,0:T(8,128)(2,1)S(1)}, bf16[256,512]{1,0:T(8,128)(2,1)S(1)}, u32[]{:S(2)}, u32[]{:S(2)}) %collective-permute-start.3) | collective-permute-done | bytes 262176 | tf_op jit(solution)/shard_map/ppermute | solution.py:44
  19.7 1.5 collective-permute-start.5
  21.2 3.0 %collective-permute-start.11 = (bf16[256,512]{1,0:T(8,128)(2,1)S(1)}, bf16[256,512]{1,0:T(8,128)(2,1)S(1)}, u32[]{:S(2)}, u32[]{:S(2)}) collective-permute-start(bf16[256,512]{1,0:T(8,128)(2,1)S(1)} %maximum_select_fusion.1), channel_id=1, source_target_pairs={{0,192},{64,0},{128,64},{192,128},{1,193},{65,1},{129,65},{193,129... | collective-permute-start | bytes 786440 | tf_op jit(solution)/shard_map/ppermute | solution.py:44
  24.6 5.5 %collective-permute-start = (bf16[80,4096]{1,0:T(8,128)(2,1)S(1)}, bf16[80,4096]{1,0:T(8,128)(2,1)S(1)}, u32[]{:S(2)}, u32[]{:S(2)}) collective-permute-start(bf16[80,4096]{1,0:T(8,128)(2,1)S(1)} %get-tuple-element.35), channel_id=1, source_target_pairs={{0,38},{32,2},{2,32},{34,4},{4,34},{36,6},{6,36},{38,0},{1,39},{33... | collective-permute-start | bytes 1966088 | tf_op jit(solution)/shard_map/ppermute | solution.py:55
  30.8 2.7 %collective-permute-start.7 = (bf16[1024,512]{1,0:T(8,128)(2,1)S(1)}, bf16[1024,512]{1,0:T(8,128)(2,1)S(1)}, u32[]{:S(2)}, u32[]{:S(2)}) collective-permute-start(bf16[1024,512]{1,0:T(8,128)(2,1)S(1)} %pad_maximum_fusion.refs_0_), channel_id=1, source_target_pairs={{0,192},{64,0},{128,64},{192,128},{1,193},{65,1},{129,65},{193,129... | collective-permute-start | bytes 3145736 | tf_op jit(solution)/shard_map/ppermute | solution.py:44
  33.6 1.3 collective-permute-start.13
  35.7 6.7 %collective-permute-done.oth_ref = bf16[80,4096]{1,0:T(8,128)(2,1)S(1)} collective-permute-done((bf16[80,4096]{1,0:T(8,128)(2,1)S(1)}, bf16[80,4096]{1,0:T(8,128)(2,1)S(1)}, u32[]{:S(2)}, u32[]{:S(2)}) %collective-permute-start) | collective-permute-done | bytes 655392 | tf_op jit(solution)/shard_map/ppermute | solution.py:55
  42.5 2.1 %collective-permute-done.1.oth_core_ref = bf16[80,4096]{1,0:T(8,128)(2,1)S(1)} collective-permute-done((bf16[80,4096]{1,0:T(8,128)(2,1)S(1)}, bf16[80,4096]{1,0:T(8,128)(2,1)S(1)}, u32[]{:S(2)}, u32[]{:S(2)}) %collective-permute-start.1) | collective-permute-done | bytes 655392 | tf_op jit(solution)/shard_map/ppermute | solution.py:48
  44.6 1.0 arrange.1
  45.6 8.7 %collective-permute-done.6.refs_1_.below_ref = bf16[1024,512]{1,0:T(8,128)(2,1)S(1)} collective-permute-done((bf16[1024,512]{1,0:T(8,128)(2,1)S(1)}, bf16[1024,512]{1,0:T(8,128)(2,1)S(1)}, u32[]{:S(2)}, u32[]{:S(2)}) %collective-permute-start.6) | collective-permute-done | bytes 1048608 | tf_op jit(solution)/shard_map/ppermute | solution.py:44
  55.0 2.6 %collective-permute-start.9 = (bf16[512,512]{1,0:T(8,128)(2,1)S(1)}, bf16[512,512]{1,0:T(8,128)(2,1)S(1)}, u32[]{:S(2)}, u32[]{:S(2)}) collective-permute-start(bf16[512,512]{1,0:T(8,128)(2,1)S(1)} %get-tuple-element.46), channel_id=1, source_target_pairs={{0,192},{64,0},{128,64},{192,128},{1,193},{65,1},{129,65},{193,129... | collective-permute-start | bytes 1572872 | tf_op jit(solution)/shard_map/ppermute | solution.py:44
  57.7 1.3 collective-permute-start.15
  59.8 1.0 near.1.total_ref
  60.9 5.4 %collective-permute-done.8.low_ref = bf16[512,512]{1,0:T(8,128)(2,1)S(1)} collective-permute-done((bf16[512,512]{1,0:T(8,128)(2,1)S(1)}, bf16[512,512]{1,0:T(8,128)(2,1)S(1)}, u32[]{:S(2)}, u32[]{:S(2)}) %collective-permute-start.8) | collective-permute-done | bytes 524320 | tf_op jit(solution)/shard_map/ppermute | solution.py:44
  66.7 1.1 collective-permute-done.15.refs_3_
  67.9 0.9 collective-permute-done.16.refs_4_
  68.8 1.3 output.1
  70.2 2.6 %collective-permute-done.17 = bf16[8,16,4096]{2,1,0:T(8,128)(2,1)S(1)} collective-permute-done((bf16[8,16,4096]{2,1,0:T(8,128)(2,1)S(1)}, bf16[8,16,4096]{2,1,0:T(8,128)(2,1)S(1)}, u32[]{:S(2)}, u32[]{:S(2)}) %collective-permute-start.17) | collective-permute-done | bytes 1048608 | tf_op jit(solution)/shard_map/ppermute | solution.py:48
  73.9 4.9 %collective-permute-start.19 = (bf16[4,16,2048]{2,1,0:T(8,128)(2,1)S(1)}, bf16[4,16,2048]{2,1,0:T(8,128)(2,1)S(1)}, u32[]{:S(2)}, u32[]{:S(2)}) collective-permute-start(bf16[4,16,2048]{2,1,0:T(8,128)(2,1)S(1)} %get-tuple-element.67), channel_id=1, source_target_pairs={{0,38},{32,2},{2,32},{34,4},{4,34},{36,6},{6,36},{38,0},{1,39},{33... | collective-permute-start | bytes 786440 | tf_op jit(solution)/shard_map/ppermute | solution.py:55
  78.9 2.7 %collective-permute-done.18.left_ref = bf16[4,16,2048]{2,1,0:T(8,128)(2,1)S(1)} collective-permute-done((bf16[4,16,2048]{2,1,0:T(8,128)(2,1)S(1)}, bf16[4,16,2048]{2,1,0:T(8,128)(2,1)S(1)}, u32[]{:S(2)}, u32[]{:S(2)}) %collective-permute-start.18) | collective-permute-done | bytes 262176 | tf_op jit(solution)/shard_map/ppermute | solution.py:48
  81.7 3.5 %collective-permute-done.19.right_ref = bf16[4,16,2048]{2,1,0:T(8,128)(2,1)S(1)} collective-permute-done((bf16[4,16,2048]{2,1,0:T(8,128)(2,1)S(1)}, bf16[4,16,2048]{2,1,0:T(8,128)(2,1)S(1)}, u32[]{:S(2)}, u32[]{:S(2)}) %collective-permute-start.19) | collective-permute-done | bytes 262176 | tf_op jit(solution)/shard_map/ppermute | solution.py:55
  85.3 1.4 collective-permute-start.20
  86.7 3.2 %collective-permute-start.21 = (bf16[16,4096]{1,0:T(8,128)(2,1)S(1)}, bf16[16,4096]{1,0:T(8,128)(2,1)S(1)}, u32[]{:S(2)}, u32[]{:S(2)}) collective-permute-start(bf16[16,4096]{1,0:T(8,128)(2,1)S(1)} %get-tuple-element.55), channel_id=1, source_target_pairs={{0,4},{2,6},{4,0},{6,2},{1,5},{3,7},{5,1},{7,3},{8,12},{10,14},{12... | collective-permute-start | bytes 393224 | tf_op jit(solution)/shard_map/ppermute | solution.py:44
  89.9 3.9 %collective-permute-start.22 = (bf16[16,4096]{1,0:T(8,128)(2,1)S(1)}, bf16[16,4096]{1,0:T(8,128)(2,1)S(1)}, u32[]{:S(2)}, u32[]{:S(2)}) collective-permute-start(bf16[16,4096]{1,0:T(8,128)(2,1)S(1)} %get-tuple-element.56), channel_id=1, source_target_pairs={{0,6},{2,0},{4,2},{6,4},{1,7},{3,1},{5,3},{7,5},{8,14},{10,8},{12,... | collective-permute-start | bytes 393224 | tf_op jit(solution)/shard_map/ppermute | solution.py:44
  93.9 5.2 %collective-permute-done.20 = bf16[16,4096]{1,0:T(8,128)(2,1)S(1)} collective-permute-done((bf16[16,4096]{1,0:T(8,128)(2,1)S(1)}, bf16[16,4096]{1,0:T(8,128)(2,1)S(1)}, u32[]{:S(2)}, u32[]{:S(2)}) %collective-permute-start.20) | collective-permute-done | bytes 131104 | tf_op jit(solution)/shard_map/ppermute | solution.py:44
  99.1 3.4 %collective-permute-done.22 = bf16[16,4096]{1,0:T(8,128)(2,1)S(1)} collective-permute-done((bf16[16,4096]{1,0:T(8,128)(2,1)S(1)}, bf16[16,4096]{1,0:T(8,128)(2,1)S(1)}, u32[]{:S(2)}, u32[]{:S(2)}) %collective-permute-start.22) | collective-permute-done | bytes 131104 | tf_op jit(solution)/shard_map/ppermute | solution.py:44
  102.7 20.0 %all_to_all.10.q_ref = bf16[4,16,4096]{2,1,0:T(8,128)(2,1)S(1)} all-to-all(bf16[4,16,4096]{2,1,0:T(8,128)(2,1)S(1)} %broadcast_in_dim.7), channel_id=1, replica_groups=mesh['y'=4,'l'=2,'x'=4,'h'=4,'c'=2] {'h'}, dimensions={0} | all-to-all | bytes 1048576 | tf_op jit(solution)/shard_map/all_to_all | solution.py:382
  123.6 6.8 %collective-permute-done.24.left_ref = bf16[4,16,2048]{2,1,0:T(8,128)(2,1)S(1)} collective-permute-done((bf16[4,16,2048]{2,1,0:T(8,128)(2,1)S(1)}, bf16[4,16,2048]{2,1,0:T(8,128)(2,1)S(1)}, u32[]{:S(2)}, u32[]{:S(2)}) %collective-permute-start.24) | collective-permute-done | bytes 262176 | tf_op jit(solution)/shard_map/ppermute | solution.py:48
  130.4 2.5 %collective-permute-done.26.right_ref = bf16[4,16,2048]{2,1,0:T(8,128)(2,1)S(1)} collective-permute-done((bf16[4,16,2048]{2,1,0:T(8,128)(2,1)S(1)}, bf16[4,16,2048]{2,1,0:T(8,128)(2,1)S(1)}, u32[]{:S(2)}, u32[]{:S(2)}) %collective-permute-start.26) | collective-permute-done | bytes 262176 | tf_op jit(solution)/shard_map/ppermute | solution.py:55
  132.9 1.5 collective-permute-done.27.rightc_ref
  134.4 1.5 backward.1
  136.3 1.0 collective-permute-done.28
  138.1 3.0 %collective-permute-done.29 = f32[16,128]{1,0:T(8,128)S(1)} collective-permute-done((f32[16,128]{1,0:T(8,128)S(1)}, f32[16,128]{1,0:T(8,128)S(1)}, u32[]{:S(2)}, u32[]{:S(2)}) %collective-permute-start.29) | collective-permute-done | bytes 8224 | tf_op jit(solution)/shard_map/ppermute | solution.py:48
  141.4 2.0 %collective-permute-start.31 = (f32[16,128]{1,0:T(8,128)S(1)}, f32[16,128]{1,0:T(8,128)S(1)}, u32[]{:S(2)}, u32[]{:S(2)}) collective-permute-start(f32[16,128]{1,0:T(8,128)S(1)} %fusion.t0_ref), channel_id=1, source_target_pairs={{0,4},{2,6},{4,0},{6,2},{1,5},{3,7},{5,1},{7,3},{8,12},{10,14},{12... | collective-permute-start | bytes 24584 | tf_op jit(solution)/shard_map/ppermute | solution.py:294
  143.5 4.1 %collective-permute-start.32 = (f32[16,128]{1,0:T(8,128)S(1)}, f32[16,128]{1,0:T(8,128)S(1)}, u32[]{:S(2)}, u32[]{:S(2)}) collective-permute-start(f32[16,128]{1,0:T(8,128)S(1)} %fusion.t0_ref), channel_id=1, source_target_pairs={{0,6},{2,4},{4,2},{6,0},{1,7},{3,5},{5,3},{7,1},{8,14},{10,12},{12... | collective-permute-start | bytes 24584 | tf_op jit(solution)/shard_map/ppermute | solution.py:294
  147.5 1.5 collective-permute-done.31.t2_ref
  149.2 1.5 down.1
  150.7 8.1 %all-to-all-start.1 = ((bf16[32,16,1152]{2,1,0:T(8,128)(2,1)}), bf16[32,16,1152]{2,1,0:T(8,128)(2,1)S(1)}, u32[]{:S(2)}, u32[]{:S(2)}) async-start(bf16[32,16,1152]{2,1,0:T(8,128)(2,1)} %get-tuple-element.61), calls=%async_computation.1 | async-start | bytes 2359296 | tf_op jit(solution)/shard_map/all_to_all | solution.py:412
  158.8 1.6 collective-permute-start.33
  160.4 11.0 %collective-permute-done.33 = f32[16,512]{1,0:T(8,128)S(1)} collective-permute-done((f32[16,512]{1,0:T(8,128)S(1)}, f32[16,512]{1,0:T(8,128)S(1)}, u32[]{:S(2)}, u32[]{:S(2)}) %collective-permute-start.33) | collective-permute-done | bytes 32800 | tf_op jit(solution)/shard_map/ppermute | solution.py:48
  172.0 2.7 %all-to-all-done.1.wire_ref = bf16[32,16,1152]{2,1,0:T(8,128)(2,1)S(1)} async-done(((bf16[32,16,1152]{2,1,0:T(8,128)(2,1)}), bf16[32,16,1152]{2,1,0:T(8,128)(2,1)S(1)}, u32[]{:S(2)}, u32[]{:S(2)}) %all-to-all-start.1) | async-done | bytes 1179680 | tf_op jit(solution)/shard_map/all_to_all | solution.py:412
  174.7 1.1 merge.1
  (67 shorter events, 10.6 us)
Async XLA Ops:
  0.6 23.6 %copy-start = (bf16[128,4096]{1,0:T(8,128)(2,1)S(1)}, bf16[128,4096]{1,0:T(8,128)(2,1)}, u32[]{:S(2)}) copy-start(bf16[128,4096]{1,0:T(8,128)(2,1)} %x_ref.1) | copy-start | bytes 3145732
  0.6 1.0 copy-start.1
  1.7 0.9 copy-start.3
  2.6 0.8 copy-start.6
  3.4 20.8 %copy-start.5 = (bf16[1,16,4096]{2,1,0:T(8,128)(2,1)S(1)}, bf16[1,16,4096]{2,1,0:T(8,128)(2,1)}, u32[]{:S(2)}) copy-start(bf16[1,16,4096]{2,1,0:T(8,128)(2,1)} %param.10) | copy-start | bytes 393220
  3.5 8.7 %collective-permute-start.2 = (bf16[272,512]{1,0:T(8,128)(2,1)S(1)}, bf16[272,512]{1,0:T(8,128)(2,1)S(1)}, u32[]{:S(2)}, u32[]{:S(2)}) collective-permute-start(bf16[272,512]{1,0:T(8,128)(2,1)S(1)} %send.1.send_ref), channel_id=1, source_target_pairs={{0,32},{32,0},{1,33},{33,1},{2,34},{34,2},{3,35},{35,3},{4,36},{36... | collective-permute-start | bytes 835592 | tf_op jit(solution)/shard_map/ppermute | solution.py:48
  12.2 7.4 %collective-permute-start.3 = (bf16[256,512]{1,0:T(8,128)(2,1)S(1)}, bf16[256,512]{1,0:T(8,128)(2,1)S(1)}, u32[]{:S(2)}, u32[]{:S(2)}) collective-permute-start(bf16[256,512]{1,0:T(8,128)(2,1)S(1)} %maximum_select_fusion), channel_id=1, source_target_pairs={{0,8},{8,16},{16,24},{24,0},{1,9},{9,17},{17,25},{25,1},{2,10},{10... | collective-permute-start | bytes 786440 | tf_op jit(solution)/shard_map/ppermute | solution.py:44
  13.9 10.3 %collective-permute-start.10 = (bf16[256,512]{1,0:T(8,128)(2,1)S(1)}, bf16[256,512]{1,0:T(8,128)(2,1)S(1)}, u32[]{:S(2)}, u32[]{:S(2)}) collective-permute-start(bf16[256,512]{1,0:T(8,128)(2,1)S(1)} %maximum_select_fusion.1), channel_id=1, source_target_pairs={{0,64},{64,128},{128,192},{192,0},{1,65},{65,129},{129,193},{193,1... | collective-permute-start | bytes 786440 | tf_op jit(solution)/shard_map/ppermute | solution.py:44
  15.5 14.6 %collective-permute-start.4 = (bf16[256,512]{1,0:T(8,128)(2,1)S(1)}, bf16[256,512]{1,0:T(8,128)(2,1)S(1)}, u32[]{:S(2)}, u32[]{:S(2)}) collective-permute-start(bf16[256,512]{1,0:T(8,128)(2,1)S(1)} %maximum_select_fusion), channel_id=1, source_target_pairs={{0,24},{8,0},{16,8},{24,16},{1,25},{9,1},{17,9},{25,17},{2,26},{10... | collective-permute-start | bytes 786440 | tf_op jit(solution)/shard_map/ppermute | solution.py:44
  19.7 10.4 %collective-permute-start.5 = (bf16[256,512]{1,0:T(8,128)(2,1)S(1)}, bf16[256,512]{1,0:T(8,128)(2,1)S(1)}, u32[]{:S(2)}, u32[]{:S(2)}) collective-permute-start(bf16[256,512]{1,0:T(8,128)(2,1)S(1)} %collective-permute-done.3), channel_id=1, source_target_pairs={{0,8},{8,16},{16,24},{24,0},{1,9},{9,17},{17,25},{25,1},{2,10},{10... | collective-permute-start | bytes 786440 | tf_op jit(solution)/shard_map/ppermute | solution.py:44
  21.2 12.4 %collective-permute-start.11 = (bf16[256,512]{1,0:T(8,128)(2,1)S(1)}, bf16[256,512]{1,0:T(8,128)(2,1)S(1)}, u32[]{:S(2)}, u32[]{:S(2)}) collective-permute-start(bf16[256,512]{1,0:T(8,128)(2,1)S(1)} %maximum_select_fusion.1), channel_id=1, source_target_pairs={{0,192},{64,0},{128,64},{192,128},{1,193},{65,1},{129,65},{193,129... | collective-permute-start | bytes 786440 | tf_op jit(solution)/shard_map/ppermute | solution.py:44
  24.2 9.4 %collective-permute-start.12 = (bf16[256,512]{1,0:T(8,128)(2,1)S(1)}, bf16[256,512]{1,0:T(8,128)(2,1)S(1)}, u32[]{:S(2)}, u32[]{:S(2)}) collective-permute-start(bf16[256,512]{1,0:T(8,128)(2,1)S(1)} %collective-permute-done.10), channel_id=1, source_target_pairs={{0,64},{64,128},{128,192},{192,0},{1,65},{65,129},{129,193},{193,1... | collective-permute-start | bytes 786440 | tf_op jit(solution)/shard_map/ppermute | solution.py:44
  24.6 17.9 %collective-permute-start = (bf16[80,4096]{1,0:T(8,128)(2,1)S(1)}, bf16[80,4096]{1,0:T(8,128)(2,1)S(1)}, u32[]{:S(2)}, u32[]{:S(2)}) collective-permute-start(bf16[80,4096]{1,0:T(8,128)(2,1)S(1)} %get-tuple-element.35), channel_id=1, source_target_pairs={{0,38},{32,2},{2,32},{34,4},{4,34},{36,6},{6,36},{38,0},{1,39},{33... | collective-permute-start | bytes 1966088 | tf_op jit(solution)/shard_map/ppermute | solution.py:55
  30.2 24.1 %collective-permute-start.6 = (bf16[1024,512]{1,0:T(8,128)(2,1)S(1)}, bf16[1024,512]{1,0:T(8,128)(2,1)S(1)}, u32[]{:S(2)}, u32[]{:S(2)}) collective-permute-start(bf16[1024,512]{1,0:T(8,128)(2,1)S(1)} %pad_maximum_fusion.refs_0_), channel_id=1, source_target_pairs={{0,64},{64,128},{128,192},{192,0},{1,65},{65,129},{129,193},{193,1... | collective-permute-start | bytes 3145736 | tf_op jit(solution)/shard_map/ppermute | solution.py:44
  30.8 23.4 %collective-permute-start.7 = (bf16[1024,512]{1,0:T(8,128)(2,1)S(1)}, bf16[1024,512]{1,0:T(8,128)(2,1)S(1)}, u32[]{:S(2)}, u32[]{:S(2)}) collective-permute-start(bf16[1024,512]{1,0:T(8,128)(2,1)S(1)} %pad_maximum_fusion.refs_0_), channel_id=1, source_target_pairs={{0,192},{64,0},{128,64},{192,128},{1,193},{65,1},{129,65},{193,129... | collective-permute-start | bytes 3145736 | tf_op jit(solution)/shard_map/ppermute | solution.py:44
  33.6 24.0 %collective-permute-start.13 = (bf16[1024,512]{1,0:T(8,128)(2,1)S(1)}, bf16[1024,512]{1,0:T(8,128)(2,1)S(1)}, u32[]{:S(2)}, u32[]{:S(2)}) collective-permute-start(bf16[1024,512]{1,0:T(8,128)(2,1)S(1)} %pad_maximum_fusion.1.refs_0_), channel_id=1, source_target_pairs={{0,8},{8,16},{16,24},{24,0},{1,9},{9,17},{17,25},{25,1},{2,10},{10... | collective-permute-start | bytes 3145736 | tf_op jit(solution)/shard_map/ppermute | solution.py:44
  34.9 22.7 %collective-permute-start.14 = (bf16[1024,512]{1,0:T(8,128)(2,1)S(1)}, bf16[1024,512]{1,0:T(8,128)(2,1)S(1)}, u32[]{:S(2)}, u32[]{:S(2)}) collective-permute-start(bf16[1024,512]{1,0:T(8,128)(2,1)S(1)} %pad_maximum_fusion.1.refs_0_), channel_id=1, source_target_pairs={{0,24},{8,0},{16,8},{24,16},{1,25},{9,1},{17,9},{25,17},{2,26},{10... | collective-permute-start | bytes 3145736 | tf_op jit(solution)/shard_map/ppermute | solution.py:44
  42.5 2.1 %collective-permute-start.1 = (bf16[80,4096]{1,0:T(8,128)(2,1)S(1)}, bf16[80,4096]{1,0:T(8,128)(2,1)S(1)}, u32[]{:S(2)}, u32[]{:S(2)}) collective-permute-start(bf16[80,4096]{1,0:T(8,128)(2,1)S(1)} %collective-permute-done.oth_ref), channel_id=1, source_target_pairs={{0,1},{1,0},{2,3},{3,2},{4,5},{5,4},{6,7},{7,6},{8,9},{9,8},{10,11... | collective-permute-start | bytes 1966088 | tf_op jit(solution)/shard_map/ppermute | solution.py:48
  54.3 11.9 %collective-permute-start.8 = (bf16[512,512]{1,0:T(8,128)(2,1)S(1)}, bf16[512,512]{1,0:T(8,128)(2,1)S(1)}, u32[]{:S(2)}, u32[]{:S(2)}) collective-permute-start(bf16[512,512]{1,0:T(8,128)(2,1)S(1)} %get-tuple-element.45), channel_id=1, source_target_pairs={{0,64},{64,128},{128,192},{192,0},{1,65},{65,129},{129,193},{193,1... | collective-permute-start | bytes 1572872 | tf_op jit(solution)/shard_map/ppermute | solution.py:44
  55.0 11.3 %collective-permute-start.9 = (bf16[512,512]{1,0:T(8,128)(2,1)S(1)}, bf16[512,512]{1,0:T(8,128)(2,1)S(1)}, u32[]{:S(2)}, u32[]{:S(2)}) collective-permute-start(bf16[512,512]{1,0:T(8,128)(2,1)S(1)} %get-tuple-element.46), channel_id=1, source_target_pairs={{0,192},{64,0},{128,64},{192,128},{1,193},{65,1},{129,65},{193,129... | collective-permute-start | bytes 1572872 | tf_op jit(solution)/shard_map/ppermute | solution.py:44
  57.7 10.2 %collective-permute-start.15 = (bf16[512,512]{1,0:T(8,128)(2,1)S(1)}, bf16[512,512]{1,0:T(8,128)(2,1)S(1)}, u32[]{:S(2)}, u32[]{:S(2)}) collective-permute-start(bf16[512,512]{1,0:T(8,128)(2,1)S(1)} %get-tuple-element.49), channel_id=1, source_target_pairs={{0,8},{8,16},{16,24},{24,0},{1,9},{9,17},{17,25},{25,1},{2,10},{10... | collective-permute-start | bytes 1572872 | tf_op jit(solution)/shard_map/ppermute | solution.py:44
  59.0 9.8 %collective-permute-start.16 = (bf16[512,512]{1,0:T(8,128)(2,1)S(1)}, bf16[512,512]{1,0:T(8,128)(2,1)S(1)}, u32[]{:S(2)}, u32[]{:S(2)}) collective-permute-start(bf16[512,512]{1,0:T(8,128)(2,1)S(1)} %get-tuple-element.50), channel_id=1, source_target_pairs={{0,24},{8,0},{16,8},{24,16},{1,25},{9,1},{17,9},{25,17},{2,26},{10... | collective-permute-start | bytes 1572872 | tf_op jit(solution)/shard_map/ppermute | solution.py:44
  70.1 2.7 %collective-permute-start.17 = (bf16[8,16,4096]{2,1,0:T(8,128)(2,1)S(1)}, bf16[8,16,4096]{2,1,0:T(8,128)(2,1)S(1)}, u32[]{:S(2)}, u32[]{:S(2)}) collective-permute-start(bf16[8,16,4096]{2,1,0:T(8,128)(2,1)S(1)} %get-tuple-element.52), channel_id=1, source_target_pairs={{0,1},{1,0},{2,3},{3,2},{4,5},{5,4},{6,7},{7,6},{8,9},{9,8},{10,11... | collective-permute-start | bytes 3145736 | tf_op jit(solution)/shard_map/ppermute | solution.py:48
  73.2 20.6 %copy-start.4 = (bf16[128,4096]{1,0:T(8,128)(2,1)S(1)}, bf16[128,4096]{1,0:T(8,128)(2,1)}, u32[]{:S(2)}) copy-start(bf16[128,4096]{1,0:T(8,128)(2,1)} %targets_ref.1) | copy-start | bytes 3145732
  73.2 8.4 %collective-permute-start.18 = (bf16[4,16,2048]{2,1,0:T(8,128)(2,1)S(1)}, bf16[4,16,2048]{2,1,0:T(8,128)(2,1)S(1)}, u32[]{:S(2)}, u32[]{:S(2)}) collective-permute-start(bf16[4,16,2048]{2,1,0:T(8,128)(2,1)S(1)} %get-tuple-element.68), channel_id=1, source_target_pairs={{0,32},{32,0},{1,33},{33,1},{2,34},{34,2},{3,35},{35,3},{4,36},{36... | collective-permute-start | bytes 786440 | tf_op jit(solution)/shard_map/ppermute | solution.py:48
  73.9 11.3 %collective-permute-start.19 = (bf16[4,16,2048]{2,1,0:T(8,128)(2,1)S(1)}, bf16[4,16,2048]{2,1,0:T(8,128)(2,1)S(1)}, u32[]{:S(2)}, u32[]{:S(2)}) collective-permute-start(bf16[4,16,2048]{2,1,0:T(8,128)(2,1)S(1)} %get-tuple-element.67), channel_id=1, source_target_pairs={{0,38},{32,2},{2,32},{34,4},{4,34},{36,6},{6,36},{38,0},{1,39},{33... | collective-permute-start | bytes 786440 | tf_op jit(solution)/shard_map/ppermute | solution.py:55
  85.3 13.8 %collective-permute-start.20 = (bf16[16,4096]{1,0:T(8,128)(2,1)S(1)}, bf16[16,4096]{1,0:T(8,128)(2,1)S(1)}, u32[]{:S(2)}, u32[]{:S(2)}) collective-permute-start(bf16[16,4096]{1,0:T(8,128)(2,1)S(1)} %get-tuple-element.54), channel_id=1, source_target_pairs={{0,2},{2,4},{4,6},{6,0},{1,3},{3,5},{5,7},{7,1},{8,10},{10,12},{12... | collective-permute-start | bytes 393224 | tf_op jit(solution)/shard_map/ppermute | solution.py:44
  86.7 12.4 %collective-permute-start.21 = (bf16[16,4096]{1,0:T(8,128)(2,1)S(1)}, bf16[16,4096]{1,0:T(8,128)(2,1)S(1)}, u32[]{:S(2)}, u32[]{:S(2)}) collective-permute-start(bf16[16,4096]{1,0:T(8,128)(2,1)S(1)} %get-tuple-element.55), channel_id=1, source_target_pairs={{0,4},{2,6},{4,0},{6,2},{1,5},{3,7},{5,1},{7,3},{8,12},{10,14},{12... | collective-permute-start | bytes 393224 | tf_op jit(solution)/shard_map/ppermute | solution.py:44
  89.9 12.6 %collective-permute-start.22 = (bf16[16,4096]{1,0:T(8,128)(2,1)S(1)}, bf16[16,4096]{1,0:T(8,128)(2,1)S(1)}, u32[]{:S(2)}, u32[]{:S(2)}) collective-permute-start(bf16[16,4096]{1,0:T(8,128)(2,1)S(1)} %get-tuple-element.56), channel_id=1, source_target_pairs={{0,6},{2,0},{4,2},{6,4},{1,7},{3,1},{5,3},{7,5},{8,14},{10,8},{12,... | collective-permute-start | bytes 393224 | tf_op jit(solution)/shard_map/ppermute | solution.py:44
  122.7 7.7 %collective-permute-start.24 = (bf16[4,16,2048]{2,1,0:T(8,128)(2,1)S(1)}, bf16[4,16,2048]{2,1,0:T(8,128)(2,1)S(1)}, u32[]{:S(2)}, u32[]{:S(2)}) collective-permute-start(bf16[4,16,2048]{2,1,0:T(8,128)(2,1)S(1)} %get-tuple-element.70), channel_id=1, source_target_pairs={{0,32},{32,0},{1,33},{33,1},{2,34},{34,2},{3,35},{35,3},{4,36},{36... | collective-permute-start | bytes 786440 | tf_op jit(solution)/shard_map/ppermute | solution.py:48
  122.8 10.0 %collective-permute-start.23 = (bf16[4,16,4096]{2,1,0:T(8,128)(2,1)S(1)}, bf16[4,16,4096]{2,1,0:T(8,128)(2,1)S(1)}, u32[]{:S(2)}, u32[]{:S(2)}) collective-permute-start(bf16[4,16,4096]{2,1,0:T(8,128)(2,1)S(1)} %all_to_all.10.q_ref), channel_id=1, source_target_pairs={{0,1},{1,0},{2,3},{3,2},{4,5},{5,4},{6,7},{7,6},{8,9},{9,8},{10,11... | collective-permute-start | bytes 1572872 | tf_op jit(solution)/shard_map/ppermute | solution.py:48
  122.9 9.9 %collective-permute-start.26 = (bf16[4,16,2048]{2,1,0:T(8,128)(2,1)S(1)}, bf16[4,16,2048]{2,1,0:T(8,128)(2,1)S(1)}, u32[]{:S(2)}, u32[]{:S(2)}) collective-permute-start(bf16[4,16,2048]{2,1,0:T(8,128)(2,1)S(1)} %get-tuple-element.69), channel_id=1, source_target_pairs={{0,38},{32,2},{2,32},{34,4},{4,34},{36,6},{6,36},{38,0},{1,39},{33... | collective-permute-start | bytes 786440 | tf_op jit(solution)/shard_map/ppermute | solution.py:55
  130.4 2.5 %collective-permute-start.25 = (bf16[4,16,2048]{2,1,0:T(8,128)(2,1)S(1)}, bf16[4,16,2048]{2,1,0:T(8,128)(2,1)S(1)}, u32[]{:S(2)}, u32[]{:S(2)}) collective-permute-start(bf16[4,16,2048]{2,1,0:T(8,128)(2,1)S(1)} %collective-permute-done.24.left_ref), channel_id=1, source_target_pairs={{0,1},{1,0},{2,3},{3,2},{4,5},{5,4},{6,7},{7,6},{8,9},{9,8},{10,11... | collective-permute-start | bytes 786440 | tf_op jit(solution)/shard_map/ppermute | solution.py:48
  132.9 1.5 collective-permute-start.27
  135.9 38.8 %copy-start.2 = (bf16[128,1024]{1,0:T(8,128)(2,1)S(1)}, bf16[128,1024]{1,0:T(8,128)(2,1)}, u32[]{:S(2)}) copy-start(bf16[128,1024]{1,0:T(8,128)(2,1)} %w_ref.1) | copy-start | bytes 786436
  135.9 1.4 collective-permute-start.28
  137.4 3.7 %collective-permute-start.29 = (f32[16,128]{1,0:T(8,128)S(1)}, f32[16,128]{1,0:T(8,128)S(1)}, u32[]{:S(2)}, u32[]{:S(2)}) collective-permute-start(f32[16,128]{1,0:T(8,128)S(1)} %slice_bitcast_fusion), channel_id=1, source_target_pairs={{0,32},{32,0},{1,33},{33,1},{2,34},{34,2},{3,35},{35,3},{4,36},{36... | collective-permute-start | bytes 24584 | tf_op jit(solution)/shard_map/ppermute | solution.py:48
  141.0 6.5 %collective-permute-start.30 = (f32[16,128]{1,0:T(8,128)S(1)}, f32[16,128]{1,0:T(8,128)S(1)}, u32[]{:S(2)}, u32[]{:S(2)}) collective-permute-start(f32[16,128]{1,0:T(8,128)S(1)} %fusion.t0_ref), channel_id=1, source_target_pairs={{0,2},{2,0},{4,6},{6,4},{1,3},{3,1},{5,7},{7,5},{8,10},{10,8},{12,... | collective-permute-start | bytes 24584 | tf_op jit(solution)/shard_map/ppermute | solution.py:294
  141.4 7.6 %collective-permute-start.31 = (f32[16,128]{1,0:T(8,128)S(1)}, f32[16,128]{1,0:T(8,128)S(1)}, u32[]{:S(2)}, u32[]{:S(2)}) collective-permute-start(f32[16,128]{1,0:T(8,128)S(1)} %fusion.t0_ref), channel_id=1, source_target_pairs={{0,4},{2,6},{4,0},{6,2},{1,5},{3,7},{5,1},{7,3},{8,12},{10,14},{12... | collective-permute-start | bytes 24584 | tf_op jit(solution)/shard_map/ppermute | solution.py:294
  143.5 5.8 %collective-permute-start.32 = (f32[16,128]{1,0:T(8,128)S(1)}, f32[16,128]{1,0:T(8,128)S(1)}, u32[]{:S(2)}, u32[]{:S(2)}) collective-permute-start(f32[16,128]{1,0:T(8,128)S(1)} %fusion.t0_ref), channel_id=1, source_target_pairs={{0,6},{2,4},{4,2},{6,0},{1,7},{3,5},{5,3},{7,1},{8,14},{10,12},{12... | collective-permute-start | bytes 24584 | tf_op jit(solution)/shard_map/ppermute | solution.py:294
  150.7 24.0 %all-to-all-start.1 = ((bf16[32,16,1152]{2,1,0:T(8,128)(2,1)}), bf16[32,16,1152]{2,1,0:T(8,128)(2,1)S(1)}, u32[]{:S(2)}, u32[]{:S(2)}) async-start(bf16[32,16,1152]{2,1,0:T(8,128)(2,1)} %get-tuple-element.61), calls=%async_computation.1 | async-start | bytes 2359296 | tf_op jit(solution)/shard_map/all_to_all | solution.py:412
  158.8 12.5 %collective-permute-start.33 = (f32[16,512]{1,0:T(8,128)S(1)}, f32[16,512]{1,0:T(8,128)S(1)}, u32[]{:S(2)}, u32[]{:S(2)}) collective-permute-start(f32[16,512]{1,0:T(8,128)S(1)} %get-tuple-element.64), channel_id=1, source_target_pairs={{0,32},{32,0},{1,33},{33,1},{2,34},{34,2},{3,35},{35,3},{4,36},{36... | collective-permute-start | bytes 98312 | tf_op jit(solution)/shard_map/ppermute | solution.py:48

commit v11 on v10

--- a/solution.py
+++ b/solution.py
@@ -188,14 +188,15 @@
                     b_own_ref, b_oth_ref, *refs):
     pieces, (up_own_ref, up_oth_ref, wire_ref, back_ref, grad_ref, own_ref, oth_ref) = refs[:5], refs[5:]
     l = lax.axis_index("l")
+    h = lax.axis_index("h")
     for i in range(16):
         j, e = (i // 2) % 4, i % 2
         here = slice(i * ROWS, (i + 1) * ROWS)
         if i < 8:
-            grad_ref[here, :] = (q_ref, qc_ref)[e][j]
+            grad_ref[here, :] = (q_ref, qc_ref)[e][(j + 4 - h) % 4]
         else:
-            grad_ref[here, :SIDE] = (left_ref, leftc_ref)[e][j]
-            grad_ref[here, SIDE:] = (right_ref, rightc_ref)[e][j]
+            grad_ref[here, :SIDE] = (left_ref, leftc_ref)[e][(j + 4 - h) % 4]
+            grad_ref[here, SIDE:] = (right_ref, rightc_ref)[e][(j + 5 - h + 2 * l) % 4]
     total = None
     for cols, piece in spans(pieces):
         term = dot(grad_ref[:, cols], piece[...])
@@ -379,7 +380,7 @@
     share = ((mine + steps[0]) + (steps[1] + steps[2])) * FF ** (-0.5)
     grad_rows = ((share - my_targets.astype(F32)) / TOK).astype(BF16)
 
-    q = lax.all_to_all(jnp.broadcast_to(grad_rows, (4, ROWS, MODEL_WIDTH)), "h", 0, 0, tiled=True)
+    q = jnp.stack([grad_rows] + [shift(grad_rows, "h", -j) for j in (1, 2, 3)])
     left = partner(q[:, :, :SIDE], "l")
     right = near_z(q[:, :, SIDE:])
     q_far, left_far, right_far = partner(q, "c"), partner(left, "c"), partner(right, "c")

time: 176 us -> 175 us (level)
  blocking collectives: 20 us -> 0 us
  waiting for transfers between devices: 82.9 us -> 94.4 us
  starting transfers between devices: 59 us -> 66.7 us
    all_to_all x1 -> x0, blocking collectives: 20 us -> none  [shards(): lax.all_to_all(jnp.broadcast_to(grad_rows, (4, ROWS, MODEL_WIDTH)), 'h',...]
    ppermute x17 -> x20, waiting for transfers between devices: 28.4 us -> 39.8 us  [shift(): return lax.ppermute(value, axis, [(i, (i + by) % n) for i in range(n)])]
    ppermute x17 -> x20, starting transfers between devices: 27.7 us -> 34.5 us  [shift(): return lax.ppermute(value, axis, [(i, (i + by) % n) for i in range(n)])]
    ppermute x3, waiting for transfers between devices: 1.71 us -> 4.2 us  [swap(): return lax.ppermute(value, 'h', [(i, i ^ mask) for i in range(4)])]
    ppermute x3, starting transfers between devices: 11.1 us -> 13.6 us  [near_z(): lax.ppermute(value, Z, [(place(z), place(z + 1 if z % 2 else z - 1)) for...]
  transfers between devices with their start and end apart: 35 -> 38, of which waited for: 22 -> 26; matrix products, arithmetic and copies ran while one was open for 1% -> 1% of each run, Pallas kernels for 2% -> 2%
where the time goes in v11:
time: 175 us
  waiting for transfers between devices  94.4 us (54%)
  starting transfers between devices  66.7 us (38%)
  Pallas kernels  8.71 us (5%)
  local copies, waits for them, and re-layouts  2.93 us (2%)
    ppermute x20, waiting for transfers between devices, shift(): return lax.ppermute(value, axis, [(i, (i + by) % n) for i in range(n)])  39.8 us
    ppermute x11, waiting for transfers between devices, partner(): return lax.ppermute(value, axis, [(0, 1), (1, 0)])  36.3 us
    ppermute x20, starting transfers between devices, shift(): return lax.ppermute(value, axis, [(i, (i + by) % n) for i in range(n)])  34.5 us
    ppermute x3, starting transfers between devices, near_z(): lax.ppermute(value, Z, [(place(z), place(z + 1 if z % 2 else z - 1)) for...  13.6 us
    ppermute x3, waiting for transfers between devices, near_z(): lax.ppermute(value, Z, [(place(z), place(z + 1 if z % 2 else z - 1)) for...  11.4 us
    pallas_call x12, Pallas kernels, call(): pl.pallas_call(kernel, out_shape=out_shape, in_specs=[vmem] * len(args) +...  8.58 us
    all_to_all x1, starting transfers between devices, shards(): wires = lax.all_to_all(wire, REP, 0, 0, tiled=True)  6.87 us
    ppermute x3, starting transfers between devices, swap(): return lax.ppermute(value, 'h', [(i, i ^ mask) for i in range(4)])  6.5 us
  transfers between devices with their start and end apart: 38, of which 26 were waited for; matrix products, arithmetic and copies ran while one was open for 1% of the time, Pallas kernels for 2%

profile of v11, /device:TPU:2, one launch (start us, length us, event | category | flops | bytes accessed | tf_op | source)
XLA Modules:
  0.0 174.9 jit_solution(1665434627135364777)
XLA Ops:
  3.5 2.0 %collective-permute-start.2 = (bf16[272,512]{1,0:T(8,128)(2,1)S(1)}, bf16[272,512]{1,0:T(8,128)(2,1)S(1)}, u32[]{:S(2)}, u32[]{:S(2)}) collective-permute-start(bf16[272,512]{1,0:T(8,128)(2,1)S(1)} %send.1.send_ref), channel_id=1, source_target_pairs={{0,32},{32,0},{1,33},{33,1},{2,34},{34,2},{3,35},{35,3},{4,36},{36... | collective-permute-start | bytes 835592 | tf_op jit(solution)/shard_map/ppermute | solution.py:48
  5.6 6.6 %collective-permute-done.2 = bf16[272,512]{1,0:T(8,128)(2,1)S(1)} collective-permute-done((bf16[272,512]{1,0:T(8,128)(2,1)S(1)}, bf16[272,512]{1,0:T(8,128)(2,1)S(1)}, u32[]{:S(2)}, u32[]{:S(2)}) %collective-permute-start.2) | collective-permute-done | bytes 278560 | tf_op jit(solution)/shard_map/ppermute | solution.py:48
  12.2 1.6 collective-permute-start.3
  13.9 1.7 collective-permute-start.10
  16.1 3.6 %collective-permute-done.3 = bf16[256,512]{1,0:T(8,128)(2,1)S(1)} collective-permute-done((bf16[256,512]{1,0:T(8,128)(2,1)S(1)}, bf16[256,512]{1,0:T(8,128)(2,1)S(1)}, u32[]{:S(2)}, u32[]{:S(2)}) %collective-permute-start.3) | collective-permute-done | bytes 262176 | tf_op jit(solution)/shard_map/ppermute | solution.py:44
  19.7 1.5 collective-permute-start.5
  21.2 3.0 %collective-permute-start.11 = (bf16[256,512]{1,0:T(8,128)(2,1)S(1)}, bf16[256,512]{1,0:T(8,128)(2,1)S(1)}, u32[]{:S(2)}, u32[]{:S(2)}) collective-permute-start(bf16[256,512]{1,0:T(8,128)(2,1)S(1)} %maximum_select_fusion.1), channel_id=1, source_target_pairs={{0,192},{64,0},{128,64},{192,128},{1,193},{65,1},{129,65},{193,129... | collective-permute-start | bytes 786440 | tf_op jit(solution)/shard_map/ppermute | solution.py:44
  24.6 5.5 %collective-permute-start = (bf16[80,4096]{1,0:T(8,128)(2,1)S(1)}, bf16[80,4096]{1,0:T(8,128)(2,1)S(1)}, u32[]{:S(2)}, u32[]{:S(2)}) collective-permute-start(bf16[80,4096]{1,0:T(8,128)(2,1)S(1)} %get-tuple-element.35), channel_id=1, source_target_pairs={{0,38},{32,2},{2,32},{34,4},{4,34},{36,6},{6,36},{38,0},{1,39},{33... | collective-permute-start | bytes 1966088 | tf_op jit(solution)/shard_map/ppermute | solution.py:55
  30.8 2.7 %collective-permute-start.7 = (bf16[1024,512]{1,0:T(8,128)(2,1)S(1)}, bf16[1024,512]{1,0:T(8,128)(2,1)S(1)}, u32[]{:S(2)}, u32[]{:S(2)}) collective-permute-start(bf16[1024,512]{1,0:T(8,128)(2,1)S(1)} %pad_maximum_fusion.refs_0_), channel_id=1, source_target_pairs={{0,192},{64,0},{128,64},{192,128},{1,193},{65,1},{129,65},{193,129... | collective-permute-start | bytes 3145736 | tf_op jit(solution)/shard_map/ppermute | solution.py:44
  33.6 1.3 collective-permute-start.13
  35.7 6.7 %collective-permute-done.oth_ref = bf16[80,4096]{1,0:T(8,128)(2,1)S(1)} collective-permute-done((bf16[80,4096]{1,0:T(8,128)(2,1)S(1)}, bf16[80,4096]{1,0:T(8,128)(2,1)S(1)}, u32[]{:S(2)}, u32[]{:S(2)}) %collective-permute-start) | collective-permute-done | bytes 655392 | tf_op jit(solution)/shard_map/ppermute | solution.py:55
  42.5 2.1 %collective-permute-done.1.oth_core_ref = bf16[80,4096]{1,0:T(8,128)(2,1)S(1)} collective-permute-done((bf16[80,4096]{1,0:T(8,128)(2,1)S(1)}, bf16[80,4096]{1,0:T(8,128)(2,1)S(1)}, u32[]{:S(2)}, u32[]{:S(2)}) %collective-permute-start.1) | collective-permute-done | bytes 655392 | tf_op jit(solution)/shard_map/ppermute | solution.py:48
  45.6 8.7 %collective-permute-done.6.refs_1_.below_ref = bf16[1024,512]{1,0:T(8,128)(2,1)S(1)} collective-permute-done((bf16[1024,512]{1,0:T(8,128)(2,1)S(1)}, bf16[1024,512]{1,0:T(8,128)(2,1)S(1)}, u32[]{:S(2)}, u32[]{:S(2)}) %collective-permute-start.6) | collective-permute-done | bytes 1048608 | tf_op jit(solution)/shard_map/ppermute | solution.py:44
  55.0 2.6 %collective-permute-start.9 = (bf16[512,512]{1,0:T(8,128)(2,1)S(1)}, bf16[512,512]{1,0:T(8,128)(2,1)S(1)}, u32[]{:S(2)}, u32[]{:S(2)}) collective-permute-start(bf16[512,512]{1,0:T(8,128)(2,1)S(1)} %get-tuple-element.46), channel_id=1, source_target_pairs={{0,192},{64,0},{128,64},{192,128},{1,193},{65,1},{129,65},{193,129... | collective-permute-start | bytes 1572872 | tf_op jit(solution)/shard_map/ppermute | solution.py:44
  57.7 1.3 collective-permute-start.15
  60.9 5.4 %collective-permute-done.8.low_ref = bf16[512,512]{1,0:T(8,128)(2,1)S(1)} collective-permute-done((bf16[512,512]{1,0:T(8,128)(2,1)S(1)}, bf16[512,512]{1,0:T(8,128)(2,1)S(1)}, u32[]{:S(2)}, u32[]{:S(2)}) %collective-permute-start.8) | collective-permute-done | bytes 524320 | tf_op jit(solution)/shard_map/ppermute | solution.py:44
  66.7 1.1 collective-permute-done.15.refs_3_
  68.8 1.3 output.1
  70.2 2.6 %collective-permute-done.17 = bf16[8,16,4096]{2,1,0:T(8,128)(2,1)S(1)} collective-permute-done((bf16[8,16,4096]{2,1,0:T(8,128)(2,1)S(1)}, bf16[8,16,4096]{2,1,0:T(8,128)(2,1)S(1)}, u32[]{:S(2)}, u32[]{:S(2)}) %collective-permute-start.17) | collective-permute-done | bytes 1048608 | tf_op jit(solution)/shard_map/ppermute | solution.py:48
  73.9 4.9 %collective-permute-start.19 = (bf16[4,16,2048]{2,1,0:T(8,128)(2,1)S(1)}, bf16[4,16,2048]{2,1,0:T(8,128)(2,1)S(1)}, u32[]{:S(2)}, u32[]{:S(2)}) collective-permute-start(bf16[4,16,2048]{2,1,0:T(8,128)(2,1)S(1)} %get-tuple-element.67), channel_id=1, source_target_pairs={{0,38},{32,2},{2,32},{34,4},{4,34},{36,6},{6,36},{38,0},{1,39},{33... | collective-permute-start | bytes 786440 | tf_op jit(solution)/shard_map/ppermute | solution.py:55
  78.9 2.7 %collective-permute-done.18.left_ref = bf16[4,16,2048]{2,1,0:T(8,128)(2,1)S(1)} collective-permute-done((bf16[4,16,2048]{2,1,0:T(8,128)(2,1)S(1)}, bf16[4,16,2048]{2,1,0:T(8,128)(2,1)S(1)}, u32[]{:S(2)}, u32[]{:S(2)}) %collective-permute-start.18) | collective-permute-done | bytes 262176 | tf_op jit(solution)/shard_map/ppermute | solution.py:48
  81.7 3.5 %collective-permute-done.19.right_ref = bf16[4,16,2048]{2,1,0:T(8,128)(2,1)S(1)} collective-permute-done((bf16[4,16,2048]{2,1,0:T(8,128)(2,1)S(1)}, bf16[4,16,2048]{2,1,0:T(8,128)(2,1)S(1)}, u32[]{:S(2)}, u32[]{:S(2)}) %collective-permute-start.19) | collective-permute-done | bytes 262176 | tf_op jit(solution)/shard_map/ppermute | solution.py:55
  85.3 1.4 collective-permute-start.20
  86.7 3.2 %collective-permute-start.21 = (bf16[16,4096]{1,0:T(8,128)(2,1)S(1)}, bf16[16,4096]{1,0:T(8,128)(2,1)S(1)}, u32[]{:S(2)}, u32[]{:S(2)}) collective-permute-start(bf16[16,4096]{1,0:T(8,128)(2,1)S(1)} %get-tuple-element.55), channel_id=1, source_target_pairs={{0,4},{2,6},{4,0},{6,2},{1,5},{3,7},{5,1},{7,3},{8,12},{10,14},{12... | collective-permute-start | bytes 393224 | tf_op jit(solution)/shard_map/ppermute | solution.py:44
  89.9 3.9 %collective-permute-start.22 = (bf16[16,4096]{1,0:T(8,128)(2,1)S(1)}, bf16[16,4096]{1,0:T(8,128)(2,1)S(1)}, u32[]{:S(2)}, u32[]{:S(2)}) collective-permute-start(bf16[16,4096]{1,0:T(8,128)(2,1)S(1)} %get-tuple-element.56), channel_id=1, source_target_pairs={{0,6},{2,0},{4,2},{6,4},{1,7},{3,1},{5,3},{7,5},{8,14},{10,8},{12,... | collective-permute-start | bytes 393224 | tf_op jit(solution)/shard_map/ppermute | solution.py:44
  93.9 5.2 %collective-permute-done.20 = bf16[16,4096]{1,0:T(8,128)(2,1)S(1)} collective-permute-done((bf16[16,4096]{1,0:T(8,128)(2,1)S(1)}, bf16[16,4096]{1,0:T(8,128)(2,1)S(1)}, u32[]{:S(2)}, u32[]{:S(2)}) %collective-permute-start.20) | collective-permute-done | bytes 131104 | tf_op jit(solution)/shard_map/ppermute | solution.py:44
  99.1 3.4 %collective-permute-done.22 = bf16[16,4096]{1,0:T(8,128)(2,1)S(1)} collective-permute-done((bf16[16,4096]{1,0:T(8,128)(2,1)S(1)}, bf16[16,4096]{1,0:T(8,128)(2,1)S(1)}, u32[]{:S(2)}, u32[]{:S(2)}) %collective-permute-start.22) | collective-permute-done | bytes 131104 | tf_op jit(solution)/shard_map/ppermute | solution.py:44
  102.6 4.3 %collective-permute-start.23 = (bf16[16,4096]{1,0:T(8,128)(2,1)S(1)}, bf16[16,4096]{1,0:T(8,128)(2,1)S(1)}, u32[]{:S(2)}, u32[]{:S(2)}) collective-permute-start(bf16[16,4096]{1,0:T(8,128)(2,1)S(1)} %multiply_convert_fusion), channel_id=1, source_target_pairs={{0,6},{2,0},{4,2},{6,4},{1,7},{3,1},{5,3},{7,5},{8,14},{10,8},{12,... | collective-permute-start | bytes 393224 | tf_op jit(solution)/shard_map/ppermute | solution.py:44
  106.9 2.0 %collective-permute-start.24 = (bf16[16,4096]{1,0:T(8,128)(2,1)S(1)}, bf16[16,4096]{1,0:T(8,128)(2,1)S(1)}, u32[]{:S(2)}, u32[]{:S(2)}) collective-permute-start(bf16[16,4096]{1,0:T(8,128)(2,1)S(1)} %multiply_convert_fusion), channel_id=1, source_target_pairs={{0,4},{2,6},{4,0},{6,2},{1,5},{3,7},{5,1},{7,3},{8,12},{10,14},{12... | collective-permute-start | bytes 393224 | tf_op jit(solution)/shard_map/ppermute | solution.py:44
  109.4 4.4 %collective-permute-done.23 = bf16[16,4096]{1,0:T(8,128)(2,1)S(1)} collective-permute-done((bf16[16,4096]{1,0:T(8,128)(2,1)S(1)}, bf16[16,4096]{1,0:T(8,128)(2,1)S(1)}, u32[]{:S(2)}, u32[]{:S(2)}) %collective-permute-start.23) | collective-permute-done | bytes 131104 | tf_op jit(solution)/shard_map/ppermute | solution.py:44
  113.8 6.2 %collective-permute-done.24 = bf16[16,4096]{1,0:T(8,128)(2,1)S(1)} collective-permute-done((bf16[16,4096]{1,0:T(8,128)(2,1)S(1)}, bf16[16,4096]{1,0:T(8,128)(2,1)S(1)}, u32[]{:S(2)}, u32[]{:S(2)}) %collective-permute-start.24) | collective-permute-done | bytes 131104 | tf_op jit(solution)/shard_map/ppermute | solution.py:44
  121.1 3.1 %collective-permute-start.29 = (bf16[4,16,2048]{2,1,0:T(8,128)(2,1)S(1)}, bf16[4,16,2048]{2,1,0:T(8,128)(2,1)S(1)}, u32[]{:S(2)}, u32[]{:S(2)}) collective-permute-start(bf16[4,16,2048]{2,1,0:T(8,128)(2,1)S(1)} %get-tuple-element.69), channel_id=1, source_target_pairs={{0,38},{32,2},{2,32},{34,4},{4,34},{36,6},{6,36},{38,0},{1,39},{33... | collective-permute-start | bytes 786440 | tf_op jit(solution)/shard_map/ppermute | solution.py:55
  124.2 5.5 %collective-permute-done.27.left_ref = bf16[4,16,2048]{2,1,0:T(8,128)(2,1)S(1)} collective-permute-done((bf16[4,16,2048]{2,1,0:T(8,128)(2,1)S(1)}, bf16[4,16,2048]{2,1,0:T(8,128)(2,1)S(1)}, u32[]{:S(2)}, u32[]{:S(2)}) %collective-permute-start.27) | collective-permute-done | bytes 262176 | tf_op jit(solution)/shard_map/ppermute | solution.py:48
  129.7 1.2 collective-permute-done.29.right_ref
  131.2 1.2 collective-permute-done.30.rightc_ref
  132.4 1.5 backward.1
  135.7 3.1 %collective-permute-done.32 = f32[16,128]{1,0:T(8,128)S(1)} collective-permute-done((f32[16,128]{1,0:T(8,128)S(1)}, f32[16,128]{1,0:T(8,128)S(1)}, u32[]{:S(2)}, u32[]{:S(2)}) %collective-permute-start.32) | collective-permute-done | bytes 8224 | tf_op jit(solution)/shard_map/ppermute | solution.py:48
  138.8 1.1 collective-permute-start.33
  140.0 3.8 %collective-permute-start.34 = (f32[16,128]{1,0:T(8,128)S(1)}, f32[16,128]{1,0:T(8,128)S(1)}, u32[]{:S(2)}, u32[]{:S(2)}) collective-permute-start(f32[16,128]{1,0:T(8,128)S(1)} %fusion.t0_ref), channel_id=1, source_target_pairs={{0,4},{2,6},{4,0},{6,2},{1,5},{3,7},{5,1},{7,3},{8,12},{10,14},{12... | collective-permute-start | bytes 24584 | tf_op jit(solution)/shard_map/ppermute | solution.py:295
  143.7 1.6 collective-permute-start.35
  145.3 2.2 %collective-permute-done.34.t2_ref = f32[16,128]{1,0:T(8,128)S(1)} collective-permute-done((f32[16,128]{1,0:T(8,128)S(1)}, f32[16,128]{1,0:T(8,128)S(1)}, u32[]{:S(2)}, u32[]{:S(2)}) %collective-permute-start.34) | collective-permute-done | bytes 8224 | tf_op jit(solution)/shard_map/ppermute | solution.py:295
  147.5 2.0 %collective-permute-done.35.t3_ref = f32[16,128]{1,0:T(8,128)S(1)} collective-permute-done((f32[16,128]{1,0:T(8,128)S(1)}, f32[16,128]{1,0:T(8,128)S(1)}, u32[]{:S(2)}, u32[]{:S(2)}) %collective-permute-start.35) | collective-permute-done | bytes 8224 | tf_op jit(solution)/shard_map/ppermute | solution.py:295
  149.5 1.4 down.1
  150.9 6.9 %all-to-all-start = ((bf16[32,16,1152]{2,1,0:T(8,128)(2,1)}), bf16[32,16,1152]{2,1,0:T(8,128)(2,1)S(1)}, u32[]{:S(2)}, u32[]{:S(2)}) async-start(bf16[32,16,1152]{2,1,0:T(8,128)(2,1)} %get-tuple-element.61), calls=%async_computation | async-start | bytes 2359296 | tf_op jit(solution)/shard_map/all_to_all | solution.py:413
  157.8 1.6 collective-permute-start.36
  159.4 11.1 %collective-permute-done.36 = f32[16,512]{1,0:T(8,128)S(1)} collective-permute-done((f32[16,512]{1,0:T(8,128)S(1)}, f32[16,512]{1,0:T(8,128)S(1)}, u32[]{:S(2)}, u32[]{:S(2)}) %collective-permute-start.36) | collective-permute-done | bytes 32800 | tf_op jit(solution)/shard_map/ppermute | solution.py:48
  171.1 2.7 %all-to-all-done.wire_ref = bf16[32,16,1152]{2,1,0:T(8,128)(2,1)S(1)} async-done(((bf16[32,16,1152]{2,1,0:T(8,128)(2,1)}), bf16[32,16,1152]{2,1,0:T(8,128)(2,1)S(1)}, u32[]{:S(2)}, u32[]{:S(2)}) %all-to-all-start) | async-done | bytes 1179680 | tf_op jit(solution)/shard_map/all_to_all | solution.py:413
  173.8 1.1 merge.1
  (72 shorter events, 16.5 us)
Async XLA Ops:
  0.6 23.6 %copy-start = (bf16[128,4096]{1,0:T(8,128)(2,1)S(1)}, bf16[128,4096]{1,0:T(8,128)(2,1)}, u32[]{:S(2)}) copy-start(bf16[128,4096]{1,0:T(8,128)(2,1)} %x_ref.1) | copy-start | bytes 3145732
  0.6 1.0 copy-start.1
  1.7 0.9 copy-start.3
  2.6 0.8 copy-start.6
  3.4 20.8 %copy-start.5 = (bf16[1,16,4096]{2,1,0:T(8,128)(2,1)S(1)}, bf16[1,16,4096]{2,1,0:T(8,128)(2,1)}, u32[]{:S(2)}) copy-start(bf16[1,16,4096]{2,1,0:T(8,128)(2,1)} %param.10) | copy-start | bytes 393220
  3.5 8.7 %collective-permute-start.2 = (bf16[272,512]{1,0:T(8,128)(2,1)S(1)}, bf16[272,512]{1,0:T(8,128)(2,1)S(1)}, u32[]{:S(2)}, u32[]{:S(2)}) collective-permute-start(bf16[272,512]{1,0:T(8,128)(2,1)S(1)} %send.1.send_ref), channel_id=1, source_target_pairs={{0,32},{32,0},{1,33},{33,1},{2,34},{34,2},{3,35},{35,3},{4,36},{36... | collective-permute-start | bytes 835592 | tf_op jit(solution)/shard_map/ppermute | solution.py:48
  12.2 7.4 %collective-permute-start.3 = (bf16[256,512]{1,0:T(8,128)(2,1)S(1)}, bf16[256,512]{1,0:T(8,128)(2,1)S(1)}, u32[]{:S(2)}, u32[]{:S(2)}) collective-permute-start(bf16[256,512]{1,0:T(8,128)(2,1)S(1)} %maximum_select_fusion), channel_id=1, source_target_pairs={{0,8},{8,16},{16,24},{24,0},{1,9},{9,17},{17,25},{25,1},{2,10},{10... | collective-permute-start | bytes 786440 | tf_op jit(solution)/shard_map/ppermute | solution.py:44
  13.9 10.3 %collective-permute-start.10 = (bf16[256,512]{1,0:T(8,128)(2,1)S(1)}, bf16[256,512]{1,0:T(8,128)(2,1)S(1)}, u32[]{:S(2)}, u32[]{:S(2)}) collective-permute-start(bf16[256,512]{1,0:T(8,128)(2,1)S(1)} %maximum_select_fusion.1), channel_id=1, source_target_pairs={{0,64},{64,128},{128,192},{192,0},{1,65},{65,129},{129,193},{193,1... | collective-permute-start | bytes 786440 | tf_op jit(solution)/shard_map/ppermute | solution.py:44
  15.5 14.6 %collective-permute-start.4 = (bf16[256,512]{1,0:T(8,128)(2,1)S(1)}, bf16[256,512]{1,0:T(8,128)(2,1)S(1)}, u32[]{:S(2)}, u32[]{:S(2)}) collective-permute-start(bf16[256,512]{1,0:T(8,128)(2,1)S(1)} %maximum_select_fusion), channel_id=1, source_target_pairs={{0,24},{8,0},{16,8},{24,16},{1,25},{9,1},{17,9},{25,17},{2,26},{10... | collective-permute-start | bytes 786440 | tf_op jit(solution)/shard_map/ppermute | solution.py:44
  19.7 10.4 %collective-permute-start.5 = (bf16[256,512]{1,0:T(8,128)(2,1)S(1)}, bf16[256,512]{1,0:T(8,128)(2,1)S(1)}, u32[]{:S(2)}, u32[]{:S(2)}) collective-permute-start(bf16[256,512]{1,0:T(8,128)(2,1)S(1)} %collective-permute-done.3), channel_id=1, source_target_pairs={{0,8},{8,16},{16,24},{24,0},{1,9},{9,17},{17,25},{25,1},{2,10},{10... | collective-permute-start | bytes 786440 | tf_op jit(solution)/shard_map/ppermute | solution.py:44
  21.2 12.4 %collective-permute-start.11 = (bf16[256,512]{1,0:T(8,128)(2,1)S(1)}, bf16[256,512]{1,0:T(8,128)(2,1)S(1)}, u32[]{:S(2)}, u32[]{:S(2)}) collective-permute-start(bf16[256,512]{1,0:T(8,128)(2,1)S(1)} %maximum_select_fusion.1), channel_id=1, source_target_pairs={{0,192},{64,0},{128,64},{192,128},{1,193},{65,1},{129,65},{193,129... | collective-permute-start | bytes 786440 | tf_op jit(solution)/shard_map/ppermute | solution.py:44
  24.2 9.4 %collective-permute-start.12 = (bf16[256,512]{1,0:T(8,128)(2,1)S(1)}, bf16[256,512]{1,0:T(8,128)(2,1)S(1)}, u32[]{:S(2)}, u32[]{:S(2)}) collective-permute-start(bf16[256,512]{1,0:T(8,128)(2,1)S(1)} %collective-permute-done.10), channel_id=1, source_target_pairs={{0,64},{64,128},{128,192},{192,0},{1,65},{65,129},{129,193},{193,1... | collective-permute-start | bytes 786440 | tf_op jit(solution)/shard_map/ppermute | solution.py:44
  24.6 17.9 %collective-permute-start = (bf16[80,4096]{1,0:T(8,128)(2,1)S(1)}, bf16[80,4096]{1,0:T(8,128)(2,1)S(1)}, u32[]{:S(2)}, u32[]{:S(2)}) collective-permute-start(bf16[80,4096]{1,0:T(8,128)(2,1)S(1)} %get-tuple-element.35), channel_id=1, source_target_pairs={{0,38},{32,2},{2,32},{34,4},{4,34},{36,6},{6,36},{38,0},{1,39},{33... | collective-permute-start | bytes 1966088 | tf_op jit(solution)/shard_map/ppermute | solution.py:55
  30.2 24.1 %collective-permute-start.6 = (bf16[1024,512]{1,0:T(8,128)(2,1)S(1)}, bf16[1024,512]{1,0:T(8,128)(2,1)S(1)}, u32[]{:S(2)}, u32[]{:S(2)}) collective-permute-start(bf16[1024,512]{1,0:T(8,128)(2,1)S(1)} %pad_maximum_fusion.refs_0_), channel_id=1, source_target_pairs={{0,64},{64,128},{128,192},{192,0},{1,65},{65,129},{129,193},{193,1... | collective-permute-start | bytes 3145736 | tf_op jit(solution)/shard_map/ppermute | solution.py:44
  30.8 23.4 %collective-permute-start.7 = (bf16[1024,512]{1,0:T(8,128)(2,1)S(1)}, bf16[1024,512]{1,0:T(8,128)(2,1)S(1)}, u32[]{:S(2)}, u32[]{:S(2)}) collective-permute-start(bf16[1024,512]{1,0:T(8,128)(2,1)S(1)} %pad_maximum_fusion.refs_0_), channel_id=1, source_target_pairs={{0,192},{64,0},{128,64},{192,128},{1,193},{65,1},{129,65},{193,129... | collective-permute-start | bytes 3145736 | tf_op jit(solution)/shard_map/ppermute | solution.py:44
  33.6 24.0 %collective-permute-start.13 = (bf16[1024,512]{1,0:T(8,128)(2,1)S(1)}, bf16[1024,512]{1,0:T(8,128)(2,1)S(1)}, u32[]{:S(2)}, u32[]{:S(2)}) collective-permute-start(bf16[1024,512]{1,0:T(8,128)(2,1)S(1)} %pad_maximum_fusion.1.refs_0_), channel_id=1, source_target_pairs={{0,8},{8,16},{16,24},{24,0},{1,9},{9,17},{17,25},{25,1},{2,10},{10... | collective-permute-start | bytes 3145736 | tf_op jit(solution)/shard_map/ppermute | solution.py:44
  34.9 22.7 %collective-permute-start.14 = (bf16[1024,512]{1,0:T(8,128)(2,1)S(1)}, bf16[1024,512]{1,0:T(8,128)(2,1)S(1)}, u32[]{:S(2)}, u32[]{:S(2)}) collective-permute-start(bf16[1024,512]{1,0:T(8,128)(2,1)S(1)} %pad_maximum_fusion.1.refs_0_), channel_id=1, source_target_pairs={{0,24},{8,0},{16,8},{24,16},{1,25},{9,1},{17,9},{25,17},{2,26},{10... | collective-permute-start | bytes 3145736 | tf_op jit(solution)/shard_map/ppermute | solution.py:44
  42.5 2.1 %collective-permute-start.1 = (bf16[80,4096]{1,0:T(8,128)(2,1)S(1)}, bf16[80,4096]{1,0:T(8,128)(2,1)S(1)}, u32[]{:S(2)}, u32[]{:S(2)}) collective-permute-start(bf16[80,4096]{1,0:T(8,128)(2,1)S(1)} %collective-permute-done.oth_ref), channel_id=1, source_target_pairs={{0,1},{1,0},{2,3},{3,2},{4,5},{5,4},{6,7},{7,6},{8,9},{9,8},{10,11... | collective-permute-start | bytes 1966088 | tf_op jit(solution)/shard_map/ppermute | solution.py:48
  54.3 11.9 %collective-permute-start.8 = (bf16[512,512]{1,0:T(8,128)(2,1)S(1)}, bf16[512,512]{1,0:T(8,128)(2,1)S(1)}, u32[]{:S(2)}, u32[]{:S(2)}) collective-permute-start(bf16[512,512]{1,0:T(8,128)(2,1)S(1)} %get-tuple-element.45), channel_id=1, source_target_pairs={{0,64},{64,128},{128,192},{192,0},{1,65},{65,129},{129,193},{193,1... | collective-permute-start | bytes 1572872 | tf_op jit(solution)/shard_map/ppermute | solution.py:44
  55.0 11.3 %collective-permute-start.9 = (bf16[512,512]{1,0:T(8,128)(2,1)S(1)}, bf16[512,512]{1,0:T(8,128)(2,1)S(1)}, u32[]{:S(2)}, u32[]{:S(2)}) collective-permute-start(bf16[512,512]{1,0:T(8,128)(2,1)S(1)} %get-tuple-element.46), channel_id=1, source_target_pairs={{0,192},{64,0},{128,64},{192,128},{1,193},{65,1},{129,65},{193,129... | collective-permute-start | bytes 1572872 | tf_op jit(solution)/shard_map/ppermute | solution.py:44
  57.7 10.2 %collective-permute-start.15 = (bf16[512,512]{1,0:T(8,128)(2,1)S(1)}, bf16[512,512]{1,0:T(8,128)(2,1)S(1)}, u32[]{:S(2)}, u32[]{:S(2)}) collective-permute-start(bf16[512,512]{1,0:T(8,128)(2,1)S(1)} %get-tuple-element.49), channel_id=1, source_target_pairs={{0,8},{8,16},{16,24},{24,0},{1,9},{9,17},{17,25},{25,1},{2,10},{10... | collective-permute-start | bytes 1572872 | tf_op jit(solution)/shard_map/ppermute | solution.py:44
  59.0 9.8 %collective-permute-start.16 = (bf16[512,512]{1,0:T(8,128)(2,1)S(1)}, bf16[512,512]{1,0:T(8,128)(2,1)S(1)}, u32[]{:S(2)}, u32[]{:S(2)}) collective-permute-start(bf16[512,512]{1,0:T(8,128)(2,1)S(1)} %get-tuple-element.50), channel_id=1, source_target_pairs={{0,24},{8,0},{16,8},{24,16},{1,25},{9,1},{17,9},{25,17},{2,26},{10... | collective-permute-start | bytes 1572872 | tf_op jit(solution)/shard_map/ppermute | solution.py:44
  70.1 2.7 %collective-permute-start.17 = (bf16[8,16,4096]{2,1,0:T(8,128)(2,1)S(1)}, bf16[8,16,4096]{2,1,0:T(8,128)(2,1)S(1)}, u32[]{:S(2)}, u32[]{:S(2)}) collective-permute-start(bf16[8,16,4096]{2,1,0:T(8,128)(2,1)S(1)} %get-tuple-element.52), channel_id=1, source_target_pairs={{0,1},{1,0},{2,3},{3,2},{4,5},{5,4},{6,7},{7,6},{8,9},{9,8},{10,11... | collective-permute-start | bytes 3145736 | tf_op jit(solution)/shard_map/ppermute | solution.py:48
  73.2 20.6 %copy-start.4 = (bf16[128,4096]{1,0:T(8,128)(2,1)S(1)}, bf16[128,4096]{1,0:T(8,128)(2,1)}, u32[]{:S(2)}) copy-start(bf16[128,4096]{1,0:T(8,128)(2,1)} %targets_ref.1) | copy-start | bytes 3145732
  73.2 8.4 %collective-permute-start.18 = (bf16[4,16,2048]{2,1,0:T(8,128)(2,1)S(1)}, bf16[4,16,2048]{2,1,0:T(8,128)(2,1)S(1)}, u32[]{:S(2)}, u32[]{:S(2)}) collective-permute-start(bf16[4,16,2048]{2,1,0:T(8,128)(2,1)S(1)} %get-tuple-element.68), channel_id=1, source_target_pairs={{0,32},{32,0},{1,33},{33,1},{2,34},{34,2},{3,35},{35,3},{4,36},{36... | collective-permute-start | bytes 786440 | tf_op jit(solution)/shard_map/ppermute | solution.py:48
  73.9 11.3 %collective-permute-start.19 = (bf16[4,16,2048]{2,1,0:T(8,128)(2,1)S(1)}, bf16[4,16,2048]{2,1,0:T(8,128)(2,1)S(1)}, u32[]{:S(2)}, u32[]{:S(2)}) collective-permute-start(bf16[4,16,2048]{2,1,0:T(8,128)(2,1)S(1)} %get-tuple-element.67), channel_id=1, source_target_pairs={{0,38},{32,2},{2,32},{34,4},{4,34},{36,6},{6,36},{38,0},{1,39},{33... | collective-permute-start | bytes 786440 | tf_op jit(solution)/shard_map/ppermute | solution.py:55
  85.3 13.8 %collective-permute-start.20 = (bf16[16,4096]{1,0:T(8,128)(2,1)S(1)}, bf16[16,4096]{1,0:T(8,128)(2,1)S(1)}, u32[]{:S(2)}, u32[]{:S(2)}) collective-permute-start(bf16[16,4096]{1,0:T(8,128)(2,1)S(1)} %get-tuple-element.54), channel_id=1, source_target_pairs={{0,2},{2,4},{4,6},{6,0},{1,3},{3,5},{5,7},{7,1},{8,10},{10,12},{12... | collective-permute-start | bytes 393224 | tf_op jit(solution)/shard_map/ppermute | solution.py:44
  86.7 12.4 %collective-permute-start.21 = (bf16[16,4096]{1,0:T(8,128)(2,1)S(1)}, bf16[16,4096]{1,0:T(8,128)(2,1)S(1)}, u32[]{:S(2)}, u32[]{:S(2)}) collective-permute-start(bf16[16,4096]{1,0:T(8,128)(2,1)S(1)} %get-tuple-element.55), channel_id=1, source_target_pairs={{0,4},{2,6},{4,0},{6,2},{1,5},{3,7},{5,1},{7,3},{8,12},{10,14},{12... | collective-permute-start | bytes 393224 | tf_op jit(solution)/shard_map/ppermute | solution.py:44
  89.9 12.6 %collective-permute-start.22 = (bf16[16,4096]{1,0:T(8,128)(2,1)S(1)}, bf16[16,4096]{1,0:T(8,128)(2,1)S(1)}, u32[]{:S(2)}, u32[]{:S(2)}) collective-permute-start(bf16[16,4096]{1,0:T(8,128)(2,1)S(1)} %get-tuple-element.56), channel_id=1, source_target_pairs={{0,6},{2,0},{4,2},{6,4},{1,7},{3,1},{5,3},{7,5},{8,14},{10,8},{12,... | collective-permute-start | bytes 393224 | tf_op jit(solution)/shard_map/ppermute | solution.py:44
  102.6 11.2 %collective-permute-start.23 = (bf16[16,4096]{1,0:T(8,128)(2,1)S(1)}, bf16[16,4096]{1,0:T(8,128)(2,1)S(1)}, u32[]{:S(2)}, u32[]{:S(2)}) collective-permute-start(bf16[16,4096]{1,0:T(8,128)(2,1)S(1)} %multiply_convert_fusion), channel_id=1, source_target_pairs={{0,6},{2,0},{4,2},{6,4},{1,7},{3,1},{5,3},{7,5},{8,14},{10,8},{12,... | collective-permute-start | bytes 393224 | tf_op jit(solution)/shard_map/ppermute | solution.py:44
  106.9 13.1 %collective-permute-start.24 = (bf16[16,4096]{1,0:T(8,128)(2,1)S(1)}, bf16[16,4096]{1,0:T(8,128)(2,1)S(1)}, u32[]{:S(2)}, u32[]{:S(2)}) collective-permute-start(bf16[16,4096]{1,0:T(8,128)(2,1)S(1)} %multiply_convert_fusion), channel_id=1, source_target_pairs={{0,4},{2,6},{4,0},{6,2},{1,5},{3,7},{5,1},{7,3},{8,12},{10,14},{12... | collective-permute-start | bytes 393224 | tf_op jit(solution)/shard_map/ppermute | solution.py:44
  108.9 11.8 %collective-permute-start.25 = (bf16[16,4096]{1,0:T(8,128)(2,1)S(1)}, bf16[16,4096]{1,0:T(8,128)(2,1)S(1)}, u32[]{:S(2)}, u32[]{:S(2)}) collective-permute-start(bf16[16,4096]{1,0:T(8,128)(2,1)S(1)} %multiply_convert_fusion), channel_id=1, source_target_pairs={{0,2},{2,4},{4,6},{6,0},{1,3},{3,5},{5,7},{7,1},{8,10},{10,12},{12... | collective-permute-start | bytes 393224 | tf_op jit(solution)/shard_map/ppermute | solution.py:44
  120.9 10.0 %collective-permute-start.26 = (bf16[4,16,4096]{2,1,0:T(8,128)(2,1)S(1)}, bf16[4,16,4096]{2,1,0:T(8,128)(2,1)S(1)}, u32[]{:S(2)}, u32[]{:S(2)}) collective-permute-start(bf16[4,16,4096]{2,1,0:T(8,128)(2,1)S(1)} %pad_maximum_fusion.2.q_ref), channel_id=1, source_target_pairs={{0,1},{1,0},{2,3},{3,2},{4,5},{5,4},{6,7},{7,6},{8,9},{9,8},{10,11... | collective-permute-start | bytes 1572872 | tf_op jit(solution)/shard_map/ppermute | solution.py:48
  121.0 8.7 %collective-permute-start.27 = (bf16[4,16,2048]{2,1,0:T(8,128)(2,1)S(1)}, bf16[4,16,2048]{2,1,0:T(8,128)(2,1)S(1)}, u32[]{:S(2)}, u32[]{:S(2)}) collective-permute-start(bf16[4,16,2048]{2,1,0:T(8,128)(2,1)S(1)} %get-tuple-element.70), channel_id=1, source_target_pairs={{0,32},{32,0},{1,33},{33,1},{2,34},{34,2},{3,35},{35,3},{4,36},{36... | collective-permute-start | bytes 786440 | tf_op jit(solution)/shard_map/ppermute | solution.py:48
  121.1 9.8 %collective-permute-start.29 = (bf16[4,16,2048]{2,1,0:T(8,128)(2,1)S(1)}, bf16[4,16,2048]{2,1,0:T(8,128)(2,1)S(1)}, u32[]{:S(2)}, u32[]{:S(2)}) collective-permute-start(bf16[4,16,2048]{2,1,0:T(8,128)(2,1)S(1)} %get-tuple-element.69), channel_id=1, source_target_pairs={{0,38},{32,2},{2,32},{34,4},{4,34},{36,6},{6,36},{38,0},{1,39},{33... | collective-permute-start | bytes 786440 | tf_op jit(solution)/shard_map/ppermute | solution.py:55
  129.7 1.5 collective-permute-start.28
  130.9 1.5 collective-permute-start.30
  133.9 39.8 %copy-start.2 = (bf16[128,1024]{1,0:T(8,128)(2,1)S(1)}, bf16[128,1024]{1,0:T(8,128)(2,1)}, u32[]{:S(2)}) copy-start(bf16[128,1024]{1,0:T(8,128)(2,1)} %w_ref.1) | copy-start | bytes 786436
  133.9 1.2 collective-permute-start.31
  135.2 3.7 %collective-permute-start.32 = (f32[16,128]{1,0:T(8,128)S(1)}, f32[16,128]{1,0:T(8,128)S(1)}, u32[]{:S(2)}, u32[]{:S(2)}) collective-permute-start(f32[16,128]{1,0:T(8,128)S(1)} %slice_bitcast_fusion), channel_id=1, source_target_pairs={{0,32},{32,0},{1,33},{33,1},{2,34},{34,2},{3,35},{35,3},{4,36},{36... | collective-permute-start | bytes 24584 | tf_op jit(solution)/shard_map/ppermute | solution.py:48
  138.8 6.5 %collective-permute-start.33 = (f32[16,128]{1,0:T(8,128)S(1)}, f32[16,128]{1,0:T(8,128)S(1)}, u32[]{:S(2)}, u32[]{:S(2)}) collective-permute-start(f32[16,128]{1,0:T(8,128)S(1)} %fusion.t0_ref), channel_id=1, source_target_pairs={{0,2},{2,0},{4,6},{6,4},{1,3},{3,1},{5,7},{7,5},{8,10},{10,8},{12,... | collective-permute-start | bytes 24584 | tf_op jit(solution)/shard_map/ppermute | solution.py:295
  140.0 7.6 %collective-permute-start.34 = (f32[16,128]{1,0:T(8,128)S(1)}, f32[16,128]{1,0:T(8,128)S(1)}, u32[]{:S(2)}, u32[]{:S(2)}) collective-permute-start(f32[16,128]{1,0:T(8,128)S(1)} %fusion.t0_ref), channel_id=1, source_target_pairs={{0,4},{2,6},{4,0},{6,2},{1,5},{3,7},{5,1},{7,3},{8,12},{10,14},{12... | collective-permute-start | bytes 24584 | tf_op jit(solution)/shard_map/ppermute | solution.py:295
  143.7 5.8 %collective-permute-start.35 = (f32[16,128]{1,0:T(8,128)S(1)}, f32[16,128]{1,0:T(8,128)S(1)}, u32[]{:S(2)}, u32[]{:S(2)}) collective-permute-start(f32[16,128]{1,0:T(8,128)S(1)} %fusion.t0_ref), channel_id=1, source_target_pairs={{0,6},{2,4},{4,2},{6,0},{1,7},{3,5},{5,3},{7,1},{8,14},{10,12},{12... | collective-permute-start | bytes 24584 | tf_op jit(solution)/shard_map/ppermute | solution.py:295
  150.9 22.8 %all-to-all-start = ((bf16[32,16,1152]{2,1,0:T(8,128)(2,1)}), bf16[32,16,1152]{2,1,0:T(8,128)(2,1)S(1)}, u32[]{:S(2)}, u32[]{:S(2)}) async-start(bf16[32,16,1152]{2,1,0:T(8,128)(2,1)} %get-tuple-element.61), calls=%async_computation | async-start | bytes 2359296 | tf_op jit(solution)/shard_map/all_to_all | solution.py:413
  157.8 12.6 %collective-permute-start.36 = (f32[16,512]{1,0:T(8,128)S(1)}, f32[16,512]{1,0:T(8,128)S(1)}, u32[]{:S(2)}, u32[]{:S(2)}) collective-permute-start(f32[16,512]{1,0:T(8,128)S(1)} %get-tuple-element.64), channel_id=1, source_target_pairs={{0,32},{32,0},{1,33},{33,1},{2,34},{34,2},{3,35},{35,3},{4,36},{36... | collective-permute-start | bytes 98312 | tf_op jit(solution)/shard_map/ppermute | solution.py:48

commit v12 on v11

--- a/solution.py
+++ b/solution.py
@@ -91,11 +91,11 @@
     return (((y + dy) % 4) * 8 + side * 4 + (x + dx) % 4) * BLOCK
 
 
-def send_kernel(w_in_ref, w_out_ref, b_ref, send_ref):
+def send_kernel(w_in_ref, w_out_ref, b_ref, in_ref, out_ref):
     other = (1 - lax.axis_index("l")) * HID
-    send_ref[:TOK] = w_in_ref[:, lanes(other, HID)]
-    send_ref[TOK : 2 * TOK] = w_out_ref[lanes(other, HID), :].T
-    send_ref[2 * TOK :] = b_ref[:, lanes(other, HID)]
+    in_ref[...] = w_in_ref[:, lanes(other, HID)]
+    out_ref[:TOK] = w_out_ref[lanes(other, HID), :].T
+    out_ref[TOK:] = b_ref[:, lanes(other, HID)]
 
 
 def own_kernel(w_in_ref, w_out_ref, b_ref, send_ref, in_ref, out_ref, b_own_ref):
@@ -300,15 +300,18 @@
     a = factor_down[0]
     b = factor_up[0]
 
-    w_send = call(send_kernel, shape(2 * TOK + RANK, HID), w_in, w_out, b, name="send")
-    w_oth = partner(w_send, "l")
+    in_send, out_send = call(
+        send_kernel, (shape(TOK, HID), shape(TOK + RANK, HID)), w_in, w_out, b, name="send"
+    )
+    in_oth = partner(in_send, "l")
+    out_oth = partner(out_send, "l")
     in_own, out_own, b_own = call(
         own_kernel,
         (shape(TOK, HID), shape(TOK, HID), shape(RANK, HID)),
-        w_in, w_out, b, w_send,
+        w_in, w_out, b, in_send,
         name="own",
     )
-    b_oth = w_oth[2 * TOK :]
+    b_oth = out_oth[TOK:]
     packed, p_own = call(
         pack_kernel,
         (shape(HALF + RANK, MODEL_WIDTH), shape(RANK, TOK)),
@@ -324,8 +327,8 @@
             l == 0, jnp.concatenate([own, oth], axis=0), jnp.concatenate([oth, own], axis=0)
         )
 
-    in_line = jnp.concatenate(ring(joined(in_own, w_oth[:TOK]), "x"), axis=0)
-    out_line = jnp.concatenate(ring(joined(out_own, w_oth[TOK : 2 * TOK]), "y"), axis=0)
+    in_line = jnp.concatenate(ring(joined(in_own, in_oth), "x"), axis=0)
+    out_line = jnp.concatenate(ring(joined(out_own, out_oth[:TOK]), "y"), axis=0)
     in_near = [in_line, shift(in_line, "y", 1), shift(in_line, "y", -1)]
     out_near = [out_line, shift(out_line, "x", 1), shift(out_line, "x", -1)]
 

time: 175 us -> 172 us (0.983)
  waiting for transfers between devices: 94.4 us -> 90.7 us
    ppermute x20, waiting for transfers between devices: 39.8 us -> 37.5 us  [shift(): return lax.ppermute(value, axis, [(i, (i + by) % n) for i in range(n)])]
    ppermute x11 -> x12, waiting for transfers between devices: 36.3 us -> 34.1 us  [partner(): return lax.ppermute(value, axis, [(0, 1), (1, 0)])]
    ppermute x11 -> x12, starting transfers between devices: 5.27 us -> 6.12 us  [partner(): return lax.ppermute(value, axis, [(0, 1), (1, 0)])]
  transfers between devices with their start and end apart: 38 -> 39, of which waited for: 26 -> 26; matrix products, arithmetic and copies ran while one was open for 1% -> 1% of each run, Pallas kernels for 2% -> 2%
where the time goes in v12:
time: 172 us; the launch traced here: 171 us
  waiting for transfers between devices  90.7 us (53%)
  starting transfers between devices  66.9 us (39%)
  Pallas kernels  8.71 us (5%)
  local copies, waits for them, and re-layouts  2.92 us (2%)
    ppermute x20, waiting for transfers between devices, shift(): return lax.ppermute(value, axis, [(i, (i + by) % n) for i in range(n)])  37.5 us
    ppermute x12, waiting for transfers between devices, partner(): return lax.ppermute(value, axis, [(0, 1), (1, 0)])  34.1 us
    ppermute x20, starting transfers between devices, shift(): return lax.ppermute(value, axis, [(i, (i + by) % n) for i in range(n)])  33.9 us
    ppermute x3, starting transfers between devices, near_z(): lax.ppermute(value, Z, [(place(z), place(z + 1 if z % 2 else z - 1)) for...  14 us
    ppermute x3, waiting for transfers between devices, near_z(): lax.ppermute(value, Z, [(place(z), place(z + 1 if z % 2 else z - 1)) for...  11.6 us
    pallas_call x12, Pallas kernels, call(): pl.pallas_call(kernel, out_shape=out_shape, in_specs=[vmem] * len(args) +...  8.57 us
    ppermute x3, starting transfers between devices, swap(): return lax.ppermute(value, 'h', [(i, i ^ mask) for i in range(4)])  6.5 us
    all_to_all x1, starting transfers between devices, shards(): wires = lax.all_to_all(wire, REP, 0, 0, tiled=True)  6.33 us
  transfers between devices with their start and end apart: 39, of which 26 were waited for; matrix products, arithmetic and copies ran while one was open for 1% of the time, Pallas kernels for 2%

profile of v12, /device:TPU:2, one launch (start us, length us, event | category | flops | bytes accessed | tf_op | source)
XLA Modules:
  0.0 171.4 jit_solution(4993190098211912094)
XLA Ops:
  3.5 2.0 %collective-permute-start.2 = (bf16[128,512]{1,0:T(8,128)(2,1)S(1)}, bf16[128,512]{1,0:T(8,128)(2,1)S(1)}, u32[]{:S(2)}, u32[]{:S(2)}) collective-permute-start(bf16[128,512]{1,0:T(8,128)(2,1)S(1)} %get-tuple-element.36.send_ref), channel_id=1, source_target_pairs={{0,32},{32,0},{1,33},{33,1},{2,34},{34,2},{3,35},{35,3},{4,36},{36... | collective-permute-start | bytes 393224 | tf_op jit(solution)/shard_map/ppermute | solution.py:48
  5.7 4.2 %collective-permute-done.2 = bf16[128,512]{1,0:T(8,128)(2,1)S(1)} collective-permute-done((bf16[128,512]{1,0:T(8,128)(2,1)S(1)}, bf16[128,512]{1,0:T(8,128)(2,1)S(1)}, u32[]{:S(2)}, u32[]{:S(2)}) %collective-permute-start.2) | collective-permute-done | bytes 131104 | tf_op jit(solution)/shard_map/ppermute | solution.py:48
  10.0 1.6 collective-permute-start.3
  12.2 1.7 collective-permute-start.11
  14.4 2.1 %collective-permute-done.3 = bf16[256,512]{1,0:T(8,128)(2,1)S(1)} collective-permute-done((bf16[256,512]{1,0:T(8,128)(2,1)S(1)}, bf16[256,512]{1,0:T(8,128)(2,1)S(1)}, u32[]{:S(2)}, u32[]{:S(2)}) %collective-permute-start.3) | collective-permute-done | bytes 262176 | tf_op jit(solution)/shard_map/ppermute | solution.py:44
  16.5 1.8 %collective-permute-start.5 = (bf16[256,512]{1,0:T(8,128)(2,1)S(1)}, bf16[256,512]{1,0:T(8,128)(2,1)S(1)}, u32[]{:S(2)}, u32[]{:S(2)}) collective-permute-start(bf16[256,512]{1,0:T(8,128)(2,1)S(1)} %collective-permute-done.3), channel_id=1, source_target_pairs={{0,8},{8,16},{16,24},{24,0},{1,9},{9,17},{17,25},{25,1},{2,10},{10... | collective-permute-start | bytes 786440 | tf_op jit(solution)/shard_map/ppermute | solution.py:44
  18.3 3.0 %collective-permute-start.12 = (bf16[256,512]{1,0:T(8,128)(2,1)S(1)}, bf16[256,512]{1,0:T(8,128)(2,1)S(1)}, u32[]{:S(2)}, u32[]{:S(2)}) collective-permute-start(bf16[256,512]{1,0:T(8,128)(2,1)S(1)} %maximum_select_fusion.1), channel_id=1, source_target_pairs={{0,192},{64,0},{128,64},{192,128},{1,193},{65,1},{129,65},{193,129... | collective-permute-start | bytes 786440 | tf_op jit(solution)/shard_map/ppermute | solution.py:44
  21.7 6.2 %collective-permute-start = (bf16[80,4096]{1,0:T(8,128)(2,1)S(1)}, bf16[80,4096]{1,0:T(8,128)(2,1)S(1)}, u32[]{:S(2)}, u32[]{:S(2)}) collective-permute-start(bf16[80,4096]{1,0:T(8,128)(2,1)S(1)} %get-tuple-element.38), channel_id=1, source_target_pairs={{0,38},{32,2},{2,32},{34,4},{4,34},{36,6},{6,36},{38,0},{1,39},{33... | collective-permute-start | bytes 1966088 | tf_op jit(solution)/shard_map/ppermute | solution.py:55
  28.9 2.5 %collective-permute-start.7 = (bf16[1024,512]{1,0:T(8,128)(2,1)S(1)}, bf16[1024,512]{1,0:T(8,128)(2,1)S(1)}, u32[]{:S(2)}, u32[]{:S(2)}) collective-permute-start(bf16[1024,512]{1,0:T(8,128)(2,1)S(1)} %pad_maximum_fusion.refs_0_), channel_id=1, source_target_pairs={{0,192},{64,0},{128,64},{192,128},{1,193},{65,1},{129,65},{193,129... | collective-permute-start | bytes 3145736 | tf_op jit(solution)/shard_map/ppermute | solution.py:44
  31.5 1.3 collective-permute-start.14
  33.6 6.3 %collective-permute-done.oth_ref = bf16[80,4096]{1,0:T(8,128)(2,1)S(1)} collective-permute-done((bf16[80,4096]{1,0:T(8,128)(2,1)S(1)}, bf16[80,4096]{1,0:T(8,128)(2,1)S(1)}, u32[]{:S(2)}, u32[]{:S(2)}) %collective-permute-start) | collective-permute-done | bytes 655392 | tf_op jit(solution)/shard_map/ppermute | solution.py:55
  39.8 2.1 %collective-permute-done.1.oth_core_ref = bf16[80,4096]{1,0:T(8,128)(2,1)S(1)} collective-permute-done((bf16[80,4096]{1,0:T(8,128)(2,1)S(1)}, bf16[80,4096]{1,0:T(8,128)(2,1)S(1)}, u32[]{:S(2)}, u32[]{:S(2)}) %collective-permute-start.1) | collective-permute-done | bytes 655392 | tf_op jit(solution)/shard_map/ppermute | solution.py:48
  43.0 8.4 %collective-permute-done.6.refs_1_.below_ref = bf16[1024,512]{1,0:T(8,128)(2,1)S(1)} collective-permute-done((bf16[1024,512]{1,0:T(8,128)(2,1)S(1)}, bf16[1024,512]{1,0:T(8,128)(2,1)S(1)}, u32[]{:S(2)}, u32[]{:S(2)}) %collective-permute-start.6) | collective-permute-done | bytes 1048608 | tf_op jit(solution)/shard_map/ppermute | solution.py:44
  51.8 2.9 %collective-permute-start.10 = (bf16[512,512]{1,0:T(8,128)(2,1)S(1)}, bf16[512,512]{1,0:T(8,128)(2,1)S(1)}, u32[]{:S(2)}, u32[]{:S(2)}) collective-permute-start(bf16[512,512]{1,0:T(8,128)(2,1)S(1)} %get-tuple-element.50), channel_id=1, source_target_pairs={{0,192},{64,0},{128,64},{192,128},{1,193},{65,1},{129,65},{193,129... | collective-permute-start | bytes 1572872 | tf_op jit(solution)/shard_map/ppermute | solution.py:44
  54.8 1.3 collective-permute-start.16
  57.9 4.4 %collective-permute-done.10.high_ref = bf16[512,512]{1,0:T(8,128)(2,1)S(1)} collective-permute-done((bf16[512,512]{1,0:T(8,128)(2,1)S(1)}, bf16[512,512]{1,0:T(8,128)(2,1)S(1)}, u32[]{:S(2)}, u32[]{:S(2)}) %collective-permute-start.10) | collective-permute-done | bytes 524320 | tf_op jit(solution)/shard_map/ppermute | solution.py:44
  62.4 2.7 %collective-permute-done.9.low_ref = bf16[512,512]{1,0:T(8,128)(2,1)S(1)} collective-permute-done((bf16[512,512]{1,0:T(8,128)(2,1)S(1)}, bf16[512,512]{1,0:T(8,128)(2,1)S(1)}, u32[]{:S(2)}, u32[]{:S(2)}) %collective-permute-start.9) | collective-permute-done | bytes 524320 | tf_op jit(solution)/shard_map/ppermute | solution.py:44
  65.6 1.3 output.1
  67.0 2.6 %collective-permute-done.18 = bf16[8,16,4096]{2,1,0:T(8,128)(2,1)S(1)} collective-permute-done((bf16[8,16,4096]{2,1,0:T(8,128)(2,1)S(1)}, bf16[8,16,4096]{2,1,0:T(8,128)(2,1)S(1)}, u32[]{:S(2)}, u32[]{:S(2)}) %collective-permute-start.18) | collective-permute-done | bytes 1048608 | tf_op jit(solution)/shard_map/ppermute | solution.py:48
  70.0 1.4 collective-permute-start.19
  71.5 4.8 %collective-permute-start.20 = (bf16[4,16,2048]{2,1,0:T(8,128)(2,1)S(1)}, bf16[4,16,2048]{2,1,0:T(8,128)(2,1)S(1)}, u32[]{:S(2)}, u32[]{:S(2)}) collective-permute-start(bf16[4,16,2048]{2,1,0:T(8,128)(2,1)S(1)} %get-tuple-element.71), channel_id=1, source_target_pairs={{0,38},{32,2},{2,32},{34,4},{4,34},{36,6},{6,36},{38,0},{1,39},{33... | collective-permute-start | bytes 786440 | tf_op jit(solution)/shard_map/ppermute | solution.py:55
  76.3 2.1 %collective-permute-done.19.left_ref = bf16[4,16,2048]{2,1,0:T(8,128)(2,1)S(1)} collective-permute-done((bf16[4,16,2048]{2,1,0:T(8,128)(2,1)S(1)}, bf16[4,16,2048]{2,1,0:T(8,128)(2,1)S(1)}, u32[]{:S(2)}, u32[]{:S(2)}) %collective-permute-start.19) | collective-permute-done | bytes 262176 | tf_op jit(solution)/shard_map/ppermute | solution.py:48
  78.5 4.1 %collective-permute-done.20.right_ref = bf16[4,16,2048]{2,1,0:T(8,128)(2,1)S(1)} collective-permute-done((bf16[4,16,2048]{2,1,0:T(8,128)(2,1)S(1)}, bf16[4,16,2048]{2,1,0:T(8,128)(2,1)S(1)}, u32[]{:S(2)}, u32[]{:S(2)}) %collective-permute-start.20) | collective-permute-done | bytes 262176 | tf_op jit(solution)/shard_map/ppermute | solution.py:55
  83.2 4.0 %collective-permute-start.22 = (bf16[16,4096]{1,0:T(8,128)(2,1)S(1)}, bf16[16,4096]{1,0:T(8,128)(2,1)S(1)}, u32[]{:S(2)}, u32[]{:S(2)}) collective-permute-start(bf16[16,4096]{1,0:T(8,128)(2,1)S(1)} %get-tuple-element.59), channel_id=1, source_target_pairs={{0,4},{2,6},{4,0},{6,2},{1,5},{3,7},{5,1},{7,3},{8,12},{10,14},{12... | collective-permute-start | bytes 393224 | tf_op jit(solution)/shard_map/ppermute | solution.py:44
  87.2 4.0 %collective-permute-start.23 = (bf16[16,4096]{1,0:T(8,128)(2,1)S(1)}, bf16[16,4096]{1,0:T(8,128)(2,1)S(1)}, u32[]{:S(2)}, u32[]{:S(2)}) collective-permute-start(bf16[16,4096]{1,0:T(8,128)(2,1)S(1)} %get-tuple-element.60), channel_id=1, source_target_pairs={{0,6},{2,0},{4,2},{6,4},{1,7},{3,1},{5,3},{7,5},{8,14},{10,8},{12,... | collective-permute-start | bytes 393224 | tf_op jit(solution)/shard_map/ppermute | solution.py:44
  91.3 5.1 %collective-permute-done.21 = bf16[16,4096]{1,0:T(8,128)(2,1)S(1)} collective-permute-done((bf16[16,4096]{1,0:T(8,128)(2,1)S(1)}, bf16[16,4096]{1,0:T(8,128)(2,1)S(1)}, u32[]{:S(2)}, u32[]{:S(2)}) %collective-permute-start.21) | collective-permute-done | bytes 131104 | tf_op jit(solution)/shard_map/ppermute | solution.py:44
  96.4 3.5 %collective-permute-done.23 = bf16[16,4096]{1,0:T(8,128)(2,1)S(1)} collective-permute-done((bf16[16,4096]{1,0:T(8,128)(2,1)S(1)}, bf16[16,4096]{1,0:T(8,128)(2,1)S(1)}, u32[]{:S(2)}, u32[]{:S(2)}) %collective-permute-start.23) | collective-permute-done | bytes 131104 | tf_op jit(solution)/shard_map/ppermute | solution.py:44
  100.0 3.9 %collective-permute-start.24 = (bf16[16,4096]{1,0:T(8,128)(2,1)S(1)}, bf16[16,4096]{1,0:T(8,128)(2,1)S(1)}, u32[]{:S(2)}, u32[]{:S(2)}) collective-permute-start(bf16[16,4096]{1,0:T(8,128)(2,1)S(1)} %multiply_convert_fusion), channel_id=1, source_target_pairs={{0,6},{2,0},{4,2},{6,4},{1,7},{3,1},{5,3},{7,5},{8,14},{10,8},{12,... | collective-permute-start | bytes 393224 | tf_op jit(solution)/shard_map/ppermute | solution.py:44
  103.9 2.0 %collective-permute-start.25 = (bf16[16,4096]{1,0:T(8,128)(2,1)S(1)}, bf16[16,4096]{1,0:T(8,128)(2,1)S(1)}, u32[]{:S(2)}, u32[]{:S(2)}) collective-permute-start(bf16[16,4096]{1,0:T(8,128)(2,1)S(1)} %multiply_convert_fusion), channel_id=1, source_target_pairs={{0,4},{2,6},{4,0},{6,2},{1,5},{3,7},{5,1},{7,3},{8,12},{10,14},{12... | collective-permute-start | bytes 393224 | tf_op jit(solution)/shard_map/ppermute | solution.py:44
  106.4 5.2 %collective-permute-done.24 = bf16[16,4096]{1,0:T(8,128)(2,1)S(1)} collective-permute-done((bf16[16,4096]{1,0:T(8,128)(2,1)S(1)}, bf16[16,4096]{1,0:T(8,128)(2,1)S(1)}, u32[]{:S(2)}, u32[]{:S(2)}) %collective-permute-start.24) | collective-permute-done | bytes 131104 | tf_op jit(solution)/shard_map/ppermute | solution.py:44
  111.6 5.5 %collective-permute-done.25 = bf16[16,4096]{1,0:T(8,128)(2,1)S(1)} collective-permute-done((bf16[16,4096]{1,0:T(8,128)(2,1)S(1)}, bf16[16,4096]{1,0:T(8,128)(2,1)S(1)}, u32[]{:S(2)}, u32[]{:S(2)}) %collective-permute-start.25) | collective-permute-done | bytes 131104 | tf_op jit(solution)/shard_map/ppermute | solution.py:44
  117.4 3.0 %collective-permute-start.30 = (bf16[4,16,2048]{2,1,0:T(8,128)(2,1)S(1)}, bf16[4,16,2048]{2,1,0:T(8,128)(2,1)S(1)}, u32[]{:S(2)}, u32[]{:S(2)}) collective-permute-start(bf16[4,16,2048]{2,1,0:T(8,128)(2,1)S(1)} %get-tuple-element.73), channel_id=1, source_target_pairs={{0,38},{32,2},{2,32},{34,4},{4,34},{36,6},{6,36},{38,0},{1,39},{33... | collective-permute-start | bytes 786440 | tf_op jit(solution)/shard_map/ppermute | solution.py:55
  120.4 5.6 %collective-permute-done.28.left_ref = bf16[4,16,2048]{2,1,0:T(8,128)(2,1)S(1)} collective-permute-done((bf16[4,16,2048]{2,1,0:T(8,128)(2,1)S(1)}, bf16[4,16,2048]{2,1,0:T(8,128)(2,1)S(1)}, u32[]{:S(2)}, u32[]{:S(2)}) %collective-permute-start.28) | collective-permute-done | bytes 262176 | tf_op jit(solution)/shard_map/ppermute | solution.py:48
  126.0 1.2 collective-permute-done.30.right_ref
  127.6 1.2 collective-permute-done.31.rightc_ref
  128.8 1.5 backward.1
  130.5 1.0 collective-permute-done.32
  132.1 3.1 %collective-permute-done.33 = f32[16,128]{1,0:T(8,128)S(1)} collective-permute-done((f32[16,128]{1,0:T(8,128)S(1)}, f32[16,128]{1,0:T(8,128)S(1)}, u32[]{:S(2)}, u32[]{:S(2)}) %collective-permute-start.33) | collective-permute-done | bytes 8224 | tf_op jit(solution)/shard_map/ppermute | solution.py:48
  135.2 1.8 %collective-permute-start.34 = (f32[16,128]{1,0:T(8,128)S(1)}, f32[16,128]{1,0:T(8,128)S(1)}, u32[]{:S(2)}, u32[]{:S(2)}) collective-permute-start(f32[16,128]{1,0:T(8,128)S(1)} %fusion.t0_ref), channel_id=1, source_target_pairs={{0,2},{2,0},{4,6},{6,4},{1,3},{3,1},{5,7},{7,5},{8,10},{10,8},{12,... | collective-permute-start | bytes 24584 | tf_op jit(solution)/shard_map/ppermute | solution.py:295
  136.9 3.9 %collective-permute-start.35 = (f32[16,128]{1,0:T(8,128)S(1)}, f32[16,128]{1,0:T(8,128)S(1)}, u32[]{:S(2)}, u32[]{:S(2)}) collective-permute-start(f32[16,128]{1,0:T(8,128)S(1)} %fusion.t0_ref), channel_id=1, source_target_pairs={{0,4},{2,6},{4,0},{6,2},{1,5},{3,7},{5,1},{7,3},{8,12},{10,14},{12... | collective-permute-start | bytes 24584 | tf_op jit(solution)/shard_map/ppermute | solution.py:295
  141.7 2.8 %collective-permute-done.35.t2_ref = f32[16,128]{1,0:T(8,128)S(1)} collective-permute-done((f32[16,128]{1,0:T(8,128)S(1)}, f32[16,128]{1,0:T(8,128)S(1)}, u32[]{:S(2)}, u32[]{:S(2)}) %collective-permute-start.35) | collective-permute-done | bytes 8224 | tf_op jit(solution)/shard_map/ppermute | solution.py:295
  144.5 2.1 %collective-permute-done.36.t3_ref = f32[16,128]{1,0:T(8,128)S(1)} collective-permute-done((f32[16,128]{1,0:T(8,128)S(1)}, f32[16,128]{1,0:T(8,128)S(1)}, u32[]{:S(2)}, u32[]{:S(2)}) %collective-permute-start.36) | collective-permute-done | bytes 8224 | tf_op jit(solution)/shard_map/ppermute | solution.py:295
  146.5 1.4 down.1
  148.0 6.3 %all-to-all-start = ((bf16[32,16,1152]{2,1,0:T(8,128)(2,1)}), bf16[32,16,1152]{2,1,0:T(8,128)(2,1)S(1)}, u32[]{:S(2)}, u32[]{:S(2)}) async-start(bf16[32,16,1152]{2,1,0:T(8,128)(2,1)} %get-tuple-element.65), calls=%async_computation | async-start | bytes 2359296 | tf_op jit(solution)/shard_map/all_to_all | solution.py:416
  154.3 1.6 collective-permute-start.37
  155.9 11.1 %collective-permute-done.37 = f32[16,512]{1,0:T(8,128)S(1)} collective-permute-done((f32[16,512]{1,0:T(8,128)S(1)}, f32[16,512]{1,0:T(8,128)S(1)}, u32[]{:S(2)}, u32[]{:S(2)}) %collective-permute-start.37) | collective-permute-done | bytes 32800 | tf_op jit(solution)/shard_map/ppermute | solution.py:48
  167.6 2.7 %all-to-all-done.wire_ref = bf16[32,16,1152]{2,1,0:T(8,128)(2,1)S(1)} async-done(((bf16[32,16,1152]{2,1,0:T(8,128)(2,1)}), bf16[32,16,1152]{2,1,0:T(8,128)(2,1)S(1)}, u32[]{:S(2)}, u32[]{:S(2)}) %all-to-all-start) | async-done | bytes 1179680 | tf_op jit(solution)/shard_map/all_to_all | solution.py:416
  170.3 1.1 merge.1
  (74 shorter events, 15.0 us)
Async XLA Ops:
  0.6 20.7 %copy-start = (bf16[128,4096]{1,0:T(8,128)(2,1)S(1)}, bf16[128,4096]{1,0:T(8,128)(2,1)}, u32[]{:S(2)}) copy-start(bf16[128,4096]{1,0:T(8,128)(2,1)} %x_ref.1) | copy-start | bytes 3145732
  0.6 1.0 copy-start.1
  1.7 0.9 copy-start.4
  2.6 0.8 copy-start.6
  3.4 18.0 %copy-start.5 = (bf16[1,16,4096]{2,1,0:T(8,128)(2,1)S(1)}, bf16[1,16,4096]{2,1,0:T(8,128)(2,1)}, u32[]{:S(2)}) copy-start(bf16[1,16,4096]{2,1,0:T(8,128)(2,1)} %param.10) | copy-start | bytes 393220
  3.5 6.5 %collective-permute-start.2 = (bf16[128,512]{1,0:T(8,128)(2,1)S(1)}, bf16[128,512]{1,0:T(8,128)(2,1)S(1)}, u32[]{:S(2)}, u32[]{:S(2)}) collective-permute-start(bf16[128,512]{1,0:T(8,128)(2,1)S(1)} %get-tuple-element.36.send_ref), channel_id=1, source_target_pairs={{0,32},{32,0},{1,33},{33,1},{2,34},{34,2},{3,35},{35,3},{4,36},{36... | collective-permute-start | bytes 393224 | tf_op jit(solution)/shard_map/ppermute | solution.py:48
  5.5 6.7 %collective-permute-start.8 = (bf16[144,512]{1,0:T(8,128)(2,1)S(1)}, bf16[144,512]{1,0:T(8,128)(2,1)S(1)}, u32[]{:S(2)}, u32[]{:S(2)}) collective-permute-start(bf16[144,512]{1,0:T(8,128)(2,1)S(1)} %get-tuple-element.46), channel_id=1, source_target_pairs={{0,32},{32,0},{1,33},{33,1},{2,34},{34,2},{3,35},{35,3},{4,36},{36... | collective-permute-start | bytes 442376 | tf_op jit(solution)/shard_map/ppermute | solution.py:48
  10.0 6.5 %collective-permute-start.3 = (bf16[256,512]{1,0:T(8,128)(2,1)S(1)}, bf16[256,512]{1,0:T(8,128)(2,1)S(1)}, u32[]{:S(2)}, u32[]{:S(2)}) collective-permute-start(bf16[256,512]{1,0:T(8,128)(2,1)S(1)} %maximum_select_fusion), channel_id=1, source_target_pairs={{0,8},{8,16},{16,24},{24,0},{1,9},{9,17},{17,25},{25,1},{2,10},{10... | collective-permute-start | bytes 786440 | tf_op jit(solution)/shard_map/ppermute | solution.py:44
  12.2 9.1 %collective-permute-start.11 = (bf16[256,512]{1,0:T(8,128)(2,1)S(1)}, bf16[256,512]{1,0:T(8,128)(2,1)S(1)}, u32[]{:S(2)}, u32[]{:S(2)}) collective-permute-start(bf16[256,512]{1,0:T(8,128)(2,1)S(1)} %maximum_select_fusion.1), channel_id=1, source_target_pairs={{0,64},{64,128},{128,192},{192,0},{1,65},{65,129},{129,193},{193,1... | collective-permute-start | bytes 786440 | tf_op jit(solution)/shard_map/ppermute | solution.py:44
  13.9 14.0 %collective-permute-start.4 = (bf16[256,512]{1,0:T(8,128)(2,1)S(1)}, bf16[256,512]{1,0:T(8,128)(2,1)S(1)}, u32[]{:S(2)}, u32[]{:S(2)}) collective-permute-start(bf16[256,512]{1,0:T(8,128)(2,1)S(1)} %maximum_select_fusion), channel_id=1, source_target_pairs={{0,24},{8,0},{16,8},{24,16},{1,25},{9,1},{17,9},{25,17},{2,26},{10... | collective-permute-start | bytes 786440 | tf_op jit(solution)/shard_map/ppermute | solution.py:44
  16.5 11.4 %collective-permute-start.5 = (bf16[256,512]{1,0:T(8,128)(2,1)S(1)}, bf16[256,512]{1,0:T(8,128)(2,1)S(1)}, u32[]{:S(2)}, u32[]{:S(2)}) collective-permute-start(bf16[256,512]{1,0:T(8,128)(2,1)S(1)} %collective-permute-done.3), channel_id=1, source_target_pairs={{0,8},{8,16},{16,24},{24,0},{1,9},{9,17},{17,25},{25,1},{2,10},{10... | collective-permute-start | bytes 786440 | tf_op jit(solution)/shard_map/ppermute | solution.py:44
  18.3 13.1 %collective-permute-start.12 = (bf16[256,512]{1,0:T(8,128)(2,1)S(1)}, bf16[256,512]{1,0:T(8,128)(2,1)S(1)}, u32[]{:S(2)}, u32[]{:S(2)}) collective-permute-start(bf16[256,512]{1,0:T(8,128)(2,1)S(1)} %maximum_select_fusion.1), channel_id=1, source_target_pairs={{0,192},{64,0},{128,64},{192,128},{1,193},{65,1},{129,65},{193,129... | collective-permute-start | bytes 786440 | tf_op jit(solution)/shard_map/ppermute | solution.py:44
  21.3 10.1 %collective-permute-start.13 = (bf16[256,512]{1,0:T(8,128)(2,1)S(1)}, bf16[256,512]{1,0:T(8,128)(2,1)S(1)}, u32[]{:S(2)}, u32[]{:S(2)}) collective-permute-start(bf16[256,512]{1,0:T(8,128)(2,1)S(1)} %collective-permute-done.11), channel_id=1, source_target_pairs={{0,64},{64,128},{128,192},{192,0},{1,65},{65,129},{129,193},{193,1... | collective-permute-start | bytes 786440 | tf_op jit(solution)/shard_map/ppermute | solution.py:44
  21.7 18.1 %collective-permute-start = (bf16[80,4096]{1,0:T(8,128)(2,1)S(1)}, bf16[80,4096]{1,0:T(8,128)(2,1)S(1)}, u32[]{:S(2)}, u32[]{:S(2)}) collective-permute-start(bf16[80,4096]{1,0:T(8,128)(2,1)S(1)} %get-tuple-element.38), channel_id=1, source_target_pairs={{0,38},{32,2},{2,32},{34,4},{4,34},{36,6},{6,36},{38,0},{1,39},{33... | collective-permute-start | bytes 1966088 | tf_op jit(solution)/shard_map/ppermute | solution.py:55
  28.0 23.4 %collective-permute-start.6 = (bf16[1024,512]{1,0:T(8,128)(2,1)S(1)}, bf16[1024,512]{1,0:T(8,128)(2,1)S(1)}, u32[]{:S(2)}, u32[]{:S(2)}) collective-permute-start(bf16[1024,512]{1,0:T(8,128)(2,1)S(1)} %pad_maximum_fusion.refs_0_), channel_id=1, source_target_pairs={{0,64},{64,128},{128,192},{192,0},{1,65},{65,129},{129,193},{193,1... | collective-permute-start | bytes 3145736 | tf_op jit(solution)/shard_map/ppermute | solution.py:44
  28.9 22.9 %collective-permute-start.7 = (bf16[1024,512]{1,0:T(8,128)(2,1)S(1)}, bf16[1024,512]{1,0:T(8,128)(2,1)S(1)}, u32[]{:S(2)}, u32[]{:S(2)}) collective-permute-start(bf16[1024,512]{1,0:T(8,128)(2,1)S(1)} %pad_maximum_fusion.refs_0_), channel_id=1, source_target_pairs={{0,192},{64,0},{128,64},{192,128},{1,193},{65,1},{129,65},{193,129... | collective-permute-start | bytes 3145736 | tf_op jit(solution)/shard_map/ppermute | solution.py:44
  31.5 23.3 %collective-permute-start.14 = (bf16[1024,512]{1,0:T(8,128)(2,1)S(1)}, bf16[1024,512]{1,0:T(8,128)(2,1)S(1)}, u32[]{:S(2)}, u32[]{:S(2)}) collective-permute-start(bf16[1024,512]{1,0:T(8,128)(2,1)S(1)} %pad_maximum_fusion.1.refs_0_), channel_id=1, source_target_pairs={{0,8},{8,16},{16,24},{24,0},{1,9},{9,17},{17,25},{25,1},{2,10},{10... | collective-permute-start | bytes 3145736 | tf_op jit(solution)/shard_map/ppermute | solution.py:44
  32.7 22.0 %collective-permute-start.15 = (bf16[1024,512]{1,0:T(8,128)(2,1)S(1)}, bf16[1024,512]{1,0:T(8,128)(2,1)S(1)}, u32[]{:S(2)}, u32[]{:S(2)}) collective-permute-start(bf16[1024,512]{1,0:T(8,128)(2,1)S(1)} %pad_maximum_fusion.1.refs_0_), channel_id=1, source_target_pairs={{0,24},{8,0},{16,8},{24,16},{1,25},{9,1},{17,9},{25,17},{2,26},{10... | collective-permute-start | bytes 3145736 | tf_op jit(solution)/shard_map/ppermute | solution.py:44
  39.8 2.1 %collective-permute-start.1 = (bf16[80,4096]{1,0:T(8,128)(2,1)S(1)}, bf16[80,4096]{1,0:T(8,128)(2,1)S(1)}, u32[]{:S(2)}, u32[]{:S(2)}) collective-permute-start(bf16[80,4096]{1,0:T(8,128)(2,1)S(1)} %collective-permute-done.oth_ref), channel_id=1, source_target_pairs={{0,1},{1,0},{2,3},{3,2},{4,5},{5,4},{6,7},{7,6},{8,9},{9,8},{10,11... | collective-permute-start | bytes 1966088 | tf_op jit(solution)/shard_map/ppermute | solution.py:48
  51.8 10.5 %collective-permute-start.10 = (bf16[512,512]{1,0:T(8,128)(2,1)S(1)}, bf16[512,512]{1,0:T(8,128)(2,1)S(1)}, u32[]{:S(2)}, u32[]{:S(2)}) collective-permute-start(bf16[512,512]{1,0:T(8,128)(2,1)S(1)} %get-tuple-element.50), channel_id=1, source_target_pairs={{0,192},{64,0},{128,64},{192,128},{1,193},{65,1},{129,65},{193,129... | collective-permute-start | bytes 1572872 | tf_op jit(solution)/shard_map/ppermute | solution.py:44
  54.7 10.4 %collective-permute-start.9 = (bf16[512,512]{1,0:T(8,128)(2,1)S(1)}, bf16[512,512]{1,0:T(8,128)(2,1)S(1)}, u32[]{:S(2)}, u32[]{:S(2)}) collective-permute-start(bf16[512,512]{1,0:T(8,128)(2,1)S(1)} %get-tuple-element.49), channel_id=1, source_target_pairs={{0,64},{64,128},{128,192},{192,0},{1,65},{65,129},{129,193},{193,1... | collective-permute-start | bytes 1572872 | tf_op jit(solution)/shard_map/ppermute | solution.py:44
  54.8 10.8 %collective-permute-start.16 = (bf16[512,512]{1,0:T(8,128)(2,1)S(1)}, bf16[512,512]{1,0:T(8,128)(2,1)S(1)}, u32[]{:S(2)}, u32[]{:S(2)}) collective-permute-start(bf16[512,512]{1,0:T(8,128)(2,1)S(1)} %get-tuple-element.53), channel_id=1, source_target_pairs={{0,8},{8,16},{16,24},{24,0},{1,9},{9,17},{17,25},{25,1},{2,10},{10... | collective-permute-start | bytes 1572872 | tf_op jit(solution)/shard_map/ppermute | solution.py:44
  56.1 9.5 %collective-permute-start.17 = (bf16[512,512]{1,0:T(8,128)(2,1)S(1)}, bf16[512,512]{1,0:T(8,128)(2,1)S(1)}, u32[]{:S(2)}, u32[]{:S(2)}) collective-permute-start(bf16[512,512]{1,0:T(8,128)(2,1)S(1)} %get-tuple-element.54), channel_id=1, source_target_pairs={{0,24},{8,0},{16,8},{24,16},{1,25},{9,1},{17,9},{25,17},{2,26},{10... | collective-permute-start | bytes 1572872 | tf_op jit(solution)/shard_map/ppermute | solution.py:44
  66.9 2.7 %collective-permute-start.18 = (bf16[8,16,4096]{2,1,0:T(8,128)(2,1)S(1)}, bf16[8,16,4096]{2,1,0:T(8,128)(2,1)S(1)}, u32[]{:S(2)}, u32[]{:S(2)}) collective-permute-start(bf16[8,16,4096]{2,1,0:T(8,128)(2,1)S(1)} %get-tuple-element.56), channel_id=1, source_target_pairs={{0,1},{1,0},{2,3},{3,2},{4,5},{5,4},{6,7},{7,6},{8,9},{9,8},{10,11... | collective-permute-start | bytes 3145736 | tf_op jit(solution)/shard_map/ppermute | solution.py:48
  70.0 21.2 %copy-start.3 = (bf16[128,4096]{1,0:T(8,128)(2,1)S(1)}, bf16[128,4096]{1,0:T(8,128)(2,1)}, u32[]{:S(2)}) copy-start(bf16[128,4096]{1,0:T(8,128)(2,1)} %targets_ref.1) | copy-start | bytes 3145732
  70.0 8.4 %collective-permute-start.19 = (bf16[4,16,2048]{2,1,0:T(8,128)(2,1)S(1)}, bf16[4,16,2048]{2,1,0:T(8,128)(2,1)S(1)}, u32[]{:S(2)}, u32[]{:S(2)}) collective-permute-start(bf16[4,16,2048]{2,1,0:T(8,128)(2,1)S(1)} %get-tuple-element.72), channel_id=1, source_target_pairs={{0,32},{32,0},{1,33},{33,1},{2,34},{34,2},{3,35},{35,3},{4,36},{36... | collective-permute-start | bytes 786440 | tf_op jit(solution)/shard_map/ppermute | solution.py:48
  71.5 11.1 %collective-permute-start.20 = (bf16[4,16,2048]{2,1,0:T(8,128)(2,1)S(1)}, bf16[4,16,2048]{2,1,0:T(8,128)(2,1)S(1)}, u32[]{:S(2)}, u32[]{:S(2)}) collective-permute-start(bf16[4,16,2048]{2,1,0:T(8,128)(2,1)S(1)} %get-tuple-element.71), channel_id=1, source_target_pairs={{0,38},{32,2},{2,32},{34,4},{4,34},{36,6},{6,36},{38,0},{1,39},{33... | collective-permute-start | bytes 786440 | tf_op jit(solution)/shard_map/ppermute | solution.py:55
  82.7 13.7 %collective-permute-start.21 = (bf16[16,4096]{1,0:T(8,128)(2,1)S(1)}, bf16[16,4096]{1,0:T(8,128)(2,1)S(1)}, u32[]{:S(2)}, u32[]{:S(2)}) collective-permute-start(bf16[16,4096]{1,0:T(8,128)(2,1)S(1)} %get-tuple-element.58), channel_id=1, source_target_pairs={{0,2},{2,4},{4,6},{6,0},{1,3},{3,5},{5,7},{7,1},{8,10},{10,12},{12... | collective-permute-start | bytes 393224 | tf_op jit(solution)/shard_map/ppermute | solution.py:44
  83.2 13.2 %collective-permute-start.22 = (bf16[16,4096]{1,0:T(8,128)(2,1)S(1)}, bf16[16,4096]{1,0:T(8,128)(2,1)S(1)}, u32[]{:S(2)}, u32[]{:S(2)}) collective-permute-start(bf16[16,4096]{1,0:T(8,128)(2,1)S(1)} %get-tuple-element.59), channel_id=1, source_target_pairs={{0,4},{2,6},{4,0},{6,2},{1,5},{3,7},{5,1},{7,3},{8,12},{10,14},{12... | collective-permute-start | bytes 393224 | tf_op jit(solution)/shard_map/ppermute | solution.py:44
  87.2 12.7 %collective-permute-start.23 = (bf16[16,4096]{1,0:T(8,128)(2,1)S(1)}, bf16[16,4096]{1,0:T(8,128)(2,1)S(1)}, u32[]{:S(2)}, u32[]{:S(2)}) collective-permute-start(bf16[16,4096]{1,0:T(8,128)(2,1)S(1)} %get-tuple-element.60), channel_id=1, source_target_pairs={{0,6},{2,0},{4,2},{6,4},{1,7},{3,1},{5,3},{7,5},{8,14},{10,8},{12,... | collective-permute-start | bytes 393224 | tf_op jit(solution)/shard_map/ppermute | solution.py:44
  100.0 11.6 %collective-permute-start.24 = (bf16[16,4096]{1,0:T(8,128)(2,1)S(1)}, bf16[16,4096]{1,0:T(8,128)(2,1)S(1)}, u32[]{:S(2)}, u32[]{:S(2)}) collective-permute-start(bf16[16,4096]{1,0:T(8,128)(2,1)S(1)} %multiply_convert_fusion), channel_id=1, source_target_pairs={{0,6},{2,0},{4,2},{6,4},{1,7},{3,1},{5,3},{7,5},{8,14},{10,8},{12,... | collective-permute-start | bytes 393224 | tf_op jit(solution)/shard_map/ppermute | solution.py:44
  103.9 13.2 %collective-permute-start.25 = (bf16[16,4096]{1,0:T(8,128)(2,1)S(1)}, bf16[16,4096]{1,0:T(8,128)(2,1)S(1)}, u32[]{:S(2)}, u32[]{:S(2)}) collective-permute-start(bf16[16,4096]{1,0:T(8,128)(2,1)S(1)} %multiply_convert_fusion), channel_id=1, source_target_pairs={{0,4},{2,6},{4,0},{6,2},{1,5},{3,7},{5,1},{7,3},{8,12},{10,14},{12... | collective-permute-start | bytes 393224 | tf_op jit(solution)/shard_map/ppermute | solution.py:44
  105.9 11.2 %collective-permute-start.26 = (bf16[16,4096]{1,0:T(8,128)(2,1)S(1)}, bf16[16,4096]{1,0:T(8,128)(2,1)S(1)}, u32[]{:S(2)}, u32[]{:S(2)}) collective-permute-start(bf16[16,4096]{1,0:T(8,128)(2,1)S(1)} %multiply_convert_fusion), channel_id=1, source_target_pairs={{0,2},{2,4},{4,6},{6,0},{1,3},{3,5},{5,7},{7,1},{8,10},{10,12},{12... | collective-permute-start | bytes 393224 | tf_op jit(solution)/shard_map/ppermute | solution.py:44
  117.2 10.0 %collective-permute-start.27 = (bf16[4,16,4096]{2,1,0:T(8,128)(2,1)S(1)}, bf16[4,16,4096]{2,1,0:T(8,128)(2,1)S(1)}, u32[]{:S(2)}, u32[]{:S(2)}) collective-permute-start(bf16[4,16,4096]{2,1,0:T(8,128)(2,1)S(1)} %pad_maximum_fusion.2.q_ref), channel_id=1, source_target_pairs={{0,1},{1,0},{2,3},{3,2},{4,5},{5,4},{6,7},{7,6},{8,9},{9,8},{10,11... | collective-permute-start | bytes 1572872 | tf_op jit(solution)/shard_map/ppermute | solution.py:48
  117.3 8.7 %collective-permute-start.28 = (bf16[4,16,2048]{2,1,0:T(8,128)(2,1)S(1)}, bf16[4,16,2048]{2,1,0:T(8,128)(2,1)S(1)}, u32[]{:S(2)}, u32[]{:S(2)}) collective-permute-start(bf16[4,16,2048]{2,1,0:T(8,128)(2,1)S(1)} %get-tuple-element.74), channel_id=1, source_target_pairs={{0,32},{32,0},{1,33},{33,1},{2,34},{34,2},{3,35},{35,3},{4,36},{36... | collective-permute-start | bytes 786440 | tf_op jit(solution)/shard_map/ppermute | solution.py:48
  117.4 9.8 %collective-permute-start.30 = (bf16[4,16,2048]{2,1,0:T(8,128)(2,1)S(1)}, bf16[4,16,2048]{2,1,0:T(8,128)(2,1)S(1)}, u32[]{:S(2)}, u32[]{:S(2)}) collective-permute-start(bf16[4,16,2048]{2,1,0:T(8,128)(2,1)S(1)} %get-tuple-element.73), channel_id=1, source_target_pairs={{0,38},{32,2},{2,32},{34,4},{4,34},{36,6},{6,36},{38,0},{1,39},{33... | collective-permute-start | bytes 786440 | tf_op jit(solution)/shard_map/ppermute | solution.py:55
  126.0 1.5 collective-permute-start.29
  127.2 1.5 collective-permute-start.31
  130.3 40.0 %copy-start.2 = (bf16[128,1024]{1,0:T(8,128)(2,1)S(1)}, bf16[128,1024]{1,0:T(8,128)(2,1)}, u32[]{:S(2)}) copy-start(bf16[128,1024]{1,0:T(8,128)(2,1)} %w_ref.1) | copy-start | bytes 786436
  130.3 1.2 collective-permute-start.32
  131.5 3.7 %collective-permute-start.33 = (f32[16,128]{1,0:T(8,128)S(1)}, f32[16,128]{1,0:T(8,128)S(1)}, u32[]{:S(2)}, u32[]{:S(2)}) collective-permute-start(f32[16,128]{1,0:T(8,128)S(1)} %slice_bitcast_fusion), channel_id=1, source_target_pairs={{0,32},{32,0},{1,33},{33,1},{2,34},{34,2},{3,35},{35,3},{4,36},{36... | collective-permute-start | bytes 24584 | tf_op jit(solution)/shard_map/ppermute | solution.py:48
  135.2 6.5 %collective-permute-start.34 = (f32[16,128]{1,0:T(8,128)S(1)}, f32[16,128]{1,0:T(8,128)S(1)}, u32[]{:S(2)}, u32[]{:S(2)}) collective-permute-start(f32[16,128]{1,0:T(8,128)S(1)} %fusion.t0_ref), channel_id=1, source_target_pairs={{0,2},{2,0},{4,6},{6,4},{1,3},{3,1},{5,7},{7,5},{8,10},{10,8},{12,... | collective-permute-start | bytes 24584 | tf_op jit(solution)/shard_map/ppermute | solution.py:295
  136.9 7.6 %collective-permute-start.35 = (f32[16,128]{1,0:T(8,128)S(1)}, f32[16,128]{1,0:T(8,128)S(1)}, u32[]{:S(2)}, u32[]{:S(2)}) collective-permute-start(f32[16,128]{1,0:T(8,128)S(1)} %fusion.t0_ref), channel_id=1, source_target_pairs={{0,4},{2,6},{4,0},{6,2},{1,5},{3,7},{5,1},{7,3},{8,12},{10,14},{12... | collective-permute-start | bytes 24584 | tf_op jit(solution)/shard_map/ppermute | solution.py:295
  140.8 5.8 %collective-permute-start.36 = (f32[16,128]{1,0:T(8,128)S(1)}, f32[16,128]{1,0:T(8,128)S(1)}, u32[]{:S(2)}, u32[]{:S(2)}) collective-permute-start(f32[16,128]{1,0:T(8,128)S(1)} %fusion.t0_ref), channel_id=1, source_target_pairs={{0,6},{2,4},{4,2},{6,0},{1,7},{3,5},{5,3},{7,1},{8,14},{10,12},{12... | collective-permute-start | bytes 24584 | tf_op jit(solution)/shard_map/ppermute | solution.py:295
  148.0 22.3 %all-to-all-start = ((bf16[32,16,1152]{2,1,0:T(8,128)(2,1)}), bf16[32,16,1152]{2,1,0:T(8,128)(2,1)S(1)}, u32[]{:S(2)}, u32[]{:S(2)}) async-start(bf16[32,16,1152]{2,1,0:T(8,128)(2,1)} %get-tuple-element.65), calls=%async_computation | async-start | bytes 2359296 | tf_op jit(solution)/shard_map/all_to_all | solution.py:416
  154.3 12.7 %collective-permute-start.37 = (f32[16,512]{1,0:T(8,128)S(1)}, f32[16,512]{1,0:T(8,128)S(1)}, u32[]{:S(2)}, u32[]{:S(2)}) collective-permute-start(f32[16,512]{1,0:T(8,128)S(1)} %get-tuple-element.68), channel_id=1, source_target_pairs={{0,32},{32,0},{1,33},{33,1},{2,34},{34,2},{3,35},{35,3},{4,36},{36... | collective-permute-start | bytes 98312 | tf_op jit(solution)/shard_map/ppermute | solution.py:48
